TPU v7x, 32 devices: a whole 2x2x4 slice. The times are simulated.
32 devices in a mesh: clip: 8 (over y, x, core), tm: 4 (over z).
Axes of the slice: x: 2, y: 2, z: 4, core: 2. Of those that a mesh axis runs over, the one named last changes fastest.
Arguments:
- latent: bfloat16 [8, 32, 8, 32, 16], P('clip', 'tm'), may hold values from -6 to 6
- offsets: int32 [8], P('clip'), may hold values from 0 to 16
- teacher: bfloat16 [8, 32, 8, 16, 384], P('clip', 'tm'), may hold values from -6 to 6
- w_in: bfloat16 [432, 384], replicated, may hold values from -0.3125 to 0.3125
- w_mid: bfloat16 [10368, 384], P('clip'), may hold values from -0.0625 to 0.0625
Outputs:
- grad_mid: float32 [10368, 384], P('clip')
- grad_in: float32 [432, 384], replicated
Inputs may be any that keep to these rules, and one draw needn't show every extreme that they name: `offsets`: each clip's crop start among the latent columns.
All inputs are finite; a program needn't handle non-finite values.
Results may differ from a plain program's by a relative error of at most 0.00095.
Values may be sent and summed in bfloat16 or wider, within the bound.
No kernel may reach another device: no remote copies, remote signals or barrier semaphores. Data moves between devices by JAX's collectives and lax.ppermute only.
A program may use at most 192 MiB of HBM per device.

v0:
```python
import math

import jax
import jax.numpy as jnp
from jax import lax
from jax.sharding import PartitionSpec as P


def passed_along(block, axis, distance):
    devices = range(lax.axis_size(axis))
    route = [(i - distance, i) for i in devices if i - distance in devices]
    return lax.ppermute(block, axis, route)


def tap_masks(count, rows, cols):
    place = jnp.arange(count, dtype=jnp.int32) % (rows * cols)
    row_pos = place // cols
    col_pos = place % cols
    masks = []
    for row_off in range(3):
        for col_off in range(3):
            good_row = (row_pos + row_off - 1 >= 0) & (row_pos + row_off - 1 < rows)
            good_col = (col_pos + col_off - 1 >= 0) & (col_pos + col_off - 1 < cols)
            masks.append((good_row & good_col).astype(jnp.bfloat16).reshape(count, 1))
    return masks


def tap_slices(extended, count, rows, cols, masks):
    margin = jnp.zeros((cols + 1, extended.shape[1]), extended.dtype)
    padded = jnp.concatenate([margin, extended, margin], axis=0)
    plane = rows * cols
    pieces = []
    for depth in range(3):
        for row_off in range(3):
            for col_off in range(3):
                first = depth * plane + row_off * cols + col_off
                pieces.append(padded[first : first + count] * masks[row_off * 3 + col_off])
    return pieces


def cross_dot(left, right):
    return lax.dot_general(
        left, right, (((0,), (0,)), ((), ())), preferred_element_type=jnp.float32
    )


def shards(latent, offsets, teacher, w_in, w_mid):
    frames = teacher.shape[1]
    rows = teacher.shape[2]
    cols = teacher.shape[3]
    chans = teacher.shape[4]
    plane = rows * cols
    count = frames * plane
    lat_chans = latent.shape[4]
    total_cells = lax.axis_size("clip") * lax.axis_size("tm") * count
    scale = 2.0 / math.sqrt(total_cells)
    masks = tap_masks(count, rows, cols)
    crop = lax.dynamic_slice_in_dim(latent[0], offsets[0], cols, axis=2).reshape(count, lat_chans)
    earlier = passed_along(crop[count - 2 * plane :], "tm", 1)
    crop_ext = jnp.concatenate([earlier, crop], axis=0)
    patch_in = jnp.concatenate(tap_slices(crop_ext, count, rows, cols, masks), axis=1)
    z_first = jnp.dot(patch_in, w_in, preferred_element_type=jnp.float32)
    act = jax.nn.silu(z_first).astype(jnp.bfloat16)
    act_prev = passed_along(act[count - 2 * plane :], "tm", 1)
    act_ext = jnp.concatenate([act_prev, act], axis=0)
    act_taps = tap_slices(act_ext, count, rows, cols, masks)
    w_full = lax.all_gather(w_mid, "clip", axis=0, tiled=True)
    output = jnp.zeros((count, chans), jnp.float32)
    for k in range(27):
        output = output + jnp.dot(
            act_taps[k], w_full[k * chans : (k + 1) * chans], preferred_element_type=jnp.float32
        )
    target_rows = teacher[0].reshape(count, chans).astype(jnp.float32)
    grad_low = ((output - target_rows) * scale).astype(jnp.bfloat16)
    local_mid = jnp.concatenate([cross_dot(act_taps[k], grad_low) for k in range(27)], axis=0)
    lead = 2 * plane + cols + 1
    masked_pads = []
    for k in range(9):
        masked_pads.append(jnp.pad(grad_low * masks[k], ((lead, lead), (0, 0))))
    ext_count = count + 2 * plane
    adjoint = jnp.zeros((ext_count, chans), jnp.float32)
    for depth in range(3):
        for row_off in range(3):
            for col_off in range(3):
                k = depth * 9 + row_off * 3 + col_off
                first = (2 - depth) * plane + (2 - row_off) * cols + (2 - col_off)
                piece = masked_pads[row_off * 3 + col_off][first : first + ext_count]
                adjoint = adjoint + lax.dot_general(
                    piece,
                    w_full[k * chans : (k + 1) * chans],
                    (((1,), (1,)), ((), ())),
                    preferred_element_type=jnp.float32,
                )
    outgoing = adjoint[: 2 * plane]
    incoming = passed_along(outgoing.astype(jnp.bfloat16), "tm", -1).astype(outgoing.dtype)
    own = adjoint[2 * plane :]
    dact = jnp.concatenate([own[: count - 2 * plane], own[count - 2 * plane :] + incoming], axis=0)
    sig = jax.nn.sigmoid(z_first)
    dz_first = (dact * sig * (1.0 + z_first * (1.0 - sig))).astype(jnp.bfloat16)
    grad_in = lax.psum(cross_dot(patch_in, dz_first), ("clip", "tm"))
    summed = lax.psum(local_mid, "tm")
    grad_mid = lax.psum_scatter(summed, "clip", scatter_dimension=0, tiled=True)
    return (grad_mid, grad_in)


def solution(mesh):
    return jax.shard_map(
        shards,
        mesh=mesh,
        in_specs=(
            P("clip", "tm", None, None, None),
            P("clip"),
            P("clip", "tm", None, None, None),
            P(),
            P("clip", None),
        ),
        out_specs=(P("clip", None), P()),
        check_vma=False,
    )
```

profile of v0, /device:TPU:0, one launch (start us, length us, event | category | flops | bytes accessed | tf_op | source)
XLA Modules:
  0.0 524.9 jit_solution(12850490637867089896)
XLA Ops:
  9.7 4.9 collective-permute-start
  18.5 2.0 multiply_convert_fusion
  20.5 3.9 collective-permute-start.1
  24.4 3.4 collective-permute-done.1
  27.8 2.3 concatenate.47
  30.2 35.1 %all-gather.2.cloned.1.call-done = bf16[10368,384]{1,0:T(8,128)(2,1)} async-done(((bf16[1296,384]{1,0:T(8,128)(2,1)}), bf16[10368,384]{1,0:T(8,128)(2,1)}) %all-gather.2.cloned.1.call-update) | async-done | bytes 7962640 | tf_op jit(solution)/shard_map/all_gather | solution.py:67
  65.3 3.0 fusion.52
  68.3 2.8 fusion.51
  71.1 2.8 fusion.50
  75.8 1.9 fusion.132
  81.4 1.9 fusion.123
  90.7 1.9 fusion.108
  96.4 2.0 fusion.99
  98.4 1.9 fusion.96
  100.2 2.1 fusion.93
  102.3 1.9 fusion.90
  106.1 1.9 fusion.84
  108.0 1.9 fusion.46
  111.8 1.9 fusion.48
  113.7 1.9 fusion.45
  117.4 17.8 %broadcast_multiply_fusion = (bf16[1024,384]{1,0:T(8,128)(2,1)S(1)}, bf16[1024,384]{1,0:T(8,128)(2,1)S(1)}, bf16[1024,384]{1,0:T(8,128)(2,1)S(1)}, bf16[1024,384...) fusion(bf16[1024]{0:T(1024)(128)(2,1)S(1)} %get-tuple-element.1, ...), kind=kOutput, calls=%fused_computation.165 | convolution fusion | flops 319684608 | bytes 50843648 | tf_op jit(solution)/shard_map/dot_general | solution.py:70
  135.3 3.1 convolution_dynamic-update-slice_fusion.26
  171.2 1.9 convolution_dynamic-update-slice_fusion.5
  181.4 2.0 fusion.4
  183.5 1.9 convolution_add_fusion.25
  185.4 1.9 convolution_add_fusion.24
  187.3 1.9 convolution_add_fusion.23
  210.1 7.5 %collective-permute-done.2 = bf16[256,384]{1,0:T(8,128)(2,1)S(1)} collective-permute-done((bf16[256,384]{1,0:T(8,128)(2,1)S(1)}, bf16[256,384]{1,0:T(8,128)(2,1)S(1)}, u32[]{:S(2)}, u32[]{:S(2)}) %collective-permute-start.2) | collective-permute-done | bytes 196640 | tf_op jit(solution)/shard_map/ppermute | solution.py:12
  219.6 74.8 %reduce-scatter.2.cloned.1.call-done = f32[1296,384]{1,0:T(8,128)} async-done(((f32[10368,384]{1,0:T(8,128)}), f32[1296,384]{1,0:T(8,128)}) %reduce-scatter.2.cloned.1.call-update) | async-done | bytes 1990672 | tf_op jit(solution)/shard_map/reduce_scatter | solution.py:102
  294.4 133.7 %all-reduce.14.cloned.1.call-done = f32[432,384]{1,0:T(8,128)} async-done(((f32[432,384]{1,0:T(8,128)}), f32[432,384]{1,0:T(8,128)}) %all-reduce.14.cloned.1.call-update) | async-done | bytes 663568 | tf_op jit(solution)/shard_map/psum | solution.py:100
  428.1 86.2 %all-reduce.16.cloned.1.call-done = f32[1296,384]{1,0:T(8,128)} async-done(((f32[1296,384]{1,0:T(8,128)}), f32[1296,384]{1,0:T(8,128)}) %all-reduce.16.cloned.1.call-update) | async-done | bytes 1990672 | tf_op jit(solution)/shard_map/psum | solution.py:101
  514.3 3.0 copy.65
  (157 shorter events, 92.3 us)
Async XLA Ops:
  7.2 11.3 %copy-start = (bf16[432,384]{1,0:T(8,128)(2,1)S(1)}, bf16[432,384]{1,0:T(8,128)(2,1)}, u32[]{:S(2)}) copy-start(bf16[432,384]{1,0:T(8,128)(2,1)} %param.8) | copy-start | bytes 995332
  7.2 58.1 %all-gather.2.cloned.1.call-start = ((), (), s32[]{:S(2)}) async-start(), calls=%async_computation.1 | async-start | bytes 8957952 | tf_op jit(solution)/shard_map/all_gather | solution.py:67
  7.9 286.4 %reduce-scatter.2.cloned.1.call-start = ((), (), s32[]{:S(2)}) async-start(), calls=%async_computation.3 | async-start | bytes 17915904 | tf_op jit(solution)/shard_map/reduce_scatter | solution.py:102
  9.7 6.6 %collective-permute-start = (bf16[256,16]{0,1:T(8,128)(2,1)S(1)}, bf16[256,16]{0,1:T(8,128)(2,1)S(1)}, u32[]{:S(2)}, u32[]{:S(2)}) collective-permute-start(bf16[256,16]{0,1:T(8,128)(2,1)S(1)} %slice.384), channel_id=1, source_target_pairs={{0,1},{1,2},{2,3},{4,5},{5,6},{6,7},{8,9},{9,10},{10,11},{12,13},{... | collective-permute-start | bytes 24584 | tf_op jit(solution)/shard_map/ppermute | solution.py:12
  18.5 2.0 copy-start.13
  20.5 7.4 %collective-permute-start.1 = (bf16[256,384]{1,0:T(8,128)(2,1)S(1)}, bf16[256,384]{1,0:T(8,128)(2,1)S(1)}, u32[]{:S(2)}, u32[]{:S(2)}) collective-permute-start(bf16[256,384]{1,0:T(8,128)(2,1)S(1)} %slice.517), channel_id=1, source_target_pairs={{0,1},{1,2},{2,3},{4,5},{5,6},{6,7},{8,9},{9,10},{10,11},{12,13},{... | collective-permute-start | bytes 589832 | tf_op jit(solution)/shard_map/ppermute | solution.py:12
  30.2 43.8 %copy-start.9 = (bf16[1297,384]{1,0:T(8,128)(2,1)}, bf16[1297,384]{1,0:T(8,128)(2,1)S(1)}, u32[]{:S(2)}) copy-start(bf16[1297,384]{1,0:T(8,128)(2,1)S(1)} %concatenate.47) | copy-start | bytes 2988292
  65.3 8.7 %copy-start.2 = (bf16[10368,384]{1,0:T(8,128)(2,1)S(1)}, bf16[10368,384]{1,0:T(8,128)(2,1)}, u32[]{:S(2)}) copy-start(bf16[10368,384]{1,0:T(8,128)(2,1)} %all-gather.2.cloned.1.call-done) | copy-start | bytes 23887876
  135.3 3.1 copy-start.10
  135.3 3.1 copy-start.11
  181.3 2.1 copy-start.7
  181.3 246.8 %all-reduce.14.cloned.1.call-start = ((), (), s32[]{:S(2)}) async-start(), calls=%async_computation.2 | async-start | bytes 1327104 | tf_op jit(solution)/shard_map/psum | solution.py:100
  183.4 1.9 copy-start.6
  183.4 5.7 %slice-start = ((s8[7962624]{0:T(1024)(128)(4,1)}), s8[4194304]{0:T(1024)(128)(4,1)S(1)}, s32[]{:S(2)}) async-start(s8[7962624]{0:T(1024)(128)(4,1)} %bitcast.44), calls=%async_computation.5 | async-start | bytes 8388608
  185.4 1.9 copy-start.5
  185.4 3.8 slice-start.1
  187.3 1.9 copy-start.4
  189.2 1.3 copy-start.3
  192.8 1.3 copy-start.8
  208.5 9.2 %copy-start.14 = (bf16[1024,432]{0,1:T(8,128)(2,1)S(1)}, bf16[1024,432]{0,1:T(8,128)(2,1)}, u32[]{:S(2)}) copy-start(bf16[1024,432]{0,1:T(8,128)(2,1)} %copy-done.13) | copy-start | bytes 2654212
  208.5 9.2 %copy-start.15 = (f32[1024,384]{1,0:T(8,128)S(1)}, f32[1024,384]{1,0:T(8,128)}, u32[]{:S(2)}) copy-start(f32[1024,384]{1,0:T(8,128)} %get-tuple-element.12) | copy-start | bytes 4718596
  208.5 9.2 %collective-permute-start.2 = (bf16[256,384]{1,0:T(8,128)(2,1)S(1)}, bf16[256,384]{1,0:T(8,128)(2,1)S(1)}, u32[]{:S(2)}, u32[]{:S(2)}) collective-permute-start(bf16[256,384]{1,0:T(8,128)(2,1)S(1)} %slice.1014), channel_id=1, source_target_pairs={{1,0},{2,1},{3,2},{5,4},{6,5},{7,6},{9,8},{10,9},{11,10},{13,12},{... | collective-permute-start | bytes 589832 | tf_op jit(solution)/shard_map/ppermute | solution.py:12
  219.5 294.8 %all-reduce.16.cloned.1.call-start = ((), (), s32[]{:S(2)}) async-start(), calls=%async_computation.4 | async-start | bytes 3981312 | tf_op jit(solution)/shard_map/psum | solution.py:101
  428.1 89.2 %copy-start.12 = (f32[432,384]{1,0:T(8,128)S(1)}, f32[432,384]{1,0:T(8,128)}, u32[]{:S(2)}) copy-start(f32[432,384]{1,0:T(8,128)} %all-reduce.14.cloned.1.call-done) | copy-start | bytes 1990660
  514.3 3.9 copy-start.1
Sparse Core Ops, SparseCore 0:
  9.9 55.3 all-gather.1
  181.4 112.8 reduce-scatter.1
  301.0 127.0 all-reduce.13
  430.4 83.9 all-reduce.15
where the time goes:
time: 528 us; the launch traced here: 525 us
  waiting for transfers between devices  342 us (65%)
  matrix products  145 us (27%)
  between operations  15.4 us (3%)
  starting transfers between devices  10.6 us (2%)
  local copies, waits for them, and re-layouts  10 us (2%)
    psum x1, waiting for transfers between devices, shards(): grad_in = lax.psum(cross_dot(patch_in, dz_first), ('clip', 'tm'))  134 us
    psum x1, waiting for transfers between devices, shards(): summed = lax.psum(local_mid, 'tm')  86.2 us
    reduce_scatter x1, waiting for transfers between devices, shards(): grad_mid = lax.psum_scatter(summed, 'clip', scatter_dimension=0, tiled=True)  74.8 us
    dot_general x27, matrix products, shards(): jnp.dot(act_taps[k], w_full[k * chans:(k + 1) * chans], preferred_element...  70 us
    dot_general x28, matrix products, cross_dot(): lax.dot_general(left, right, (((0,), (0,)), ((), ())), preferred_element_...  47.7 us
    all_gather x1, waiting for transfers between devices, shards(): w_full = lax.all_gather(w_mid, 'clip', axis=0, tiled=True)  35.1 us
    dot_general x27, matrix products, shards(): lax.dot_general(piece, w_full[k * chans:(k + 1) * chans], (((1,), (1,)),...  25.7 us
    ppermute x3, waiting for transfers between devices, passed_along(): return lax.ppermute(block, axis, route)  11 us
  transfers between devices with their start and end apart: 7, of which 6 were waited for; matrix products, arithmetic and copies ran while one was open for 7% of the time, Pallas kernels for 0%

commit v1 on v0

v1 whole, which is shorter than its diff:
```python
import math

import jax
import jax.numpy as jnp
from jax import lax
from jax.experimental import pallas as pl
from jax.experimental.pallas import tpu as pltpu
from jax.sharding import PartitionSpec as P

F32 = jnp.float32
BF16 = jnp.bfloat16
CHUNKS = 3
VMEM = 56 * 1024 * 1024


def passed_along(block, axis, distance):
    devices = range(lax.axis_size(axis))
    route = [(i - distance, i) for i in devices if i - distance in devices]
    return lax.ppermute(block, axis, route)


def shifted(x, row_off, col_off, rows, cols):
    lanes = x.shape[1]
    lane = lax.broadcasted_iota(jnp.int32, (1, lanes), 1)
    row = (lane // cols) % rows + row_off
    col = lane % cols + col_off
    good = (row >= 0) & (row < rows) & (col >= 0) & (col < cols)
    shift = row_off * cols + col_off
    return jnp.where(good, pltpu.roll(x, (lanes - shift) % lanes, axis=1), 0.0)


def contract(left, right, dims):
    return lax.dot_general(left, right, (dims, ((), ())), preferred_element_type=F32)


def front_kernel(crop_ref, w_ref, patch_ref, z_ref, taps_ref, full_ref, *, rows, cols):
    plane = rows * cols
    lat = crop_ref.shape[0]
    count = patch_ref.shape[1]
    ext = count + 2 * plane

    @pl.when(pl.program_id(0) == 0)
    def _():
        crop = crop_ref[...].astype(F32)
        for spot in range(9):
            moved = shifted(crop, spot // 3 - 1, spot % 3 - 1, rows, cols).astype(BF16)
            for depth in range(3):
                first = (depth * 9 + spot) * lat
                full_ref[first : first + lat, :] = moved[:, depth * plane : depth * plane + ext]
        patch_ref[...] = full_ref[:, 2 * plane :]

    z = contract(w_ref[...], full_ref[...], ((0,), (0,)))
    z_ref[...] = z[:, 2 * plane :]
    act = (z * (1.0 / (1.0 + jnp.exp(-z)))).astype(BF16).astype(F32)
    for spot in range(9):
        moved = shifted(act, spot // 3 - 1, spot % 3 - 1, rows, cols).astype(BF16)
        for depth in range(3):
            taps_ref[depth * 9 + spot] = moved[:, depth * plane : depth * plane + count]


def front(crop_t, w_in, rows, cols, count):
    chans = w_in.shape[1]
    depth_in = w_in.shape[0]
    plane = rows * cols
    block = 128
    return pl.pallas_call(
        lambda *refs: front_kernel(*refs, rows=rows, cols=cols),
        grid=(chans // block,),
        in_specs=[
            pl.BlockSpec(crop_t.shape, lambda i: (0, 0)),
            pl.BlockSpec((depth_in, block), lambda i: (0, i)),
        ],
        out_specs=[
            pl.BlockSpec((depth_in, count), lambda i: (0, 0)),
            pl.BlockSpec((block, count), lambda i: (i, 0)),
            pl.BlockSpec((27, block, count), lambda i: (0, i, 0)),
        ],
        out_shape=[
            jax.ShapeDtypeStruct((depth_in, count), BF16),
            jax.ShapeDtypeStruct((chans, count), F32),
            jax.ShapeDtypeStruct((27, chans, count), BF16),
        ],
        scratch_shapes=[pltpu.VMEM((depth_in, count + 2 * plane), BF16)],
        compiler_params=pltpu.CompilerParams(vmem_limit_bytes=VMEM),
        name="front",
    )(crop_t, w_in)


def grad_kernel(order_ref, taps_ref, g_ref, out_ref):
    out_ref[0] = contract(taps_ref[...], g_ref[...], ((1,), (1,)))


def grad_chunk(order, taps, g_t, parts, which):
    blocks = order.shape[0]
    total, count = taps.shape
    chans = g_t.shape[0]
    rows = total // blocks // parts
    return pl.pallas_call(
        grad_kernel,
        grid_spec=pltpu.PrefetchScalarGridSpec(
            num_scalar_prefetch=1,
            grid=(blocks,),
            in_specs=[
                pl.BlockSpec((rows, count), lambda i, order: (order[i] * parts + which, 0)),
                pl.BlockSpec((chans, count), lambda i, order: (0, 0)),
            ],
            out_specs=pl.BlockSpec((1, rows, chans), lambda i, order: (i, 0, 0)),
        ),
        out_shape=jax.ShapeDtypeStruct((blocks, rows, chans), F32),
        compiler_params=pltpu.CompilerParams(vmem_limit_bytes=VMEM),
        name="grad",
    )(order, taps, g_t)


def back_kernel(g_ref, w_ref, z_ref, patch_ref, out_ref, acc_ref, *, rows, cols):
    plane = rows * cols
    count = z_ref.shape[1]
    spot = pl.program_id(0)
    moved = shifted(g_ref[...].astype(F32), 1 - spot // 3, 1 - spot % 3, rows, cols).astype(BF16)
    total = contract(w_ref[0, 0], moved[:, 2 * plane : 2 * plane + count], ((1,), (0,)))
    total += contract(w_ref[1, 0], moved[:, plane : plane + count], ((1,), (0,)))
    total += contract(w_ref[2, 0], moved[:, :count], ((1,), (0,)))

    @pl.when(spot == 0)
    def _():
        acc_ref[...] = total

    @pl.when(spot > 0)
    def _():
        acc_ref[...] += total

    @pl.when(spot == 8)
    def _():
        z = z_ref[...]
        sig = 1.0 / (1.0 + jnp.exp(-z))
        dz = (acc_ref[...] * sig * (1.0 + z * (1.0 - sig))).astype(BF16)
        out_ref[...] = contract(patch_ref[...], dz, ((1,), (1,)))


def back(g_ext, w_taps, z_t, patch_t, rows, cols):
    chans, count = z_t.shape
    depth_in = patch_t.shape[0]
    return pl.pallas_call(
        lambda *refs: back_kernel(*refs, rows=rows, cols=cols),
        grid=(9,),
        in_specs=[
            pl.BlockSpec(g_ext.shape, lambda i: (0, 0)),
            pl.BlockSpec((3, 1, chans, chans), lambda i: (0, i, 0, 0)),
            pl.BlockSpec((chans, count), lambda i: (0, 0)),
            pl.BlockSpec((depth_in, count), lambda i: (0, 0)),
        ],
        out_specs=pl.BlockSpec((depth_in, chans), lambda i: (0, 0)),
        out_shape=jax.ShapeDtypeStruct((depth_in, chans), F32),
        scratch_shapes=[pltpu.VMEM((chans, count), F32)],
        compiler_params=pltpu.CompilerParams(vmem_limit_bytes=VMEM),
        name="back",
    )(g_ext, w_taps, z_t, patch_t)


def reduced(part):
    half = part.shape[0] // 2
    clips = lax.axis_size("clip")
    swap = [(i, i ^ 1) for i in range(clips)]
    mine = part[half:] + lax.ppermute(part[:half], "clip", swap)
    groups = [[2 * p + core for p in range(half)] for core in range(2)]
    block = lax.all_to_all(mine, "clip", 0, 0, axis_index_groups=groups, tiled=True).sum(axis=0)
    depth = lax.axis_size("tm")
    rows, chans = block.shape
    piece = lax.all_to_all(block.reshape(depth, rows // depth, chans), "tm", 0, 0, tiled=True).sum(axis=0)
    spread = jnp.broadcast_to(piece[None], (depth,) + piece.shape)
    return lax.all_to_all(spread, "tm", 0, 0, tiled=True).reshape(rows, chans)


def shards(latent, offsets, teacher, w_in, w_mid):
    frames = teacher.shape[1]
    rows = teacher.shape[2]
    cols = teacher.shape[3]
    chans = teacher.shape[4]
    plane = rows * cols
    count = frames * plane
    lat_chans = latent.shape[4]
    clips = lax.axis_size("clip")
    total_cells = clips * lax.axis_size("tm") * count
    scale = 2.0 / math.sqrt(total_cells)
    w_full = lax.all_gather(w_mid, "clip", axis=0, tiled=True)
    crop = lax.dynamic_slice_in_dim(latent[0], offsets[0], cols, axis=2).reshape(count, lat_chans).T
    earlier = passed_along(crop[:, count - 4 * plane :], "tm", 1)
    crop_ext = jnp.concatenate([earlier, crop], axis=1)
    patch_t, z_t, taps = front(crop_ext, w_in, rows, cols, count)
    taps = taps.reshape(27 * chans, count)
    teacher_t = teacher[0].reshape(count, chans).T.astype(F32)
    h_t = contract(w_full, taps, ((0,), (0,)))
    g_t = ((h_t - teacher_t) * scale).astype(BF16)
    later = passed_along(g_t[:, : 2 * plane], "tm", -1)
    g_ext = jnp.concatenate([g_t, later], axis=1)

    core = lax.axis_index("clip") % 2
    even = 2 * jnp.arange(clips // 2, dtype=jnp.int32)
    order = jnp.concatenate([even + 1 - core, even + core])
    parts = [grad_chunk(order, taps, g_t, CHUNKS, j) for j in range(CHUNKS)]
    in_part = back(g_ext, w_full.reshape(3, 9, chans, chans), z_t, patch_t, rows, cols)
    done = [reduced(part) for part in parts]
    grad_mid = jnp.concatenate(done, axis=0)
    grad_in = lax.psum(in_part, ("clip", "tm"))
    return (grad_mid, grad_in)


def solution(mesh):
    return jax.shard_map(
        shards,
        mesh=mesh,
        in_specs=(
            P("clip", "tm", None, None, None),
            P("clip"),
            P("clip", "tm", None, None, None),
            P(),
            P("clip", None),
        ),
        out_specs=(P("clip", None), P()),
        check_vma=False,
    )
```

time: 528 us -> 509 us (0.964)
  matrix products: 145 us -> 15.8 us
  Pallas kernels: 0 us -> 65.1 us
  starting transfers between devices: 10.6 us -> 42.3 us
  other arithmetic: 2.07 us -> 22.2 us
  waiting for transfers between devices: 342 us -> 326 us
  local copies, waits for them, and re-layouts: 10 us -> 20 us
    all_to_all x0 -> x9, waiting for transfers between devices: none -> 145 us  [the longest x3 64.9 us: reduced(): lax.all_to_all(mine, 'clip', 0, 0, axis_index_groups=groups, tiled=True)]
    dot_general x83 -> x1, matrix products: 145 us -> 15.8 us  [contract(): lax.dot_general(left, right, (dims, ((), ())), preferred_element_type=F32)]
    psum x2 -> x1, waiting for transfers between devices: 220 us -> 128 us  [shards(): grad_in = lax.psum(in_part, ('clip', 'tm'))]
    reduce_scatter x1 -> x0, waiting for transfers between devices: 74.8 us -> none  [shards(): grad_mid = lax.psum_scatter(summed, 'clip', scatter_dimension=0, tiled=True)]
    pallas_call x0 -> x5, Pallas kernels: none -> 65.1 us  [the longest x3 32.4 us: grad_chunk(): pl.pallas_call(grad_kernel, grid_spec=pltpu.PrefetchScalarGridSpec(num_sc...]
    all_to_all x0 -> x9, starting transfers between devices: none -> 35.2 us  [the longest x3 13 us: reduced(): lax.all_to_all(mine, 'clip', 0, 0, axis_index_groups=groups, tiled=True)]
    add x1 -> x3, other arithmetic: 0.04 us -> 11.3 us  [reduced(): mine = part[half:] + lax.ppermute(part[:half], 'clip', swap)]
    slice x6 -> x5, local copies, waits for them, and re-layouts: 1.19 us -> 9.01 us  [the longest x3 8.98 us: reduced(): mine = part[half:] + lax.ppermute(part[:half], 'clip', swap)]
  transfers between devices with their start and end apart: 7 -> 16, of which waited for: 6 -> 12; matrix products, arithmetic and copies ran while one was open for 7% -> 7% of each run, Pallas kernels for 0% -> 11%
where the time goes in v1:
time: 509 us; the launch traced here: 506 us
  waiting for transfers between devices  326 us (64%)
  Pallas kernels  65.1 us (13%)
  starting transfers between devices  42.3 us (8%)
  other arithmetic  22.2 us (4%)
  local copies, waits for them, and re-layouts  20 us (4%)
  matrix products  15.8 us (3%)
  between operations  15 us (3%)
    psum x1, waiting for transfers between devices, shards(): grad_in = lax.psum(in_part, ('clip', 'tm'))  128 us
    all_to_all x3, waiting for transfers between devices, reduced(): lax.all_to_all(mine, 'clip', 0, 0, axis_index_groups=groups, tiled=True)  64.9 us
    all_to_all x3, waiting for transfers between devices, reduced(): lax.all_to_all(block.reshape(depth, rows // depth, chans), 'tm', 0, 0, ti...  44.9 us
    all_gather x1, waiting for transfers between devices, shards(): w_full = lax.all_gather(w_mid, 'clip', axis=0, tiled=True)  38.5 us
    all_to_all x3, waiting for transfers between devices, reduced(): return lax.all_to_all(spread, 'tm', 0, 0, tiled=True).reshape(rows, chans)  34.8 us
    pallas_call x3, Pallas kernels, grad_chunk(): pl.pallas_call(grad_kernel, grid_spec=pltpu.PrefetchScalarGridSpec(num_sc...  32.4 us
    pallas_call x1, Pallas kernels, back(): pl.pallas_call(lambda *refs: back_kernel(*refs, rows=rows, cols=cols), gr...  22 us
    dot_general x1, matrix products, contract(): lax.dot_general(left, right, (dims, ((), ())), preferred_element_type=F32)  15.8 us
  transfers between devices with their start and end apart: 16, of which 12 were waited for; matrix products, arithmetic and copies ran while one was open for 7% of the time, Pallas kernels for 11%

profile of v1, /device:TPU:0, one launch (start us, length us, event | category | flops | bytes accessed | tf_op | source)
XLA Modules:
  0.0 506.5 jit_solution(11076243988924394763)
XLA Ops:
  9.1 4.9 collective-permute-start
  16.1 10.6 %front.1 = (bf16[432,1024]{1,0:T(8,128)(2,1)}, f32[384,1024]{1,0:T(8,128)}, bf16[27,384,1024]{2,1,0:T(8,128)(2,1)}) custom-call(bf16[16,1536]{1,0:T(8,128)(2,1)} %pad_maximum_fusion.2.refs_0_, bf16[432,384]{1,0:T(8,128)(2,1)} %refs_1_.1), custom_call_target="tpu_custom_call" | custom-call | tf_op jit(solution)/shard_map/front/pallas_call | solution.py:66
  26.7 38.5 %all-gather.2.cloned.1.call-done = bf16[10368,384]{1,0:T(8,128)(2,1)} async-done(((bf16[1296,384]{1,0:T(8,128)(2,1)}), bf16[10368,384]{1,0:T(8,128)(2,1)}) %all-gather.2.cloned.1.call-update) | async-done | bytes 7962640 | tf_op jit(solution)/shard_map/all_gather | solution.py:185
  65.2 15.8 %fusion.g_ref = bf16[384,1024]{1,0:T(8,128)(2,1)} fusion(f32[1024,384]{0,1:T(8,128)S(1)} %copy.12, bf16[10368,1024]{1,0:T(8,128)(2,1)} %bitcast.18, bf16[10368,384]{1,0:T(8,128)(2,1)} %all-gather.2.cloned.1.call-done), kind=kOutput, calls=%fused_computation.5 | convolution fusion | flops 8154906624 | bytes 31555584 | tf_op jit(solution)/shard_map/dot_general | solution.py:33
  81.0 10.6 %grad.5 = f32[8,432,384]{2,1,0:T(8,128)} custom-call(s32[8]{0:T(128)} %pad_add_fusion.order_ref, bf16[10368,1024]{1,0:T(8,128)(2,1)} %bitcast.19, bf16[384,1024]{1,0:T(8,128)(2,1)} %fusion.g_ref), custom_call_target="tpu_custom_call" | custom-call | tf_op jit(solution)/shard_map/grad/pallas_call | solution.py:98
  94.1 10.7 %grad.4 = f32[8,432,384]{2,1,0:T(8,128)} custom-call(s32[8]{0:T(128)} %pad_add_fusion.order_ref, bf16[10368,1024]{1,0:T(8,128)(2,1)} %bitcast.20, bf16[384,1024]{1,0:T(8,128)(2,1)} %fusion.g_ref), custom_call_target="tpu_custom_call" | custom-call | tf_op jit(solution)/shard_map/grad/pallas_call | solution.py:98
  104.7 3.4 slice.36
  108.6 3.5 slice_add_fusion
  112.1 4.7 all-to-all-start.6
  116.8 11.2 %grad.3 = f32[8,432,384]{2,1,0:T(8,128)} custom-call(s32[8]{0:T(128)} %pad_add_fusion.order_ref, bf16[10368,1024]{1,0:T(8,128)(2,1)} %bitcast.21, bf16[384,1024]{1,0:T(8,128)(2,1)} %fusion.g_ref), custom_call_target="tpu_custom_call" | custom-call | tf_op jit(solution)/shard_map/grad/pallas_call | solution.py:98
  128.0 3.5 slice.34
  131.6 3.5 slice_add_fusion.1
  135.1 13.2 %all-to-all-done.6 = f32[4,432,384]{2,1,0:T(8,128)} async-done(((f32[4,432,384]{2,1,0:T(8,128)}), f32[4,432,384]{2,1,0:T(8,128)}, u32[]{:S(2)}, u32[]{:S(2)}) %all-to-all-start.6) | async-done | bytes 2654240 | tf_op jit(solution)/shard_map/all_to_all | solution.py:166
  148.3 3.7 all-to-all-start.3
  151.9 4.3 slice_add_fusion.2
  156.2 26.2 %all-to-all-done.3 = f32[4,432,384]{2,1,0:T(8,128)S(1)} async-done(((f32[4,432,384]{2,1,0:T(8,128)}), f32[4,432,384]{2,1,0:T(8,128)S(1)}, u32[]{:S(2)}, u32[]{:S(2)}) %all-to-all-start.3) | async-done | bytes 2654240 | tf_op jit(solution)/shard_map/all_to_all | solution.py:166
  182.5 4.6 all-to-all-start
  191.9 25.5 %all-to-all-done = f32[4,432,384]{2,1,0:T(8,128)} async-done(((f32[4,432,384]{2,1,0:T(8,128)}), f32[4,432,384]{2,1,0:T(8,128)}, u32[]{:S(2)}, u32[]{:S(2)}) %all-to-all-start) | async-done | bytes 2654240 | tf_op jit(solution)/shard_map/all_to_all | solution.py:166
  217.4 4.6 all-to-all-start.7
  225.1 14.2 %all-to-all-done.7 = f32[4,108,384]{2,1,0:T(8,128)} async-done(((f32[4,108,384]{2,1,0:T(8,128)}), f32[4,108,384]{2,1,0:T(8,128)}, u32[]{:S(2)}, u32[]{:S(2)}) %all-to-all-start.7) | async-done | bytes 663584 | tf_op jit(solution)/shard_map/all_to_all | solution.py:169
  239.3 3.7 all-to-all-start.4
  245.9 14.3 %all-to-all-done.4 = f32[4,108,384]{2,1,0:T(8,128)S(1)} async-done(((f32[4,108,384]{2,1,0:T(8,128)}), f32[4,108,384]{2,1,0:T(8,128)S(1)}, u32[]{:S(2)}, u32[]{:S(2)}) %all-to-all-start.4) | async-done | bytes 663584 | tf_op jit(solution)/shard_map/all_to_all | solution.py:169
  260.2 3.5 all-to-all-start.1
  264.9 16.3 %all-to-all-done.1 = f32[4,108,384]{2,1,0:T(8,128)S(1)} async-done(((f32[4,108,384]{2,1,0:T(8,128)}), f32[4,108,384]{2,1,0:T(8,128)S(1)}, u32[]{:S(2)}, u32[]{:S(2)}) %all-to-all-start.1) | async-done | bytes 663584 | tf_op jit(solution)/shard_map/all_to_all | solution.py:169
  282.1 3.5 all-to-all-start.8
  285.7 17.4 %all-to-all-done.8 = f32[4,108,384]{2,1,0:T(8,128)S(1)} async-done(((f32[4,108,384]{2,1,0:T(8,128)}), f32[4,108,384]{2,1,0:T(8,128)S(1)}, u32[]{:S(2)}, u32[]{:S(2)}) %all-to-all-start.8) | async-done | bytes 663584 | tf_op jit(solution)/shard_map/all_to_all | solution.py:171
  304.0 3.5 all-to-all-start.5
  307.5 17.4 %all-to-all-done.5 = f32[4,108,384]{2,1,0:T(8,128)S(1)} async-done(((f32[4,108,384]{2,1,0:T(8,128)}), f32[4,108,384]{2,1,0:T(8,128)S(1)}, u32[]{:S(2)}, u32[]{:S(2)}) %all-to-all-start.5) | async-done | bytes 663584 | tf_op jit(solution)/shard_map/all_to_all | solution.py:171
  325.9 3.5 all-to-all-start.2
  330.7 14.5 %collective-permute-done.4 = bf16[384,256]{1,0:T(8,128)(2,1)S(1)} collective-permute-done((bf16[384,256]{1,0:T(8,128)(2,1)S(1)}, bf16[384,256]{1,0:T(8,128)(2,1)S(1)}, u32[]{:S(2)}, u32[]{:S(2)}) %collective-permute-start.4) | collective-permute-done | bytes 196640 | tf_op jit(solution)/shard_map/ppermute | solution.py:19
  346.3 22.0 %back.1 = f32[432,384]{1,0:T(8,128)} custom-call(bf16[384,1280]{1,0:T(8,128)(2,1)} %pad_maximum_fusion.1.refs_0_, bf16[3,9,384,384]{3,2,1,0:T(8,128)(2,1)} %bitcast.26, f32[384,1024]{1,0:T(8,128)} %get-tuple-element.6.refs_2_, bf16[432,1024]{1,0:T(8,128)(2,1)} %get-tuple-element.7.refs_3_), custom_call_target="tpu_custom_call" | custom-call | tf_op jit(solution)/shard_map/back/pallas_call | solution.py:143
  370.0 127.7 %all-reduce.2.cloned.1.call-done = f32[432,384]{1,0:T(8,128)} async-done(((f32[432,384]{1,0:T(8,128)}), f32[432,384]{1,0:T(8,128)}) %all-reduce.2.cloned.1.call-update) | async-done | bytes 663568 | tf_op jit(solution)/shard_map/psum | solution.py:204
  (60 shorter events, 27.0 us)
Async XLA Ops:
  7.2 1.4 copy-start
  7.2 6.9 %copy-start.3 = (bf16[1,8,8,16,384]{4,3,2,1,0:T(8,128)(2,1)S(1)}, bf16[1,8,8,16,384]{4,3,2,1,0:T(8,128)(2,1)}, u32[]{:S(2)}) copy-start(bf16[1,8,8,16,384]{4,3,2,1,0:T(8,128)(2,1)} %param.7) | copy-start | bytes 2359300
  7.2 58.0 %all-gather.2.cloned.1.call-start = ((), (), s32[]{:S(2)}) async-start(), calls=%async_computation.9 | async-start | bytes 8957952 | tf_op jit(solution)/shard_map/all_gather | solution.py:185
  9.1 6.4 %collective-permute-start = (bf16[16,512]{1,0:T(8,128)(2,1)S(1)}, bf16[16,512]{1,0:T(8,128)(2,1)S(1)}, u32[]{:S(2)}, u32[]{:S(2)}) collective-permute-start(bf16[16,512]{1,0:T(8,128)(2,1)S(1)} %slice.32), channel_id=1, source_target_pairs={{0,1},{1,2},{2,3},{4,5},{5,6},{6,7},{8,9},{9,10},{10,11},{12,13},{... | collective-permute-start | bytes 49160 | tf_op jit(solution)/shard_map/ppermute | solution.py:19
  91.7 16.9 %slice-start.2 = ((s8[5308416]{0:T(1024)(128)(4,1)}), s8[4194304]{0:T(1024)(128)(4,1)S(1)}, s32[]{:S(2)}) async-start(s8[5308416]{0:T(1024)(128)(4,1)} %bitcast.24), calls=%async_computation.13 | async-start | bytes 8388608
  93.7 14.8 %slice-start.3 = ((s8[5308416]{0:T(1024)(128)(4,1)}), s8[1114112]{0:T(1024)(128)(4,1)S(1)}, s32[]{:S(2)}) async-start(s8[5308416]{0:T(1024)(128)(4,1)} %bitcast.24), calls=%async_computation.14 | async-start | bytes 2228224
  93.7 14.8 %collective-permute-start.3 = (f32[4,432,384]{2,1,0:T(8,128)S(1)}, f32[4,432,384]{2,1,0:T(8,128)}, u32[]{:S(2)}, u32[]{:S(2)}) collective-permute-start(f32[4,432,384]{2,1,0:T(8,128)S(1)} %slice.38), channel_id=1, source_target_pairs={{0,4},{4,0},{8,12},{12,8},{16,20},{20,16},{24,28},{28,24},{1,5},{5... | collective-permute-start | bytes 7962632 | tf_op jit(solution)/shard_map/ppermute | solution.py:164
  108.1 23.5 %collective-permute-start.2 = (f32[4,432,384]{2,1,0:T(8,128)}, f32[4,432,384]{2,1,0:T(8,128)}, u32[]{:S(2)}, u32[]{:S(2)}) collective-permute-start(f32[4,432,384]{2,1,0:T(8,128)} %slice.36), channel_id=1, source_target_pairs={{0,4},{4,0},{8,12},{12,8},{16,20},{20,16},{24,28},{28,24},{1,5},{5... | collective-permute-start | bytes 7962632 | tf_op jit(solution)/shard_map/ppermute | solution.py:164
  112.1 19.5 %slice-start = ((s8[5308416]{0:T(1024)(128)(4,1)}), s8[1114112]{0:T(1024)(128)(4,1)S(1)}, s32[]{:S(2)}) async-start(s8[5308416]{0:T(1024)(128)(4,1)} %bitcast.22), calls=%async_computation.11 | async-start | bytes 2228224
  112.1 36.2 %all-to-all-start.6 = ((f32[4,432,384]{2,1,0:T(8,128)}), f32[4,432,384]{2,1,0:T(8,128)}, u32[]{:S(2)}, u32[]{:S(2)}) async-start(f32[4,432,384]{2,1,0:T(8,128)} %slice_add_fusion), calls=%async_computation.6 | async-start | bytes 5308416 | tf_op jit(solution)/shard_map/all_to_all | solution.py:166
  116.8 14.8 %slice-start.1 = ((s8[5308416]{0:T(1024)(128)(4,1)}), s8[4194304]{0:T(1024)(128)(4,1)S(1)}, s32[]{:S(2)}) async-start(s8[5308416]{0:T(1024)(128)(4,1)} %bitcast.22), calls=%async_computation.12 | async-start | bytes 8388608
  131.5 20.5 %collective-permute-start.1 = (f32[4,432,384]{2,1,0:T(8,128)}, f32[4,432,384]{2,1,0:T(8,128)}, u32[]{:S(2)}, u32[]{:S(2)}) collective-permute-start(f32[4,432,384]{2,1,0:T(8,128)} %slice.34), channel_id=1, source_target_pairs={{0,4},{4,0},{8,12},{12,8},{16,20},{20,16},{24,28},{28,24},{1,5},{5... | collective-permute-start | bytes 7962632 | tf_op jit(solution)/shard_map/ppermute | solution.py:164
  148.3 34.2 %all-to-all-start.3 = ((f32[4,432,384]{2,1,0:T(8,128)}), f32[4,432,384]{2,1,0:T(8,128)S(1)}, u32[]{:S(2)}, u32[]{:S(2)}) async-start(f32[4,432,384]{2,1,0:T(8,128)} %slice_add_fusion.1), calls=%async_computation.3 | async-start | bytes 5308416 | tf_op jit(solution)/shard_map/all_to_all | solution.py:166
  182.5 34.9 %all-to-all-start = ((f32[4,432,384]{2,1,0:T(8,128)}), f32[4,432,384]{2,1,0:T(8,128)}, u32[]{:S(2)}, u32[]{:S(2)}) async-start(f32[4,432,384]{2,1,0:T(8,128)} %slice_add_fusion.2), calls=%async_computation | async-start | bytes 5308416 | tf_op jit(solution)/shard_map/all_to_all | solution.py:166
  217.4 21.9 %all-to-all-start.7 = ((f32[4,108,384]{2,1,0:T(8,128)}), f32[4,108,384]{2,1,0:T(8,128)}, u32[]{:S(2)}, u32[]{:S(2)}) async-start(f32[4,108,384]{2,1,0:T(8,128)} %reshape.44), calls=%async_computation.7 | async-start | bytes 1376256 | tf_op jit(solution)/shard_map/all_to_all | solution.py:169
  239.3 21.0 %all-to-all-start.4 = ((f32[4,108,384]{2,1,0:T(8,128)}), f32[4,108,384]{2,1,0:T(8,128)S(1)}, u32[]{:S(2)}, u32[]{:S(2)}) async-start(f32[4,108,384]{2,1,0:T(8,128)} %reshape.42), calls=%async_computation.4 | async-start | bytes 1376256 | tf_op jit(solution)/shard_map/all_to_all | solution.py:169
  260.2 20.9 %all-to-all-start.1 = ((f32[4,108,384]{2,1,0:T(8,128)}), f32[4,108,384]{2,1,0:T(8,128)S(1)}, u32[]{:S(2)}, u32[]{:S(2)}) async-start(f32[4,108,384]{2,1,0:T(8,128)} %reshape.40), calls=%async_computation.1 | async-start | bytes 1376256 | tf_op jit(solution)/shard_map/all_to_all | solution.py:169
  282.1 20.9 %all-to-all-start.8 = ((f32[4,108,384]{2,1,0:T(8,128)}), f32[4,108,384]{2,1,0:T(8,128)S(1)}, u32[]{:S(2)}, u32[]{:S(2)}) async-start(f32[4,108,384]{2,1,0:T(8,128)} %broadcast_in_dim.8), calls=%async_computation.8 | async-start | bytes 1376256 | tf_op jit(solution)/shard_map/all_to_all | solution.py:171
  285.6 43.8 %copy-start.2 = (bf16[384,1024]{1,0:T(8,128)(2,1)S(1)}, bf16[384,1024]{1,0:T(8,128)(2,1)}, u32[]{:S(2)}) copy-start(bf16[384,1024]{1,0:T(8,128)(2,1)} %fusion.g_ref) | copy-start | bytes 2359300
  304.0 20.9 %all-to-all-start.5 = ((f32[4,108,384]{2,1,0:T(8,128)}), f32[4,108,384]{2,1,0:T(8,128)S(1)}, u32[]{:S(2)}, u32[]{:S(2)}) async-start(f32[4,108,384]{2,1,0:T(8,128)} %broadcast_in_dim.7), calls=%async_computation.5 | async-start | bytes 1376256 | tf_op jit(solution)/shard_map/all_to_all | solution.py:171
  325.9 42.6 %all-to-all-start.2 = ((f32[4,108,384]{2,1,0:T(8,128)}), f32[4,108,384]{2,1,0:T(8,128)S(1)}, u32[]{:S(2)}, u32[]{:S(2)}) async-start(f32[4,108,384]{2,1,0:T(8,128)} %broadcast_in_dim.6), calls=%async_computation.2 | async-start | bytes 1376256 | tf_op jit(solution)/shard_map/all_to_all | solution.py:171
  329.3 168.3 %all-reduce.2.cloned.1.call-start = ((), (), s32[]{:S(2)}) async-start(), calls=%async_computation.10 | async-start | bytes 1327104 | tf_op jit(solution)/shard_map/psum | solution.py:204
  329.4 15.8 %collective-permute-start.4 = (bf16[384,256]{1,0:T(8,128)(2,1)S(1)}, bf16[384,256]{1,0:T(8,128)(2,1)S(1)}, u32[]{:S(2)}, u32[]{:S(2)}) collective-permute-start(bf16[384,256]{1,0:T(8,128)(2,1)S(1)} %slice.39), channel_id=1, source_target_pairs={{1,0},{2,1},{3,2},{5,4},{6,5},{7,6},{9,8},{10,9},{11,10},{13,12},{... | collective-permute-start | bytes 589832 | tf_op jit(solution)/shard_map/ppermute | solution.py:19
  368.5 131.2 %copy-start.1 = (bf16[1,8,8,32,16]{3,4,2,1,0:T(8,128)(2,1)S(1)}, bf16[1,8,8,32,16]{3,4,2,1,0:T(8,128)(2,1)}, u32[]{:S(2)}) copy-start(bf16[1,8,8,32,16]{3,4,2,1,0:T(8,128)(2,1)} %param.5) | copy-start | bytes 196612
Sparse Core Ops, SparseCore 0:
  9.9 55.2 all-gather.1
  368.4 129.1 all-reduce.1

commit v2 on v1

--- a/solution.py
+++ b/solution.py
@@ -9,7 +9,7 @@
 
 F32 = jnp.float32
 BF16 = jnp.bfloat16
-CHUNKS = 3
+F16 = jnp.float16
 VMEM = 56 * 1024 * 1024
 
 
@@ -17,6 +17,14 @@
     devices = range(lax.axis_size(axis))
     route = [(i - distance, i) for i in devices if i - distance in devices]
     return lax.ppermute(block, axis, route)
+
+
+def swapped(block):
+    return lax.ppermute(block, "clip", [(i, i ^ 1) for i in range(lax.axis_size("clip"))])
+
+
+def padded(rows):
+    return (rows // 16 + 1) * 16
 
 
 def shifted(x, row_off, col_off, rows, cols):
@@ -33,7 +41,7 @@
     return lax.dot_general(left, right, (dims, ((), ())), preferred_element_type=F32)
 
 
-def front_kernel(crop_ref, w_ref, patch_ref, z_ref, taps_ref, full_ref, *, rows, cols):
+def front_kernel(crop_ref, w_ref, patch_ref, z_ref, taps_ref, top_ref, full_ref, *, rows, cols):
     plane = rows * cols
     lat = crop_ref.shape[0]
     count = patch_ref.shape[1]
@@ -52,6 +60,7 @@
     z = contract(w_ref[...], full_ref[...], ((0,), (0,)))
     z_ref[...] = z[:, 2 * plane :]
     act = (z * (1.0 / (1.0 + jnp.exp(-z)))).astype(BF16).astype(F32)
+    top_ref[...] = jnp.broadcast_to(jnp.max(jnp.abs(act), axis=1, keepdims=True), top_ref.shape)
     for spot in range(9):
         moved = shifted(act, spot // 3 - 1, spot % 3 - 1, rows, cols).astype(BF16)
         for depth in range(3):
@@ -74,11 +83,13 @@
             pl.BlockSpec((depth_in, count), lambda i: (0, 0)),
             pl.BlockSpec((block, count), lambda i: (i, 0)),
             pl.BlockSpec((27, block, count), lambda i: (0, i, 0)),
+            pl.BlockSpec((block, 128), lambda i: (i, 0)),
         ],
         out_shape=[
             jax.ShapeDtypeStruct((depth_in, count), BF16),
             jax.ShapeDtypeStruct((chans, count), F32),
             jax.ShapeDtypeStruct((27, chans, count), BF16),
+            jax.ShapeDtypeStruct((chans, 128), F32),
         ],
         scratch_shapes=[pltpu.VMEM((depth_in, count + 2 * plane), BF16)],
         compiler_params=pltpu.CompilerParams(vmem_limit_bytes=VMEM),
@@ -86,30 +97,39 @@
     )(crop_t, w_in)
 
 
-def grad_kernel(order_ref, taps_ref, g_ref, out_ref):
-    out_ref[0] = contract(taps_ref[...], g_ref[...], ((1,), (1,)))
+def grad_kernel(order_ref, *refs):
+    out_ref = refs[-1]
+    blocks = out_ref.shape[0]
+    rows = refs[0].shape[0]
+    for i in range(blocks):
+        total = contract(refs[2 * i][...], refs[2 * blocks][...], ((1,), (1,)))
+        total += contract(refs[2 * i + 1][...], refs[2 * blocks + 1][...], ((1,), (1,)))
+        out_ref[i, :rows, :] = total
 
 
 def grad_chunk(order, taps, g_t, parts, which):
     blocks = order.shape[0]
-    total, count = taps.shape
-    chans = g_t.shape[0]
-    rows = total // blocks // parts
+    total, count = taps[0].shape
+    chans = g_t[0].shape[0]
+    rows = total // (2 * blocks) // parts
+    at_once = 2
+    tap_specs = []
+    for i in range(at_once):
+        spec = pl.BlockSpec((rows, count), lambda s, order, i=i: (order[s * at_once + i] * parts + which, 0))
+        tap_specs += [spec, spec]
+    whole = pl.BlockSpec((chans, count), lambda s, order: (0, 0))
     return pl.pallas_call(
         grad_kernel,
         grid_spec=pltpu.PrefetchScalarGridSpec(
             num_scalar_prefetch=1,
-            grid=(blocks,),
-            in_specs=[
-                pl.BlockSpec((rows, count), lambda i, order: (order[i] * parts + which, 0)),
-                pl.BlockSpec((chans, count), lambda i, order: (0, 0)),
-            ],
-            out_specs=pl.BlockSpec((1, rows, chans), lambda i, order: (i, 0, 0)),
+            grid=(blocks // at_once,),
+            in_specs=tap_specs + [whole, whole],
+            out_specs=pl.BlockSpec((at_once, padded(rows), chans), lambda s, order: (s, 0, 0)),
         ),
-        out_shape=jax.ShapeDtypeStruct((blocks, rows, chans), F32),
+        out_shape=jax.ShapeDtypeStruct((blocks, padded(rows), chans), F32),
         compiler_params=pltpu.CompilerParams(vmem_limit_bytes=VMEM),
         name="grad",
-    )(order, taps, g_t)
+    )(order, *(list(taps) * at_once), *g_t)
 
 
 def back_kernel(g_ref, w_ref, z_ref, patch_ref, out_ref, acc_ref, *, rows, cols):
@@ -157,18 +177,52 @@
     )(g_ext, w_taps, z_t, patch_t)
 
 
-def reduced(part):
-    half = part.shape[0] // 2
+def packed(x, rows, bound):
+    power = jnp.ceil(jnp.log2(jnp.maximum(bound, 1e-30)))
+    row = lax.broadcasted_iota(jnp.int32, x.shape, 1)
+    return jnp.where(row < rows, x * jnp.exp2(14.0 - power), power).astype(F16)
+
+
+def unpacked(x, rows):
+    power = x[:, rows : rows + 1, :1].astype(F32)
+    return x[:, :rows].astype(F32) * jnp.exp2(power - 14.0), jnp.sum(jnp.exp2(power[:, 0, 0]))
+
+
+def across_plane(part, rows, bound):
     clips = lax.axis_size("clip")
-    swap = [(i, i ^ 1) for i in range(clips)]
-    mine = part[half:] + lax.ppermute(part[:half], "clip", swap)
-    groups = [[2 * p + core for p in range(half)] for core in range(2)]
-    block = lax.all_to_all(mine, "clip", 0, 0, axis_index_groups=groups, tiled=True).sum(axis=0)
-    depth = lax.axis_size("tm")
-    rows, chans = block.shape
-    piece = lax.all_to_all(block.reshape(depth, rows // depth, chans), "tm", 0, 0, tiled=True).sum(axis=0)
-    spread = jnp.broadcast_to(piece[None], (depth,) + piece.shape)
-    return lax.all_to_all(spread, "tm", 0, 0, tiled=True).reshape(rows, chans)
+    groups = [[2 * p + core for p in range(clips // 2)] for core in range(2)]
+    return lax.all_to_all(packed(part, rows, bound), "clip", 0, 0, axis_index_groups=groups, tiled=True)
+
+
+def to_depth(pieces, rows, bound):
+    extra = padded(rows) - rows
+    return lax.all_to_all(packed(jnp.pad(pieces, ((0, 0), (0, extra), (0, 0))), rows, bound), "tm", 0, 0, tiled=True)
+
+
+def across_depth(got, rows):
+    terms, bound = unpacked(got, rows)
+    block = terms.sum(axis=0)
+    depth = lax.axis_size("tm")
+    chans = block.shape[1]
+    small = rows // depth
+    return to_depth(block.reshape(depth, small, chans), small, bound)
+
+
+def spread(got, small):
+    terms, bound = unpacked(got, small)
+    piece = terms.sum(axis=0)
+    depth = lax.axis_size("tm")
+    return to_depth(jnp.broadcast_to(piece[None], (depth,) + piece.shape), small, bound)
+
+
+def everywhere(part):
+    clips = lax.axis_size("clip")
+    depth = lax.axis_size("tm")
+    rows, chans = part.shape
+    mine = lax.all_to_all(part.reshape(clips, rows // clips, chans), "clip", 0, 0, tiled=True).sum(axis=0)
+    mine = lax.all_to_all(jnp.broadcast_to(mine[None], (depth,) + mine.shape), "tm", 0, 0, tiled=True).sum(axis=0)
+    mine = lax.all_to_all(jnp.broadcast_to(mine[None], (clips,) + mine.shape), "clip", 0, 0, tiled=True)
+    return mine.reshape(rows, chans)
 
 
 def shards(latent, offsets, teacher, w_in, w_mid):
@@ -186,22 +240,36 @@
     crop = lax.dynamic_slice_in_dim(latent[0], offsets[0], cols, axis=2).reshape(count, lat_chans).T
     earlier = passed_along(crop[:, count - 4 * plane :], "tm", 1)
     crop_ext = jnp.concatenate([earlier, crop], axis=1)
-    patch_t, z_t, taps = front(crop_ext, w_in, rows, cols, count)
+    patch_t, z_t, taps, top = front(crop_ext, w_in, rows, cols, count)
     taps = taps.reshape(27 * chans, count)
+    _, _, pair_taps, pair_top = front(swapped(crop_ext), w_in, rows, cols, count)
+    pair_taps = pair_taps.reshape(27 * chans, count)
     teacher_t = teacher[0].reshape(count, chans).T.astype(F32)
     h_t = contract(w_full, taps, ((0,), (0,)))
     g_t = ((h_t - teacher_t) * scale).astype(BF16)
+    pair_g = swapped(g_t)
     later = passed_along(g_t[:, : 2 * plane], "tm", -1)
-    g_ext = jnp.concatenate([g_t, later], axis=1)
 
     core = lax.axis_index("clip") % 2
-    even = 2 * jnp.arange(clips // 2, dtype=jnp.int32)
-    order = jnp.concatenate([even + 1 - core, even + core])
-    parts = [grad_chunk(order, taps, g_t, CHUNKS, j) for j in range(CHUNKS)]
+    order = 2 * jnp.arange(clips // 2, dtype=jnp.int32) + core
+    depth = lax.axis_size("tm")
+    block_rows = 27 * chans // clips
+    chunks = next(c for c in (2, 3, 1) if block_rows % (8 * c) == 0 and block_rows % (depth * c) == 0)
+    part_rows = block_rows // chunks
+    parts = [grad_chunk(order, (taps, pair_taps), (g_t, pair_g), chunks, j) for j in range(chunks)]
+    size = jnp.max(jnp.sum(jnp.abs(g_t.astype(F32)), axis=1))
+    pair_size = jnp.max(jnp.sum(jnp.abs(pair_g.astype(F32)), axis=1))
+    bound = (jnp.max(top) * size + jnp.max(pair_top) * pair_size) * 1.01
+    g_ext, _ = lax.optimization_barrier((jnp.concatenate([g_t, later], axis=1), parts[1]))
     in_part = back(g_ext, w_full.reshape(3, 9, chans, chans), z_t, patch_t, rows, cols)
-    done = [reduced(part) for part in parts]
+    plane_got = [across_plane(part, part_rows, bound) for part in parts]
+    plane_got[0], in_part = lax.optimization_barrier((plane_got[0], in_part))
+    depth_got = [across_depth(got, part_rows) for got in plane_got]
+    grad_in = everywhere(in_part)
+    small = part_rows // depth
+    last_got = [spread(got, small) for got in depth_got]
+    done = [unpacked(got, small)[0].reshape(part_rows, chans) for got in last_got]
     grad_mid = jnp.concatenate(done, axis=0)
-    grad_in = lax.psum(in_part, ("clip", "tm"))
     return (grad_mid, grad_in)
 
 

time: 509 us -> 317 us (0.62)
  waiting for transfers between devices: 326 us -> 95 us
  blocking collectives: 0 us -> 43.2 us
  local copies, waits for them, and re-layouts: 20 us -> 8.05 us
  between operations: 15 us -> 20.6 us
    psum x1 -> x0, waiting for transfers between devices: 128 us -> none  [shards(): grad_in = lax.psum(in_part, ('clip', 'tm'))]
    all_to_all x9 -> x7, waiting for transfers between devices: 145 us -> 47.8 us  [the longest x3 32.2 us: to_depth(): lax.all_to_all(packed(jnp.pad(pieces, ((0, 0), (0, extra), (0, 0))), rows...]
    all_to_all x0 -> x2, blocking collectives: none -> 43.2 us  [the longest x1 28.6 us: across_plane(): lax.all_to_all(packed(part, rows, bound), 'clip', 0, 0, axis_index_groups...]
    add x3 -> x1, other arithmetic: 11.3 us -> 0.52 us  [shards(): order = 2 * jnp.arange(clips // 2, dtype=jnp.int32) + core]
    pallas_call x1 -> x2, Pallas kernels: 10.6 us -> 21.3 us  [front(): pl.pallas_call(lambda *refs: front_kernel(*refs, rows=rows, cols=cols), g...]
    pallas_call x3 -> x2, Pallas kernels: 32.4 us -> 23.1 us  [grad_chunk(): pl.pallas_call(grad_kernel, grid_spec=pltpu.PrefetchScalarGridSpec(num_sc...]
    slice x3 -> x0, local copies, waits for them, and re-layouts: 8.98 us -> none  [reduced(): mine = part[half:] + lax.ppermute(part[:half], 'clip', swap)]
    convert_element_type x0 -> x4, other arithmetic: none -> 7.68 us  [packed(): return jnp.where(row < rows, x * jnp.exp2(14.0 - power), power).astype(F16)]
  transfers between devices with their start and end apart: 16 -> 12, of which waited for: 12 -> 10; matrix products, arithmetic and copies ran while one was open for 7% -> 8% of each run, Pallas kernels for 11% -> 14%
where the time goes in v2:
time: 317 us; the launch traced here: 315 us
  waiting for transfers between devices  95 us (30%)
  Pallas kernels  66.4 us (21%)
  blocking collectives  43.2 us (14%)
  starting transfers between devices  40.6 us (13%)
  other arithmetic  26 us (8%)
  between operations  20.6 us (6%)
  matrix products  15.2 us (5%)
  local copies, waits for them, and re-layouts  8.05 us (3%)
    all_gather x1, waiting for transfers between devices, shards(): w_full = lax.all_gather(w_mid, 'clip', axis=0, tiled=True)  38.4 us
    all_to_all x3, waiting for transfers between devices, to_depth(): lax.all_to_all(packed(jnp.pad(pieces, ((0, 0), (0, extra), (0, 0))), rows...  32.2 us
    all_to_all x1, blocking collectives, across_plane(): lax.all_to_all(packed(part, rows, bound), 'clip', 0, 0, axis_index_groups...  28.6 us
    pallas_call x2, Pallas kernels, grad_chunk(): pl.pallas_call(grad_kernel, grid_spec=pltpu.PrefetchScalarGridSpec(num_sc...  23.1 us
    pallas_call x1, Pallas kernels, back(): pl.pallas_call(lambda *refs: back_kernel(*refs, rows=rows, cols=cols), gr...  22 us
    pallas_call x2, Pallas kernels, front(): pl.pallas_call(lambda *refs: front_kernel(*refs, rows=rows, cols=cols), g...  21.3 us
    dot_general x1, matrix products, contract(): lax.dot_general(left, right, (dims, ((), ())), preferred_element_type=F32)  15.2 us
    all_to_all x1, blocking collectives, to_depth(): lax.all_to_all(packed(jnp.pad(pieces, ((0, 0), (0, extra), (0, 0))), rows...  14.6 us
  transfers between devices with their start and end apart: 12, of which 10 were waited for; matrix products, arithmetic and copies ran while one was open for 8% of the time, Pallas kernels for 14%

profile of v2, /device:TPU:0, one launch (start us, length us, event | category | flops | bytes accessed | tf_op | source)
XLA Modules:
  0.0 315.1 jit_solution(17529425704248957704)
XLA Ops:
  9.1 4.9 %collective-permute-start = (bf16[16,512]{1,0:T(8,128)(2,1)S(1)}, bf16[16,512]{1,0:T(8,128)(2,1)S(1)}, u32[]{:S(2)}, u32[]{:S(2)}) collective-permute-start(bf16[16,512]{1,0:T(8,128)(2,1)S(1)} %slice.56), channel_id=1, source_target_pairs={{0,1},{1,2},{2,3},{4,5},{5,6},{6,7},{8,9},{9,10},{10,11},{12,13},{... | collective-permute-start | bytes 49160 | tf_op jit(solution)/shard_map/ppermute | solution.py:19
  16.1 10.7 %front.2 = (bf16[432,1024]{1,0:T(8,128)(2,1)}, f32[384,1024]{1,0:T(8,128)}, bf16[27,384,1024]{2,1,0:T(8,128)(2,1)}, f32[384,128]{1,0:T(8,128)}) custom-call(bf16[16,1536]{1,0:T(8,128)(2,1)} %pad_maximum_fusion.2.refs_0_, bf16[432,384]{1,0:T(8,128)(2,1)} %refs_1_.3), custom_call_target="tpu_custom_call" | custom-call | tf_op jit(solution)/shard_map/front/pallas_call | solution.py:75
  26.8 38.4 %all-gather.2.cloned.1.call-done = bf16[10368,384]{1,0:T(8,128)(2,1)} async-done(((bf16[1296,384]{1,0:T(8,128)(2,1)}), bf16[10368,384]{1,0:T(8,128)(2,1)}) %all-gather.2.cloned.1.call-update) | async-done | bytes 7962640 | tf_op jit(solution)/shard_map/all_gather | solution.py:239
  65.3 15.2 %abs_reduce_fusion.1 = (f32[384]{0:T(512)S(1)}, bf16[384,1024]{1,0:T(8,128)(2,1)S(1)}) fusion(f32[1024,384]{0,1:T(8,128)S(1)} %copy.18, bf16[10368,1024]{1,0:T(8,128)(2,1)} %bitcast.19, bf16[10368,384]{1,0:T(8,128)(2,1)} %all-gather.2.cloned.1.call-done), kind=kOutput, calls=%fused_computation.6 | convolution fusion | flops 8156085760 | bytes 31557120 | tf_op jit(solution)/shard_map/dot_general | solution.py:41
  83.5 10.6 %front.3 = (bf16[432,1024]{1,0:T(8,128)(2,1)}, f32[384,1024]{1,0:T(8,128)}, bf16[27,384,1024]{2,1,0:T(8,128)(2,1)}, f32[384,128]{1,0:T(8,128)}) custom-call(bf16[16,1536]{1,0:T(8,128)(2,1)} %copy-done.9, bf16[432,384]{1,0:T(8,128)(2,1)} %refs_1_.3), custom_call_target="tpu_custom_call" | custom-call | tf_op jit(solution)/shard_map/front/pallas_call | solution.py:75
  94.1 1.6 reduce_max.38
  99.8 11.3 %grad.2 = f32[4,656,384]{2,1,0:T(8,128)} custom-call(s32[4]{0:T(128)} %multiply_add_fusion.order_ref, bf16[10368,1024]{1,0:T(8,128)(2,1)} %bitcast.20, bf16[10368,1024]{1,0:T(8,128)(2,1)} %bitcast.24, bf16[10368,1024]{1,0:T(8,128)(2,1)} %bitcast.21, bf16[10368,1024]{1,0:T(8,128)(2,1)} %bitcast.25, bf16[384,1024]{1,0:T(8,128)(2,1)} %copy-done.3, ...), custom_call_target="tpu_custom_call" | custom-call | tf_op jit(solution)/shard_map/grad/pallas_call | solution.py:121
  111.1 11.8 %grad.3 = f32[4,656,384]{2,1,0:T(8,128)} custom-call(s32[4]{0:T(128)} %multiply_add_fusion.order_ref, bf16[10368,1024]{1,0:T(8,128)(2,1)} %bitcast.22, bf16[10368,1024]{1,0:T(8,128)(2,1)} %bitcast.26, bf16[10368,1024]{1,0:T(8,128)(2,1)} %bitcast.23, bf16[10368,1024]{1,0:T(8,128)(2,1)} %bitcast.27, bf16[384,1024]{1,0:T(8,128)(2,1)} %copy-done.3, ...), custom_call_target="tpu_custom_call" | custom-call | tf_op jit(solution)/shard_map/grad/pallas_call | solution.py:121
  123.0 4.6 %select_convert_fusion.1 = (f16[4,656,384]{2,1,0:T(8,128)(2,1)S(1)}, f16[4,656,384]{2,1,0:T(8,128)(2,1)}) fusion(f32[4,656,384]{2,1,0:T(8,128)S(1)} %copy-done.2, f32[]{:T(128)S(6)} %ceil.16, f32[]{:T(128)S(6)} %exp2.101, pred[656]{0:T(1024)(128)(4,1)S(1)} %iota_compare_fusion, f32[4,656,384]{2,1,0:T(8,128)} %grad.3), kind=kLoop, calls=%fused_computation.1 | loop fusion | flops 6045696 | bytes 12092056 | tf_op jit(solution)/shard_map/convert_element_type | solution.py:183
  127.5 28.6 %all_to_all.45 = f16[4,656,384]{2,1,0:T(8,128)(2,1)} all-to-all(f16[4,656,384]{2,1,0:T(8,128)(2,1)S(1)} %get-tuple-element.28), channel_id=1, replica_groups={{0,8,16,24},{4,12,20,28},{1,9,17,25},{5,13,21,29},{2,10,18,26},{6,14,22..., dimensions={0} | all-to-all | bytes 4030464 | tf_op jit(solution)/shard_map/all_to_all | solution.py:194
  156.2 3.7 %all-to-all-start.3 = ((f16[4,656,384]{2,1,0:T(8,128)(2,1)}), f16[4,656,384]{2,1,0:T(8,128)(2,1)S(1)}, u32[]{:S(2)}, u32[]{:S(2)}) async-start(f16[4,656,384]{2,1,0:T(8,128)(2,1)} %get-tuple-element.29), calls=%async_computation.3 | async-start | bytes 4030464 | tf_op jit(solution)/shard_map/all_to_all | solution.py:194
  161.3 6.7 %collective-permute-done.3 = bf16[384,256]{1,0:T(8,128)(2,1)S(1)} collective-permute-done((bf16[384,256]{1,0:T(8,128)(2,1)S(1)}, bf16[384,256]{1,0:T(8,128)(2,1)S(1)}, u32[]{:S(2)}, u32[]{:S(2)}) %collective-permute-start.3) | collective-permute-done | bytes 196640 | tf_op jit(solution)/shard_map/ppermute | solution.py:19
  169.0 22.0 %back.1 = f32[432,384]{1,0:T(8,128)} custom-call(bf16[384,1280]{1,0:T(8,128)(2,1)} %pad_maximum_fusion.1.refs_0_, bf16[3,9,384,384]{3,2,1,0:T(8,128)(2,1)} %bitcast.28, f32[384,1024]{1,0:T(8,128)} %get-tuple-element.16.refs_2_, bf16[432,1024]{1,0:T(8,128)(2,1)} %get-tuple-element.17.refs_3_), custom_call_target="tpu_custom_call" | custom-call | tf_op jit(solution)/shard_map/back/pallas_call | solution.py:163
  191.0 2.0 reshape.62
  193.0 4.2 %all-to-all-start.6 = ((f32[8,54,384]{2,1,0:T(8,128)}), f32[8,54,384]{2,1,0:T(8,128)}, u32[]{:S(2)}, u32[]{:S(2)}) async-start(f32[8,54,384]{2,1,0:T(8,128)} %reshape.62), calls=%async_computation.6 | async-start | bytes 1376256 | tf_op jit(solution)/shard_map/all_to_all | solution.py:222
  197.3 1.4 exponential_reduce_fusion.6
  198.7 3.1 multiply_reduce_fusion.1
  201.8 1.3 reshape.58
  204.8 3.9 %all-to-all-done.6 = f32[8,54,384]{2,1,0:T(8,128)} async-done(((f32[8,54,384]{2,1,0:T(8,128)}), f32[8,54,384]{2,1,0:T(8,128)}, u32[]{:S(2)}, u32[]{:S(2)}) %all-to-all-start.6) | async-done | bytes 663584 | tf_op jit(solution)/shard_map/all_to_all | solution.py:222
  208.8 4.1 %all-to-all-start.1 = ((f16[4,176,384]{2,1,0:T(8,128)(2,1)}), f16[4,176,384]{2,1,0:T(8,128)(2,1)}, u32[]{:S(2)}, u32[]{:S(2)}) async-start(f16[4,176,384]{2,1,0:T(8,128)(2,1)} %select_convert_fusion.5), calls=%async_computation.1 | async-start | bytes 1081344 | tf_op jit(solution)/shard_map/all_to_all | solution.py:199
  216.1 9.1 %all-to-all-done.1 = f16[4,176,384]{2,1,0:T(8,128)(2,1)} async-done(((f16[4,176,384]{2,1,0:T(8,128)(2,1)}), f16[4,176,384]{2,1,0:T(8,128)(2,1)}, u32[]{:S(2)}, u32[]{:S(2)}) %all-to-all-start.1) | async-done | bytes 540704 | tf_op jit(solution)/shard_map/all_to_all | solution.py:199
  225.9 3.5 %all-to-all-start.7 = ((f32[4,54,384]{2,1,0:T(8,128)}), f32[4,54,384]{2,1,0:T(8,128)S(1)}, u32[]{:S(2)}, u32[]{:S(2)}) async-start(f32[4,54,384]{2,1,0:T(8,128)} %broadcast_in_dim.49), calls=%async_computation.7 | async-start | bytes 688128 | tf_op jit(solution)/shard_map/all_to_all | solution.py:223
  229.3 1.4 exponential_reduce_fusion.4
  234.0 2.8 all-to-all-done.7
  236.8 14.6 %all_to_all.46 = f16[4,176,384]{2,1,0:T(8,128)(2,1)S(1)} all-to-all(f16[4,176,384]{2,1,0:T(8,128)(2,1)S(1)} %get-tuple-element.31), channel_id=1, replica_groups=mesh['clip'=8,'tm'=4] {'tm'}, dimensions={0} | all-to-all | bytes 1081344 | tf_op jit(solution)/shard_map/all_to_all | solution.py:199
  251.3 3.5 %all-to-all-start.2 = ((f16[4,176,384]{2,1,0:T(8,128)(2,1)}), f16[4,176,384]{2,1,0:T(8,128)(2,1)S(1)}, u32[]{:S(2)}, u32[]{:S(2)}) async-start(f16[4,176,384]{2,1,0:T(8,128)(2,1)} %get-tuple-element.30), calls=%async_computation.2 | async-start | bytes 1081344 | tf_op jit(solution)/shard_map/all_to_all | solution.py:199
  254.8 12.1 %all-to-all-done.2 = f16[4,176,384]{2,1,0:T(8,128)(2,1)S(1)} async-done(((f16[4,176,384]{2,1,0:T(8,128)(2,1)}), f16[4,176,384]{2,1,0:T(8,128)(2,1)S(1)}, u32[]{:S(2)}, u32[]{:S(2)}) %all-to-all-start.2) | async-done | bytes 540704 | tf_op jit(solution)/shard_map/all_to_all | solution.py:199
  267.9 11.3 %all-to-all-start.8 = ((f32[8,54,384]{2,1,0:T(8,128)}), f32[8,54,384]{2,1,0:T(8,128)S(1)}, u32[]{:S(2)}, u32[]{:S(2)}) async-start(f32[8,54,384]{2,1,0:T(8,128)} %broadcast_in_dim.50), calls=%async_computation.8 | async-start | bytes 1376256 | tf_op jit(solution)/shard_map/all_to_all | solution.py:224
  281.8 8.9 %all-to-all-done.8 = f32[8,54,384]{2,1,0:T(8,128)S(1)} async-done(((f32[8,54,384]{2,1,0:T(8,128)}), f32[8,54,384]{2,1,0:T(8,128)S(1)}, u32[]{:S(2)}, u32[]{:S(2)}) %all-to-all-start.8) | async-done | bytes 663584 | tf_op jit(solution)/shard_map/all_to_all | solution.py:224
  290.7 3.5 %all-to-all-start.5 = ((f16[4,176,384]{2,1,0:T(8,128)(2,1)}), f16[4,176,384]{2,1,0:T(8,128)(2,1)S(1)}, u32[]{:S(2)}, u32[]{:S(2)}) async-start(f16[4,176,384]{2,1,0:T(8,128)(2,1)} %select_convert_fusion.2), calls=%async_computation.5 | async-start | bytes 1081344 | tf_op jit(solution)/shard_map/all_to_all | solution.py:199
  295.5 11.0 %all-to-all-done.5 = f16[4,176,384]{2,1,0:T(8,128)(2,1)S(1)} async-done(((f16[4,176,384]{2,1,0:T(8,128)(2,1)}), f16[4,176,384]{2,1,0:T(8,128)(2,1)S(1)}, u32[]{:S(2)}, u32[]{:S(2)}) %all-to-all-start.5) | async-done | bytes 540704 | tf_op jit(solution)/shard_map/all_to_all | solution.py:199
  306.9 1.4 pad_maximum_fusion
  (67 shorter events, 21.2 us)
Async XLA Ops:
  7.2 1.4 copy-start
  7.2 6.9 %copy-start.6 = (bf16[1,8,8,16,384]{4,3,2,1,0:T(8,128)(2,1)S(1)}, bf16[1,8,8,16,384]{4,3,2,1,0:T(8,128)(2,1)}, u32[]{:S(2)}) copy-start(bf16[1,8,8,16,384]{4,3,2,1,0:T(8,128)(2,1)} %param.7) | copy-start | bytes 2359300
  7.2 58.1 %all-gather.2.cloned.1.call-start = ((), (), s32[]{:S(2)}) async-start(), calls=%async_computation.9 | async-start | bytes 8957952 | tf_op jit(solution)/shard_map/all_gather | solution.py:239
  9.1 6.4 %collective-permute-start = (bf16[16,512]{1,0:T(8,128)(2,1)S(1)}, bf16[16,512]{1,0:T(8,128)(2,1)S(1)}, u32[]{:S(2)}, u32[]{:S(2)}) collective-permute-start(bf16[16,512]{1,0:T(8,128)(2,1)S(1)} %slice.56), channel_id=1, source_target_pairs={{0,1},{1,2},{2,3},{4,5},{5,6},{6,7},{8,9},{9,10},{10,11},{12,13},{... | collective-permute-start | bytes 49160 | tf_op jit(solution)/shard_map/ppermute | solution.py:19
  65.2 15.6 %copy-start.7 = (bf16[16,1536]{1,0:T(8,128)(2,1)S(1)}, bf16[16,1536]{1,0:T(8,128)(2,1)}, u32[]{:S(2)}) copy-start(bf16[16,1536]{1,0:T(8,128)(2,1)} %pad_maximum_fusion.2.refs_0_) | copy-start | bytes 147460
  65.3 16.4 %copy-start.8 = (f32[384,128]{1,0:T(8,128)S(1)}, f32[384,128]{1,0:T(8,128)}, u32[]{:S(2)}) copy-start(f32[384,128]{1,0:T(8,128)} %get-tuple-element.13) | copy-start | bytes 589828
  80.5 19.3 %copy-start.3 = (bf16[384,1024]{1,0:T(8,128)(2,1)}, bf16[384,1024]{1,0:T(8,128)(2,1)S(1)}, u32[]{:S(2)}) copy-start(bf16[384,1024]{1,0:T(8,128)(2,1)S(1)} %get-tuple-element.33.refs_4_) | copy-start | bytes 2359300
  80.5 17.1 %collective-permute-start.2 = (bf16[384,1024]{1,0:T(8,128)(2,1)S(1)}, bf16[384,1024]{1,0:T(8,128)(2,1)S(1)}, u32[]{:S(2)}, u32[]{:S(2)}) collective-permute-start(bf16[384,1024]{1,0:T(8,128)(2,1)S(1)} %get-tuple-element.33.refs_4_), channel_id=1, source_target_pairs={{0,4},{4,0},{8,12},{12,8},{16,20},{20,16},{24,28},{28,24},{1,5},{5... | collective-permute-start | bytes 2359304 | tf_op jit(solution)/shard_map/ppermute | solution.py:23
  80.8 2.1 collective-permute-start.1
  82.9 0.6 copy-start.9
  97.6 2.2 copy-start.5
  111.1 11.8 %copy-start.2 = (f32[4,656,384]{2,1,0:T(8,128)S(1)}, f32[4,656,384]{2,1,0:T(8,128)}, u32[]{:S(2)}) copy-start(f32[4,656,384]{2,1,0:T(8,128)} %grad.2) | copy-start | bytes 12091396
  156.2 3.7 %copy-start.4 = (bf16[384,1024]{1,0:T(8,128)(2,1)S(1)}, bf16[384,1024]{1,0:T(8,128)(2,1)}, u32[]{:S(2)}) copy-start(bf16[384,1024]{1,0:T(8,128)(2,1)} %copy-done.3) | copy-start | bytes 2359300
  156.2 36.9 %all-to-all-start.3 = ((f16[4,656,384]{2,1,0:T(8,128)(2,1)}), f16[4,656,384]{2,1,0:T(8,128)(2,1)S(1)}, u32[]{:S(2)}, u32[]{:S(2)}) async-start(f16[4,656,384]{2,1,0:T(8,128)(2,1)} %get-tuple-element.29), calls=%async_computation.3 | async-start | bytes 4030464 | tf_op jit(solution)/shard_map/all_to_all | solution.py:194
  160.0 8.0 %collective-permute-start.3 = (bf16[384,256]{1,0:T(8,128)(2,1)S(1)}, bf16[384,256]{1,0:T(8,128)(2,1)S(1)}, u32[]{:S(2)}, u32[]{:S(2)}) collective-permute-start(bf16[384,256]{1,0:T(8,128)(2,1)S(1)} %slice.57), channel_id=1, source_target_pairs={{1,0},{2,1},{3,2},{5,4},{6,5},{7,6},{9,8},{10,9},{11,10},{13,12},{... | collective-permute-start | bytes 589832 | tf_op jit(solution)/shard_map/ppermute | solution.py:19
  193.0 15.7 %all-to-all-start.6 = ((f32[8,54,384]{2,1,0:T(8,128)}), f32[8,54,384]{2,1,0:T(8,128)}, u32[]{:S(2)}, u32[]{:S(2)}) async-start(f32[8,54,384]{2,1,0:T(8,128)} %reshape.62), calls=%async_computation.6 | async-start | bytes 1376256 | tf_op jit(solution)/shard_map/all_to_all | solution.py:222
  208.8 16.4 %all-to-all-start.1 = ((f16[4,176,384]{2,1,0:T(8,128)(2,1)}), f16[4,176,384]{2,1,0:T(8,128)(2,1)}, u32[]{:S(2)}, u32[]{:S(2)}) async-start(f16[4,176,384]{2,1,0:T(8,128)(2,1)} %select_convert_fusion.5), calls=%async_computation.1 | async-start | bytes 1081344 | tf_op jit(solution)/shard_map/all_to_all | solution.py:199
  225.9 10.9 %all-to-all-start.7 = ((f32[4,54,384]{2,1,0:T(8,128)}), f32[4,54,384]{2,1,0:T(8,128)S(1)}, u32[]{:S(2)}, u32[]{:S(2)}) async-start(f32[4,54,384]{2,1,0:T(8,128)} %broadcast_in_dim.49), calls=%async_computation.7 | async-start | bytes 688128 | tf_op jit(solution)/shard_map/all_to_all | solution.py:223
  251.3 15.6 %all-to-all-start.2 = ((f16[4,176,384]{2,1,0:T(8,128)(2,1)}), f16[4,176,384]{2,1,0:T(8,128)(2,1)S(1)}, u32[]{:S(2)}, u32[]{:S(2)}) async-start(f16[4,176,384]{2,1,0:T(8,128)(2,1)} %get-tuple-element.30), calls=%async_computation.2 | async-start | bytes 1081344 | tf_op jit(solution)/shard_map/all_to_all | solution.py:199
  267.9 22.8 %all-to-all-start.8 = ((f32[8,54,384]{2,1,0:T(8,128)}), f32[8,54,384]{2,1,0:T(8,128)S(1)}, u32[]{:S(2)}, u32[]{:S(2)}) async-start(f32[8,54,384]{2,1,0:T(8,128)} %broadcast_in_dim.50), calls=%async_computation.8 | async-start | bytes 1376256 | tf_op jit(solution)/shard_map/all_to_all | solution.py:224
  290.7 15.8 %all-to-all-start.5 = ((f16[4,176,384]{2,1,0:T(8,128)(2,1)}), f16[4,176,384]{2,1,0:T(8,128)(2,1)S(1)}, u32[]{:S(2)}, u32[]{:S(2)}) async-start(f16[4,176,384]{2,1,0:T(8,128)(2,1)} %select_convert_fusion.2), calls=%async_computation.5 | async-start | bytes 1081344 | tf_op jit(solution)/shard_map/all_to_all | solution.py:199
  306.7 1.5 copy-start.1
Sparse Core Ops, SparseCore 0:
  9.9 55.2 all-gather.1

commit v3 on v2

--- a/solution.py
+++ b/solution.py
@@ -23,8 +23,12 @@
     return lax.ppermute(block, "clip", [(i, i ^ 1) for i in range(lax.axis_size("clip"))])
 
 
+def piece_rows(rows):
+    return rows // lax.axis_size("tm") // 16 * 16 + 16
+
+
 def padded(rows):
-    return (rows // 16 + 1) * 16
+    return piece_rows(rows) * lax.axis_size("tm") + 16
 
 
 def shifted(x, row_off, col_off, rows, cols):
@@ -105,6 +109,7 @@
         total = contract(refs[2 * i][...], refs[2 * blocks][...], ((1,), (1,)))
         total += contract(refs[2 * i + 1][...], refs[2 * blocks + 1][...], ((1,), (1,)))
         out_ref[i, :rows, :] = total
+        out_ref[i, rows:, :] = jnp.zeros((out_ref.shape[1] - rows, out_ref.shape[2]), F32)
 
 
 def grad_chunk(order, taps, g_t, parts, which):
@@ -179,40 +184,71 @@
 
 def packed(x, rows, bound):
     power = jnp.ceil(jnp.log2(jnp.maximum(bound, 1e-30)))
-    row = lax.broadcasted_iota(jnp.int32, x.shape, 1)
+    row = lax.broadcasted_iota(jnp.int32, x.shape, 0)
     return jnp.where(row < rows, x * jnp.exp2(14.0 - power), power).astype(F16)
 
 
-def unpacked(x, rows):
-    power = x[:, rows : rows + 1, :1].astype(F32)
-    return x[:, :rows].astype(F32) * jnp.exp2(power - 14.0), jnp.sum(jnp.exp2(power[:, 0, 0]))
-
-
-def across_plane(part, rows, bound):
+def power_of(x, rows):
+    return jnp.exp2(x[rows, 0].astype(F32))
+
+
+def across_plane(part, rows, bound, after):
     clips = lax.axis_size("clip")
-    groups = [[2 * p + core for p in range(clips // 2)] for core in range(2)]
-    return lax.all_to_all(packed(part, rows, bound), "clip", 0, 0, axis_index_groups=groups, tiled=True)
-
-
-def to_depth(pieces, rows, bound):
-    extra = padded(rows) - rows
-    return lax.all_to_all(packed(jnp.pad(pieces, ((0, 0), (0, extra), (0, 0))), rows, bound), "tm", 0, 0, tiled=True)
-
-
-def across_depth(got, rows):
-    terms, bound = unpacked(got, rows)
-    block = terms.sum(axis=0)
-    depth = lax.axis_size("tm")
-    chans = block.shape[1]
-    small = rows // depth
-    return to_depth(block.reshape(depth, small, chans), small, bound)
-
-
-def spread(got, small):
-    terms, bound = unpacked(got, small)
-    piece = terms.sum(axis=0)
-    depth = lax.axis_size("tm")
-    return to_depth(jnp.broadcast_to(piece[None], (depth,) + piece.shape), small, bound)
+    payloads = [packed(part[q], rows, bound) for q in range(1, clips // 2)]
+    payloads, after = lax.optimization_barrier((payloads, after))
+    got = []
+    for q in range(1, clips // 2):
+        route = [(i, i ^ (2 * q)) for i in range(clips)]
+        got.append(lax.ppermute(payloads[q - 1], "clip", route))
+    return (part[0], got), after
+
+
+def around(blocks, distance):
+    depth = lax.axis_size("tm")
+    return lax.ppermute(blocks, "tm", [(i, (i + distance) % depth) for i in range(depth)])
+
+
+def across_depth(own, got, rows, bound):
+    depth = lax.axis_size("tm")
+    me = lax.axis_index("tm")
+    small = piece_rows(rows)
+    powers = [power_of(x, rows) for x in got]
+    total = (bound + sum(powers)) * 1.01
+
+    def piece(place):
+        first = place * small
+        terms = lax.dynamic_slice_in_dim(own, first, small + 16, axis=0)
+        for x, power in zip(got, powers):
+            terms = terms + lax.dynamic_slice_in_dim(x, first, small + 16, axis=0).astype(F32) * (power * 2.0**-14)
+        return terms
+
+    others = [around(packed(piece((me + d) % depth), small, total), d) for d in range(1, depth)]
+    return piece(me), others, total
+
+
+def spread(own, got, small, bound):
+    depth = lax.axis_size("tm")
+    powers = [power_of(x, small) for x in got]
+    total = (bound + sum(powers)) * 1.01
+    for x, power in zip(got, powers):
+        own = own + x.astype(F32) * (power * 2.0**-14)
+    payload = packed(own, small, total)
+    return [payload] + [around(payload, depth - k) for k in range(1, depth)]
+
+
+def assembled(pieces, small, rows):
+    depth = lax.axis_size("tm")
+    me = lax.axis_index("tm")
+    out = []
+    for place in range(depth):
+        x = pieces[0]
+        for k in range(1, depth):
+            x = jnp.where((me + k) % depth == place, pieces[k], x)
+        count = min(small, rows - place * small)
+        if count <= 0:
+            break
+        out.append(x[:count].astype(F32) * (power_of(x, small) * 2.0**-14))
+    return out
 
 
 def everywhere(part):
@@ -245,32 +281,37 @@
     _, _, pair_taps, pair_top = front(swapped(crop_ext), w_in, rows, cols, count)
     pair_taps = pair_taps.reshape(27 * chans, count)
     teacher_t = teacher[0].reshape(count, chans).T.astype(F32)
+    w_full, pair_taps, pair_top = lax.optimization_barrier((w_full, pair_taps, pair_top))
     h_t = contract(w_full, taps, ((0,), (0,)))
     g_t = ((h_t - teacher_t) * scale).astype(BF16)
     pair_g = swapped(g_t)
     later = passed_along(g_t[:, : 2 * plane], "tm", -1)
 
-    core = lax.axis_index("clip") % 2
-    order = 2 * jnp.arange(clips // 2, dtype=jnp.int32) + core
-    depth = lax.axis_size("tm")
+    order = lax.axis_index("clip") ^ (2 * jnp.arange(clips // 2, dtype=jnp.int32))
     block_rows = 27 * chans // clips
-    chunks = next(c for c in (2, 3, 1) if block_rows % (8 * c) == 0 and block_rows % (depth * c) == 0)
+    chunks = next(c for c in (2, 3, 1) if block_rows % (8 * c) == 0)
     part_rows = block_rows // chunks
-    parts = [grad_chunk(order, (taps, pair_taps), (g_t, pair_g), chunks, j) for j in range(chunks)]
     size = jnp.max(jnp.sum(jnp.abs(g_t.astype(F32)), axis=1))
     pair_size = jnp.max(jnp.sum(jnp.abs(pair_g.astype(F32)), axis=1))
     bound = (jnp.max(top) * size + jnp.max(pair_top) * pair_size) * 1.01
-    g_ext, _ = lax.optimization_barrier((jnp.concatenate([g_t, later], axis=1), parts[1]))
+    plane_got = []
+    g_now = g_t
+    for j in range(chunks):
+        part = grad_chunk(order, (taps, pair_taps), (g_now, pair_g), chunks, j)
+        got, g_now = across_plane(part, part_rows, bound, g_now)
+        plane_got.append(got)
+    g_ext = jnp.concatenate([g_now, later], axis=1)
     in_part = back(g_ext, w_full.reshape(3, 9, chans, chans), z_t, patch_t, rows, cols)
-    plane_got = [across_plane(part, part_rows, bound) for part in parts]
     plane_got[0], in_part = lax.optimization_barrier((plane_got[0], in_part))
-    depth_got = [across_depth(got, part_rows) for got in plane_got]
+    (own, got), in_part = lax.optimization_barrier((plane_got[0], in_part))
+    plane_got[0] = (own, got)
+    depth_got = [across_depth(own, got, part_rows, bound) for own, got in plane_got]
     grad_in = everywhere(in_part)
-    small = part_rows // depth
-    last_got = [spread(got, small) for got in depth_got]
-    done = [unpacked(got, small)[0].reshape(part_rows, chans) for got in last_got]
-    grad_mid = jnp.concatenate(done, axis=0)
-    return (grad_mid, grad_in)
+    small = piece_rows(part_rows)
+    pieces = []
+    for own, got, total in depth_got:
+        pieces += assembled(spread(own, got, small, total), small, part_rows)
+    return (jnp.concatenate(pieces, axis=0), grad_in)
 
 
 def solution(mesh):

time: 317 us -> 261 us (0.82)
  waiting for transfers between devices: 95 us -> 44.4 us
  blocking collectives: 43.2 us -> 0 us
  local copies, waits for them, and re-layouts: 8.05 us -> 25.1 us
  between operations: 20.6 us -> 32.1 us
  starting transfers between devices: 40.6 us -> 50.8 us
    all_to_all x2 -> x0, blocking collectives: 43.2 us -> none  [the longest x1 28.6 us: across_plane(): lax.all_to_all(packed(part, rows, bound), 'clip', 0, 0, axis_index_groups...]
    all_to_all x4 -> x0, waiting for transfers between devices: 32.2 us -> none  [the longest x3 32.2 us: to_depth(): lax.all_to_all(packed(jnp.pad(pieces, ((0, 0), (0, extra), (0, 0))), rows...]
    ppermute x0 -> x18, starting transfers between devices: none -> 30.7 us  [the longest x12 23.6 us: around(): lax.ppermute(blocks, 'tm', [(i, (i + distance) % depth) for i in range(de...]
    slice x0 -> x21, local copies, waits for them, and re-layouts: none -> 17.7 us  [the longest x20 16.4 us: power_of(): return jnp.exp2(x[rows, 0].astype(F32))]
    all_to_all x4 -> x0, starting transfers between devices: 14.8 us -> none  [the longest x3 11.1 us: to_depth(): lax.all_to_all(packed(jnp.pad(pieces, ((0, 0), (0, extra), (0, 0))), rows...]
    all_gather x1, waiting for transfers between devices: 38.4 us -> 27.3 us  [shards(): w_full = lax.all_gather(w_mid, 'clip', axis=0, tiled=True)]
    reduce_sum x8 -> x0, other arithmetic: 9.18 us -> none  [the longest x4 4.06 us: unpacked(): jnp.sum(jnp.exp2(power[:, 0, 0]))]
    all_to_all x1, starting transfers between devices: 11.3 us -> 3.54 us  [everywhere(): lax.all_to_all(jnp.broadcast_to(mine[None], (clips,) + mine.shape), 'clip...]
  transfers between devices with their start and end apart: 12 -> 26, of which waited for: 10 -> 5; matrix products, arithmetic and copies ran while one was open for 8% -> 17% of each run, Pallas kernels for 14% -> 21%
where the time goes in v3:
time: 261 us; the launch traced here: 260 us
  Pallas kernels  66 us (25%)
  starting transfers between devices  50.8 us (19%)
  waiting for transfers between devices  44.4 us (17%)
  between operations  32.1 us (12%)
  other arithmetic  26.5 us (10%)
  local copies, waits for them, and re-layouts  25.1 us (10%)
  matrix products  15.2 us (6%)
    all_gather x1, waiting for transfers between devices, shards(): w_full = lax.all_gather(w_mid, 'clip', axis=0, tiled=True)  27.3 us
    ppermute x12, starting transfers between devices, around(): lax.ppermute(blocks, 'tm', [(i, (i + distance) % depth) for i in range(de...  23.6 us
    pallas_call x2, Pallas kernels, grad_chunk(): pl.pallas_call(grad_kernel, grid_spec=pltpu.PrefetchScalarGridSpec(num_sc...  22.8 us
    pallas_call x1, Pallas kernels, back(): pl.pallas_call(lambda *refs: back_kernel(*refs, rows=rows, cols=cols), gr...  22.1 us
    pallas_call x2, Pallas kernels, front(): pl.pallas_call(lambda *refs: front_kernel(*refs, rows=rows, cols=cols), g...  21.1 us
    slice x20, local copies, waits for them, and re-layouts, power_of(): return jnp.exp2(x[rows, 0].astype(F32))  16.4 us
    dot_general x1, matrix products, contract(): lax.dot_general(left, right, (dims, ((), ())), preferred_element_type=F32)  15.2 us
    convert_element_type x6, other arithmetic, packed(): return jnp.where(row < rows, x * jnp.exp2(14.0 - power), power).astype(F16)  14.8 us
  transfers between devices with their start and end apart: 26, of which 5 were waited for; matrix products, arithmetic and copies ran while one was open for 17% of the time, Pallas kernels for 21%

profile of v3, /device:TPU:0, one launch (start us, length us, event | category | flops | bytes accessed | tf_op | source)
XLA Modules:
  0.0 260.0 jit_solution(5066616899714748227)
XLA Ops:
  9.1 4.9 %collective-permute-start = (bf16[16,512]{1,0:T(8,128)(2,1)S(1)}, bf16[16,512]{1,0:T(8,128)(2,1)S(1)}, u32[]{:S(2)}, u32[]{:S(2)}) collective-permute-start(bf16[16,512]{1,0:T(8,128)(2,1)S(1)} %slice.152), channel_id=1, source_target_pairs={{0,1},{1,2},{2,3},{4,5},{5,6},{6,7},{8,9},{9,10},{10,11},{12,13},{... | collective-permute-start | bytes 49160 | tf_op jit(solution)/shard_map/ppermute | solution.py:19
  14.1 1.4 collective-permute-done
  16.2 10.7 %front.2 = (bf16[432,1024]{1,0:T(8,128)(2,1)}, f32[384,1024]{1,0:T(8,128)}, bf16[27,384,1024]{2,1,0:T(8,128)(2,1)}, f32[384,128]{1,0:T(8,128)}) custom-call(bf16[16,1536]{1,0:T(8,128)(2,1)} %copy-done.9, bf16[432,384]{1,0:T(8,128)(2,1)} %refs_1_.3), custom_call_target="tpu_custom_call" | custom-call | tf_op jit(solution)/shard_map/front/pallas_call | solution.py:79
  27.5 10.4 %front.3 = (bf16[432,1024]{1,0:T(8,128)(2,1)}, f32[384,1024]{1,0:T(8,128)}, bf16[27,384,1024]{2,1,0:T(8,128)(2,1)}, f32[384,128]{1,0:T(8,128)}) custom-call(bf16[16,1536]{1,0:T(8,128)(2,1)} %copy-done.12, bf16[432,384]{1,0:T(8,128)(2,1)} %refs_1_.3), custom_call_target="tpu_custom_call" | custom-call | tf_op jit(solution)/shard_map/front/pallas_call | solution.py:79
  38.0 27.3 %all-gather.2.cloned.1.call-done = bf16[10368,384]{1,0:T(8,128)(2,1)} async-done(((bf16[1296,384]{1,0:T(8,128)(2,1)}), bf16[10368,384]{1,0:T(8,128)(2,1)}) %all-gather.2.cloned.1.call-update) | async-done | bytes 7962640 | tf_op jit(solution)/shard_map/all_gather | solution.py:275
  65.2 15.2 %fusion.4 = (f32[384]{0:T(512)S(1)}, bf16[384,1024]{1,0:T(8,128)(2,1)S(1)}) fusion(f32[1024,384]{0,1:T(8,128)S(1)} %copy.14, bf16[10368,384]{1,0:T(8,128)(2,1)} %all-gather.2.cloned.1.call-done, bf16[10368,1024]{1,0:T(8,128)(2,1)} %bitcast.145), kind=kOutput, calls=%fused_computation.5 | convolution fusion | flops 8156085760 | bytes 31557120 | tf_op jit(solution)/shard_map/dot_general | solution.py:45
  82.6 1.6 reduce_max.38
  87.6 11.4 %grad.2 = f32[4,720,384]{2,1,0:T(8,128)} custom-call(s32[4]{0:T(128)} %multiply_xor_fusion.order_ref, bf16[10368,1024]{1,0:T(8,128)(2,1)} %bitcast.146, bf16[10368,1024]{1,0:T(8,128)(2,1)} %bitcast.150, bf16[10368,1024]{1,0:T(8,128)(2,1)} %bitcast.147, bf16[10368,1024]{1,0:T(8,128)(2,1)} %bitcast.151, bf16[384,1024]{1,0:T(8,128)(2,1)} %copy-done.2, ...), custom_call_target="tpu_custom_call" | custom-call | tf_op jit(solution)/shard_map/grad/pallas_call | solution.py:126
  99.0 3.4 %fusion.16 = (f16[720,384]{1,0:T(8,128)(2,1)}, f16[720,384]{1,0:T(8,128)(2,1)}, f16[720,384]{1,0:T(8,128)(2,1)S(1)}) fusion(f32[4,720,384]{2,1,0:T(8,128)} %grad.2, f32[]{:T(128)S(6)} %ceil.10, f32[]{:T(128)S(6)} %exp2.217, pred[720]{0:T(1024)(128)(4,1)S(1)} %iota_compare_fusion), kind=kLoop, calls=%fused_computation.22 | loop fusion | flops 2488320 | bytes 4977368 | tf_op jit(solution)/shard_map/convert_element_type | solution.py:188
  102.4 1.5 collective-permute-start.3
  104.8 1.5 collective-permute-start.6
  106.9 1.5 collective-permute-start.5
  108.4 11.4 %grad.3 = f32[4,720,384]{2,1,0:T(8,128)} custom-call(s32[4]{0:T(128)} %multiply_xor_fusion.order_ref, bf16[10368,1024]{1,0:T(8,128)(2,1)} %bitcast.148, bf16[10368,1024]{1,0:T(8,128)(2,1)} %bitcast.152, bf16[10368,1024]{1,0:T(8,128)(2,1)} %bitcast.149, bf16[10368,1024]{1,0:T(8,128)(2,1)} %bitcast.153, bf16[384,1024]{1,0:T(8,128)(2,1)} %copy-done.2, ...), custom_call_target="tpu_custom_call" | custom-call | tf_op jit(solution)/shard_map/grad/pallas_call | solution.py:126
  119.8 3.6 %fusion.7 = (f16[720,384]{1,0:T(8,128)(2,1)}, f16[720,384]{1,0:T(8,128)(2,1)}, f16[720,384]{1,0:T(8,128)(2,1)}) fusion(f32[4,720,384]{2,1,0:T(8,128)} %grad.3, f32[]{:T(128)S(6)} %ceil.10, f32[]{:T(128)S(6)} %exp2.217, pred[720]{0:T(1024)(128)(4,1)S(1)} %iota_compare_fusion), kind=kLoop, calls=%fused_computation.10 | loop fusion | flops 2488320 | bytes 4977368 | tf_op jit(solution)/shard_map/convert_element_type | solution.py:188
  123.4 1.5 collective-permute-start.13
  125.4 1.5 collective-permute-start.15
  129.3 22.1 %back.1 = f32[432,384]{1,0:T(8,128)} custom-call(bf16[384,1280]{1,0:T(8,128)(2,1)} %pad_maximum_fusion.refs_0_, bf16[3,9,384,384]{3,2,1,0:T(8,128)(2,1)} %bitcast.154, f32[384,1024]{1,0:T(8,128)} %get-tuple-element.36.refs_2_, bf16[432,1024]{1,0:T(8,128)(2,1)} %get-tuple-element.37.refs_3_), custom_call_target="tpu_custom_call" | custom-call | tf_op jit(solution)/shard_map/back/pallas_call | solution.py:168
  162.0 2.5 select_convert_fusion.3
  164.5 4.5 %collective-permute-start.9 = (f16[192,384]{1,0:T(8,128)(2,1)}, f16[192,384]{1,0:T(8,128)(2,1)S(1)}, u32[]{:S(2)}, u32[]{:S(2)}) collective-permute-start(f16[192,384]{1,0:T(8,128)(2,1)} %get-tuple-element.58), channel_id=1, source_target_pairs={{0,3},{1,0},{2,1},{3,2},{4,7},{5,4},{6,5},{7,6},{8,11},{9,8},{10,9... | collective-permute-start | bytes 442376 | tf_op jit(solution)/shard_map/ppermute | solution.py:208
  172.2 2.5 fusion.37
  174.7 2.7 %collective-permute-start.18 = (f16[192,384]{1,0:T(8,128)(2,1)}, f16[192,384]{1,0:T(8,128)(2,1)S(1)}, u32[]{:S(2)}, u32[]{:S(2)}) collective-permute-start(f16[192,384]{1,0:T(8,128)(2,1)} %get-tuple-element.55), channel_id=1, source_target_pairs={{0,3},{1,0},{2,1},{3,2},{4,7},{5,4},{6,5},{7,6},{8,11},{9,8},{10,9... | collective-permute-start | bytes 442376 | tf_op jit(solution)/shard_map/ppermute | solution.py:208
  179.5 3.5 %all-to-all-start = ((f32[8,54,384]{2,1,0:T(8,128)}), f32[8,54,384]{2,1,0:T(8,128)S(1)}, u32[]{:S(2)}, u32[]{:S(2)}) async-start(f32[8,54,384]{2,1,0:T(8,128)} %reshape.164), calls=%async_computation | async-start | bytes 1376256 | tf_op jit(solution)/shard_map/all_to_all | solution.py:258
  183.0 5.3 %collective-permute-start.16 = (f16[192,384]{1,0:T(8,128)(2,1)}, f16[192,384]{1,0:T(8,128)(2,1)}, u32[]{:S(2)}, u32[]{:S(2)}) collective-permute-start(f16[192,384]{1,0:T(8,128)(2,1)} %get-tuple-element.54), channel_id=1, source_target_pairs={{0,1},{1,2},{2,3},{3,0},{4,5},{5,6},{6,7},{7,4},{8,9},{9,10},{10,1... | collective-permute-start | bytes 442376 | tf_op jit(solution)/shard_map/ppermute | solution.py:208
  193.6 1.5 select_convert_fusion
  195.1 2.5 collective-permute-start.10
  197.6 2.4 collective-permute-start.12
  205.9 2.5 collective-permute-start.20
  215.1 5.3 %collective-permute-done.20 = f16[192,384]{1,0:T(8,128)(2,1)S(1)} collective-permute-done((f16[192,384]{1,0:T(8,128)(2,1)S(1)}, f16[192,384]{1,0:T(8,128)(2,1)S(1)}, u32[]{:S(2)}, u32[]{:S(2)}) %collective-permute-start.20) | collective-permute-done | bytes 147488 | tf_op jit(solution)/shard_map/ppermute | solution.py:208
  221.5 6.2 %all-to-all-start.1 = ((f32[4,54,384]{2,1,0:T(8,128)}), f32[4,54,384]{2,1,0:T(8,128)S(1)}, u32[]{:S(2)}, u32[]{:S(2)}) async-start(f32[4,54,384]{2,1,0:T(8,128)} %broadcast_in_dim.43), calls=%async_computation.1 | async-start | bytes 688128 | tf_op jit(solution)/shard_map/all_to_all | solution.py:259
  233.5 2.8 %all-to-all-done.1 = f32[4,54,384]{2,1,0:T(8,128)S(1)} async-done(((f32[4,54,384]{2,1,0:T(8,128)}), f32[4,54,384]{2,1,0:T(8,128)S(1)}, u32[]{:S(2)}, u32[]{:S(2)}) %all-to-all-start.1) | async-done | bytes 331808 | tf_op jit(solution)/shard_map/all_to_all | solution.py:259
  237.3 3.5 %all-to-all-start.2 = ((f32[8,54,384]{2,1,0:T(8,128)}), f32[8,54,384]{2,1,0:T(8,128)S(1)}, u32[]{:S(2)}, u32[]{:S(2)}) async-start(f32[8,54,384]{2,1,0:T(8,128)} %broadcast_in_dim.44), calls=%async_computation.2 | async-start | bytes 1376256 | tf_op jit(solution)/shard_map/all_to_all | solution.py:260
  245.4 6.8 %all-to-all-done.2 = f32[8,54,384]{2,1,0:T(8,128)S(1)} async-done(((f32[8,54,384]{2,1,0:T(8,128)}), f32[8,54,384]{2,1,0:T(8,128)S(1)}, u32[]{:S(2)}, u32[]{:S(2)}) %all-to-all-start.2) | async-done | bytes 663584 | tf_op jit(solution)/shard_map/all_to_all | solution.py:260
  (114 shorter events, 42.4 us)
Async XLA Ops:
  7.2 8.3 %copy-start.6 = (bf16[1,8,8,16,384]{4,3,2,1,0:T(8,128)(2,1)S(1)}, bf16[1,8,8,16,384]{4,3,2,1,0:T(8,128)(2,1)}, u32[]{:S(2)}) copy-start(bf16[1,8,8,16,384]{4,3,2,1,0:T(8,128)(2,1)} %param.7) | copy-start | bytes 2359300
  7.2 58.0 %all-gather.2.cloned.1.call-start = ((), (), s32[]{:S(2)}) async-start(), calls=%async_computation.3 | async-start | bytes 8957952 | tf_op jit(solution)/shard_map/all_gather | solution.py:275
  9.1 6.4 %collective-permute-start = (bf16[16,512]{1,0:T(8,128)(2,1)S(1)}, bf16[16,512]{1,0:T(8,128)(2,1)S(1)}, u32[]{:S(2)}, u32[]{:S(2)}) collective-permute-start(bf16[16,512]{1,0:T(8,128)(2,1)S(1)} %slice.152), channel_id=1, source_target_pairs={{0,1},{1,2},{2,3},{4,5},{5,6},{6,7},{8,9},{9,10},{10,11},{12,13},{... | collective-permute-start | bytes 49160 | tf_op jit(solution)/shard_map/ppermute | solution.py:19
  15.5 11.4 %collective-permute-start.1 = (bf16[16,1536]{1,0:T(8,128)(2,1)S(1)}, bf16[16,1536]{1,0:T(8,128)(2,1)S(1)}, u32[]{:S(2)}, u32[]{:S(2)}) collective-permute-start(bf16[16,1536]{1,0:T(8,128)(2,1)S(1)} %pad_maximum_fusion.1.refs_0_), channel_id=1, source_target_pairs={{0,4},{4,0},{8,12},{12,8},{16,20},{20,16},{24,28},{28,24},{1,5},{5... | collective-permute-start | bytes 147464 | tf_op jit(solution)/shard_map/ppermute | solution.py:23
  65.2 16.1 %copy-start.10 = (f32[384,128]{1,0:T(8,128)S(1)}, f32[384,128]{1,0:T(8,128)}, u32[]{:S(2)}) copy-start(f32[384,128]{1,0:T(8,128)} %get-tuple-element.29) | copy-start | bytes 589828
  80.5 7.2 %copy-start.2 = (bf16[384,1024]{1,0:T(8,128)(2,1)}, bf16[384,1024]{1,0:T(8,128)(2,1)S(1)}, u32[]{:S(2)}) copy-start(bf16[384,1024]{1,0:T(8,128)(2,1)S(1)} %get-tuple-element.35.refs_4_) | copy-start | bytes 2359300
  80.5 4.9 %collective-permute-start.2 = (bf16[384,1024]{1,0:T(8,128)(2,1)S(1)}, bf16[384,1024]{1,0:T(8,128)(2,1)S(1)}, u32[]{:S(2)}, u32[]{:S(2)}) collective-permute-start(bf16[384,1024]{1,0:T(8,128)(2,1)S(1)} %get-tuple-element.35.refs_4_), channel_id=1, source_target_pairs={{0,4},{4,0},{8,12},{12,8},{16,20},{20,16},{24,28},{28,24},{1,5},{5... | collective-permute-start | bytes 2359304 | tf_op jit(solution)/shard_map/ppermute | solution.py:23
  102.4 23.0 %collective-permute-start.3 = (f16[720,384]{1,0:T(8,128)(2,1)S(1)}, f16[720,384]{1,0:T(8,128)(2,1)S(1)}, u32[]{:S(2)}, u32[]{:S(2)}) collective-permute-start(f16[720,384]{1,0:T(8,128)(2,1)S(1)} %get-tuple-element.31), channel_id=1, source_target_pairs={{0,8},{4,12},{8,0},{12,4},{16,24},{20,28},{24,16},{28,20},{1,9},{5... | collective-permute-start | bytes 1658888 | tf_op jit(solution)/shard_map/ppermute | solution.py:202
  104.8 20.0 %collective-permute-start.6 = (bf16[384,256]{1,0:T(8,128)(2,1)S(1)}, bf16[384,256]{1,0:T(8,128)(2,1)S(1)}, u32[]{:S(2)}, u32[]{:S(2)}) collective-permute-start(bf16[384,256]{1,0:T(8,128)(2,1)S(1)} %slice.160), channel_id=1, source_target_pairs={{1,0},{2,1},{3,2},{5,4},{6,5},{7,6},{9,8},{10,9},{11,10},{13,12},{... | collective-permute-start | bytes 589832 | tf_op jit(solution)/shard_map/ppermute | solution.py:19
  106.3 46.4 %collective-permute-start.4 = (f16[720,384]{1,0:T(8,128)(2,1)}, f16[720,384]{1,0:T(8,128)(2,1)}, u32[]{:S(2)}, u32[]{:S(2)}) collective-permute-start(f16[720,384]{1,0:T(8,128)(2,1)} %get-tuple-element.32), channel_id=1, source_target_pairs={{0,16},{4,20},{8,24},{12,28},{16,0},{20,4},{24,8},{28,12},{1,17},{... | collective-permute-start | bytes 1658888 | tf_op jit(solution)/shard_map/ppermute | solution.py:202
  106.9 45.8 %collective-permute-start.5 = (f16[720,384]{1,0:T(8,128)(2,1)}, f16[720,384]{1,0:T(8,128)(2,1)}, u32[]{:S(2)}, u32[]{:S(2)}) collective-permute-start(f16[720,384]{1,0:T(8,128)(2,1)} %get-tuple-element.33), channel_id=1, source_target_pairs={{0,24},{4,28},{8,16},{12,20},{16,8},{20,12},{24,0},{28,4},{1,25},{... | collective-permute-start | bytes 1658888 | tf_op jit(solution)/shard_map/ppermute | solution.py:202
  119.8 7.2 %copy-start.3 = (bf16[384,1024]{1,0:T(8,128)(2,1)S(1)}, bf16[384,1024]{1,0:T(8,128)(2,1)}, u32[]{:S(2)}) copy-start(bf16[384,1024]{1,0:T(8,128)(2,1)} %copy-done.2) | copy-start | bytes 2359300
  123.4 33.1 %collective-permute-start.13 = (f16[720,384]{1,0:T(8,128)(2,1)}, f16[720,384]{1,0:T(8,128)(2,1)S(1)}, u32[]{:S(2)}, u32[]{:S(2)}) collective-permute-start(f16[720,384]{1,0:T(8,128)(2,1)} %get-tuple-element.42), channel_id=1, source_target_pairs={{0,8},{4,12},{8,0},{12,4},{16,24},{20,28},{24,16},{28,20},{1,9},{5... | collective-permute-start | bytes 1658888 | tf_op jit(solution)/shard_map/ppermute | solution.py:202
  124.8 33.0 %collective-permute-start.14 = (f16[720,384]{1,0:T(8,128)(2,1)}, f16[720,384]{1,0:T(8,128)(2,1)}, u32[]{:S(2)}, u32[]{:S(2)}) collective-permute-start(f16[720,384]{1,0:T(8,128)(2,1)} %get-tuple-element.43), channel_id=1, source_target_pairs={{0,16},{4,20},{8,24},{12,28},{16,0},{20,4},{24,8},{28,12},{1,17},{... | collective-permute-start | bytes 1658888 | tf_op jit(solution)/shard_map/ppermute | solution.py:202
  125.4 44.7 %collective-permute-start.15 = (f16[720,384]{1,0:T(8,128)(2,1)}, f16[720,384]{1,0:T(8,128)(2,1)}, u32[]{:S(2)}, u32[]{:S(2)}) collective-permute-start(f16[720,384]{1,0:T(8,128)(2,1)} %get-tuple-element.44), channel_id=1, source_target_pairs={{0,24},{4,28},{8,16},{12,20},{16,8},{20,12},{24,0},{28,4},{1,25},{... | collective-permute-start | bytes 1658888 | tf_op jit(solution)/shard_map/ppermute | solution.py:202
  164.5 14.1 %copy-start.5 = (f32[432,384]{1,0:T(8,128)S(1)}, f32[432,384]{1,0:T(8,128)}, u32[]{:S(2)}) copy-start(f32[432,384]{1,0:T(8,128)} %back.1) | copy-start | bytes 1990660
  164.5 27.6 %collective-permute-start.9 = (f16[192,384]{1,0:T(8,128)(2,1)}, f16[192,384]{1,0:T(8,128)(2,1)S(1)}, u32[]{:S(2)}, u32[]{:S(2)}) collective-permute-start(f16[192,384]{1,0:T(8,128)(2,1)} %get-tuple-element.58), channel_id=1, source_target_pairs={{0,3},{1,0},{2,1},{3,2},{4,7},{5,4},{6,5},{7,6},{8,11},{9,8},{10,9... | collective-permute-start | bytes 442376 | tf_op jit(solution)/shard_map/ppermute | solution.py:208
  169.0 21.2 %collective-permute-start.8 = (f16[192,384]{1,0:T(8,128)(2,1)}, f16[192,384]{1,0:T(8,128)(2,1)}, u32[]{:S(2)}, u32[]{:S(2)}) collective-permute-start(f16[192,384]{1,0:T(8,128)(2,1)} %get-tuple-element.59), channel_id=1, source_target_pairs={{0,2},{1,3},{2,0},{3,1},{4,6},{5,7},{6,4},{7,5},{8,10},{9,11},{10,... | collective-permute-start | bytes 442376 | tf_op jit(solution)/shard_map/ppermute | solution.py:208
  169.0 14.0 %collective-permute-start.7 = (f16[192,384]{1,0:T(8,128)(2,1)}, f16[192,384]{1,0:T(8,128)(2,1)}, u32[]{:S(2)}, u32[]{:S(2)}) collective-permute-start(f16[192,384]{1,0:T(8,128)(2,1)} %get-tuple-element.57), channel_id=1, source_target_pairs={{0,1},{1,2},{2,3},{3,0},{4,5},{5,6},{6,7},{7,4},{8,9},{9,10},{10,1... | collective-permute-start | bytes 442376 | tf_op jit(solution)/shard_map/ppermute | solution.py:208
  174.7 28.5 %collective-permute-start.18 = (f16[192,384]{1,0:T(8,128)(2,1)}, f16[192,384]{1,0:T(8,128)(2,1)S(1)}, u32[]{:S(2)}, u32[]{:S(2)}) collective-permute-start(f16[192,384]{1,0:T(8,128)(2,1)} %get-tuple-element.55), channel_id=1, source_target_pairs={{0,3},{1,0},{2,1},{3,2},{4,7},{5,4},{6,5},{7,6},{8,11},{9,8},{10,9... | collective-permute-start | bytes 442376 | tf_op jit(solution)/shard_map/ppermute | solution.py:208
  177.4 24.5 %collective-permute-start.17 = (f16[192,384]{1,0:T(8,128)(2,1)}, f16[192,384]{1,0:T(8,128)(2,1)S(1)}, u32[]{:S(2)}, u32[]{:S(2)}) collective-permute-start(f16[192,384]{1,0:T(8,128)(2,1)} %get-tuple-element.56), channel_id=1, source_target_pairs={{0,2},{1,3},{2,0},{3,1},{4,6},{5,7},{6,4},{7,5},{8,10},{9,11},{10,... | collective-permute-start | bytes 442376 | tf_op jit(solution)/shard_map/ppermute | solution.py:208
  179.5 41.2 %all-to-all-start = ((f32[8,54,384]{2,1,0:T(8,128)}), f32[8,54,384]{2,1,0:T(8,128)S(1)}, u32[]{:S(2)}, u32[]{:S(2)}) async-start(f32[8,54,384]{2,1,0:T(8,128)} %reshape.164), calls=%async_computation | async-start | bytes 1376256 | tf_op jit(solution)/shard_map/all_to_all | solution.py:258
  183.0 14.6 %collective-permute-start.16 = (f16[192,384]{1,0:T(8,128)(2,1)}, f16[192,384]{1,0:T(8,128)(2,1)}, u32[]{:S(2)}, u32[]{:S(2)}) collective-permute-start(f16[192,384]{1,0:T(8,128)(2,1)} %get-tuple-element.54), channel_id=1, source_target_pairs={{0,1},{1,2},{2,3},{3,0},{4,5},{5,6},{6,7},{7,4},{8,9},{9,10},{10,1... | collective-permute-start | bytes 442376 | tf_op jit(solution)/shard_map/ppermute | solution.py:208
  195.1 13.3 %collective-permute-start.10 = (f16[192,384]{1,0:T(8,128)(2,1)S(1)}, f16[192,384]{1,0:T(8,128)(2,1)S(1)}, u32[]{:S(2)}, u32[]{:S(2)}) collective-permute-start(f16[192,384]{1,0:T(8,128)(2,1)S(1)} %select_convert_fusion), channel_id=1, source_target_pairs={{0,1},{1,2},{2,3},{3,0},{4,5},{5,6},{6,7},{7,4},{8,9},{9,10},{10,1... | collective-permute-start | bytes 442376 | tf_op jit(solution)/shard_map/ppermute | solution.py:208
  197.6 12.1 %collective-permute-start.11 = (f16[192,384]{1,0:T(8,128)(2,1)S(1)}, f16[192,384]{1,0:T(8,128)(2,1)S(1)}, u32[]{:S(2)}, u32[]{:S(2)}) collective-permute-start(f16[192,384]{1,0:T(8,128)(2,1)S(1)} %select_convert_fusion), channel_id=1, source_target_pairs={{0,2},{1,3},{2,0},{3,1},{4,6},{5,7},{6,4},{7,5},{8,10},{9,11},{10,... | collective-permute-start | bytes 442376 | tf_op jit(solution)/shard_map/ppermute | solution.py:208
  197.6 12.1 %collective-permute-start.12 = (f16[192,384]{1,0:T(8,128)(2,1)S(1)}, f16[192,384]{1,0:T(8,128)(2,1)S(1)}, u32[]{:S(2)}, u32[]{:S(2)}) collective-permute-start(f16[192,384]{1,0:T(8,128)(2,1)S(1)} %select_convert_fusion), channel_id=1, source_target_pairs={{0,3},{1,0},{2,1},{3,2},{4,7},{5,4},{6,5},{7,6},{8,11},{9,8},{10,9... | collective-permute-start | bytes 442376 | tf_op jit(solution)/shard_map/ppermute | solution.py:208
  205.8 9.3 %collective-permute-start.19 = (f16[192,384]{1,0:T(8,128)(2,1)S(1)}, f16[192,384]{1,0:T(8,128)(2,1)S(1)}, u32[]{:S(2)}, u32[]{:S(2)}) collective-permute-start(f16[192,384]{1,0:T(8,128)(2,1)S(1)} %fusion.45), channel_id=1, source_target_pairs={{0,1},{1,2},{2,3},{3,0},{4,5},{5,6},{6,7},{7,4},{8,9},{9,10},{10,1... | collective-permute-start | bytes 442376 | tf_op jit(solution)/shard_map/ppermute | solution.py:208
  205.9 14.5 %collective-permute-start.20 = (f16[192,384]{1,0:T(8,128)(2,1)S(1)}, f16[192,384]{1,0:T(8,128)(2,1)S(1)}, u32[]{:S(2)}, u32[]{:S(2)}) collective-permute-start(f16[192,384]{1,0:T(8,128)(2,1)S(1)} %fusion.45), channel_id=1, source_target_pairs={{0,2},{1,3},{2,0},{3,1},{4,6},{5,7},{6,4},{7,5},{8,10},{9,11},{10,... | collective-permute-start | bytes 442376 | tf_op jit(solution)/shard_map/ppermute | solution.py:208
  208.4 12.0 %collective-permute-start.21 = (f16[192,384]{1,0:T(8,128)(2,1)S(1)}, f16[192,384]{1,0:T(8,128)(2,1)S(1)}, u32[]{:S(2)}, u32[]{:S(2)}) collective-permute-start(f16[192,384]{1,0:T(8,128)(2,1)S(1)} %fusion.45), channel_id=1, source_target_pairs={{0,3},{1,0},{2,1},{3,2},{4,7},{5,4},{6,5},{7,6},{8,11},{9,8},{10,9... | collective-permute-start | bytes 442376 | tf_op jit(solution)/shard_map/ppermute | solution.py:208
  221.5 14.9 %all-to-all-start.1 = ((f32[4,54,384]{2,1,0:T(8,128)}), f32[4,54,384]{2,1,0:T(8,128)S(1)}, u32[]{:S(2)}, u32[]{:S(2)}) async-start(f32[4,54,384]{2,1,0:T(8,128)} %broadcast_in_dim.43), calls=%async_computation.1 | async-start | bytes 688128 | tf_op jit(solution)/shard_map/all_to_all | solution.py:259
  237.3 15.0 %all-to-all-start.2 = ((f32[8,54,384]{2,1,0:T(8,128)}), f32[8,54,384]{2,1,0:T(8,128)S(1)}, u32[]{:S(2)}, u32[]{:S(2)}) async-start(f32[8,54,384]{2,1,0:T(8,128)} %broadcast_in_dim.44), calls=%async_computation.2 | async-start | bytes 1376256 | tf_op jit(solution)/shard_map/all_to_all | solution.py:260
  240.8 12.3 %copy-start.1 = (bf16[1,8,8,32,16]{3,4,2,1,0:T(8,128)(2,1)S(1)}, bf16[1,8,8,32,16]{3,4,2,1,0:T(8,128)(2,1)}, u32[]{:S(2)}) copy-start(bf16[1,8,8,32,16]{3,4,2,1,0:T(8,128)(2,1)} %param.5) | copy-start | bytes 196612
  (7 other events, 13.4 us)
Sparse Core Ops, SparseCore 0:
  9.9 55.2 all-gather.1

commit v4 on v3

--- a/solution.py
+++ b/solution.py
@@ -188,10 +188,6 @@
     return jnp.where(row < rows, x * jnp.exp2(14.0 - power), power).astype(F16)
 
 
-def power_of(x, rows):
-    return jnp.exp2(x[rows, 0].astype(F32))
-
-
 def across_plane(part, rows, bound, after):
     clips = lax.axis_size("clip")
     payloads = [packed(part[q], rows, bound) for q in range(1, clips // 2)]
@@ -208,37 +204,41 @@
     return lax.ppermute(blocks, "tm", [(i, (i + distance) % depth) for i in range(depth)])
 
 
-def across_depth(own, got, rows, bound):
+def scales(got, rows, bound):
+    powers = [jnp.exp2(x[rows : rows + 1].astype(F32)) for x in got]
+    return [power * 2.0**-14 for power in powers], (bound + sum(powers)) * 1.01
+
+
+def across_depth(own, got, rows, factors, total, after):
     depth = lax.axis_size("tm")
     me = lax.axis_index("tm")
     small = piece_rows(rows)
-    powers = [power_of(x, rows) for x in got]
-    total = (bound + sum(powers)) * 1.01
 
     def piece(place):
         first = place * small
         terms = lax.dynamic_slice_in_dim(own, first, small + 16, axis=0)
-        for x, power in zip(got, powers):
-            terms = terms + lax.dynamic_slice_in_dim(x, first, small + 16, axis=0).astype(F32) * (power * 2.0**-14)
+        for x, factor in zip(got, factors):
+            terms = terms + lax.dynamic_slice_in_dim(x, first, small + 16, axis=0).astype(F32) * factor
         return terms
 
-    others = [around(packed(piece((me + d) % depth), small, total), d) for d in range(1, depth)]
-    return piece(me), others, total
-
-
-def spread(own, got, small, bound):
-    depth = lax.axis_size("tm")
-    powers = [power_of(x, small) for x in got]
-    total = (bound + sum(powers)) * 1.01
-    for x, power in zip(got, powers):
-        own = own + x.astype(F32) * (power * 2.0**-14)
+    payloads = [packed(piece((me + d) % depth), small, total) for d in range(1, depth)]
+    payloads, after = lax.optimization_barrier((payloads, after))
+    others = [around(payloads[d - 1], d) for d in range(1, depth)]
+    return (piece(me), others), after
+
+
+def spread(own, got, small, factors, total):
+    depth = lax.axis_size("tm")
+    for x, factor in zip(got, factors):
+        own = own + x.astype(F32) * factor
     payload = packed(own, small, total)
     return [payload] + [around(payload, depth - k) for k in range(1, depth)]
 
 
-def assembled(pieces, small, rows):
+def assembled(pieces, factors, small, rows):
     depth = lax.axis_size("tm")
     me = lax.axis_index("tm")
+    pieces = [x[:small].astype(F32) * factor for x, factor in zip(pieces, factors)]
     out = []
     for place in range(depth):
         x = pieces[0]
@@ -247,7 +247,7 @@
         count = min(small, rows - place * small)
         if count <= 0:
             break
-        out.append(x[:count].astype(F32) * (power_of(x, small) * 2.0**-14))
+        out.append(x[:count])
     return out
 
 
@@ -300,17 +300,27 @@
         part = grad_chunk(order, (taps, pair_taps), (g_now, pair_g), chunks, j)
         got, g_now = across_plane(part, part_rows, bound, g_now)
         plane_got.append(got)
+    factors, total = scales(plane_got[0][1], part_rows, bound)
+    first, g_now = across_depth(*plane_got[0], part_rows, factors, total, g_now)
+    depth_got = [first]
     g_ext = jnp.concatenate([g_now, later], axis=1)
     in_part = back(g_ext, w_full.reshape(3, 9, chans, chans), z_t, patch_t, rows, cols)
-    plane_got[0], in_part = lax.optimization_barrier((plane_got[0], in_part))
-    (own, got), in_part = lax.optimization_barrier((plane_got[0], in_part))
-    plane_got[0] = (own, got)
-    depth_got = [across_depth(own, got, part_rows, bound) for own, got in plane_got]
+    for own, got in plane_got[1:]:
+        got, in_part = lax.optimization_barrier((got, in_part))
+        more, in_part = across_depth(own, got, part_rows, factors, total, in_part)
+        depth_got.append(more)
     grad_in = everywhere(in_part)
     small = piece_rows(part_rows)
+    factors, total = scales(depth_got[0][1], small, total)
+    last = []
+    for own, got in depth_got:
+        if last:
+            got, last[-1][0] = lax.optimization_barrier((got, last[-1][0]))
+        last.append(spread(own, got, small, factors, total))
+    factors, _ = scales(last[0], small, 0.0)
     pieces = []
-    for own, got, total in depth_got:
-        pieces += assembled(spread(own, got, small, total), small, part_rows)
+    for got in last:
+        pieces += assembled(got, factors, small, part_rows)
     return (jnp.concatenate(pieces, axis=0), grad_in)
 
 

time: 261 us -> 239 us (0.916)
  local copies, waits for them, and re-layouts: 25.1 us -> 9.33 us
  between operations: 32.1 us -> 17.6 us
  waiting for transfers between devices: 44.4 us -> 58.6 us
  starting transfers between devices: 50.8 us -> 46.2 us
    slice x20 -> x0, local copies, waits for them, and re-layouts: 16.4 us -> none  [power_of(): return jnp.exp2(x[rows, 0].astype(F32))]
    ppermute x12, waiting for transfers between devices: 5.32 us -> 9.31 us  [around(): lax.ppermute(blocks, 'tm', [(i, (i + distance) % depth) for i in range(de...]
    ppermute x6, waiting for transfers between devices: 0.02 us -> 3.96 us  [across_plane(): got.append(lax.ppermute(payloads[q - 1], 'clip', route))]
    all_to_all x1, waiting for transfers between devices: 2.81 us -> 6.72 us  [everywhere(): lax.all_to_all(jnp.broadcast_to(mine[None], (depth,) + mine.shape), 'tm',...]
    all_to_all x1, starting transfers between devices: 6.16 us -> 3.46 us  [everywhere(): lax.all_to_all(jnp.broadcast_to(mine[None], (depth,) + mine.shape), 'tm',...]
    convert_element_type x6, other arithmetic: 14.8 us -> 12.2 us  [packed(): return jnp.where(row < rows, x * jnp.exp2(14.0 - power), power).astype(F16)]
  transfers between devices with their start and end apart: 26 -> 26, of which waited for: 5 -> 7; matrix products, arithmetic and copies ran while one was open for 17% -> 11% of each run, Pallas kernels for 21% -> 23%
where the time goes in v4:
time: 239 us; the launch traced here: 238 us
  Pallas kernels  66 us (28%)
  waiting for transfers between devices  58.6 us (25%)
  starting transfers between devices  46.2 us (19%)
  other arithmetic  24.9 us (10%)
  between operations  17.6 us (7%)
  matrix products  15.2 us (6%)
  local copies, waits for them, and re-layouts  9.33 us (4%)
    all_gather x1, waiting for transfers between devices, shards(): w_full = lax.all_gather(w_mid, 'clip', axis=0, tiled=True)  27.3 us
    pallas_call x2, Pallas kernels, grad_chunk(): pl.pallas_call(grad_kernel, grid_spec=pltpu.PrefetchScalarGridSpec(num_sc...  22.9 us
    ppermute x12, starting transfers between devices, around(): lax.ppermute(blocks, 'tm', [(i, (i + distance) % depth) for i in range(de...  22.4 us
    pallas_call x1, Pallas kernels, back(): pl.pallas_call(lambda *refs: back_kernel(*refs, rows=rows, cols=cols), gr...  22 us
    pallas_call x2, Pallas kernels, front(): pl.pallas_call(lambda *refs: front_kernel(*refs, rows=rows, cols=cols), g...  21.1 us
    dot_general x1, matrix products, contract(): lax.dot_general(left, right, (dims, ((), ())), preferred_element_type=F32)  15.2 us
    convert_element_type x6, other arithmetic, packed(): return jnp.where(row < rows, x * jnp.exp2(14.0 - power), power).astype(F16)  12.2 us
    ppermute x12, waiting for transfers between devices, around(): lax.ppermute(blocks, 'tm', [(i, (i + distance) % depth) for i in range(de...  9.31 us
  transfers between devices with their start and end apart: 26, of which 7 were waited for; matrix products, arithmetic and copies ran while one was open for 11% of the time, Pallas kernels for 23%

profile of v4, /device:TPU:0, one launch (start us, length us, event | category | flops | bytes accessed | tf_op | source)
XLA Modules:
  0.0 237.8 jit_solution(17860883409595587750)
XLA Ops:
  9.1 4.9 %collective-permute-start = (bf16[16,512]{1,0:T(8,128)(2,1)S(1)}, bf16[16,512]{1,0:T(8,128)(2,1)S(1)}, u32[]{:S(2)}, u32[]{:S(2)}) collective-permute-start(bf16[16,512]{1,0:T(8,128)(2,1)S(1)} %slice.120), channel_id=1, source_target_pairs={{0,1},{1,2},{2,3},{4,5},{5,6},{6,7},{8,9},{9,10},{10,11},{12,13},{... | collective-permute-start | bytes 49160 | tf_op jit(solution)/shard_map/ppermute | solution.py:19
  14.1 1.4 collective-permute-done
  16.2 10.7 %front.2 = (bf16[432,1024]{1,0:T(8,128)(2,1)}, f32[384,1024]{1,0:T(8,128)}, bf16[27,384,1024]{2,1,0:T(8,128)(2,1)}, f32[384,128]{1,0:T(8,128)}) custom-call(bf16[16,1536]{1,0:T(8,128)(2,1)} %copy-done.11, bf16[432,384]{1,0:T(8,128)(2,1)} %refs_1_.3), custom_call_target="tpu_custom_call" | custom-call | tf_op jit(solution)/shard_map/front/pallas_call | solution.py:79
  27.5 10.4 %front.3 = (bf16[432,1024]{1,0:T(8,128)(2,1)}, f32[384,1024]{1,0:T(8,128)}, bf16[27,384,1024]{2,1,0:T(8,128)(2,1)}, f32[384,128]{1,0:T(8,128)}) custom-call(bf16[16,1536]{1,0:T(8,128)(2,1)} %copy-done.14, bf16[432,384]{1,0:T(8,128)(2,1)} %refs_1_.3), custom_call_target="tpu_custom_call" | custom-call | tf_op jit(solution)/shard_map/front/pallas_call | solution.py:79
  37.9 27.3 %all-gather.2.cloned.1.call-done = bf16[10368,384]{1,0:T(8,128)(2,1)} async-done(((bf16[1296,384]{1,0:T(8,128)(2,1)}), bf16[10368,384]{1,0:T(8,128)(2,1)}) %all-gather.2.cloned.1.call-update) | async-done | bytes 7962640 | tf_op jit(solution)/shard_map/all_gather | solution.py:275
  65.2 15.2 %fusion.4 = (f32[384]{0:T(512)S(1)}, bf16[384,1024]{1,0:T(8,128)(2,1)S(1)}) fusion(f32[1024,384]{0,1:T(8,128)S(1)} %copy.14, bf16[10368,384]{1,0:T(8,128)(2,1)} %all-gather.2.cloned.1.call-done, bf16[10368,1024]{1,0:T(8,128)(2,1)} %bitcast.173), kind=kOutput, calls=%fused_computation.5 | convolution fusion | flops 8156085760 | bytes 31557120 | tf_op jit(solution)/shard_map/dot_general | solution.py:45
  82.0 1.6 reduce_max.38
  87.6 11.4 %grad.2 = f32[4,720,384]{2,1,0:T(8,128)} custom-call(s32[4]{0:T(128)} %multiply_xor_fusion.order_ref, bf16[10368,1024]{1,0:T(8,128)(2,1)} %bitcast.174, bf16[10368,1024]{1,0:T(8,128)(2,1)} %bitcast.178, bf16[10368,1024]{1,0:T(8,128)(2,1)} %bitcast.175, bf16[10368,1024]{1,0:T(8,128)(2,1)} %bitcast.179, bf16[384,1024]{1,0:T(8,128)(2,1)} %copy-done.2, ...), custom_call_target="tpu_custom_call" | custom-call | tf_op jit(solution)/shard_map/grad/pallas_call | solution.py:126
  99.1 3.5 %fusion.16 = (f16[720,384]{1,0:T(8,128)(2,1)}, f16[720,384]{1,0:T(8,128)(2,1)}, f16[720,384]{1,0:T(8,128)(2,1)}) fusion(f32[4,720,384]{2,1,0:T(8,128)} %grad.2, f32[]{:T(128)S(6)} %ceil.6, f32[]{:T(128)S(6)} %exp2.101, pred[720]{0:T(1024)(128)(4,1)S(1)} %iota_compare_fusion), kind=kLoop, calls=%fused_computation.22 | loop fusion | flops 2488320 | bytes 4977368 | tf_op jit(solution)/shard_map/convert_element_type | solution.py:188
  102.6 1.5 collective-permute-start.3
  104.6 1.5 collective-permute-start.5
  107.1 1.5 collective-permute-start.15
  109.9 11.4 %grad.3 = f32[4,720,384]{2,1,0:T(8,128)} custom-call(s32[4]{0:T(128)} %multiply_xor_fusion.order_ref, bf16[10368,1024]{1,0:T(8,128)(2,1)} %bitcast.176, bf16[10368,1024]{1,0:T(8,128)(2,1)} %bitcast.180, bf16[10368,1024]{1,0:T(8,128)(2,1)} %bitcast.177, bf16[10368,1024]{1,0:T(8,128)(2,1)} %bitcast.181, bf16[384,1024]{1,0:T(8,128)(2,1)} %copy-done.2, ...), custom_call_target="tpu_custom_call" | custom-call | tf_op jit(solution)/shard_map/grad/pallas_call | solution.py:126
  122.6 2.4 fusion.7
  125.0 1.6 collective-permute-start.12
  127.1 3.9 %collective-permute-done.4 = f16[720,384]{1,0:T(8,128)(2,1)} collective-permute-done((f16[720,384]{1,0:T(8,128)(2,1)}, f16[720,384]{1,0:T(8,128)(2,1)}, u32[]{:S(2)}, u32[]{:S(2)}) %collective-permute-start.4) | collective-permute-done | bytes 552992 | tf_op jit(solution)/shard_map/ppermute | solution.py:198
  131.8 2.4 fusion.50
  134.2 1.5 collective-permute-start.6
  135.7 2.4 %collective-permute-start.7 = (f16[192,384]{1,0:T(8,128)(2,1)}, f16[192,384]{1,0:T(8,128)(2,1)S(1)}, u32[]{:S(2)}, u32[]{:S(2)}) collective-permute-start(f16[192,384]{1,0:T(8,128)(2,1)} %get-tuple-element.48), channel_id=1, source_target_pairs={{0,2},{1,3},{2,0},{3,1},{4,6},{5,7},{6,4},{7,5},{8,10},{9,11},{10,... | collective-permute-start | bytes 442376 | tf_op jit(solution)/shard_map/ppermute | solution.py:204
  139.2 22.0 %back.1 = f32[432,384]{1,0:T(8,128)} custom-call(bf16[384,1280]{1,0:T(8,128)(2,1)} %pad_maximum_fusion.refs_0_, bf16[3,9,384,384]{3,2,1,0:T(8,128)(2,1)} %bitcast.182, f32[384,1024]{1,0:T(8,128)} %get-tuple-element.54.refs_2_, bf16[432,1024]{1,0:T(8,128)(2,1)} %get-tuple-element.55.refs_3_), custom_call_target="tpu_custom_call" | custom-call | tf_op jit(solution)/shard_map/back/pallas_call | solution.py:168
  161.2 1.5 collective-permute-start.8
  166.1 4.2 %all-to-all-start = ((f32[8,54,384]{2,1,0:T(8,128)}), f32[8,54,384]{2,1,0:T(8,128)S(1)}, u32[]{:S(2)}, u32[]{:S(2)}) async-start(f32[8,54,384]{2,1,0:T(8,128)} %reshape.52), calls=%async_computation | async-start | bytes 1376256 | tf_op jit(solution)/shard_map/all_to_all | solution.py:258
  170.3 2.6 %collective-permute-start.18 = (f16[192,384]{1,0:T(8,128)(2,1)}, f16[192,384]{1,0:T(8,128)(2,1)S(1)}, u32[]{:S(2)}, u32[]{:S(2)}) collective-permute-start(f16[192,384]{1,0:T(8,128)(2,1)} %get-tuple-element.62), channel_id=1, source_target_pairs={{0,3},{1,0},{2,1},{3,2},{4,7},{5,4},{6,5},{7,6},{8,11},{9,8},{10,9... | collective-permute-start | bytes 442376 | tf_op jit(solution)/shard_map/ppermute | solution.py:204
  176.1 1.9 collective-permute-start.10
  179.2 1.4 fusion.30
  180.6 2.8 %collective-permute-start.21 = (f16[192,384]{1,0:T(8,128)(2,1)S(1)}, f16[192,384]{1,0:T(8,128)(2,1)S(1)}, u32[]{:S(2)}, u32[]{:S(2)}) collective-permute-start(f16[192,384]{1,0:T(8,128)(2,1)S(1)} %fusion.30), channel_id=1, source_target_pairs={{0,3},{1,0},{2,1},{3,2},{4,7},{5,4},{6,5},{7,6},{8,11},{9,8},{10,9... | collective-permute-start | bytes 442376 | tf_op jit(solution)/shard_map/ppermute | solution.py:204
  183.4 6.2 %collective-permute-start.19 = (f16[192,384]{1,0:T(8,128)(2,1)S(1)}, f16[192,384]{1,0:T(8,128)(2,1)S(1)}, u32[]{:S(2)}, u32[]{:S(2)}) collective-permute-start(f16[192,384]{1,0:T(8,128)(2,1)S(1)} %fusion.30), channel_id=1, source_target_pairs={{0,1},{1,2},{2,3},{3,0},{4,5},{5,6},{6,7},{7,4},{8,9},{9,10},{10,1... | collective-permute-start | bytes 442376 | tf_op jit(solution)/shard_map/ppermute | solution.py:204
  189.6 9.1 %collective-permute-done.10 = f16[192,384]{1,0:T(8,128)(2,1)S(1)} collective-permute-done((f16[192,384]{1,0:T(8,128)(2,1)S(1)}, f16[192,384]{1,0:T(8,128)(2,1)S(1)}, u32[]{:S(2)}, u32[]{:S(2)}) %collective-permute-start.10) | collective-permute-done | bytes 147488 | tf_op jit(solution)/shard_map/ppermute | solution.py:204
  201.2 3.5 %all-to-all-start.1 = ((f32[4,54,384]{2,1,0:T(8,128)}), f32[4,54,384]{2,1,0:T(8,128)S(1)}, u32[]{:S(2)}, u32[]{:S(2)}) async-start(f32[4,54,384]{2,1,0:T(8,128)} %broadcast_in_dim.61), calls=%async_computation.1 | async-start | bytes 688128 | tf_op jit(solution)/shard_map/all_to_all | solution.py:259
  207.0 6.7 %all-to-all-done.1 = f32[4,54,384]{2,1,0:T(8,128)S(1)} async-done(((f32[4,54,384]{2,1,0:T(8,128)}), f32[4,54,384]{2,1,0:T(8,128)S(1)}, u32[]{:S(2)}, u32[]{:S(2)}) %all-to-all-start.1) | async-done | bytes 331808 | tf_op jit(solution)/shard_map/all_to_all | solution.py:259
  214.7 3.8 %all-to-all-start.2 = ((f32[8,54,384]{2,1,0:T(8,128)}), f32[8,54,384]{2,1,0:T(8,128)S(1)}, u32[]{:S(2)}, u32[]{:S(2)}) async-start(f32[8,54,384]{2,1,0:T(8,128)} %broadcast_in_dim.62), calls=%async_computation.2 | async-start | bytes 1376256 | tf_op jit(solution)/shard_map/all_to_all | solution.py:260
  220.8 9.2 %all-to-all-done.2 = f32[8,54,384]{2,1,0:T(8,128)S(1)} async-done(((f32[8,54,384]{2,1,0:T(8,128)}), f32[8,54,384]{2,1,0:T(8,128)S(1)}, u32[]{:S(2)}, u32[]{:S(2)}) %all-to-all-start.2) | async-done | bytes 663584 | tf_op jit(solution)/shard_map/all_to_all | solution.py:260
  (103 shorter events, 28.8 us)
Async XLA Ops:
  7.2 8.3 %copy-start.6 = (bf16[1,8,8,16,384]{4,3,2,1,0:T(8,128)(2,1)S(1)}, bf16[1,8,8,16,384]{4,3,2,1,0:T(8,128)(2,1)}, u32[]{:S(2)}) copy-start(bf16[1,8,8,16,384]{4,3,2,1,0:T(8,128)(2,1)} %param.7) | copy-start | bytes 2359300
  7.2 58.0 %all-gather.2.cloned.1.call-start = ((), (), s32[]{:S(2)}) async-start(), calls=%async_computation.3 | async-start | bytes 8957952 | tf_op jit(solution)/shard_map/all_gather | solution.py:275
  9.1 6.4 %collective-permute-start = (bf16[16,512]{1,0:T(8,128)(2,1)S(1)}, bf16[16,512]{1,0:T(8,128)(2,1)S(1)}, u32[]{:S(2)}, u32[]{:S(2)}) collective-permute-start(bf16[16,512]{1,0:T(8,128)(2,1)S(1)} %slice.120), channel_id=1, source_target_pairs={{0,1},{1,2},{2,3},{4,5},{5,6},{6,7},{8,9},{9,10},{10,11},{12,13},{... | collective-permute-start | bytes 49160 | tf_op jit(solution)/shard_map/ppermute | solution.py:19
  15.5 11.4 %collective-permute-start.1 = (bf16[16,1536]{1,0:T(8,128)(2,1)S(1)}, bf16[16,1536]{1,0:T(8,128)(2,1)S(1)}, u32[]{:S(2)}, u32[]{:S(2)}) collective-permute-start(bf16[16,1536]{1,0:T(8,128)(2,1)S(1)} %pad_maximum_fusion.1.refs_0_), channel_id=1, source_target_pairs={{0,4},{4,0},{8,12},{12,8},{16,20},{20,16},{24,28},{28,24},{1,5},{5... | collective-permute-start | bytes 147464 | tf_op jit(solution)/shard_map/ppermute | solution.py:23
  65.2 16.1 %copy-start.12 = (f32[384,128]{1,0:T(8,128)S(1)}, f32[384,128]{1,0:T(8,128)}, u32[]{:S(2)}) copy-start(f32[384,128]{1,0:T(8,128)} %get-tuple-element.40) | copy-start | bytes 589828
  80.5 7.2 %copy-start.2 = (bf16[384,1024]{1,0:T(8,128)(2,1)}, bf16[384,1024]{1,0:T(8,128)(2,1)S(1)}, u32[]{:S(2)}) copy-start(bf16[384,1024]{1,0:T(8,128)(2,1)S(1)} %get-tuple-element.53.refs_4_) | copy-start | bytes 2359300
  80.5 5.0 %collective-permute-start.2 = (bf16[384,1024]{1,0:T(8,128)(2,1)S(1)}, bf16[384,1024]{1,0:T(8,128)(2,1)S(1)}, u32[]{:S(2)}, u32[]{:S(2)}) collective-permute-start(bf16[384,1024]{1,0:T(8,128)(2,1)S(1)} %get-tuple-element.53.refs_4_), channel_id=1, source_target_pairs={{0,4},{4,0},{8,12},{12,8},{16,20},{20,16},{24,28},{28,24},{1,5},{5... | collective-permute-start | bytes 2359304 | tf_op jit(solution)/shard_map/ppermute | solution.py:23
  102.6 23.9 %collective-permute-start.3 = (f16[720,384]{1,0:T(8,128)(2,1)}, f16[720,384]{1,0:T(8,128)(2,1)S(1)}, u32[]{:S(2)}, u32[]{:S(2)}) collective-permute-start(f16[720,384]{1,0:T(8,128)(2,1)} %get-tuple-element.42), channel_id=1, source_target_pairs={{0,8},{4,12},{8,0},{12,4},{16,24},{20,28},{24,16},{28,20},{1,9},{5... | collective-permute-start | bytes 1658888 | tf_op jit(solution)/shard_map/ppermute | solution.py:198
  104.1 27.0 %collective-permute-start.4 = (f16[720,384]{1,0:T(8,128)(2,1)}, f16[720,384]{1,0:T(8,128)(2,1)}, u32[]{:S(2)}, u32[]{:S(2)}) collective-permute-start(f16[720,384]{1,0:T(8,128)(2,1)} %get-tuple-element.43), channel_id=1, source_target_pairs={{0,16},{4,20},{8,24},{12,28},{16,0},{20,4},{24,8},{28,12},{1,17},{... | collective-permute-start | bytes 1658888 | tf_op jit(solution)/shard_map/ppermute | solution.py:198
  104.6 26.4 %collective-permute-start.5 = (f16[720,384]{1,0:T(8,128)(2,1)}, f16[720,384]{1,0:T(8,128)(2,1)}, u32[]{:S(2)}, u32[]{:S(2)}) collective-permute-start(f16[720,384]{1,0:T(8,128)(2,1)} %get-tuple-element.44), channel_id=1, source_target_pairs={{0,24},{4,28},{8,16},{12,20},{16,8},{20,12},{24,0},{28,4},{1,25},{... | collective-permute-start | bytes 1658888 | tf_op jit(solution)/shard_map/ppermute | solution.py:198
  107.1 28.7 %collective-permute-start.15 = (bf16[384,256]{1,0:T(8,128)(2,1)S(1)}, bf16[384,256]{1,0:T(8,128)(2,1)S(1)}, u32[]{:S(2)}, u32[]{:S(2)}) collective-permute-start(bf16[384,256]{1,0:T(8,128)(2,1)S(1)} %slice.141), channel_id=1, source_target_pairs={{1,0},{2,1},{3,2},{5,4},{6,5},{7,6},{9,8},{10,9},{11,10},{13,12},{... | collective-permute-start | bytes 589832 | tf_op jit(solution)/shard_map/ppermute | solution.py:19
  125.0 13.2 %copy-start.3 = (bf16[384,1024]{1,0:T(8,128)(2,1)S(1)}, bf16[384,1024]{1,0:T(8,128)(2,1)}, u32[]{:S(2)}) copy-start(bf16[384,1024]{1,0:T(8,128)(2,1)} %copy-done.2) | copy-start | bytes 2359300
  125.0 36.2 %collective-permute-start.12 = (f16[720,384]{1,0:T(8,128)(2,1)S(1)}, f16[720,384]{1,0:T(8,128)(2,1)S(1)}, u32[]{:S(2)}, u32[]{:S(2)}) collective-permute-start(f16[720,384]{1,0:T(8,128)(2,1)S(1)} %get-tuple-element.50), channel_id=1, source_target_pairs={{0,8},{4,12},{8,0},{12,4},{16,24},{20,28},{24,16},{28,20},{1,9},{5... | collective-permute-start | bytes 1658888 | tf_op jit(solution)/shard_map/ppermute | solution.py:198
  126.6 12.6 %copy-start.7 = (f16[720,384]{1,0:T(8,128)(2,1)}, f16[720,384]{1,0:T(8,128)(2,1)S(1)}, u32[]{:S(2)}) copy-start(f16[720,384]{1,0:T(8,128)(2,1)S(1)} %collective-permute-done.3) | copy-start | bytes 1658884
  126.6 36.1 %collective-permute-start.13 = (f16[720,384]{1,0:T(8,128)(2,1)S(1)}, f16[720,384]{1,0:T(8,128)(2,1)S(1)}, u32[]{:S(2)}, u32[]{:S(2)}) collective-permute-start(f16[720,384]{1,0:T(8,128)(2,1)S(1)} %get-tuple-element.51), channel_id=1, source_target_pairs={{0,16},{4,20},{8,24},{12,28},{16,0},{20,4},{24,8},{28,12},{1,17},{... | collective-permute-start | bytes 1658888 | tf_op jit(solution)/shard_map/ppermute | solution.py:198
  131.1 31.6 %collective-permute-start.14 = (f16[720,384]{1,0:T(8,128)(2,1)S(1)}, f16[720,384]{1,0:T(8,128)(2,1)S(1)}, u32[]{:S(2)}, u32[]{:S(2)}) collective-permute-start(f16[720,384]{1,0:T(8,128)(2,1)S(1)} %get-tuple-element.52), channel_id=1, source_target_pairs={{0,24},{4,28},{8,16},{12,20},{16,8},{20,12},{24,0},{28,4},{1,25},{... | collective-permute-start | bytes 1658888 | tf_op jit(solution)/shard_map/ppermute | solution.py:198
  134.2 36.0 %collective-permute-start.6 = (f16[192,384]{1,0:T(8,128)(2,1)}, f16[192,384]{1,0:T(8,128)(2,1)S(1)}, u32[]{:S(2)}, u32[]{:S(2)}) collective-permute-start(f16[192,384]{1,0:T(8,128)(2,1)} %get-tuple-element.47), channel_id=1, source_target_pairs={{0,1},{1,2},{2,3},{3,0},{4,5},{5,6},{6,7},{7,4},{8,9},{9,10},{10,1... | collective-permute-start | bytes 442376 | tf_op jit(solution)/shard_map/ppermute | solution.py:204
  135.7 37.1 %collective-permute-start.7 = (f16[192,384]{1,0:T(8,128)(2,1)}, f16[192,384]{1,0:T(8,128)(2,1)S(1)}, u32[]{:S(2)}, u32[]{:S(2)}) collective-permute-start(f16[192,384]{1,0:T(8,128)(2,1)} %get-tuple-element.48), channel_id=1, source_target_pairs={{0,2},{1,3},{2,0},{3,1},{4,6},{5,7},{6,4},{7,5},{8,10},{9,11},{10,... | collective-permute-start | bytes 442376 | tf_op jit(solution)/shard_map/ppermute | solution.py:204
  161.2 11.7 %collective-permute-start.8 = (f16[192,384]{1,0:T(8,128)(2,1)}, f16[192,384]{1,0:T(8,128)(2,1)S(1)}, u32[]{:S(2)}, u32[]{:S(2)}) collective-permute-start(f16[192,384]{1,0:T(8,128)(2,1)} %get-tuple-element.49), channel_id=1, source_target_pairs={{0,3},{1,0},{2,1},{3,2},{4,7},{5,4},{6,5},{7,6},{8,11},{9,8},{10,9... | collective-permute-start | bytes 442376 | tf_op jit(solution)/shard_map/ppermute | solution.py:204
  163.8 14.2 %collective-permute-start.16 = (f16[192,384]{1,0:T(8,128)(2,1)}, f16[192,384]{1,0:T(8,128)(2,1)}, u32[]{:S(2)}, u32[]{:S(2)}) collective-permute-start(f16[192,384]{1,0:T(8,128)(2,1)} %get-tuple-element.60), channel_id=1, source_target_pairs={{0,1},{1,2},{2,3},{3,0},{4,5},{5,6},{6,7},{7,4},{8,9},{9,10},{10,1... | collective-permute-start | bytes 442376 | tf_op jit(solution)/shard_map/ppermute | solution.py:204
  164.4 14.6 %collective-permute-start.17 = (f16[192,384]{1,0:T(8,128)(2,1)}, f16[192,384]{1,0:T(8,128)(2,1)}, u32[]{:S(2)}, u32[]{:S(2)}) collective-permute-start(f16[192,384]{1,0:T(8,128)(2,1)} %get-tuple-element.61), channel_id=1, source_target_pairs={{0,2},{1,3},{2,0},{3,1},{4,6},{5,7},{6,4},{7,5},{8,10},{9,11},{10,... | collective-permute-start | bytes 442376 | tf_op jit(solution)/shard_map/ppermute | solution.py:204
  166.1 34.3 %all-to-all-start = ((f32[8,54,384]{2,1,0:T(8,128)}), f32[8,54,384]{2,1,0:T(8,128)S(1)}, u32[]{:S(2)}, u32[]{:S(2)}) async-start(f32[8,54,384]{2,1,0:T(8,128)} %reshape.52), calls=%async_computation | async-start | bytes 1376256 | tf_op jit(solution)/shard_map/all_to_all | solution.py:258
  170.3 8.9 %collective-permute-start.18 = (f16[192,384]{1,0:T(8,128)(2,1)}, f16[192,384]{1,0:T(8,128)(2,1)S(1)}, u32[]{:S(2)}, u32[]{:S(2)}) collective-permute-start(f16[192,384]{1,0:T(8,128)(2,1)} %get-tuple-element.62), channel_id=1, source_target_pairs={{0,3},{1,0},{2,1},{3,2},{4,7},{5,4},{6,5},{7,6},{8,11},{9,8},{10,9... | collective-permute-start | bytes 442376 | tf_op jit(solution)/shard_map/ppermute | solution.py:204
  174.9 8.5 %collective-permute-start.11 = (f16[192,384]{1,0:T(8,128)(2,1)S(1)}, f16[192,384]{1,0:T(8,128)(2,1)S(1)}, u32[]{:S(2)}, u32[]{:S(2)}) collective-permute-start(f16[192,384]{1,0:T(8,128)(2,1)S(1)} %fusion.68), channel_id=1, source_target_pairs={{0,3},{1,0},{2,1},{3,2},{4,7},{5,4},{6,5},{7,6},{8,11},{9,8},{10,9... | collective-permute-start | bytes 442376 | tf_op jit(solution)/shard_map/ppermute | solution.py:204
  176.1 22.6 %collective-permute-start.10 = (f16[192,384]{1,0:T(8,128)(2,1)S(1)}, f16[192,384]{1,0:T(8,128)(2,1)S(1)}, u32[]{:S(2)}, u32[]{:S(2)}) collective-permute-start(f16[192,384]{1,0:T(8,128)(2,1)S(1)} %fusion.68), channel_id=1, source_target_pairs={{0,2},{1,3},{2,0},{3,1},{4,6},{5,7},{6,4},{7,5},{8,10},{9,11},{10,... | collective-permute-start | bytes 442376 | tf_op jit(solution)/shard_map/ppermute | solution.py:204
  178.0 20.7 %collective-permute-start.9 = (f16[192,384]{1,0:T(8,128)(2,1)S(1)}, f16[192,384]{1,0:T(8,128)(2,1)S(1)}, u32[]{:S(2)}, u32[]{:S(2)}) collective-permute-start(f16[192,384]{1,0:T(8,128)(2,1)S(1)} %fusion.68), channel_id=1, source_target_pairs={{0,1},{1,2},{2,3},{3,0},{4,5},{5,6},{6,7},{7,4},{8,9},{9,10},{10,1... | collective-permute-start | bytes 442376 | tf_op jit(solution)/shard_map/ppermute | solution.py:204
  180.6 25.6 %collective-permute-start.21 = (f16[192,384]{1,0:T(8,128)(2,1)S(1)}, f16[192,384]{1,0:T(8,128)(2,1)S(1)}, u32[]{:S(2)}, u32[]{:S(2)}) collective-permute-start(f16[192,384]{1,0:T(8,128)(2,1)S(1)} %fusion.30), channel_id=1, source_target_pairs={{0,3},{1,0},{2,1},{3,2},{4,7},{5,4},{6,5},{7,6},{8,11},{9,8},{10,9... | collective-permute-start | bytes 442376 | tf_op jit(solution)/shard_map/ppermute | solution.py:204
  183.4 22.8 %collective-permute-start.20 = (f16[192,384]{1,0:T(8,128)(2,1)S(1)}, f16[192,384]{1,0:T(8,128)(2,1)S(1)}, u32[]{:S(2)}, u32[]{:S(2)}) collective-permute-start(f16[192,384]{1,0:T(8,128)(2,1)S(1)} %fusion.30), channel_id=1, source_target_pairs={{0,2},{1,3},{2,0},{3,1},{4,6},{5,7},{6,4},{7,5},{8,10},{9,11},{10,... | collective-permute-start | bytes 442376 | tf_op jit(solution)/shard_map/ppermute | solution.py:204
  183.4 22.8 %collective-permute-start.19 = (f16[192,384]{1,0:T(8,128)(2,1)S(1)}, f16[192,384]{1,0:T(8,128)(2,1)S(1)}, u32[]{:S(2)}, u32[]{:S(2)}) collective-permute-start(f16[192,384]{1,0:T(8,128)(2,1)S(1)} %fusion.30), channel_id=1, source_target_pairs={{0,1},{1,2},{2,3},{3,0},{4,5},{5,6},{6,7},{7,4},{8,9},{9,10},{10,1... | collective-permute-start | bytes 442376 | tf_op jit(solution)/shard_map/ppermute | solution.py:204
  201.2 12.5 %all-to-all-start.1 = ((f32[4,54,384]{2,1,0:T(8,128)}), f32[4,54,384]{2,1,0:T(8,128)S(1)}, u32[]{:S(2)}, u32[]{:S(2)}) async-start(f32[4,54,384]{2,1,0:T(8,128)} %broadcast_in_dim.61), calls=%async_computation.1 | async-start | bytes 688128 | tf_op jit(solution)/shard_map/all_to_all | solution.py:259
  214.7 15.3 %all-to-all-start.2 = ((f32[8,54,384]{2,1,0:T(8,128)}), f32[8,54,384]{2,1,0:T(8,128)S(1)}, u32[]{:S(2)}, u32[]{:S(2)}) async-start(f32[8,54,384]{2,1,0:T(8,128)} %broadcast_in_dim.62), calls=%async_computation.2 | async-start | bytes 1376256 | tf_op jit(solution)/shard_map/all_to_all | solution.py:260
  219.3 11.6 %copy-start.1 = (bf16[1,8,8,32,16]{3,4,2,1,0:T(8,128)(2,1)S(1)}, bf16[1,8,8,32,16]{3,4,2,1,0:T(8,128)(2,1)}, u32[]{:S(2)}) copy-start(bf16[1,8,8,32,16]{3,4,2,1,0:T(8,128)(2,1)} %param.5) | copy-start | bytes 196612
  (9 other events, 13.3 us)
Sparse Core Ops, SparseCore 0:
  9.9 55.2 all-gather.1

commit v5 on v4

v5 whole, which is shorter than its diff:
```python
import math

import jax
import jax.numpy as jnp
from jax import lax
from jax.experimental import pallas as pl
from jax.experimental.pallas import tpu as pltpu
from jax.sharding import PartitionSpec as P

F32 = jnp.float32
BF16 = jnp.bfloat16
F16 = jnp.float16
VMEM = 56 * 1024 * 1024


def passed_along(block, axis, distance):
    devices = range(lax.axis_size(axis))
    route = [(i - distance, i) for i in devices if i - distance in devices]
    return lax.ppermute(block, axis, route)


def swapped(block):
    return lax.ppermute(block, "clip", [(i, i ^ 1) for i in range(lax.axis_size("clip"))])


def piece_rows(rows):
    return rows // lax.axis_size("tm") // 16 * 16 + 16


def padded(rows):
    return piece_rows(rows) * lax.axis_size("tm") + 16


def shifted(x, row_off, col_off, rows, cols):
    lanes = x.shape[1]
    lane = lax.broadcasted_iota(jnp.int32, (1, lanes), 1)
    row = (lane // cols) % rows + row_off
    col = lane % cols + col_off
    good = (row >= 0) & (row < rows) & (col >= 0) & (col < cols)
    shift = row_off * cols + col_off
    return jnp.where(good, pltpu.roll(x, (lanes - shift) % lanes, axis=1), 0.0)


def contract(left, right, dims):
    return lax.dot_general(left, right, (dims, ((), ())), preferred_element_type=F32)


def fill_columns(out_ref, x, rows, cols):
    cells, chans = x.shape
    frames = cells // (rows * cols)
    zero = jnp.zeros((frames, cols, chans), BF16)
    place = lax.broadcasted_iota(jnp.int32, (cells, 1), 0) % cols
    for c in range(3):
        moved = x
        if c != 1:
            good = (place + c - 1 >= 0) & (place + c - 1 < cols)
            moved = jnp.where(good, pltpu.roll(x, (1 - c) % cells, axis=0), 0.0)
        out_ref[c, :, 0] = zero
        out_ref[c, :, rows + 1] = zero
        out_ref[c, :, 1 : rows + 1] = moved.astype(BF16).reshape(frames, rows, cols, chans)


def window(ref, column, frame, row, frames, rows):
    x = ref[column, pl.ds(frame, frames), pl.ds(row, rows)]
    return x.reshape(frames * rows * x.shape[2], x.shape[3])


def front_kernel(crop_ref, w_ref, *refs, rows, cols, first):
    if first:
        patch_ref, z_ref, cells_ref, taps_ref, top_ref, full_ref = refs
    else:
        taps_ref, top_ref, full_ref = refs
    plane = rows * cols
    lat = crop_ref.shape[0]
    ext = full_ref.shape[1]
    count = ext - 2 * plane

    @pl.when(pl.program_id(0) == 0)
    def _():
        crop = crop_ref[...].astype(F32)
        for spot in range(9):
            moved = shifted(crop, spot // 3 - 1, spot % 3 - 1, rows, cols).astype(BF16)
            for depth in range(3):
                at = (depth * 9 + spot) * lat
                full_ref[at : at + lat, :] = moved[:, depth * plane : depth * plane + ext]
        if first:
            patch_ref[...] = full_ref[:, 2 * plane :]

    z = contract(w_ref[...], full_ref[...], ((0,), (0,)))
    act = (z * (1.0 / (1.0 + jnp.exp(-z)))).astype(BF16).astype(F32)
    top_ref[...] = jnp.broadcast_to(jnp.max(jnp.abs(act), axis=1, keepdims=True), top_ref.shape)
    for spot in range(9):
        moved = shifted(act, spot // 3 - 1, spot % 3 - 1, rows, cols).astype(BF16)
        for depth in range(3):
            taps_ref[depth * 9 + spot] = moved[:, depth * plane : depth * plane + count]
    if first:
        z_ref[...] = z[:, 2 * plane :].T
        fill_columns(cells_ref, act.T, rows, cols)


def front(crop_t, w_in, rows, cols, count, first):
    chans = w_in.shape[1]
    depth_in = w_in.shape[0]
    plane = rows * cols
    block = 128
    frames = count // plane + 2
    specs = [
        pl.BlockSpec((27, block, count), lambda i: (0, i, 0)),
        pl.BlockSpec((block, 128), lambda i: (i, 0)),
    ]
    shapes = [
        jax.ShapeDtypeStruct((27, chans, count), BF16),
        jax.ShapeDtypeStruct((chans, 128), F32),
    ]
    if first:
        specs = [
            pl.BlockSpec((depth_in, count), lambda i: (0, 0)),
            pl.BlockSpec((count, block), lambda i: (0, i)),
            pl.BlockSpec((3, frames, rows + 2, cols, block), lambda i: (0, 0, 0, 0, i)),
        ] + specs
        shapes = [
            jax.ShapeDtypeStruct((depth_in, count), BF16),
            jax.ShapeDtypeStruct((count, chans), F32),
            jax.ShapeDtypeStruct((3, frames, rows + 2, cols, chans), BF16),
        ] + shapes
    return pl.pallas_call(
        lambda *refs: front_kernel(*refs, rows=rows, cols=cols, first=first),
        grid=(chans // block,),
        in_specs=[
            pl.BlockSpec(crop_t.shape, lambda i: (0, 0)),
            pl.BlockSpec((depth_in, block), lambda i: (0, i)),
        ],
        out_specs=specs,
        out_shape=shapes,
        scratch_shapes=[pltpu.VMEM((depth_in, count + 2 * plane), BF16)],
        compiler_params=pltpu.CompilerParams(vmem_limit_bytes=VMEM),
        name="front",
    )(crop_t, w_in)


def middle_kernel(cells_ref, w_ref, teacher_ref, g_ref, size_ref, acc_ref, *, scale):
    depth = pl.program_id(0)
    frames = cells_ref.shape[1] - 2
    rows = cells_ref.shape[2] - 2
    chans = w_ref.shape[2]
    left = jnp.concatenate(
        [window(cells_ref, k % 3, depth, k // 3, frames, rows) for k in range(9)], axis=1
    )
    total = contract(left, w_ref[...].reshape(9 * chans, chans), ((1,), (0,)))

    @pl.when(depth == 0)
    def _():
        acc_ref[...] = total

    @pl.when(depth == 1)
    def _():
        acc_ref[...] += total

    @pl.when(depth == 2)
    def _():
        g = ((acc_ref[...] + total - teacher_ref[...].astype(F32)) * scale).astype(BF16)
        g_ref[...] = g
        size = jnp.max(jnp.sum(jnp.abs(g.astype(F32)), axis=0, keepdims=True), axis=1, keepdims=True)
        size_ref[...] = jnp.broadcast_to(size, size_ref.shape)


def middle(cells, w_taps, teacher, scale):
    count, chans = teacher.shape
    return pl.pallas_call(
        lambda *refs: middle_kernel(*refs, scale=scale),
        grid=(3,),
        in_specs=[
            pl.BlockSpec(cells.shape, lambda i: (0,) * 5),
            pl.BlockSpec((9, chans, chans), lambda i: (i, 0, 0)),
            pl.BlockSpec((count, chans), lambda i: (0, 0)),
        ],
        out_specs=[
            pl.BlockSpec((count, chans), lambda i: (0, 0)),
            pl.BlockSpec((8, 128), lambda i: (0, 0)),
        ],
        out_shape=[
            jax.ShapeDtypeStruct((count, chans), BF16),
            jax.ShapeDtypeStruct((8, 128), F32),
        ],
        scratch_shapes=[pltpu.VMEM((count, chans), F32)],
        compiler_params=pltpu.CompilerParams(vmem_limit_bytes=VMEM),
        name="middle",
    )(cells, w_taps, teacher)


def grad_kernel(order_ref, *refs):
    own_ref, out_ref = refs[-2:]
    at_once = (len(refs) - 4) // 2
    rows = refs[0].shape[0]
    zero = jnp.zeros((own_ref.shape[0] - rows, own_ref.shape[1]), F32)
    for i in range(at_once):
        total = contract(refs[2 * i][...], refs[2 * at_once][...], ((1,), (0,)))
        total += contract(refs[2 * i + 1][...], refs[2 * at_once + 1][...], ((1,), (0,)))
        if i == 0:
            @pl.when(pl.program_id(0) == 0)
            def _():
                own_ref[:rows, :] = total
                own_ref[rows:, :] = zero

        out_ref[i, :rows, :] = total
        out_ref[i, rows:, :] = zero


def grad_chunk(order, taps, g, parts, which):
    blocks = order.shape[0]
    total, count = taps[0].shape
    chans = g[0].shape[1]
    rows = total // (2 * blocks) // parts
    at_once = 2
    tap_specs = []
    for i in range(at_once):
        spec = pl.BlockSpec((rows, count), lambda s, order, i=i: (order[s * at_once + i] * parts + which, 0))
        tap_specs += [spec, spec]
    whole = pl.BlockSpec((count, chans), lambda s, order: (0, 0))
    return pl.pallas_call(
        grad_kernel,
        grid_spec=pltpu.PrefetchScalarGridSpec(
            num_scalar_prefetch=1,
            grid=(blocks // at_once,),
            in_specs=tap_specs + [whole, whole],
            out_specs=[
                pl.BlockSpec((padded(rows), chans), lambda s, order: (0, 0)),
                pl.BlockSpec((at_once, padded(rows), chans), lambda s, order: (s, 0, 0)),
            ],
        ),
        out_shape=[
            jax.ShapeDtypeStruct((padded(rows), chans), F32),
            jax.ShapeDtypeStruct((blocks, padded(rows), chans), F32),
        ],
        compiler_params=pltpu.CompilerParams(vmem_limit_bytes=VMEM),
        name="grad",
    )(order, *(list(taps) * at_once), *g)


def back_kernel(g_ref, later_ref, w_ref, z_ref, patch_ref, out_ref, cells_ref, acc_ref, *, rows, cols):
    depth = pl.program_id(0)
    frames = cells_ref.shape[1] - 2

    @pl.when(depth == 0)
    def _():
        g = jnp.concatenate([g_ref[...], later_ref[...]], axis=0).astype(F32)
        fill_columns(cells_ref, g, rows, cols)

    left = jnp.concatenate(
        [window(cells_ref, 2 - k % 3, 2 - depth, 2 - k // 3, frames, rows) for k in range(9)], axis=1
    )
    right = jnp.concatenate([w_ref[k] for k in range(9)], axis=1)
    total = contract(left, right, ((1,), (1,)))

    @pl.when(depth == 0)
    def _():
        acc_ref[...] = total

    @pl.when(depth == 1)
    def _():
        acc_ref[...] += total

    @pl.when(depth == 2)
    def _():
        z = z_ref[...]
        sig = 1.0 / (1.0 + jnp.exp(-z))
        dz = ((acc_ref[...] + total) * sig * (1.0 + z * (1.0 - sig))).astype(BF16)
        out_ref[...] = contract(patch_ref[...], dz, ((1,), (0,)))


def back(g, later, w_taps, z, patch_t, rows, cols):
    count, chans = z.shape
    depth_in = patch_t.shape[0]
    frames = count // (rows * cols) + 2
    return pl.pallas_call(
        lambda *refs: back_kernel(*refs, rows=rows, cols=cols),
        grid=(3,),
        in_specs=[
            pl.BlockSpec(g.shape, lambda i: (0, 0)),
            pl.BlockSpec(later.shape, lambda i: (0, 0)),
            pl.BlockSpec((9, chans, chans), lambda i: (i, 0, 0)),
            pl.BlockSpec((count, chans), lambda i: (0, 0)),
            pl.BlockSpec((depth_in, count), lambda i: (0, 0)),
        ],
        out_specs=pl.BlockSpec((depth_in, chans), lambda i: (0, 0)),
        out_shape=jax.ShapeDtypeStruct((depth_in, chans), F32),
        scratch_shapes=[
            pltpu.VMEM((3, frames, rows + 2, cols, chans), BF16),
            pltpu.VMEM((count, chans), F32),
        ],
        compiler_params=pltpu.CompilerParams(vmem_limit_bytes=VMEM),
        name="back",
    )(g, later, w_taps, z, patch_t)


def packed(x, rows, bound):
    power = jnp.ceil(jnp.log2(jnp.maximum(bound, 1e-30)))
    row = lax.broadcasted_iota(jnp.int32, x.shape, 0)
    return jnp.where(row < rows, x * jnp.exp2(14.0 - power), power).astype(F16)


def across_plane(part, rows, bound, after):
    clips = lax.axis_size("clip")
    payloads = [packed(part[q], rows, bound) for q in range(1, clips // 2)]
    payloads, after = lax.optimization_barrier((payloads, after))
    got = []
    for q in range(1, clips // 2):
        route = [(i, i ^ (2 * q)) for i in range(clips)]
        got.append(lax.ppermute(payloads[q - 1], "clip", route))
    return got, after


def around(blocks, distance):
    depth = lax.axis_size("tm")
    return lax.ppermute(blocks, "tm", [(i, (i + distance) % depth) for i in range(depth)])


def scales(got, rows, bound):
    powers = [jnp.exp2(x[rows : rows + 1].astype(F32)) for x in got]
    return [power * 2.0**-14 for power in powers], (bound + sum(powers)) * 1.01


def across_depth(own, got, rows, factors, total, after, at_once):
    depth = lax.axis_size("tm")
    me = lax.axis_index("tm")
    small = piece_rows(rows)

    def piece(place):
        first = place * small
        terms = lax.dynamic_slice_in_dim(own, first, small + 16, axis=0)
        for x, factor in zip(got, factors):
            terms = terms + lax.dynamic_slice_in_dim(x, first, small + 16, axis=0).astype(F32) * factor
        return terms

    if at_once:
        payload = jnp.concatenate([packed(piece(d), small, total) for d in range(depth)], axis=0)
        payload, after = lax.optimization_barrier((payload, after))
        got = lax.all_to_all(payload, "tm", 0, 0, tiled=True)
        return (None, [got[d * (small + 16) : (d + 1) * (small + 16)] for d in range(depth)]), after
    payloads = [packed(piece((me + d) % depth), small, total) for d in range(1, depth)]
    payloads, after = lax.optimization_barrier((payloads, after))
    others = [around(payloads[d - 1], d) for d in range(1, depth)]
    return (piece(me), others), after


def spread(own, got, small, factors, total):
    depth = lax.axis_size("tm")
    terms = [x.astype(F32) * factor for x, factor in zip(got, factors)]
    own = sum(terms) if own is None else own + sum(terms)
    payload = packed(own, small, total)
    return [payload] + [around(payload, depth - k) for k in range(1, depth)]


def assembled(pieces, factors, small, rows):
    depth = lax.axis_size("tm")
    me = lax.axis_index("tm")
    pieces = [x[:small].astype(F32) * factor for x, factor in zip(pieces, factors)]
    out = []
    for place in range(depth):
        x = pieces[0]
        for k in range(1, depth):
            x = jnp.where((me + k) % depth == place, pieces[k], x)
        count = min(small, rows - place * small)
        if count <= 0:
            break
        out.append(x[:count])
    return out


def cast_to_all(block, axis):
    size = lax.axis_size(axis)
    return lax.all_to_all(jnp.broadcast_to(block[None], (size,) + block.shape), axis, 0, 0, tiled=True)


def shards(latent, offsets, teacher, w_in, w_mid):
    frames = teacher.shape[1]
    rows = teacher.shape[2]
    cols = teacher.shape[3]
    chans = teacher.shape[4]
    plane = rows * cols
    count = frames * plane
    lat_chans = latent.shape[4]
    clips = lax.axis_size("clip")
    total_cells = clips * lax.axis_size("tm") * count
    scale = 2.0 / math.sqrt(total_cells)
    w_full = lax.all_gather(w_mid, "clip", axis=0, tiled=True)
    crop = lax.dynamic_slice_in_dim(latent[0], offsets[0], cols, axis=2).reshape(count, lat_chans).T
    earlier = passed_along(crop[:, count - 4 * plane :], "tm", 1)
    crop_ext = jnp.concatenate([earlier, crop], axis=1)
    patch_t, z, cells, taps, top = front(crop_ext, w_in, rows, cols, count, True)
    pair_taps, pair_top = front(swapped(crop_ext), w_in, rows, cols, count, False)
    taps = taps.reshape(27 * chans, count)
    pair_taps = pair_taps.reshape(27 * chans, count)
    w_full, pair_taps, pair_top = lax.optimization_barrier((w_full, pair_taps, pair_top))
    w_taps = w_full.reshape(27, chans, chans)
    g, size = middle(cells, w_taps, teacher[0].reshape(count, chans), scale)
    pair_g = swapped(g)
    pair_size = swapped(size)
    later = passed_along(g[: 2 * plane], "tm", -1)

    order = lax.axis_index("clip") ^ (2 * jnp.arange(clips // 2, dtype=jnp.int32))
    block_rows = 27 * chans // clips
    chunks = next(c for c in (2, 3, 1) if block_rows % (8 * c) == 0)
    part_rows = block_rows // chunks
    bound = (jnp.max(top) * size[:1, :1] + jnp.max(pair_top) * pair_size[:1, :1]) * 1.01
    plane_got = []
    g_now = g
    for j in range(chunks):
        own, part = grad_chunk(order, (taps, pair_taps), (g_now, pair_g), chunks, j)
        got, g_now = across_plane(part, part_rows, bound, g_now)
        later, g_now = lax.optimization_barrier((later, g_now))
        plane_got.append((own, got))
    factors, total = scales(plane_got[0][1], part_rows, bound)
    first, g_now = across_depth(*plane_got[0], part_rows, factors, total, g_now, True)
    depth_got = [first]
    in_part = back(g_now, later, w_taps, z, patch_t, rows, cols)
    for own, got in plane_got[1:]:
        got, in_part = lax.optimization_barrier((got, in_part))
        more, in_part = across_depth(own, got, part_rows, factors, total, in_part, False)
        depth_got.append(more)
    in_rows = in_part.shape[0]
    in_got = lax.all_to_all(in_part.reshape(clips, in_rows // clips, chans), "clip", 0, 0, tiled=True)
    small = piece_rows(part_rows)
    factors, total = scales(depth_got[0][1], small, 0.0)
    last = []
    for own, got in depth_got:
        if last:
            in_got, got, last[-1][0] = lax.optimization_barrier((in_got, got, last[-1][0]))
            factors, _ = scales(got, small, 0.0)
        last.append(spread(own, got, small, factors, total))
        if len(last) == 2:
            in_got = cast_to_all(in_got.sum(axis=0), "tm")
    if len(last) == 1:
        in_got = cast_to_all(in_got.sum(axis=0), "tm")
    grad_in = cast_to_all(in_got.sum(axis=0), "clip").reshape(in_rows, chans)
    factors, _ = scales(last[0], small, 0.0)
    pieces = []
    for got in last:
        pieces += assembled(got, factors, small, part_rows)
    return (jnp.concatenate(pieces, axis=0), grad_in)


def solution(mesh):
    return jax.shard_map(
        shards,
        mesh=mesh,
        in_specs=(
            P("clip", "tm", None, None, None),
            P("clip"),
            P("clip", "tm", None, None, None),
            P(),
            P("clip", None),
        ),
        out_specs=(P("clip", None), P()),
        check_vma=False,
    )
```

time: 239 us -> 247 us (1.033)
  matrix products: 15.2 us -> 0 us
  Pallas kernels: 66 us -> 80.3 us
  starting transfers between devices: 46.2 us -> 56.9 us
  other arithmetic: 24.9 us -> 20.6 us
  waiting for transfers between devices: 58.6 us -> 62.1 us
    pallas_call x2 -> x3, Pallas kernels: 21.1 us -> 38.9 us  [the longest x2 22.2 us: front(): pl.pallas_call(lambda *refs: front_kernel(*refs, rows=rows, cols=cols, fi...]
    dot_general x1 -> x0, matrix products: 15.2 us -> none  [contract(): lax.dot_general(left, right, (dims, ((), ())), preferred_element_type=F32)]
    ppermute x2, waiting for transfers between devices: 1.43 us -> 8.01 us  [passed_along(): return lax.ppermute(block, axis, route)]
    ppermute x12 -> x9, starting transfers between devices: 22.4 us -> 27.4 us  [around(): lax.ppermute(blocks, 'tm', [(i, (i + distance) % depth) for i in range(de...]
    pallas_call x1, Pallas kernels: 22 us -> 17.5 us  [back(): pl.pallas_call(lambda *refs: back_kernel(*refs, rows=rows, cols=cols), gr...]
    all_to_all x3 -> x4, starting transfers between devices: 11.5 us -> 15.5 us  [the longest x2 8.06 us: cast_to_all(): lax.all_to_all(jnp.broadcast_to(block[None], (size,) + block.shape), axis...]
    all_to_all x3 -> x4, waiting for transfers between devices: 15.9 us -> 12 us  [the longest x2 11.9 us: cast_to_all(): lax.all_to_all(jnp.broadcast_to(block[None], (size,) + block.shape), axis...]
    ppermute x6, waiting for transfers between devices: 3.96 us -> 6.5 us  [across_plane(): got.append(lax.ppermute(payloads[q - 1], 'clip', route))]
  transfers between devices with their start and end apart: 26 -> 25, of which waited for: 7 -> 8; matrix products, arithmetic and copies ran while one was open for 11% -> 9% of each run, Pallas kernels for 23% -> 21%
where the time goes in v5:
time: 247 us; the launch traced here: 246 us
  Pallas kernels  80.3 us (33%)
  waiting for transfers between devices  62.1 us (25%)
  starting transfers between devices  56.9 us (23%)
  other arithmetic  20.6 us (8%)
  between operations  17.6 us (7%)
  local copies, waits for them, and re-layouts  8.83 us (4%)
    ppermute x9, starting transfers between devices, around(): lax.ppermute(blocks, 'tm', [(i, (i + distance) % depth) for i in range(de...  27.4 us
    all_gather x1, waiting for transfers between devices, shards(): w_full = lax.all_gather(w_mid, 'clip', axis=0, tiled=True)  26.3 us
    pallas_call x2, Pallas kernels, grad_chunk(): pl.pallas_call(grad_kernel, grid_spec=pltpu.PrefetchScalarGridSpec(num_sc...  23.9 us
    pallas_call x2, Pallas kernels, front(): pl.pallas_call(lambda *refs: front_kernel(*refs, rows=rows, cols=cols, fi...  22.2 us
    pallas_call x1, Pallas kernels, back(): pl.pallas_call(lambda *refs: back_kernel(*refs, rows=rows, cols=cols), gr...  17.5 us
    pallas_call x1, Pallas kernels, middle(): pl.pallas_call(lambda *refs: middle_kernel(*refs, scale=scale), grid=(3,)...  16.7 us
    all_to_all x2, waiting for transfers between devices, cast_to_all(): lax.all_to_all(jnp.broadcast_to(block[None], (size,) + block.shape), axis...  11.9 us
    convert_element_type x7, other arithmetic, packed(): return jnp.where(row < rows, x * jnp.exp2(14.0 - power), power).astype(F16)  10.4 us
  transfers between devices with their start and end apart: 25, of which 8 were waited for; matrix products, arithmetic and copies ran while one was open for 9% of the time, Pallas kernels for 21%

profile of v5, /device:TPU:0, one launch (start us, length us, event | category | flops | bytes accessed | tf_op | source)
XLA Modules:
  0.0 246.2 jit_solution(5180387788336273196)
XLA Ops:
  9.1 4.9 %collective-permute-start = (bf16[16,512]{1,0:T(8,128)(2,1)S(1)}, bf16[16,512]{1,0:T(8,128)(2,1)S(1)}, u32[]{:S(2)}, u32[]{:S(2)}) collective-permute-start(bf16[16,512]{1,0:T(8,128)(2,1)S(1)} %slice.160), channel_id=1, source_target_pairs={{0,1},{1,2},{2,3},{4,5},{5,6},{6,7},{8,9},{9,10},{10,11},{12,13},{... | collective-permute-start | bytes 49160 | tf_op jit(solution)/shard_map/ppermute | solution.py:19
  14.1 1.4 collective-permute-done
  16.1 12.2 %front.2 = (bf16[432,1024]{1,0:T(8,128)(2,1)}, f32[1024,384]{1,0:T(8,128)}, bf16[3,10,10,16,384]{4,3,2,1,0:T(8,128)(2,1)}, bf16[27,384,1024]{2,1,0:T(8,128)(2,1)}, f32[384,128]{1,0:T(8,128)}) custom-call(bf16[16,1536]{1,0:T(8,128)(2,1)} %copy-done.6, bf16[432,384]{1,0:T(8,128)(2,1)} %refs_1_.3), custom_call_target="tpu_custom_call" | custom-call | tf_op jit(solution)/shard_map/front/pallas_call | solution.py:126
  29.0 9.9 %front.3 = (bf16[27,384,1024]{2,1,0:T(8,128)(2,1)}, f32[384,128]{1,0:T(8,128)}) custom-call(bf16[16,1536]{1,0:T(8,128)(2,1)} %copy-done.10, bf16[432,384]{1,0:T(8,128)(2,1)} %refs_1_.3), custom_call_target="tpu_custom_call" | custom-call | tf_op jit(solution)/shard_map/front/pallas_call | solution.py:126
  38.9 26.3 %all-gather.2.cloned.1.call-done = bf16[10368,384]{1,0:T(8,128)(2,1)} async-done(((bf16[1296,384]{1,0:T(8,128)(2,1)}), bf16[10368,384]{1,0:T(8,128)(2,1)}) %all-gather.2.cloned.1.call-update) | async-done | bytes 7962640 | tf_op jit(solution)/shard_map/all_gather | solution.py:386
  65.2 16.7 %middle.1 = (bf16[1024,384]{1,0:T(8,128)(2,1)}, f32[8,128]{1,0:T(8,128)}) custom-call(bf16[3,10,10,16,384]{4,3,2,1,0:T(8,128)(2,1)} %get-tuple-element.49.refs_0_, bf16[27,384,384]{2,1,0:T(8,128)(2,1)} %bitcast.72, bf16[1024,384]{1,0:T(8,128)(2,1)} %bitcast.75), custom_call_target="tpu_custom_call" | custom-call | tf_op jit(solution)/shard_map/middle/pallas_call | solution.py:169
  89.6 12.0 %grad.2 = (f32[720,384]{1,0:T(8,128)}, f32[4,720,384]{2,1,0:T(8,128)}) custom-call(s32[4]{0:T(128)} %multiply_xor_fusion.order_ref, bf16[10368,1024]{1,0:T(8,128)(2,1)} %bitcast.64, bf16[10368,1024]{1,0:T(8,128)(2,1)} %bitcast.68, bf16[10368,1024]{1,0:T(8,128)(2,1)} %bitcast.65, bf16[10368,1024]{1,0:T(8,128)(2,1)} %bitcast.69, ...), custom_call_target="tpu_custom_call" | custom-call | tf_op jit(solution)/shard_map/grad/pallas_call | solution.py:220
  101.6 2.4 fusion.3
  103.9 1.5 collective-permute-start.6
  105.4 1.5 collective-permute-start.5
  108.5 1.5 collective-permute-start.7
  109.9 6.6 %collective-permute-done.7.refs_1_ = bf16[256,384]{1,0:T(8,128)(2,1)S(1)} collective-permute-done((bf16[256,384]{1,0:T(8,128)(2,1)S(1)}, bf16[256,384]{1,0:T(8,128)(2,1)S(1)}, u32[]{:S(2)}, u32[]{:S(2)}) %collective-permute-start.7) | collective-permute-done | bytes 196640 | tf_op jit(solution)/shard_map/ppermute | solution.py:19
  116.5 11.9 %grad.3 = (f32[720,384]{1,0:T(8,128)}, f32[4,720,384]{2,1,0:T(8,128)}) custom-call(s32[4]{0:T(128)} %multiply_xor_fusion.order_ref, bf16[10368,1024]{1,0:T(8,128)(2,1)} %bitcast.66, bf16[10368,1024]{1,0:T(8,128)(2,1)} %bitcast.70, bf16[10368,1024]{1,0:T(8,128)(2,1)} %bitcast.67, bf16[10368,1024]{1,0:T(8,128)(2,1)} %bitcast.71, ...), custom_call_target="tpu_custom_call" | custom-call | tf_op jit(solution)/shard_map/grad/pallas_call | solution.py:220
  128.5 3.6 %fusion = (f16[720,384]{1,0:T(8,128)(2,1)}, f16[720,384]{1,0:T(8,128)(2,1)}, f16[720,384]{1,0:T(8,128)(2,1)}) fusion(f32[4,720,384]{2,1,0:T(8,128)} %get-tuple-element.63, f32[]{:T(128)} %bitcast.10, f32[]{:T(128)} %bitcast.8, pred[720]{0:T(1024)(128)(4,1)S(1)} %iota_compare_fusion), kind=kLoop, calls=%fused_computation.1 | loop fusion | flops 2488320 | bytes 4977368 | tf_op jit(solution)/shard_map/convert_element_type | solution.py:299
  133.8 3.9 %all-to-all-start = ((f16[4,192,384]{2,1,0:T(8,128)(2,1)}), f16[4,192,384]{2,1,0:T(8,128)(2,1)S(1)}, u32[]{:S(2)}, u32[]{:S(2)}) async-start(f16[4,192,384]{2,1,0:T(8,128)(2,1)} %bitcast.17), calls=%async_computation | async-start | bytes 1179648 | tf_op jit(solution)/shard_map/all_to_all | solution.py:338
  137.7 1.4 collective-permute-start.11
  141.1 17.5 %back.1 = f32[432,384]{1,0:T(8,128)} custom-call(bf16[1024,384]{1,0:T(8,128)(2,1)} %get-tuple-element.71.refs_4_.refs_0_, bf16[256,384]{1,0:T(8,128)(2,1)} %copy-done.9, bf16[27,384,384]{2,1,0:T(8,128)(2,1)} %bitcast.73, f32[1024,384]{1,0:T(8,128)} %get-tuple-element.73.refs_3_, bf16[432,1024]{1,0:T(8,128)(2,1)} %get-tuple-element.74.refs_4_), custom_call_target="tpu_custom_call" | custom-call | tf_op jit(solution)/shard_map/back/pallas_call | solution.py:275
  158.6 6.5 %collective-permute-done.12 = f16[720,384]{1,0:T(8,128)(2,1)} collective-permute-done((f16[720,384]{1,0:T(8,128)(2,1)}, f16[720,384]{1,0:T(8,128)(2,1)}, u32[]{:S(2)}, u32[]{:S(2)}) %collective-permute-start.12) | collective-permute-done | bytes 552992 | tf_op jit(solution)/shard_map/ppermute | solution.py:309
  165.1 2.4 select_convert_fusion.1
  168.4 3.5 %all-to-all-start.1 = ((f32[8,54,384]{2,1,0:T(8,128)}), f32[8,54,384]{2,1,0:T(8,128)S(1)}, u32[]{:S(2)}, u32[]{:S(2)}) async-start(f32[8,54,384]{2,1,0:T(8,128)} %reshape.58), calls=%async_computation.1 | async-start | bytes 1376256 | tf_op jit(solution)/shard_map/all_to_all | solution.py:422
  172.0 1.8 collective-permute-start.14
  173.8 2.4 collective-permute-start.15
  176.1 1.5 collective-permute-start.16
  178.4 1.5 collective-permute-start.9
  180.6 11.0 %collective-permute-start.8 = (f16[192,384]{1,0:T(8,128)(2,1)S(1)}, f16[192,384]{1,0:T(8,128)(2,1)S(1)}, u32[]{:S(2)}, u32[]{:S(2)}) collective-permute-start(f16[192,384]{1,0:T(8,128)(2,1)S(1)} %fusion.9), channel_id=1, source_target_pairs={{0,1},{1,2},{2,3},{3,0},{4,5},{5,6},{6,7},{7,4},{8,9},{9,10},{10,1... | collective-permute-start | bytes 442376 | tf_op jit(solution)/shard_map/ppermute | solution.py:315
  193.6 6.7 %collective-permute-start.19 = (f16[192,384]{1,0:T(8,128)(2,1)S(1)}, f16[192,384]{1,0:T(8,128)(2,1)S(1)}, u32[]{:S(2)}, u32[]{:S(2)}) collective-permute-start(f16[192,384]{1,0:T(8,128)(2,1)S(1)} %select_convert_fusion), channel_id=1, source_target_pairs={{0,3},{1,0},{2,1},{3,2},{4,7},{5,4},{6,5},{7,6},{8,11},{9,8},{10,9... | collective-permute-start | bytes 442376 | tf_op jit(solution)/shard_map/ppermute | solution.py:315
  201.1 4.2 %all-to-all-start.2 = ((f32[4,54,384]{2,1,0:T(8,128)}), f32[4,54,384]{2,1,0:T(8,128)S(1)}, u32[]{:S(2)}, u32[]{:S(2)}) async-start(f32[4,54,384]{2,1,0:T(8,128)} %broadcast_in_dim.81), calls=%async_computation.2 | async-start | bytes 688128 | tf_op jit(solution)/shard_map/all_to_all | solution.py:372
  205.3 2.0 collective-permute-start.17
  210.6 7.9 %collective-permute-done.18 = f16[192,384]{1,0:T(8,128)(2,1)S(1)} collective-permute-done((f16[192,384]{1,0:T(8,128)(2,1)S(1)}, f16[192,384]{1,0:T(8,128)(2,1)S(1)}, u32[]{:S(2)}, u32[]{:S(2)}) %collective-permute-start.18) | collective-permute-done | bytes 147488 | tf_op jit(solution)/shard_map/ppermute | solution.py:315
  219.3 2.8 %all-to-all-done.2 = f32[4,54,384]{2,1,0:T(8,128)S(1)} async-done(((f32[4,54,384]{2,1,0:T(8,128)}), f32[4,54,384]{2,1,0:T(8,128)S(1)}, u32[]{:S(2)}, u32[]{:S(2)}) %all-to-all-start.2) | async-done | bytes 331808 | tf_op jit(solution)/shard_map/all_to_all | solution.py:372
  223.0 3.9 %all-to-all-start.3 = ((f32[8,54,384]{2,1,0:T(8,128)}), f32[8,54,384]{2,1,0:T(8,128)S(1)}, u32[]{:S(2)}, u32[]{:S(2)}) async-start(f32[8,54,384]{2,1,0:T(8,128)} %broadcast_in_dim.82), calls=%async_computation.3 | async-start | bytes 1376256 | tf_op jit(solution)/shard_map/all_to_all | solution.py:372
  229.3 9.2 %all-to-all-done.3 = f32[8,54,384]{2,1,0:T(8,128)S(1)} async-done(((f32[8,54,384]{2,1,0:T(8,128)}), f32[8,54,384]{2,1,0:T(8,128)S(1)}, u32[]{:S(2)}, u32[]{:S(2)}) %all-to-all-start.3) | async-done | bytes 663584 | tf_op jit(solution)/shard_map/all_to_all | solution.py:372
  (92 shorter events, 26.2 us)
Async XLA Ops:
  7.2 58.0 %all-gather.2.cloned.1.call-start = ((), (), s32[]{:S(2)}) async-start(), calls=%async_computation.4 | async-start | bytes 8957952 | tf_op jit(solution)/shard_map/all_gather | solution.py:386
  9.1 6.4 %collective-permute-start = (bf16[16,512]{1,0:T(8,128)(2,1)S(1)}, bf16[16,512]{1,0:T(8,128)(2,1)S(1)}, u32[]{:S(2)}, u32[]{:S(2)}) collective-permute-start(bf16[16,512]{1,0:T(8,128)(2,1)S(1)} %slice.160), channel_id=1, source_target_pairs={{0,1},{1,2},{2,3},{4,5},{5,6},{6,7},{8,9},{9,10},{10,11},{12,13},{... | collective-permute-start | bytes 49160 | tf_op jit(solution)/shard_map/ppermute | solution.py:19
  15.5 12.9 %collective-permute-start.1 = (bf16[16,1536]{1,0:T(8,128)(2,1)S(1)}, bf16[16,1536]{1,0:T(8,128)(2,1)S(1)}, u32[]{:S(2)}, u32[]{:S(2)}) collective-permute-start(bf16[16,1536]{1,0:T(8,128)(2,1)S(1)} %pad_maximum_fusion.1.refs_0_), channel_id=1, source_target_pairs={{0,4},{4,0},{8,12},{12,8},{16,20},{20,16},{24,28},{28,24},{1,5},{5... | collective-permute-start | bytes 147464 | tf_op jit(solution)/shard_map/ppermute | solution.py:23
  65.2 17.7 %copy-start.7 = (f32[384,128]{1,0:T(8,128)S(1)}, f32[384,128]{1,0:T(8,128)}, u32[]{:S(2)}) copy-start(f32[384,128]{1,0:T(8,128)} %get-tuple-element.54) | copy-start | bytes 589828
  65.2 19.6 %copy-start.8 = (f32[384,128]{1,0:T(8,128)S(1)}, f32[384,128]{1,0:T(8,128)}, u32[]{:S(2)}) copy-start(f32[384,128]{1,0:T(8,128)} %get-tuple-element.56) | copy-start | bytes 589828
  82.0 6.8 %collective-permute-start.2 = (bf16[1024,384]{1,0:T(8,128)(2,1)}, bf16[1024,384]{1,0:T(8,128)(2,1)S(1)}, u32[]{:S(2)}, u32[]{:S(2)}) collective-permute-start(bf16[1024,384]{1,0:T(8,128)(2,1)} %get-tuple-element.71.refs_4_.refs_0_), channel_id=1, source_target_pairs={{0,4},{4,0},{8,12},{12,8},{16,20},{20,16},{24,28},{28,24},{1,5},{5... | collective-permute-start | bytes 2359304 | tf_op jit(solution)/shard_map/ppermute | solution.py:23
  82.2 4.6 %collective-permute-start.3 = (f32[8,128]{1,0:T(8,128)}, f32[8,128]{1,0:T(8,128)S(1)}, u32[]{:S(2)}, u32[]{:S(2)}) collective-permute-start(f32[8,128]{1,0:T(8,128)} %get-tuple-element.55), channel_id=1, source_target_pairs={{0,4},{4,0},{8,12},{12,8},{16,20},{20,16},{24,28},{28,24},{1,5},{5... | collective-permute-start | bytes 12296 | tf_op jit(solution)/shard_map/ppermute | solution.py:23
  103.9 28.2 %collective-permute-start.6 = (f16[720,384]{1,0:T(8,128)(2,1)S(1)}, f16[720,384]{1,0:T(8,128)(2,1)S(1)}, u32[]{:S(2)}, u32[]{:S(2)}) collective-permute-start(f16[720,384]{1,0:T(8,128)(2,1)S(1)} %get-tuple-element.59), channel_id=1, source_target_pairs={{0,24},{4,28},{8,16},{12,20},{16,8},{20,12},{24,0},{28,4},{1,25},{... | collective-permute-start | bytes 1658888 | tf_op jit(solution)/shard_map/ppermute | solution.py:309
  105.4 26.7 %collective-permute-start.5 = (f16[720,384]{1,0:T(8,128)(2,1)S(1)}, f16[720,384]{1,0:T(8,128)(2,1)S(1)}, u32[]{:S(2)}, u32[]{:S(2)}) collective-permute-start(f16[720,384]{1,0:T(8,128)(2,1)S(1)} %get-tuple-element.58), channel_id=1, source_target_pairs={{0,16},{4,20},{8,24},{12,28},{16,0},{20,4},{24,8},{28,12},{1,17},{... | collective-permute-start | bytes 1658888 | tf_op jit(solution)/shard_map/ppermute | solution.py:309
  107.0 25.1 %collective-permute-start.4 = (f16[720,384]{1,0:T(8,128)(2,1)S(1)}, f16[720,384]{1,0:T(8,128)(2,1)S(1)}, u32[]{:S(2)}, u32[]{:S(2)}) collective-permute-start(f16[720,384]{1,0:T(8,128)(2,1)S(1)} %get-tuple-element.57), channel_id=1, source_target_pairs={{0,8},{4,12},{8,0},{12,4},{16,24},{20,28},{24,16},{28,20},{1,9},{5... | collective-permute-start | bytes 1658888 | tf_op jit(solution)/shard_map/ppermute | solution.py:309
  108.5 8.1 %collective-permute-start.7 = (bf16[256,384]{1,0:T(8,128)(2,1)S(1)}, bf16[256,384]{1,0:T(8,128)(2,1)S(1)}, u32[]{:S(2)}, u32[]{:S(2)}) collective-permute-start(bf16[256,384]{1,0:T(8,128)(2,1)S(1)} %slice.131), channel_id=1, source_target_pairs={{1,0},{2,1},{3,2},{5,4},{6,5},{7,6},{9,8},{10,9},{11,10},{13,12},{... | collective-permute-start | bytes 589832 | tf_op jit(solution)/shard_map/ppermute | solution.py:19
  116.5 11.9 %copy-start.9 = (bf16[256,384]{1,0:T(8,128)(2,1)}, bf16[256,384]{1,0:T(8,128)(2,1)S(1)}, u32[]{:S(2)}) copy-start(bf16[256,384]{1,0:T(8,128)(2,1)S(1)} %collective-permute-done.7.refs_1_) | copy-start | bytes 589828
  128.5 3.7 %copy-start.4 = (f32[720,384]{1,0:T(8,128)S(1)}, f32[720,384]{1,0:T(8,128)}, u32[]{:S(2)}) copy-start(f32[720,384]{1,0:T(8,128)} %get-tuple-element.52) | copy-start | bytes 3317764
  133.8 34.6 %all-to-all-start = ((f16[4,192,384]{2,1,0:T(8,128)(2,1)}), f16[4,192,384]{2,1,0:T(8,128)(2,1)S(1)}, u32[]{:S(2)}, u32[]{:S(2)}) async-start(f16[4,192,384]{2,1,0:T(8,128)(2,1)} %bitcast.17), calls=%async_computation | async-start | bytes 1179648 | tf_op jit(solution)/shard_map/all_to_all | solution.py:338
  137.7 21.0 %collective-permute-start.11 = (f16[720,384]{1,0:T(8,128)(2,1)}, f16[720,384]{1,0:T(8,128)(2,1)S(1)}, u32[]{:S(2)}, u32[]{:S(2)}) collective-permute-start(f16[720,384]{1,0:T(8,128)(2,1)} %get-tuple-element.68), channel_id=1, source_target_pairs={{0,8},{4,12},{8,0},{12,4},{16,24},{20,28},{24,16},{28,20},{1,9},{5... | collective-permute-start | bytes 1658888 | tf_op jit(solution)/shard_map/ppermute | solution.py:309
  139.1 26.0 %collective-permute-start.12 = (f16[720,384]{1,0:T(8,128)(2,1)}, f16[720,384]{1,0:T(8,128)(2,1)}, u32[]{:S(2)}, u32[]{:S(2)}) collective-permute-start(f16[720,384]{1,0:T(8,128)(2,1)} %get-tuple-element.69), channel_id=1, source_target_pairs={{0,16},{4,20},{8,24},{12,28},{16,0},{20,4},{24,8},{28,12},{1,17},{... | collective-permute-start | bytes 1658888 | tf_op jit(solution)/shard_map/ppermute | solution.py:309
  139.7 25.4 %collective-permute-start.13 = (f16[720,384]{1,0:T(8,128)(2,1)}, f16[720,384]{1,0:T(8,128)(2,1)}, u32[]{:S(2)}, u32[]{:S(2)}) collective-permute-start(f16[720,384]{1,0:T(8,128)(2,1)} %get-tuple-element.70), channel_id=1, source_target_pairs={{0,24},{4,28},{8,16},{12,20},{16,8},{20,12},{24,0},{28,4},{1,25},{... | collective-permute-start | bytes 1658888 | tf_op jit(solution)/shard_map/ppermute | solution.py:309
  141.1 24.0 %copy-start.5 = (f32[720,384]{1,0:T(8,128)S(1)}, f32[720,384]{1,0:T(8,128)}, u32[]{:S(2)}) copy-start(f32[720,384]{1,0:T(8,128)} %get-tuple-element.67) | copy-start | bytes 3317764
  158.6 8.9 %copy-start.3 = (f32[432,384]{1,0:T(8,128)S(1)}, f32[432,384]{1,0:T(8,128)}, u32[]{:S(2)}) copy-start(f32[432,384]{1,0:T(8,128)} %back.1) | copy-start | bytes 1990660
  168.4 23.2 %all-to-all-start.1 = ((f32[8,54,384]{2,1,0:T(8,128)}), f32[8,54,384]{2,1,0:T(8,128)S(1)}, u32[]{:S(2)}, u32[]{:S(2)}) async-start(f32[8,54,384]{2,1,0:T(8,128)} %reshape.58), calls=%async_computation.1 | async-start | bytes 1376256 | tf_op jit(solution)/shard_map/all_to_all | solution.py:422
  172.0 8.6 %collective-permute-start.14 = (f16[192,384]{1,0:T(8,128)(2,1)S(1)}, f16[192,384]{1,0:T(8,128)(2,1)S(1)}, u32[]{:S(2)}, u32[]{:S(2)}) collective-permute-start(f16[192,384]{1,0:T(8,128)(2,1)S(1)} %get-tuple-element.80), channel_id=1, source_target_pairs={{0,1},{1,2},{2,3},{3,0},{4,5},{5,6},{6,7},{7,4},{8,9},{9,10},{10,1... | collective-permute-start | bytes 442376 | tf_op jit(solution)/shard_map/ppermute | solution.py:315
  173.8 17.8 %collective-permute-start.15 = (f16[192,384]{1,0:T(8,128)(2,1)}, f16[192,384]{1,0:T(8,128)(2,1)S(1)}, u32[]{:S(2)}, u32[]{:S(2)}) collective-permute-start(f16[192,384]{1,0:T(8,128)(2,1)} %get-tuple-element.81), channel_id=1, source_target_pairs={{0,2},{1,3},{2,0},{3,1},{4,6},{5,7},{6,4},{7,5},{8,10},{9,11},{10,... | collective-permute-start | bytes 442376 | tf_op jit(solution)/shard_map/ppermute | solution.py:315
  176.1 15.4 %collective-permute-start.16 = (f16[192,384]{1,0:T(8,128)(2,1)}, f16[192,384]{1,0:T(8,128)(2,1)}, u32[]{:S(2)}, u32[]{:S(2)}) collective-permute-start(f16[192,384]{1,0:T(8,128)(2,1)} %get-tuple-element.82), channel_id=1, source_target_pairs={{0,3},{1,0},{2,1},{3,2},{4,7},{5,4},{6,5},{7,6},{8,11},{9,8},{10,9... | collective-permute-start | bytes 442376 | tf_op jit(solution)/shard_map/ppermute | solution.py:315
  177.8 27.5 %collective-permute-start.10 = (f16[192,384]{1,0:T(8,128)(2,1)S(1)}, f16[192,384]{1,0:T(8,128)(2,1)S(1)}, u32[]{:S(2)}, u32[]{:S(2)}) collective-permute-start(f16[192,384]{1,0:T(8,128)(2,1)S(1)} %fusion.9), channel_id=1, source_target_pairs={{0,3},{1,0},{2,1},{3,2},{4,7},{5,4},{6,5},{7,6},{8,11},{9,8},{10,9... | collective-permute-start | bytes 442376 | tf_op jit(solution)/shard_map/ppermute | solution.py:315
  178.4 28.9 %collective-permute-start.9 = (f16[192,384]{1,0:T(8,128)(2,1)S(1)}, f16[192,384]{1,0:T(8,128)(2,1)S(1)}, u32[]{:S(2)}, u32[]{:S(2)}) collective-permute-start(f16[192,384]{1,0:T(8,128)(2,1)S(1)} %fusion.9), channel_id=1, source_target_pairs={{0,2},{1,3},{2,0},{3,1},{4,6},{5,7},{6,4},{7,5},{8,10},{9,11},{10,... | collective-permute-start | bytes 442376 | tf_op jit(solution)/shard_map/ppermute | solution.py:315
  180.6 26.8 %collective-permute-start.8 = (f16[192,384]{1,0:T(8,128)(2,1)S(1)}, f16[192,384]{1,0:T(8,128)(2,1)S(1)}, u32[]{:S(2)}, u32[]{:S(2)}) collective-permute-start(f16[192,384]{1,0:T(8,128)(2,1)S(1)} %fusion.9), channel_id=1, source_target_pairs={{0,1},{1,2},{2,3},{3,0},{4,5},{5,6},{6,7},{7,4},{8,9},{9,10},{10,1... | collective-permute-start | bytes 442376 | tf_op jit(solution)/shard_map/ppermute | solution.py:315
  193.6 17.0 %collective-permute-start.19 = (f16[192,384]{1,0:T(8,128)(2,1)S(1)}, f16[192,384]{1,0:T(8,128)(2,1)S(1)}, u32[]{:S(2)}, u32[]{:S(2)}) collective-permute-start(f16[192,384]{1,0:T(8,128)(2,1)S(1)} %select_convert_fusion), channel_id=1, source_target_pairs={{0,3},{1,0},{2,1},{3,2},{4,7},{5,4},{6,5},{7,6},{8,11},{9,8},{10,9... | collective-permute-start | bytes 442376 | tf_op jit(solution)/shard_map/ppermute | solution.py:315
  200.3 18.2 %collective-permute-start.18 = (f16[192,384]{1,0:T(8,128)(2,1)S(1)}, f16[192,384]{1,0:T(8,128)(2,1)S(1)}, u32[]{:S(2)}, u32[]{:S(2)}) collective-permute-start(f16[192,384]{1,0:T(8,128)(2,1)S(1)} %select_convert_fusion), channel_id=1, source_target_pairs={{0,2},{1,3},{2,0},{3,1},{4,6},{5,7},{6,4},{7,5},{8,10},{9,11},{10,... | collective-permute-start | bytes 442376 | tf_op jit(solution)/shard_map/ppermute | solution.py:315
  201.1 21.0 %all-to-all-start.2 = ((f32[4,54,384]{2,1,0:T(8,128)}), f32[4,54,384]{2,1,0:T(8,128)S(1)}, u32[]{:S(2)}, u32[]{:S(2)}) async-start(f32[4,54,384]{2,1,0:T(8,128)} %broadcast_in_dim.81), calls=%async_computation.2 | async-start | bytes 688128 | tf_op jit(solution)/shard_map/all_to_all | solution.py:372
  205.3 13.2 %collective-permute-start.17 = (f16[192,384]{1,0:T(8,128)(2,1)S(1)}, f16[192,384]{1,0:T(8,128)(2,1)S(1)}, u32[]{:S(2)}, u32[]{:S(2)}) collective-permute-start(f16[192,384]{1,0:T(8,128)(2,1)S(1)} %select_convert_fusion), channel_id=1, source_target_pairs={{0,1},{1,2},{2,3},{3,0},{4,5},{5,6},{6,7},{7,4},{8,9},{9,10},{10,1... | collective-permute-start | bytes 442376 | tf_op jit(solution)/shard_map/ppermute | solution.py:315
  223.0 15.4 %all-to-all-start.3 = ((f32[8,54,384]{2,1,0:T(8,128)}), f32[8,54,384]{2,1,0:T(8,128)S(1)}, u32[]{:S(2)}, u32[]{:S(2)}) async-start(f32[8,54,384]{2,1,0:T(8,128)} %broadcast_in_dim.82), calls=%async_computation.3 | async-start | bytes 1376256 | tf_op jit(solution)/shard_map/all_to_all | solution.py:372
  226.9 12.4 %copy-start.1 = (bf16[1,8,8,32,16]{3,4,2,1,0:T(8,128)(2,1)S(1)}, bf16[1,8,8,32,16]{3,4,2,1,0:T(8,128)(2,1)}, u32[]{:S(2)}) copy-start(bf16[1,8,8,32,16]{3,4,2,1,0:T(8,128)(2,1)} %param.5) | copy-start | bytes 196612
  (4 other events, 3.5 us)
Sparse Core Ops, SparseCore 0:
  9.9 55.2 all-gather.1

commit v6 on v5

--- a/solution.py
+++ b/solution.py
@@ -188,53 +188,59 @@
     )(cells, w_taps, teacher)
 
 
-def grad_kernel(order_ref, *refs):
+def grad_kernel(order_ref, *refs, units):
     own_ref, out_ref = refs[-2:]
-    at_once = (len(refs) - 4) // 2
+    g_refs = refs[-4:-2]
+    at_once = out_ref.shape[0]
     rows = refs[0].shape[0]
-    zero = jnp.zeros((own_ref.shape[0] - rows, own_ref.shape[1]), F32)
+    spare = own_ref.shape[0] - units * rows
+    zero = jnp.zeros((spare, own_ref.shape[1]), F32)
     for i in range(at_once):
-        total = contract(refs[2 * i][...], refs[2 * at_once][...], ((1,), (0,)))
-        total += contract(refs[2 * i + 1][...], refs[2 * at_once + 1][...], ((1,), (0,)))
-        if i == 0:
-            @pl.when(pl.program_id(0) == 0)
-            def _():
-                own_ref[:rows, :] = total
-                own_ref[rows:, :] = zero
-
-        out_ref[i, :rows, :] = total
-        out_ref[i, rows:, :] = zero
-
-
-def grad_chunk(order, taps, g, parts, which):
+        for k in range(units):
+            at = 2 * (i * units + k)
+            total = contract(refs[at][...], g_refs[0][...], ((1,), (0,)))
+            total += contract(refs[at + 1][...], g_refs[1][...], ((1,), (0,)))
+            out_ref[i, k * rows : (k + 1) * rows, :] = total
+        out_ref[i, units * rows :, :] = zero
+
+    @pl.when(pl.program_id(0) == 0)
+    def _():
+        own_ref[...] = out_ref[0]
+
+
+def grad_chunk(order, taps, g, first, units):
     blocks = order.shape[0]
     total, count = taps[0].shape
     chans = g[0].shape[1]
-    rows = total // (2 * blocks) // parts
-    at_once = 2
+    rows = total // (2 * blocks) // 3
+    at_once = 2 // units
     tap_specs = []
     for i in range(at_once):
-        spec = pl.BlockSpec((rows, count), lambda s, order, i=i: (order[s * at_once + i] * parts + which, 0))
-        tap_specs += [spec, spec]
+        for k in range(units):
+            spec = pl.BlockSpec(
+                (rows, count), lambda s, order, i=i, k=k: (order[s * at_once + i] * 3 + first + k, 0)
+            )
+            tap_specs += [spec, spec]
     whole = pl.BlockSpec((count, chans), lambda s, order: (0, 0))
+    size = padded(rows * units)
     return pl.pallas_call(
-        grad_kernel,
+        lambda *refs: grad_kernel(*refs, units=units),
         grid_spec=pltpu.PrefetchScalarGridSpec(
             num_scalar_prefetch=1,
             grid=(blocks // at_once,),
             in_specs=tap_specs + [whole, whole],
             out_specs=[
-                pl.BlockSpec((padded(rows), chans), lambda s, order: (0, 0)),
-                pl.BlockSpec((at_once, padded(rows), chans), lambda s, order: (s, 0, 0)),
+                pl.BlockSpec((size, chans), lambda s, order: (0, 0)),
+                pl.BlockSpec((at_once, size, chans), lambda s, order: (s, 0, 0)),
             ],
         ),
         out_shape=[
-            jax.ShapeDtypeStruct((padded(rows), chans), F32),
-            jax.ShapeDtypeStruct((blocks, padded(rows), chans), F32),
+            jax.ShapeDtypeStruct((size, chans), F32),
+            jax.ShapeDtypeStruct((blocks, size, chans), F32),
         ],
         compiler_params=pltpu.CompilerParams(vmem_limit_bytes=VMEM),
         name="grad",
-    )(order, *(list(taps) * at_once), *g)
+    )(order, *(list(taps) * 2), *g)
 
 
 def back_kernel(g_ref, later_ref, w_ref, z_ref, patch_ref, out_ref, cells_ref, acc_ref, *, rows, cols):
@@ -365,11 +371,6 @@
             break
         out.append(x[:count])
     return out
-
-
-def cast_to_all(block, axis):
-    size = lax.axis_size(axis)
-    return lax.all_to_all(jnp.broadcast_to(block[None], (size,) + block.shape), axis, 0, 0, tiled=True)
 
 
 def shards(latent, offsets, teacher, w_in, w_mid):
@@ -399,44 +400,41 @@
     later = passed_along(g[: 2 * plane], "tm", -1)
 
     order = lax.axis_index("clip") ^ (2 * jnp.arange(clips // 2, dtype=jnp.int32))
-    block_rows = 27 * chans // clips
-    chunks = next(c for c in (2, 3, 1) if block_rows % (8 * c) == 0)
-    part_rows = block_rows // chunks
+    third = 27 * chans // clips // 3
     bound = (jnp.max(top) * size[:1, :1] + jnp.max(pair_top) * pair_size[:1, :1]) * 1.01
-    plane_got = []
-    g_now = g
-    for j in range(chunks):
-        own, part = grad_chunk(order, (taps, pair_taps), (g_now, pair_g), chunks, j)
-        got, g_now = across_plane(part, part_rows, bound, g_now)
-        later, g_now = lax.optimization_barrier((later, g_now))
-        plane_got.append((own, got))
-    factors, total = scales(plane_got[0][1], part_rows, bound)
-    first, g_now = across_depth(*plane_got[0], part_rows, factors, total, g_now, True)
-    depth_got = [first]
-    in_part = back(g_now, later, w_taps, z, patch_t, rows, cols)
-    for own, got in plane_got[1:]:
-        got, in_part = lax.optimization_barrier((got, in_part))
-        more, in_part = across_depth(own, got, part_rows, factors, total, in_part, False)
-        depth_got.append(more)
-    in_rows = in_part.shape[0]
+    both = (taps, pair_taps)
+    in_rows = patch_t.shape[0]
+
+    own_a, part = grad_chunk(order, both, (g, pair_g), 0, 2)
+    got_a, g = across_plane(part, 2 * third, bound, g)
+    in_part = back(g, later, w_taps, z, patch_t, rows, cols)
     in_got = lax.all_to_all(in_part.reshape(clips, in_rows // clips, chans), "clip", 0, 0, tiled=True)
-    small = piece_rows(part_rows)
-    factors, total = scales(depth_got[0][1], small, 0.0)
-    last = []
-    for own, got in depth_got:
-        if last:
-            in_got, got, last[-1][0] = lax.optimization_barrier((in_got, got, last[-1][0]))
-            factors, _ = scales(got, small, 0.0)
-        last.append(spread(own, got, small, factors, total))
-        if len(last) == 2:
-            in_got = cast_to_all(in_got.sum(axis=0), "tm")
-    if len(last) == 1:
-        in_got = cast_to_all(in_got.sum(axis=0), "tm")
-    grad_in = cast_to_all(in_got.sum(axis=0), "clip").reshape(in_rows, chans)
-    factors, _ = scales(last[0], small, 0.0)
-    pieces = []
-    for got in last:
-        pieces += assembled(got, factors, small, part_rows)
+    g, in_part = lax.optimization_barrier((g, in_part))
+    own_b, part = grad_chunk(order, both, (g, pair_g), 2, 1)
+    got_b, got_a = across_plane(part, third, bound, got_a)
+
+    factors, total = scales(got_a, 2 * third, bound)
+    (_, depth_a), in_got = across_depth(own_a, got_a, 2 * third, factors, total, in_got, True)
+    in_sum = in_got.sum(axis=0)
+    got_b, _ = lax.optimization_barrier((got_b, in_sum))
+    (own_b, depth_b), _ = across_depth(own_b, got_b, third, factors, total, total, False)
+    in_sum, depth_a = lax.optimization_barrier((in_sum, depth_a))
+    in_sum = jnp.broadcast_to(in_sum[None], (lax.axis_size("tm"),) + in_sum.shape)
+    in_sum, depth_a = lax.optimization_barrier((in_sum, depth_a))
+    in_got = lax.all_to_all(in_sum, "tm", 0, 0, tiled=True)
+    small_a = piece_rows(2 * third)
+    small_b = piece_rows(third)
+    factors, total = scales(depth_a, small_a, 0.0)
+    last_a = spread(None, depth_a, small_a, factors, total)
+    depth_b, last_a[0] = lax.optimization_barrier((depth_b, last_a[0]))
+    factors, _ = scales(depth_b, small_b, 0.0)
+    last_b = spread(own_b, depth_b, small_b, factors, total)
+    in_sum = in_got.sum(axis=0)
+    in_sum = jnp.broadcast_to(in_sum[None], (clips,) + in_sum.shape)
+    in_sum, last_a = lax.optimization_barrier((in_sum, last_a))
+    grad_in = lax.all_to_all(in_sum, "clip", 0, 0, tiled=True).reshape(in_rows, chans)
+    factors, _ = scales(last_a, small_a, 0.0)
+    pieces = assembled(last_a, factors, small_a, 2 * third) + assembled(last_b, factors, small_b, third)
     return (jnp.concatenate(pieces, axis=0), grad_in)
 
 

time: 247 us -> 248 us (level)
    ppermute x6, waiting for transfers between devices: 6.5 us -> 16.2 us  [across_plane(): got.append(lax.ppermute(payloads[q - 1], 'clip', route))]
    all_to_all x2, waiting for transfers between devices: 11.9 us -> 5.08 us  [the longest x1 5.07 us: shards(): lax.all_to_all(in_sum, 'clip', 0, 0, tiled=True).reshape(in_rows, chans)]
    ppermute x9, waiting for transfers between devices: 8.62 us -> 3.41 us  [around(): lax.ppermute(blocks, 'tm', [(i, (i + distance) % depth) for i in range(de...]
    ppermute x9, starting transfers between devices: 27.4 us -> 30.7 us  [around(): lax.ppermute(blocks, 'tm', [(i, (i + distance) % depth) for i in range(de...]
  transfers between devices with their start and end apart: 25 -> 25, of which waited for: 8 -> 7; matrix products, arithmetic and copies ran while one was open for 9% -> 10% of each run, Pallas kernels for 21% -> 20%
where the time goes in v6:
time: 248 us; the launch traced here: 247 us
  Pallas kernels  78.8 us (32%)
  waiting for transfers between devices  59.8 us (24%)
  starting transfers between devices  58.9 us (24%)
  other arithmetic  21 us (8%)
  between operations  17.5 us (7%)
  local copies, waits for them, and re-layouts  10.8 us (4%)
    ppermute x9, starting transfers between devices, around(): lax.ppermute(blocks, 'tm', [(i, (i + distance) % depth) for i in range(de...  30.7 us
    all_gather x1, waiting for transfers between devices, shards(): w_full = lax.all_gather(w_mid, 'clip', axis=0, tiled=True)  26.3 us
    pallas_call x2, Pallas kernels, grad_chunk(): pl.pallas_call(lambda *refs: grad_kernel(*refs, units=units), grid_spec=p...  22.5 us
    pallas_call x2, Pallas kernels, front(): pl.pallas_call(lambda *refs: front_kernel(*refs, rows=rows, cols=cols, fi...  22.2 us
    pallas_call x1, Pallas kernels, back(): pl.pallas_call(lambda *refs: back_kernel(*refs, rows=rows, cols=cols), gr...  17.4 us
    pallas_call x1, Pallas kernels, middle(): pl.pallas_call(lambda *refs: middle_kernel(*refs, scale=scale), grid=(3,)...  16.8 us
    ppermute x6, waiting for transfers between devices, across_plane(): got.append(lax.ppermute(payloads[q - 1], 'clip', route))  16.2 us
    convert_element_type x7, other arithmetic, packed(): return jnp.where(row < rows, x * jnp.exp2(14.0 - power), power).astype(F16)  10.8 us
  transfers between devices with their start and end apart: 25, of which 7 were waited for; matrix products, arithmetic and copies ran while one was open for 10% of the time, Pallas kernels for 20%

profile of v6, /device:TPU:0, one launch (start us, length us, event | category | flops | bytes accessed | tf_op | source)
XLA Modules:
  0.0 246.8 jit_solution(14812412117927188991)
XLA Ops:
  9.1 4.9 %collective-permute-start = (bf16[16,512]{1,0:T(8,128)(2,1)S(1)}, bf16[16,512]{1,0:T(8,128)(2,1)S(1)}, u32[]{:S(2)}, u32[]{:S(2)}) collective-permute-start(bf16[16,512]{1,0:T(8,128)(2,1)S(1)} %slice.168), channel_id=1, source_target_pairs={{0,1},{1,2},{2,3},{4,5},{5,6},{6,7},{8,9},{9,10},{10,11},{12,13},{... | collective-permute-start | bytes 49160 | tf_op jit(solution)/shard_map/ppermute | solution.py:19
  16.1 12.2 %front.2 = (bf16[432,1024]{1,0:T(8,128)(2,1)}, f32[1024,384]{1,0:T(8,128)}, bf16[3,10,10,16,384]{4,3,2,1,0:T(8,128)(2,1)}, bf16[27,384,1024]{2,1,0:T(8,128)(2,1)}, f32[384,128]{1,0:T(8,128)}) custom-call(bf16[16,1536]{1,0:T(8,128)(2,1)} %copy-done.5, bf16[432,384]{1,0:T(8,128)(2,1)} %refs_1_.3), custom_call_target="tpu_custom_call" | custom-call | tf_op jit(solution)/shard_map/front/pallas_call | solution.py:126
  29.0 9.9 %front.3 = (bf16[27,384,1024]{2,1,0:T(8,128)(2,1)}, f32[384,128]{1,0:T(8,128)}) custom-call(bf16[16,1536]{1,0:T(8,128)(2,1)} %copy-done.9, bf16[432,384]{1,0:T(8,128)(2,1)} %refs_1_.3), custom_call_target="tpu_custom_call" | custom-call | tf_op jit(solution)/shard_map/front/pallas_call | solution.py:126
  38.9 26.3 %all-gather.2.cloned.1.call-done = bf16[10368,384]{1,0:T(8,128)(2,1)} async-done(((bf16[1296,384]{1,0:T(8,128)(2,1)}), bf16[10368,384]{1,0:T(8,128)(2,1)}) %all-gather.2.cloned.1.call-update) | async-done | bytes 7962640 | tf_op jit(solution)/shard_map/all_gather | solution.py:387
  65.2 16.8 %middle.1 = (bf16[1024,384]{1,0:T(8,128)(2,1)}, f32[8,128]{1,0:T(8,128)}) custom-call(bf16[3,10,10,16,384]{4,3,2,1,0:T(8,128)(2,1)} %get-tuple-element.60.refs_0_, bf16[27,384,384]{2,1,0:T(8,128)(2,1)} %bitcast.59, bf16[1024,384]{1,0:T(8,128)(2,1)} %bitcast.61), custom_call_target="tpu_custom_call" | custom-call | tf_op jit(solution)/shard_map/middle/pallas_call | solution.py:169
  89.7 13.7 %grad.2 = (f32[912,384]{1,0:T(8,128)}, f32[4,912,384]{2,1,0:T(8,128)}) custom-call(s32[4]{0:T(128)} %multiply_xor_fusion.refs_0_, bf16[10368,1024]{1,0:T(8,128)(2,1)} %bitcast.51, bf16[10368,1024]{1,0:T(8,128)(2,1)} %bitcast.55, bf16[10368,1024]{1,0:T(8,128)(2,1)} %bitcast.52, bf16[10368,1024]{1,0:T(8,128)(2,1)} %bitcast.56, ...), custom_call_target="tpu_custom_call" | custom-call | tf_op jit(solution)/shard_map/grad/pallas_call | solution.py:226
  103.4 4.1 %fusion = (f16[912,384]{1,0:T(8,128)(2,1)}, f16[912,384]{1,0:T(8,128)(2,1)}, f16[912,384]{1,0:T(8,128)(2,1)}) fusion(f32[4,912,384]{2,1,0:T(8,128)} %get-tuple-element.64, f32[]{:T(128)} %bitcast.10, f32[]{:T(128)} %bitcast.8, pred[912]{0:T(1024)(128)(4,1)S(1)} %iota_compare_fusion), kind=kLoop, calls=%fused_computation.1 | loop fusion | flops 3151872 | bytes 6304664 | tf_op jit(solution)/shard_map/convert_element_type | solution.py:305
  107.4 1.5 collective-permute-start.5
  109.4 1.5 collective-permute-start.7
  111.9 1.5 collective-permute-start.4
  113.4 6.6 %collective-permute-done.4.refs_1_ = bf16[256,384]{1,0:T(8,128)(2,1)S(1)} collective-permute-done((bf16[256,384]{1,0:T(8,128)(2,1)S(1)}, bf16[256,384]{1,0:T(8,128)(2,1)S(1)}, u32[]{:S(2)}, u32[]{:S(2)}) %collective-permute-start.4) | collective-permute-done | bytes 196640 | tf_op jit(solution)/shard_map/ppermute | solution.py:19
  120.6 17.4 %back.1 = f32[432,384]{1,0:T(8,128)} custom-call(bf16[1024,384]{1,0:T(8,128)(2,1)} %get-tuple-element.71.refs_5_.refs_0_, bf16[256,384]{1,0:T(8,128)(2,1)} %copy-done.8, bf16[27,384,384]{2,1,0:T(8,128)(2,1)} %bitcast.60, f32[1024,384]{1,0:T(8,128)} %get-tuple-element.69.refs_3_, bf16[432,1024]{1,0:T(8,128)(2,1)} %get-tuple-element.70.refs_4_), custom_call_target="tpu_custom_call" | custom-call | tf_op jit(solution)/shard_map/back/pallas_call | solution.py:281
  138.0 2.0 reshape.50
  140.1 3.5 %all-to-all-start = ((f32[8,54,384]{2,1,0:T(8,128)}), f32[8,54,384]{2,1,0:T(8,128)S(1)}, u32[]{:S(2)}, u32[]{:S(2)}) async-start(f32[8,54,384]{2,1,0:T(8,128)} %reshape.50), calls=%async_computation | async-start | bytes 1376256 | tf_op jit(solution)/shard_map/all_to_all | solution.py:411
  143.6 8.8 %grad.3 = (f32[464,384]{1,0:T(8,128)}, f32[4,464,384]{2,1,0:T(8,128)}) custom-call(s32[4]{0:T(128)} %multiply_xor_fusion.refs_0_, bf16[10368,1024]{1,0:T(8,128)(2,1)} %bitcast.53, bf16[10368,1024]{1,0:T(8,128)(2,1)} %bitcast.57, bf16[10368,1024]{1,0:T(8,128)(2,1)} %bitcast.54, bf16[10368,1024]{1,0:T(8,128)(2,1)} %bitcast.58, ...), custom_call_target="tpu_custom_call" | custom-call | tf_op jit(solution)/shard_map/grad/pallas_call | solution.py:226
  152.4 2.8 %fusion.3 = (f16[464,384]{1,0:T(8,128)(2,1)S(1)}, f16[464,384]{1,0:T(8,128)(2,1)}, f16[464,384]{1,0:T(8,128)(2,1)}) fusion(f32[4,464,384]{2,1,0:T(8,128)} %get-tuple-element.72, f32[]{:T(128)} %bitcast.10, f32[]{:T(128)} %bitcast.8, pred[464]{0:T(512)(128)(4,1)S(1)} %iota_compare_fusion.1), kind=kLoop, calls=%fused_computation.8 | loop fusion | flops 1603584 | bytes 3207640 | tf_op jit(solution)/shard_map/convert_element_type | solution.py:305
  157.1 3.7 %all-to-all-start.1 = ((f16[4,240,384]{2,1,0:T(8,128)(2,1)}), f16[4,240,384]{2,1,0:T(8,128)(2,1)S(1)}, u32[]{:S(2)}, u32[]{:S(2)}) async-start(f16[4,240,384]{2,1,0:T(8,128)(2,1)} %bitcast.17), calls=%async_computation.1 | async-start | bytes 1474560 | tf_op jit(solution)/shard_map/all_to_all | solution.py:344
  160.8 1.9 collective-permute-start.8
  162.7 1.5 collective-permute-start.9
  164.3 7.8 %collective-permute-done.8 = f16[464,384]{1,0:T(8,128)(2,1)S(1)} collective-permute-done((f16[464,384]{1,0:T(8,128)(2,1)}, f16[464,384]{1,0:T(8,128)(2,1)S(1)}, u32[]{:S(2)}, u32[]{:S(2)}) %collective-permute-start.8) | collective-permute-done | bytes 356384 | tf_op jit(solution)/shard_map/ppermute | solution.py:315
  172.1 8.4 %collective-permute-done.9 = f16[464,384]{1,0:T(8,128)(2,1)S(1)} collective-permute-done((f16[464,384]{1,0:T(8,128)(2,1)}, f16[464,384]{1,0:T(8,128)(2,1)S(1)}, u32[]{:S(2)}, u32[]{:S(2)}) %collective-permute-start.9) | collective-permute-done | bytes 356384 | tf_op jit(solution)/shard_map/ppermute | solution.py:315
  180.5 1.9 select_convert_fusion.6
  182.5 1.6 collective-permute-start.11
  184.1 2.4 collective-permute-start.12
  186.5 1.5 collective-permute-start.13
  188.8 3.5 %all-to-all-start.2 = ((f32[4,54,384]{2,1,0:T(8,128)}), f32[4,54,384]{2,1,0:T(8,128)S(1)}, u32[]{:S(2)}, u32[]{:S(2)}) async-start(f32[4,54,384]{2,1,0:T(8,128)} %broadcast_in_dim.92), calls=%async_computation.2 | async-start | bytes 688128 | tf_op jit(solution)/shard_map/all_to_all | solution.py:424
  192.6 3.8 %collective-permute-start.14 = (f16[240,384]{1,0:T(8,128)(2,1)S(1)}, f16[240,384]{1,0:T(8,128)(2,1)S(1)}, u32[]{:S(2)}, u32[]{:S(2)}) collective-permute-start(f16[240,384]{1,0:T(8,128)(2,1)S(1)} %select_convert_fusion), channel_id=1, source_target_pairs={{0,3},{1,0},{2,1},{3,2},{4,7},{5,4},{6,5},{7,6},{8,11},{9,8},{10,9... | collective-permute-start | bytes 552968 | tf_op jit(solution)/shard_map/ppermute | solution.py:321
  199.4 8.9 %collective-permute-start.19 = (f16[128,384]{1,0:T(8,128)(2,1)S(1)}, f16[128,384]{1,0:T(8,128)(2,1)S(1)}, u32[]{:S(2)}, u32[]{:S(2)}) collective-permute-start(f16[128,384]{1,0:T(8,128)(2,1)S(1)} %select_convert_fusion.5), channel_id=1, source_target_pairs={{0,3},{1,0},{2,1},{3,2},{4,7},{5,4},{6,5},{7,6},{8,11},{9,8},{10,9... | collective-permute-start | bytes 294920 | tf_op jit(solution)/shard_map/ppermute | solution.py:321
  208.3 11.4 %collective-permute-start.17 = (f16[128,384]{1,0:T(8,128)(2,1)S(1)}, f16[128,384]{1,0:T(8,128)(2,1)S(1)}, u32[]{:S(2)}, u32[]{:S(2)}) collective-permute-start(f16[128,384]{1,0:T(8,128)(2,1)S(1)} %select_convert_fusion.5), channel_id=1, source_target_pairs={{0,1},{1,2},{2,3},{3,0},{4,5},{5,6},{6,7},{7,4},{8,9},{9,10},{10,1... | collective-permute-start | bytes 294920 | tf_op jit(solution)/shard_map/ppermute | solution.py:321
  219.7 3.4 %collective-permute-done.15 = f16[240,384]{1,0:T(8,128)(2,1)S(1)} collective-permute-done((f16[240,384]{1,0:T(8,128)(2,1)S(1)}, f16[240,384]{1,0:T(8,128)(2,1)S(1)}, u32[]{:S(2)}, u32[]{:S(2)}) %collective-permute-start.15) | collective-permute-done | bytes 184352 | tf_op jit(solution)/shard_map/ppermute | solution.py:321
  224.0 3.5 %all-to-all-start.3 = ((f32[8,54,384]{2,1,0:T(8,128)}), f32[8,54,384]{2,1,0:T(8,128)S(1)}, u32[]{:S(2)}, u32[]{:S(2)}) async-start(f32[8,54,384]{2,1,0:T(8,128)} %broadcast_in_dim.93), calls=%async_computation.3 | async-start | bytes 1376256 | tf_op jit(solution)/shard_map/all_to_all | solution.py:435
  233.9 5.1 %all-to-all-done.3 = f32[8,54,384]{2,1,0:T(8,128)S(1)} async-done(((f32[8,54,384]{2,1,0:T(8,128)}), f32[8,54,384]{2,1,0:T(8,128)S(1)}, u32[]{:S(2)}, u32[]{:S(2)}) %all-to-all-start.3) | async-done | bytes 663584 | tf_op jit(solution)/shard_map/all_to_all | solution.py:435
  (90 shorter events, 25.4 us)
Async XLA Ops:
  7.2 1.4 copy-start
  7.2 58.0 %all-gather.2.cloned.1.call-start = ((), (), s32[]{:S(2)}) async-start(), calls=%async_computation.4 | async-start | bytes 8957952 | tf_op jit(solution)/shard_map/all_gather | solution.py:387
  9.1 6.4 %collective-permute-start = (bf16[16,512]{1,0:T(8,128)(2,1)S(1)}, bf16[16,512]{1,0:T(8,128)(2,1)S(1)}, u32[]{:S(2)}, u32[]{:S(2)}) collective-permute-start(bf16[16,512]{1,0:T(8,128)(2,1)S(1)} %slice.168), channel_id=1, source_target_pairs={{0,1},{1,2},{2,3},{4,5},{5,6},{6,7},{8,9},{9,10},{10,11},{12,13},{... | collective-permute-start | bytes 49160 | tf_op jit(solution)/shard_map/ppermute | solution.py:19
  15.5 12.9 %collective-permute-start.1 = (bf16[16,1536]{1,0:T(8,128)(2,1)S(1)}, bf16[16,1536]{1,0:T(8,128)(2,1)S(1)}, u32[]{:S(2)}, u32[]{:S(2)}) collective-permute-start(bf16[16,1536]{1,0:T(8,128)(2,1)S(1)} %pad_maximum_fusion.1.refs_0_), channel_id=1, source_target_pairs={{0,4},{4,0},{8,12},{12,8},{16,20},{20,16},{24,28},{28,24},{1,5},{5... | collective-permute-start | bytes 147464 | tf_op jit(solution)/shard_map/ppermute | solution.py:23
  65.2 17.9 %copy-start.6 = (f32[384,128]{1,0:T(8,128)S(1)}, f32[384,128]{1,0:T(8,128)}, u32[]{:S(2)}) copy-start(f32[384,128]{1,0:T(8,128)} %get-tuple-element.65) | copy-start | bytes 589828
  65.2 19.8 %copy-start.7 = (f32[384,128]{1,0:T(8,128)S(1)}, f32[384,128]{1,0:T(8,128)}, u32[]{:S(2)}) copy-start(f32[384,128]{1,0:T(8,128)} %get-tuple-element.67) | copy-start | bytes 589828
  82.0 6.8 %collective-permute-start.2 = (bf16[1024,384]{1,0:T(8,128)(2,1)}, bf16[1024,384]{1,0:T(8,128)(2,1)S(1)}, u32[]{:S(2)}, u32[]{:S(2)}) collective-permute-start(bf16[1024,384]{1,0:T(8,128)(2,1)} %get-tuple-element.71.refs_5_.refs_0_), channel_id=1, source_target_pairs={{0,4},{4,0},{8,12},{12,8},{16,20},{20,16},{24,28},{28,24},{1,5},{5... | collective-permute-start | bytes 2359304 | tf_op jit(solution)/shard_map/ppermute | solution.py:23
  82.3 4.7 %collective-permute-start.3 = (f32[8,128]{1,0:T(8,128)}, f32[8,128]{1,0:T(8,128)S(1)}, u32[]{:S(2)}, u32[]{:S(2)}) collective-permute-start(f32[8,128]{1,0:T(8,128)} %get-tuple-element.66), channel_id=1, source_target_pairs={{0,4},{4,0},{8,12},{12,8},{16,20},{20,16},{24,28},{28,24},{1,5},{5... | collective-permute-start | bytes 12296 | tf_op jit(solution)/shard_map/ppermute | solution.py:23
  88.8 0.9 copy-start.2
  107.4 47.8 %collective-permute-start.5 = (f16[912,384]{1,0:T(8,128)(2,1)}, f16[912,384]{1,0:T(8,128)(2,1)S(1)}, u32[]{:S(2)}, u32[]{:S(2)}) collective-permute-start(f16[912,384]{1,0:T(8,128)(2,1)} %get-tuple-element.73), channel_id=1, source_target_pairs={{0,8},{4,12},{8,0},{12,4},{16,24},{20,28},{24,16},{28,20},{1,9},{5... | collective-permute-start | bytes 2101256 | tf_op jit(solution)/shard_map/ppermute | solution.py:315
  108.9 46.3 %collective-permute-start.6 = (f16[912,384]{1,0:T(8,128)(2,1)}, f16[912,384]{1,0:T(8,128)(2,1)S(1)}, u32[]{:S(2)}, u32[]{:S(2)}) collective-permute-start(f16[912,384]{1,0:T(8,128)(2,1)} %get-tuple-element.74), channel_id=1, source_target_pairs={{0,16},{4,20},{8,24},{12,28},{16,0},{20,4},{24,8},{28,12},{1,17},{... | collective-permute-start | bytes 2101256 | tf_op jit(solution)/shard_map/ppermute | solution.py:315
  109.4 45.8 %collective-permute-start.7 = (f16[912,384]{1,0:T(8,128)(2,1)}, f16[912,384]{1,0:T(8,128)(2,1)S(1)}, u32[]{:S(2)}, u32[]{:S(2)}) collective-permute-start(f16[912,384]{1,0:T(8,128)(2,1)} %get-tuple-element.75), channel_id=1, source_target_pairs={{0,24},{4,28},{8,16},{12,20},{16,8},{20,12},{24,0},{28,4},{1,25},{... | collective-permute-start | bytes 2101256 | tf_op jit(solution)/shard_map/ppermute | solution.py:315
  111.9 8.1 %collective-permute-start.4 = (bf16[256,384]{1,0:T(8,128)(2,1)S(1)}, bf16[256,384]{1,0:T(8,128)(2,1)S(1)}, u32[]{:S(2)}, u32[]{:S(2)}) collective-permute-start(bf16[256,384]{1,0:T(8,128)(2,1)S(1)} %slice.132), channel_id=1, source_target_pairs={{1,0},{2,1},{3,2},{5,4},{6,5},{7,6},{9,8},{10,9},{11,10},{13,12},{... | collective-permute-start | bytes 589832 | tf_op jit(solution)/shard_map/ppermute | solution.py:19
  140.1 17.0 %all-to-all-start = ((f32[8,54,384]{2,1,0:T(8,128)}), f32[8,54,384]{2,1,0:T(8,128)S(1)}, u32[]{:S(2)}, u32[]{:S(2)}) async-start(f32[8,54,384]{2,1,0:T(8,128)} %reshape.50), calls=%async_computation | async-start | bytes 1376256 | tf_op jit(solution)/shard_map/all_to_all | solution.py:411
  152.4 2.9 %copy-start.3 = (f32[912,384]{1,0:T(8,128)S(1)}, f32[912,384]{1,0:T(8,128)}, u32[]{:S(2)}) copy-start(f32[912,384]{1,0:T(8,128)} %get-tuple-element.63) | copy-start | bytes 4202500
  156.0 24.6 %copy-start.4 = (f32[464,384]{1,0:T(8,128)S(1)}, f32[464,384]{1,0:T(8,128)}, u32[]{:S(2)}) copy-start(f32[464,384]{1,0:T(8,128)} %get-tuple-element.87) | copy-start | bytes 2138116
  157.1 30.8 %all-to-all-start.1 = ((f16[4,240,384]{2,1,0:T(8,128)(2,1)}), f16[4,240,384]{2,1,0:T(8,128)(2,1)S(1)}, u32[]{:S(2)}, u32[]{:S(2)}) async-start(f16[4,240,384]{2,1,0:T(8,128)(2,1)} %bitcast.17), calls=%async_computation.1 | async-start | bytes 1474560 | tf_op jit(solution)/shard_map/all_to_all | solution.py:344
  160.8 11.4 %collective-permute-start.8 = (f16[464,384]{1,0:T(8,128)(2,1)}, f16[464,384]{1,0:T(8,128)(2,1)S(1)}, u32[]{:S(2)}, u32[]{:S(2)}) collective-permute-start(f16[464,384]{1,0:T(8,128)(2,1)} %get-tuple-element.88), channel_id=1, source_target_pairs={{0,8},{4,12},{8,0},{12,4},{16,24},{20,28},{24,16},{28,20},{1,9},{5... | collective-permute-start | bytes 1069064 | tf_op jit(solution)/shard_map/ppermute | solution.py:315
  162.7 17.8 %collective-permute-start.9 = (f16[464,384]{1,0:T(8,128)(2,1)}, f16[464,384]{1,0:T(8,128)(2,1)S(1)}, u32[]{:S(2)}, u32[]{:S(2)}) collective-permute-start(f16[464,384]{1,0:T(8,128)(2,1)} %get-tuple-element.89), channel_id=1, source_target_pairs={{0,16},{4,20},{8,24},{12,28},{16,0},{20,4},{24,8},{28,12},{1,17},{... | collective-permute-start | bytes 1069064 | tf_op jit(solution)/shard_map/ppermute | solution.py:315
  164.2 16.3 %collective-permute-start.10 = (f16[464,384]{1,0:T(8,128)(2,1)S(1)}, f16[464,384]{1,0:T(8,128)(2,1)}, u32[]{:S(2)}, u32[]{:S(2)}) collective-permute-start(f16[464,384]{1,0:T(8,128)(2,1)S(1)} %get-tuple-element.90), channel_id=1, source_target_pairs={{0,24},{4,28},{8,16},{12,20},{16,8},{20,12},{24,0},{28,4},{1,25},{... | collective-permute-start | bytes 1069064 | tf_op jit(solution)/shard_map/ppermute | solution.py:315
  182.5 13.9 %collective-permute-start.11 = (f16[128,384]{1,0:T(8,128)(2,1)S(1)}, f16[128,384]{1,0:T(8,128)(2,1)S(1)}, u32[]{:S(2)}, u32[]{:S(2)}) collective-permute-start(f16[128,384]{1,0:T(8,128)(2,1)S(1)} %get-tuple-element.94), channel_id=1, source_target_pairs={{0,1},{1,2},{2,3},{3,0},{4,5},{5,6},{6,7},{7,4},{8,9},{9,10},{10,1... | collective-permute-start | bytes 294920 | tf_op jit(solution)/shard_map/ppermute | solution.py:321
  184.1 13.4 %collective-permute-start.12 = (f16[128,384]{1,0:T(8,128)(2,1)}, f16[128,384]{1,0:T(8,128)(2,1)S(1)}, u32[]{:S(2)}, u32[]{:S(2)}) collective-permute-start(f16[128,384]{1,0:T(8,128)(2,1)} %get-tuple-element.95), channel_id=1, source_target_pairs={{0,2},{1,3},{2,0},{3,1},{4,6},{5,7},{6,4},{7,5},{8,10},{9,11},{10,... | collective-permute-start | bytes 294920 | tf_op jit(solution)/shard_map/ppermute | solution.py:321
  186.5 11.1 %collective-permute-start.13 = (f16[128,384]{1,0:T(8,128)(2,1)}, f16[128,384]{1,0:T(8,128)(2,1)}, u32[]{:S(2)}, u32[]{:S(2)}) collective-permute-start(f16[128,384]{1,0:T(8,128)(2,1)} %get-tuple-element.96), channel_id=1, source_target_pairs={{0,3},{1,0},{2,1},{3,2},{4,7},{5,4},{6,5},{7,6},{8,11},{9,8},{10,9... | collective-permute-start | bytes 294920 | tf_op jit(solution)/shard_map/ppermute | solution.py:321
  188.8 19.5 %all-to-all-start.2 = ((f32[4,54,384]{2,1,0:T(8,128)}), f32[4,54,384]{2,1,0:T(8,128)S(1)}, u32[]{:S(2)}, u32[]{:S(2)}) async-start(f32[4,54,384]{2,1,0:T(8,128)} %broadcast_in_dim.92), calls=%async_computation.2 | async-start | bytes 688128 | tf_op jit(solution)/shard_map/all_to_all | solution.py:424
  192.6 15.8 %collective-permute-start.14 = (f16[240,384]{1,0:T(8,128)(2,1)S(1)}, f16[240,384]{1,0:T(8,128)(2,1)S(1)}, u32[]{:S(2)}, u32[]{:S(2)}) collective-permute-start(f16[240,384]{1,0:T(8,128)(2,1)S(1)} %select_convert_fusion), channel_id=1, source_target_pairs={{0,3},{1,0},{2,1},{3,2},{4,7},{5,4},{6,5},{7,6},{8,11},{9,8},{10,9... | collective-permute-start | bytes 552968 | tf_op jit(solution)/shard_map/ppermute | solution.py:321
  196.4 26.7 %collective-permute-start.15 = (f16[240,384]{1,0:T(8,128)(2,1)S(1)}, f16[240,384]{1,0:T(8,128)(2,1)S(1)}, u32[]{:S(2)}, u32[]{:S(2)}) collective-permute-start(f16[240,384]{1,0:T(8,128)(2,1)S(1)} %select_convert_fusion), channel_id=1, source_target_pairs={{0,2},{1,3},{2,0},{3,1},{4,6},{5,7},{6,4},{7,5},{8,10},{9,11},{10,... | collective-permute-start | bytes 552968 | tf_op jit(solution)/shard_map/ppermute | solution.py:321
  196.4 26.7 %collective-permute-start.16 = (f16[240,384]{1,0:T(8,128)(2,1)S(1)}, f16[240,384]{1,0:T(8,128)(2,1)S(1)}, u32[]{:S(2)}, u32[]{:S(2)}) collective-permute-start(f16[240,384]{1,0:T(8,128)(2,1)S(1)} %select_convert_fusion), channel_id=1, source_target_pairs={{0,1},{1,2},{2,3},{3,0},{4,5},{5,6},{6,7},{7,4},{8,9},{9,10},{10,1... | collective-permute-start | bytes 552968 | tf_op jit(solution)/shard_map/ppermute | solution.py:321
  199.4 31.6 %collective-permute-start.19 = (f16[128,384]{1,0:T(8,128)(2,1)S(1)}, f16[128,384]{1,0:T(8,128)(2,1)S(1)}, u32[]{:S(2)}, u32[]{:S(2)}) collective-permute-start(f16[128,384]{1,0:T(8,128)(2,1)S(1)} %select_convert_fusion.5), channel_id=1, source_target_pairs={{0,3},{1,0},{2,1},{3,2},{4,7},{5,4},{6,5},{7,6},{8,11},{9,8},{10,9... | collective-permute-start | bytes 294920 | tf_op jit(solution)/shard_map/ppermute | solution.py:321
  208.3 22.7 %collective-permute-start.18 = (f16[128,384]{1,0:T(8,128)(2,1)S(1)}, f16[128,384]{1,0:T(8,128)(2,1)S(1)}, u32[]{:S(2)}, u32[]{:S(2)}) collective-permute-start(f16[128,384]{1,0:T(8,128)(2,1)S(1)} %select_convert_fusion.5), channel_id=1, source_target_pairs={{0,2},{1,3},{2,0},{3,1},{4,6},{5,7},{6,4},{7,5},{8,10},{9,11},{10,... | collective-permute-start | bytes 294920 | tf_op jit(solution)/shard_map/ppermute | solution.py:321
  208.3 22.7 %collective-permute-start.17 = (f16[128,384]{1,0:T(8,128)(2,1)S(1)}, f16[128,384]{1,0:T(8,128)(2,1)S(1)}, u32[]{:S(2)}, u32[]{:S(2)}) collective-permute-start(f16[128,384]{1,0:T(8,128)(2,1)S(1)} %select_convert_fusion.5), channel_id=1, source_target_pairs={{0,1},{1,2},{2,3},{3,0},{4,5},{5,6},{6,7},{7,4},{8,9},{9,10},{10,1... | collective-permute-start | bytes 294920 | tf_op jit(solution)/shard_map/ppermute | solution.py:321
  224.0 15.0 %all-to-all-start.3 = ((f32[8,54,384]{2,1,0:T(8,128)}), f32[8,54,384]{2,1,0:T(8,128)S(1)}, u32[]{:S(2)}, u32[]{:S(2)}) async-start(f32[8,54,384]{2,1,0:T(8,128)} %broadcast_in_dim.93), calls=%async_computation.3 | async-start | bytes 1376256 | tf_op jit(solution)/shard_map/all_to_all | solution.py:435
  231.0 8.9 %copy-start.1 = (bf16[1,8,8,32,16]{3,4,2,1,0:T(8,128)(2,1)S(1)}, bf16[1,8,8,32,16]{3,4,2,1,0:T(8,128)(2,1)}, u32[]{:S(2)}) copy-start(bf16[1,8,8,32,16]{3,4,2,1,0:T(8,128)(2,1)} %param.5) | copy-start | bytes 196612
  (3 other events, 1.9 us)
Sparse Core Ops, SparseCore 0:
  9.9 55.2 all-gather.1

commit v7 on v6

--- a/solution.py
+++ b/solution.py
@@ -138,7 +138,7 @@
     )(crop_t, w_in)
 
 
-def middle_kernel(cells_ref, w_ref, teacher_ref, g_ref, size_ref, acc_ref, *, scale):
+def middle_kernel(cells_ref, w_ref, teacher_ref, g_ref, head_ref, acc_ref, *, scale):
     depth = pl.program_id(0)
     frames = cells_ref.shape[1] - 2
     rows = cells_ref.shape[2] - 2
@@ -159,12 +159,14 @@
     @pl.when(depth == 2)
     def _():
         g = ((acc_ref[...] + total - teacher_ref[...].astype(F32)) * scale).astype(BF16)
-        g_ref[...] = g
+        count = g.shape[0]
+        g_ref[:count, :] = g
+        head_ref[...] = g[: head_ref.shape[0]]
         size = jnp.max(jnp.sum(jnp.abs(g.astype(F32)), axis=0, keepdims=True), axis=1, keepdims=True)
-        size_ref[...] = jnp.broadcast_to(size, size_ref.shape)
-
-
-def middle(cells, w_taps, teacher, scale):
+        g_ref[count:, :] = jnp.broadcast_to(size, (g_ref.shape[0] - count, g.shape[1])).astype(BF16)
+
+
+def middle(cells, w_taps, teacher, scale, head):
     count, chans = teacher.shape
     return pl.pallas_call(
         lambda *refs: middle_kernel(*refs, scale=scale),
@@ -175,12 +177,12 @@
             pl.BlockSpec((count, chans), lambda i: (0, 0)),
         ],
         out_specs=[
-            pl.BlockSpec((count, chans), lambda i: (0, 0)),
-            pl.BlockSpec((8, 128), lambda i: (0, 0)),
+            pl.BlockSpec((count + 16, chans), lambda i: (0, 0)),
+            pl.BlockSpec((head, chans), lambda i: (0, 0)),
         ],
         out_shape=[
-            jax.ShapeDtypeStruct((count, chans), BF16),
-            jax.ShapeDtypeStruct((8, 128), F32),
+            jax.ShapeDtypeStruct((count + 16, chans), BF16),
+            jax.ShapeDtypeStruct((head, chans), BF16),
         ],
         scratch_shapes=[pltpu.VMEM((count, chans), F32)],
         compiler_params=pltpu.CompilerParams(vmem_limit_bytes=VMEM),
@@ -282,7 +284,7 @@
         lambda *refs: back_kernel(*refs, rows=rows, cols=cols),
         grid=(3,),
         in_specs=[
-            pl.BlockSpec(g.shape, lambda i: (0, 0)),
+            pl.BlockSpec((count, chans), lambda i: (0, 0)),
             pl.BlockSpec(later.shape, lambda i: (0, 0)),
             pl.BlockSpec((9, chans, chans), lambda i: (i, 0, 0)),
             pl.BlockSpec((count, chans), lambda i: (0, 0)),
@@ -301,7 +303,7 @@
 
 def packed(x, rows, bound):
     power = jnp.ceil(jnp.log2(jnp.maximum(bound, 1e-30)))
-    row = lax.broadcasted_iota(jnp.int32, x.shape, 0)
+    row = lax.broadcasted_iota(jnp.int32, x.shape, x.ndim - 2)
     return jnp.where(row < rows, x * jnp.exp2(14.0 - power), power).astype(F16)
 
 
@@ -316,6 +318,10 @@
     return got, after
 
 
+def behind(x, *first):
+    return lax.optimization_barrier((x, first))[0]
+
+
 def around(blocks, distance):
     depth = lax.axis_size("tm")
     return lax.ppermute(blocks, "tm", [(i, (i + distance) % depth) for i in range(depth)])
@@ -326,50 +332,51 @@
     return [power * 2.0**-14 for power in powers], (bound + sum(powers)) * 1.01
 
 
-def across_depth(own, got, rows, factors, total, after, at_once):
+def across_depth(own, got, rows, factors, total, after):
     depth = lax.axis_size("tm")
     me = lax.axis_index("tm")
     small = piece_rows(rows)
 
     def piece(place):
-        first = place * small
-        terms = lax.dynamic_slice_in_dim(own, first, small + 16, axis=0)
-        for x, factor in zip(got, factors):
-            terms = terms + lax.dynamic_slice_in_dim(x, first, small + 16, axis=0).astype(F32) * factor
-        return terms
-
-    if at_once:
-        payload = jnp.concatenate([packed(piece(d), small, total) for d in range(depth)], axis=0)
-        payload, after = lax.optimization_barrier((payload, after))
-        got = lax.all_to_all(payload, "tm", 0, 0, tiled=True)
-        return (None, [got[d * (small + 16) : (d + 1) * (small + 16)] for d in range(depth)]), after
+        cut = lambda x: lax.dynamic_slice_in_dim(x, place * small, small + 16, axis=0)
+        terms = [cut(x).astype(F32) * factor for x, factor in zip(got, factors)]
+        return sum(terms) if own is None else cut(own) + sum(terms)
+
     payloads = [packed(piece((me + d) % depth), small, total) for d in range(1, depth)]
-    payloads, after = lax.optimization_barrier((payloads, after))
+    after = behind(after, payloads)
     others = [around(payloads[d - 1], d) for d in range(1, depth)]
     return (piece(me), others), after
 
 
-def spread(own, got, small, factors, total):
+def spread(parts, smalls, factors, total):
     depth = lax.axis_size("tm")
-    terms = [x.astype(F32) * factor for x, factor in zip(got, factors)]
-    own = sum(terms) if own is None else own + sum(terms)
-    payload = packed(own, small, total)
+    sums = []
+    for (own, got), small in zip(parts, smalls):
+        terms = [x[:small].astype(F32) * factor for x, factor in zip(got, factors)]
+        sums.append(own[:small] + sum(terms))
+    rows = sum(smalls)
+    payload = packed(jnp.pad(jnp.concatenate(sums, axis=0), ((0, 16), (0, 0))), rows, total)
     return [payload] + [around(payload, depth - k) for k in range(1, depth)]
 
 
-def assembled(pieces, factors, small, rows):
+def assembled(pieces, factors, smalls, rows):
     depth = lax.axis_size("tm")
     me = lax.axis_index("tm")
-    pieces = [x[:small].astype(F32) * factor for x, factor in zip(pieces, factors)]
-    out = []
+    pieces = [x.astype(F32) * factor for x, factor in zip(pieces, factors)]
+    placed = []
     for place in range(depth):
         x = pieces[0]
         for k in range(1, depth):
             x = jnp.where((me + k) % depth == place, pieces[k], x)
-        count = min(small, rows - place * small)
-        if count <= 0:
-            break
-        out.append(x[:count])
+        placed.append(x)
+    out = []
+    at = 0
+    for small, count in zip(smalls, rows):
+        for place in range(depth):
+            left = min(small, count - place * small)
+            if left > 0:
+                out.append(placed[place][at : at + left])
+        at += small
     return out
 
 
@@ -392,49 +399,52 @@
     pair_taps, pair_top = front(swapped(crop_ext), w_in, rows, cols, count, False)
     taps = taps.reshape(27 * chans, count)
     pair_taps = pair_taps.reshape(27 * chans, count)
-    w_full, pair_taps, pair_top = lax.optimization_barrier((w_full, pair_taps, pair_top))
+    top, pair_top = jnp.max(top), jnp.max(pair_top)
+    w_full, pair_taps, top, pair_top = lax.optimization_barrier((w_full, pair_taps, top, pair_top))
     w_taps = w_full.reshape(27, chans, chans)
-    g, size = middle(cells, w_taps, teacher[0].reshape(count, chans), scale)
+    g, head = middle(cells, w_taps, teacher[0].reshape(count, chans), scale, 2 * plane)
     pair_g = swapped(g)
-    pair_size = swapped(size)
-    later = passed_along(g[: 2 * plane], "tm", -1)
-
-    order = lax.axis_index("clip") ^ (2 * jnp.arange(clips // 2, dtype=jnp.int32))
+    later = passed_along(head, "tm", -1)
+
     third = 27 * chans // clips // 3
-    bound = (jnp.max(top) * size[:1, :1] + jnp.max(pair_top) * pair_size[:1, :1]) * 1.01
+    spare = slice(count, count + 1)
+    bound = (top * g[spare, :1].astype(F32) + pair_top * pair_g[spare, :1].astype(F32)) * 1.03
     both = (taps, pair_taps)
     in_rows = patch_t.shape[0]
 
-    own_a, part = grad_chunk(order, both, (g, pair_g), 0, 2)
+    me = lax.axis_index("clip")
+    chips = jnp.arange(clips // 2, dtype=jnp.int32)
+    own_a, part = grad_chunk(me ^ (2 * chips), both, (g, pair_g), 0, 2)
+    part, later = lax.optimization_barrier((part, later))
     got_a, g = across_plane(part, 2 * third, bound, g)
+    _, part = grad_chunk(2 * chips + me % 2, both, (g, pair_g), 2, 1)
+    payload = packed(part, third, bound)
+    payload, g = lax.optimization_barrier((payload, g))
+    groups = [[2 * p + core for p in range(clips // 2)] for core in range(2)]
+    got_b = lax.all_to_all(payload, "clip", 0, 0, axis_index_groups=groups, tiled=True)
+    got_b = [got_b[p] for p in range(clips // 2)]
     in_part = back(g, later, w_taps, z, patch_t, rows, cols)
+
+    got_a = behind(got_a, in_part)
+    factors, total = scales(got_a, 2 * third, bound)
+    (own_a, depth_a), got_b = across_depth(own_a, got_a, 2 * third, factors, total, got_b)
+    factors, _ = scales(got_b, third, 0.0)
+    (own_b, depth_b), in_part = across_depth(None, got_b, third, factors, total, in_part)
     in_got = lax.all_to_all(in_part.reshape(clips, in_rows // clips, chans), "clip", 0, 0, tiled=True)
-    g, in_part = lax.optimization_barrier((g, in_part))
-    own_b, part = grad_chunk(order, both, (g, pair_g), 2, 1)
-    got_b, got_a = across_plane(part, third, bound, got_a)
-
-    factors, total = scales(got_a, 2 * third, bound)
-    (_, depth_a), in_got = across_depth(own_a, got_a, 2 * third, factors, total, in_got, True)
-    in_sum = in_got.sum(axis=0)
-    got_b, _ = lax.optimization_barrier((got_b, in_sum))
-    (own_b, depth_b), _ = across_depth(own_b, got_b, third, factors, total, total, False)
-    in_sum, depth_a = lax.optimization_barrier((in_sum, depth_a))
+    z_total = total
+    smalls = [piece_rows(2 * third), piece_rows(third)]
+    factors, total = scales(depth_a, smalls[0], z_total)
+    in_sum = behind(in_got, depth_a).sum(axis=0)
     in_sum = jnp.broadcast_to(in_sum[None], (lax.axis_size("tm"),) + in_sum.shape)
-    in_sum, depth_a = lax.optimization_barrier((in_sum, depth_a))
+    depth_b = behind(depth_b, in_sum)
     in_got = lax.all_to_all(in_sum, "tm", 0, 0, tiled=True)
-    small_a = piece_rows(2 * third)
-    small_b = piece_rows(third)
-    factors, total = scales(depth_a, small_a, 0.0)
-    last_a = spread(None, depth_a, small_a, factors, total)
-    depth_b, last_a[0] = lax.optimization_barrier((depth_b, last_a[0]))
-    factors, _ = scales(depth_b, small_b, 0.0)
-    last_b = spread(own_b, depth_b, small_b, factors, total)
-    in_sum = in_got.sum(axis=0)
+    last = spread([(own_a, depth_a), (own_b, depth_b)], smalls, factors, total)
+    in_sum = behind(in_got, last[0]).sum(axis=0)
     in_sum = jnp.broadcast_to(in_sum[None], (clips,) + in_sum.shape)
-    in_sum, last_a = lax.optimization_barrier((in_sum, last_a))
+    last[-1] = behind(last[-1], in_sum)
     grad_in = lax.all_to_all(in_sum, "clip", 0, 0, tiled=True).reshape(in_rows, chans)
-    factors, _ = scales(last_a, small_a, 0.0)
-    pieces = assembled(last_a, factors, small_a, 2 * third) + assembled(last_b, factors, small_b, third)
+    factors, _ = scales(last, sum(smalls), 0.0)
+    pieces = assembled(last, factors, smalls, [2 * third, third])
     return (jnp.concatenate(pieces, axis=0), grad_in)
 
 

time: 248 us -> 239 us (0.964)
  starting transfers between devices: 58.9 us -> 43 us
  waiting for transfers between devices: 59.8 us -> 64.2 us
  local copies, waits for them, and re-layouts: 10.8 us -> 14.6 us
    ppermute x9, waiting for transfers between devices: 3.41 us -> 27.8 us  [around(): lax.ppermute(blocks, 'tm', [(i, (i + distance) % depth) for i in range(de...]
    ppermute x9, starting transfers between devices: 30.7 us -> 16.2 us  [around(): lax.ppermute(blocks, 'tm', [(i, (i + distance) % depth) for i in range(de...]
    ppermute x6 -> x3, waiting for transfers between devices: 16.2 us -> 4.48 us  [across_plane(): got.append(lax.ppermute(payloads[q - 1], 'clip', route))]
    ppermute x2, waiting for transfers between devices: 8.04 us -> 1.43 us  [passed_along(): return lax.ppermute(block, axis, route)]
    unnamed x20 -> x35, local copies, waits for them, and re-layouts: 2.79 us -> 7.19 us
    unnamed x5 -> x0, other arithmetic: 3.97 us -> none
    all_gather x1, waiting for transfers between devices: 26.3 us -> 22.8 us  [shards(): w_full = lax.all_gather(w_mid, 'clip', axis=0, tiled=True)]
    ppermute x6 -> x3, starting transfers between devices: 6.98 us -> 3.49 us  [across_plane(): got.append(lax.ppermute(payloads[q - 1], 'clip', route))]
  transfers between devices with their start and end apart: 25 -> 21, of which waited for: 7 -> 8; matrix products, arithmetic and copies ran while one was open for 10% -> 11% of each run, Pallas kernels for 20% -> 26%
where the time goes in v7:
time: 239 us; the launch traced here: 238 us
  Pallas kernels  79.1 us (33%)
  waiting for transfers between devices  64.2 us (27%)
  starting transfers between devices  43 us (18%)
  other arithmetic  19.2 us (8%)
  between operations  17.7 us (7%)
  local copies, waits for them, and re-layouts  14.6 us (6%)
    ppermute x9, waiting for transfers between devices, around(): lax.ppermute(blocks, 'tm', [(i, (i + distance) % depth) for i in range(de...  27.8 us
    all_gather x1, waiting for transfers between devices, shards(): w_full = lax.all_gather(w_mid, 'clip', axis=0, tiled=True)  22.8 us
    pallas_call x2, Pallas kernels, grad_chunk(): pl.pallas_call(lambda *refs: grad_kernel(*refs, units=units), grid_spec=p...  22.5 us
    pallas_call x2, Pallas kernels, front(): pl.pallas_call(lambda *refs: front_kernel(*refs, rows=rows, cols=cols, fi...  22.4 us
    pallas_call x1, Pallas kernels, back(): pl.pallas_call(lambda *refs: back_kernel(*refs, rows=rows, cols=cols), gr...  17.5 us
    pallas_call x1, Pallas kernels, middle(): pl.pallas_call(lambda *refs: middle_kernel(*refs, scale=scale), grid=(3,)...  16.7 us
    ppermute x9, starting transfers between devices, around(): lax.ppermute(blocks, 'tm', [(i, (i + distance) % depth) for i in range(de...  16.2 us
    convert_element_type x5, other arithmetic, packed(): return jnp.where(row < rows, x * jnp.exp2(14.0 - power), power).astype(F16)  9.72 us
  transfers between devices with their start and end apart: 21, of which 8 were waited for; matrix products, arithmetic and copies ran while one was open for 11% of the time, Pallas kernels for 26%

profile of v7, /device:TPU:0, one launch (start us, length us, event | category | flops | bytes accessed | tf_op | source)
XLA Modules:
  0.0 237.7 jit_solution(12215832441780378818)
XLA Ops:
  9.1 4.9 %collective-permute-start = (bf16[16,512]{1,0:T(8,128)(2,1)S(1)}, bf16[16,512]{1,0:T(8,128)(2,1)S(1)}, u32[]{:S(2)}, u32[]{:S(2)}) collective-permute-start(bf16[16,512]{1,0:T(8,128)(2,1)S(1)} %slice.160), channel_id=1, source_target_pairs={{0,1},{1,2},{2,3},{4,5},{5,6},{6,7},{8,9},{9,10},{10,11},{12,13},{... | collective-permute-start | bytes 49160 | tf_op jit(solution)/shard_map/ppermute | solution.py:19
  16.1 12.2 %front.2 = (bf16[432,1024]{1,0:T(8,128)(2,1)}, f32[1024,384]{1,0:T(8,128)}, bf16[3,10,10,16,384]{4,3,2,1,0:T(8,128)(2,1)}, bf16[27,384,1024]{2,1,0:T(8,128)(2,1)}, f32[384,128]{1,0:T(8,128)}) custom-call(bf16[16,1536]{1,0:T(8,128)(2,1)} %copy-done.8, bf16[432,384]{1,0:T(8,128)(2,1)} %refs_1_.3), custom_call_target="tpu_custom_call" | custom-call | tf_op jit(solution)/shard_map/front/pallas_call | solution.py:126
  28.4 1.6 reduce_max.18
  30.6 10.2 %front.3 = (bf16[27,384,1024]{2,1,0:T(8,128)(2,1)}, f32[384,128]{1,0:T(8,128)}) custom-call(bf16[16,1536]{1,0:T(8,128)(2,1)} %copy-done.10, bf16[432,384]{1,0:T(8,128)(2,1)} %refs_1_.3), custom_call_target="tpu_custom_call" | custom-call | tf_op jit(solution)/shard_map/front/pallas_call | solution.py:126
  40.7 1.7 reduce_max.19
  42.4 22.8 %all-gather.2.cloned.1.call-done = bf16[10368,384]{1,0:T(8,128)(2,1)} async-done(((bf16[1296,384]{1,0:T(8,128)(2,1)}), bf16[10368,384]{1,0:T(8,128)(2,1)}) %all-gather.2.cloned.1.call-update) | async-done | bytes 7962640 | tf_op jit(solution)/shard_map/all_gather | solution.py:394
  65.2 16.7 %middle.1 = (bf16[1040,384]{1,0:T(8,128)(2,1)}, bf16[256,384]{1,0:T(8,128)(2,1)}) custom-call(bf16[3,10,10,16,384]{4,3,2,1,0:T(8,128)(2,1)} %get-tuple-element.45.refs_0_, bf16[27,384,384]{2,1,0:T(8,128)(2,1)} %bitcast.46, bf16[1024,384]{1,0:T(8,128)(2,1)} %bitcast.48), custom_call_target="tpu_custom_call" | custom-call | tf_op jit(solution)/shard_map/middle/pallas_call | solution.py:171
  82.8 1.5 collective-permute-start.3
  88.2 13.7 %grad.2 = (f32[912,384]{1,0:T(8,128)}, f32[4,912,384]{2,1,0:T(8,128)}) custom-call(s32[4]{0:T(128)} %fusion.26.refs_0_, bf16[10368,1024]{1,0:T(8,128)(2,1)} %bitcast.38, bf16[10368,1024]{1,0:T(8,128)(2,1)} %bitcast.42, bf16[10368,1024]{1,0:T(8,128)(2,1)} %bitcast.39, bf16[10368,1024]{1,0:T(8,128)(2,1)} %bitcast.43, ...), custom_call_target="tpu_custom_call" | custom-call | tf_op jit(solution)/shard_map/grad/pallas_call | solution.py:228
  104.5 4.1 %fusion = (f16[912,384]{1,0:T(8,128)(2,1)}, f16[912,384]{1,0:T(8,128)(2,1)}, f16[912,384]{1,0:T(8,128)(2,1)}) fusion(f32[4,912,384]{2,1,0:T(8,128)} %get-tuple-element.51, f32[]{:T(128)} %bitcast.10, f32[]{:T(128)} %bitcast.8, pred[912]{0:T(1024)(128)(4,1)S(1)} %iota_compare_fusion.1), kind=kLoop, calls=%fused_computation.2 | loop fusion | flops 3151872 | bytes 6304664 | tf_op jit(solution)/shard_map/convert_element_type | solution.py:307
  108.5 1.5 collective-permute-start.4
  110.5 1.5 collective-permute-start.6
  112.0 8.8 %grad.3 = (f32[464,384]{1,0:T(8,128)}, f32[4,464,384]{2,1,0:T(8,128)}) custom-call(s32[4]{0:T(128)} %fusion.25.refs_0_, bf16[10368,1024]{1,0:T(8,128)(2,1)} %bitcast.40, bf16[10368,1024]{1,0:T(8,128)(2,1)} %bitcast.44, bf16[10368,1024]{1,0:T(8,128)(2,1)} %bitcast.41, bf16[10368,1024]{1,0:T(8,128)(2,1)} %bitcast.45, ...), custom_call_target="tpu_custom_call" | custom-call | tf_op jit(solution)/shard_map/grad/pallas_call | solution.py:228
  120.8 3.3 %select_convert_fusion = f16[4,464,384]{2,1,0:T(8,128)(2,1)} fusion(f32[4,464,384]{2,1,0:T(8,128)} %get-tuple-element.58, f32[]{:T(128)} %bitcast.10, f32[]{:T(128)} %bitcast.8, pred[464]{0:T(512)(128)(4,1)S(1)} %iota_compare_fusion.2), kind=kLoop, calls=%fused_computation | loop fusion | flops 2138112 | bytes 4276696 | tf_op jit(solution)/shard_map/convert_element_type | solution.py:307
  124.2 3.5 %all-to-all-start = ((f16[4,464,384]{2,1,0:T(8,128)(2,1)}), f16[4,464,384]{2,1,0:T(8,128)(2,1)S(1)}, u32[]{:S(2)}, u32[]{:S(2)}) async-start(f16[4,464,384]{2,1,0:T(8,128)(2,1)} %select_convert_fusion), calls=%async_computation | async-start | bytes 2850816 | tf_op jit(solution)/shard_map/all_to_all | solution.py:424
  128.9 17.5 %back.1 = f32[432,384]{1,0:T(8,128)} custom-call(bf16[1040,384]{1,0:T(8,128)(2,1)} %get-tuple-element.59.refs_5_.refs_0_, bf16[256,384]{1,0:T(8,128)(2,1)} %copy-done.9, bf16[27,384,384]{2,1,0:T(8,128)(2,1)} %bitcast.47, f32[1024,384]{1,0:T(8,128)} %get-tuple-element.61.refs_3_, bf16[432,1024]{1,0:T(8,128)(2,1)} %get-tuple-element.62.refs_4_), custom_call_target="tpu_custom_call" | custom-call | tf_op jit(solution)/shard_map/back/pallas_call | solution.py:283
  146.4 4.5 %collective-permute-done.5 = f16[912,384]{1,0:T(8,128)(2,1)S(1)} collective-permute-done((f16[912,384]{1,0:T(8,128)(2,1)}, f16[912,384]{1,0:T(8,128)(2,1)S(1)}, u32[]{:S(2)}, u32[]{:S(2)}) %collective-permute-start.5) | collective-permute-done | bytes 700448 | tf_op jit(solution)/shard_map/ppermute | solution.py:317
  152.8 2.4 collective-permute-start.7
  155.1 2.4 %collective-permute-start.8 = (f16[240,384]{1,0:T(8,128)(2,1)}, f16[240,384]{1,0:T(8,128)(2,1)}, u32[]{:S(2)}, u32[]{:S(2)}) collective-permute-start(f16[240,384]{1,0:T(8,128)(2,1)} %get-tuple-element.87), channel_id=1, source_target_pairs={{0,2},{1,3},{2,0},{3,1},{4,6},{5,7},{6,4},{7,5},{8,10},{9,11},{10,... | collective-permute-start | bytes 552968 | tf_op jit(solution)/shard_map/ppermute | solution.py:327
  157.5 1.4 collective-permute-start.9
  161.3 3.5 %all-to-all-start.1 = ((f32[8,54,384]{2,1,0:T(8,128)}), f32[8,54,384]{2,1,0:T(8,128)S(1)}, u32[]{:S(2)}, u32[]{:S(2)}) async-start(f32[8,54,384]{2,1,0:T(8,128)} %reshape.40), calls=%async_computation.1 | async-start | bytes 1376256 | tf_op jit(solution)/shard_map/all_to_all | solution.py:433
  164.8 2.1 collective-permute-done.8
  167.8 1.6 fusion.6
  169.4 2.6 %collective-permute-start.10 = (f16[128,384]{1,0:T(8,128)(2,1)S(1)}, f16[128,384]{1,0:T(8,128)(2,1)S(1)}, u32[]{:S(2)}, u32[]{:S(2)}) collective-permute-start(f16[128,384]{1,0:T(8,128)(2,1)S(1)} %get-tuple-element.91), channel_id=1, source_target_pairs={{0,1},{1,2},{2,3},{3,0},{4,5},{5,6},{6,7},{7,4},{8,9},{9,10},{10,1... | collective-permute-start | bytes 294920 | tf_op jit(solution)/shard_map/ppermute | solution.py:327
  172.0 1.7 collective-permute-start.11
  174.4 1.8 all-to-all-done.1
  177.1 4.6 %all-to-all-start.2 = ((f32[4,54,384]{2,1,0:T(8,128)}), f32[4,54,384]{2,1,0:T(8,128)S(1)}, u32[]{:S(2)}, u32[]{:S(2)}) async-start(f32[4,54,384]{2,1,0:T(8,128)} %broadcast_in_dim.83), calls=%async_computation.2 | async-start | bytes 688128 | tf_op jit(solution)/shard_map/all_to_all | solution.py:440
  181.9 3.9 %collective-permute-start.15 = (f16[352,384]{1,0:T(8,128)(2,1)S(1)}, f16[352,384]{1,0:T(8,128)(2,1)S(1)}, u32[]{:S(2)}, u32[]{:S(2)}) collective-permute-start(f16[352,384]{1,0:T(8,128)(2,1)S(1)} %fusion.5), channel_id=1, source_target_pairs={{0,3},{1,0},{2,1},{3,2},{4,7},{5,4},{6,5},{7,6},{8,11},{9,8},{10,9... | collective-permute-start | bytes 811016 | tf_op jit(solution)/shard_map/ppermute | solution.py:327
  186.9 7.2 %collective-permute-done.15 = f16[352,384]{1,0:T(8,128)(2,1)S(1)} collective-permute-done((f16[352,384]{1,0:T(8,128)(2,1)S(1)}, f16[352,384]{1,0:T(8,128)(2,1)S(1)}, u32[]{:S(2)}, u32[]{:S(2)}) %collective-permute-start.15) | collective-permute-done | bytes 270368 | tf_op jit(solution)/shard_map/ppermute | solution.py:327
  194.2 18.4 %collective-permute-done.14 = f16[352,384]{1,0:T(8,128)(2,1)S(1)} collective-permute-done((f16[352,384]{1,0:T(8,128)(2,1)S(1)}, f16[352,384]{1,0:T(8,128)(2,1)S(1)}, u32[]{:S(2)}, u32[]{:S(2)}) %collective-permute-start.14) | collective-permute-done | bytes 270368 | tf_op jit(solution)/shard_map/ppermute | solution.py:327
  213.5 4.9 %all-to-all-start.3 = ((f32[8,54,384]{2,1,0:T(8,128)}), f32[8,54,384]{2,1,0:T(8,128)S(1)}, u32[]{:S(2)}, u32[]{:S(2)}) async-start(f32[8,54,384]{2,1,0:T(8,128)} %broadcast_in_dim.86), calls=%async_computation.3 | async-start | bytes 1376256 | tf_op jit(solution)/shard_map/all_to_all | solution.py:445
  224.8 5.1 %all-to-all-done.3 = f32[8,54,384]{2,1,0:T(8,128)S(1)} async-done(((f32[8,54,384]{2,1,0:T(8,128)}), f32[8,54,384]{2,1,0:T(8,128)S(1)}, u32[]{:S(2)}, u32[]{:S(2)}) %all-to-all-start.3) | async-done | bytes 663584 | tf_op jit(solution)/shard_map/all_to_all | solution.py:445
  (94 shorter events, 26.4 us)
Async XLA Ops:
  7.2 1.4 copy-start
  7.2 58.0 %all-gather.2.cloned.1.call-start = ((), (), s32[]{:S(2)}) async-start(), calls=%async_computation.4 | async-start | bytes 8957952 | tf_op jit(solution)/shard_map/all_gather | solution.py:394
  9.1 6.4 %collective-permute-start = (bf16[16,512]{1,0:T(8,128)(2,1)S(1)}, bf16[16,512]{1,0:T(8,128)(2,1)S(1)}, u32[]{:S(2)}, u32[]{:S(2)}) collective-permute-start(bf16[16,512]{1,0:T(8,128)(2,1)S(1)} %slice.160), channel_id=1, source_target_pairs={{0,1},{1,2},{2,3},{4,5},{5,6},{6,7},{8,9},{9,10},{10,11},{12,13},{... | collective-permute-start | bytes 49160 | tf_op jit(solution)/shard_map/ppermute | solution.py:19
  15.5 14.5 %collective-permute-start.1 = (bf16[16,1536]{1,0:T(8,128)(2,1)S(1)}, bf16[16,1536]{1,0:T(8,128)(2,1)S(1)}, u32[]{:S(2)}, u32[]{:S(2)}) collective-permute-start(bf16[16,1536]{1,0:T(8,128)(2,1)S(1)} %pad_maximum_fusion.refs_0_), channel_id=1, source_target_pairs={{0,4},{4,0},{8,12},{12,8},{16,20},{20,16},{24,28},{28,24},{1,5},{5... | collective-permute-start | bytes 147464 | tf_op jit(solution)/shard_map/ppermute | solution.py:23
  82.0 5.4 %collective-permute-start.2 = (bf16[1040,384]{1,0:T(8,128)(2,1)}, bf16[1040,384]{1,0:T(8,128)(2,1)S(1)}, u32[]{:S(2)}, u32[]{:S(2)}) collective-permute-start(bf16[1040,384]{1,0:T(8,128)(2,1)} %get-tuple-element.59.refs_5_.refs_0_), channel_id=1, source_target_pairs={{0,4},{4,0},{8,12},{12,8},{16,20},{20,16},{24,28},{28,24},{1,5},{5... | collective-permute-start | bytes 2396168 | tf_op jit(solution)/shard_map/ppermute | solution.py:23
  82.8 19.1 %collective-permute-start.3 = (bf16[256,384]{1,0:T(8,128)(2,1)}, bf16[256,384]{1,0:T(8,128)(2,1)S(1)}, u32[]{:S(2)}, u32[]{:S(2)}) collective-permute-start(bf16[256,384]{1,0:T(8,128)(2,1)} %get-tuple-element.50), channel_id=1, source_target_pairs={{1,0},{2,1},{3,2},{5,4},{6,5},{7,6},{9,8},{10,9},{11,10},{13,12},{... | collective-permute-start | bytes 589832 | tf_op jit(solution)/shard_map/ppermute | solution.py:19
  101.9 6.6 %copy-start.9 = (bf16[256,384]{1,0:T(8,128)(2,1)}, bf16[256,384]{1,0:T(8,128)(2,1)S(1)}, u32[]{:S(2)}) copy-start(bf16[256,384]{1,0:T(8,128)(2,1)S(1)} %collective-permute-done.3.refs_1_) | copy-start | bytes 589828
  108.5 37.9 %collective-permute-start.4 = (f16[912,384]{1,0:T(8,128)(2,1)}, f16[912,384]{1,0:T(8,128)(2,1)S(1)}, u32[]{:S(2)}, u32[]{:S(2)}) collective-permute-start(f16[912,384]{1,0:T(8,128)(2,1)} %get-tuple-element.54), channel_id=1, source_target_pairs={{0,8},{4,12},{8,0},{12,4},{16,24},{20,28},{24,16},{28,20},{1,9},{5... | collective-permute-start | bytes 2101256 | tf_op jit(solution)/shard_map/ppermute | solution.py:317
  110.0 40.9 %collective-permute-start.5 = (f16[912,384]{1,0:T(8,128)(2,1)}, f16[912,384]{1,0:T(8,128)(2,1)S(1)}, u32[]{:S(2)}, u32[]{:S(2)}) collective-permute-start(f16[912,384]{1,0:T(8,128)(2,1)} %get-tuple-element.55), channel_id=1, source_target_pairs={{0,16},{4,20},{8,24},{12,28},{16,0},{20,4},{24,8},{28,12},{1,17},{... | collective-permute-start | bytes 2101256 | tf_op jit(solution)/shard_map/ppermute | solution.py:317
  110.5 40.3 %collective-permute-start.6 = (f16[912,384]{1,0:T(8,128)(2,1)}, f16[912,384]{1,0:T(8,128)(2,1)S(1)}, u32[]{:S(2)}, u32[]{:S(2)}) collective-permute-start(f16[912,384]{1,0:T(8,128)(2,1)} %get-tuple-element.56), channel_id=1, source_target_pairs={{0,24},{4,28},{8,16},{12,20},{16,8},{20,12},{24,0},{28,4},{1,25},{... | collective-permute-start | bytes 2101256 | tf_op jit(solution)/shard_map/ppermute | solution.py:317
  124.2 34.8 %all-to-all-start = ((f16[4,464,384]{2,1,0:T(8,128)(2,1)}), f16[4,464,384]{2,1,0:T(8,128)(2,1)S(1)}, u32[]{:S(2)}, u32[]{:S(2)}) async-start(f16[4,464,384]{2,1,0:T(8,128)(2,1)} %select_convert_fusion), calls=%async_computation | async-start | bytes 2850816 | tf_op jit(solution)/shard_map/all_to_all | solution.py:424
  128.9 22.6 %copy-start.4 = (f32[912,384]{1,0:T(8,128)S(1)}, f32[912,384]{1,0:T(8,128)}, u32[]{:S(2)}) copy-start(f32[912,384]{1,0:T(8,128)} %get-tuple-element.48) | copy-start | bytes 4202500
  146.4 11.2 %copy-start.5 = (f16[912,384]{1,0:T(8,128)(2,1)}, f16[912,384]{1,0:T(8,128)(2,1)S(1)}, u32[]{:S(2)}) copy-start(f16[912,384]{1,0:T(8,128)(2,1)S(1)} %collective-permute-done.4) | copy-start | bytes 2101252
  150.9 8.1 %copy-start.6 = (f16[912,384]{1,0:T(8,128)(2,1)}, f16[912,384]{1,0:T(8,128)(2,1)S(1)}, u32[]{:S(2)}) copy-start(f16[912,384]{1,0:T(8,128)(2,1)S(1)} %collective-permute-done.5) | copy-start | bytes 2101252
  150.9 8.1 %copy-start.7 = (f16[912,384]{1,0:T(8,128)(2,1)}, f16[912,384]{1,0:T(8,128)(2,1)S(1)}, u32[]{:S(2)}) copy-start(f16[912,384]{1,0:T(8,128)(2,1)S(1)} %collective-permute-done.6) | copy-start | bytes 2101252
  151.5 7.8 %copy-start.11 = (f32[384]{0:T(512)}, f32[384]{0:T(512)S(1)}, u32[]{:S(2)}) copy-start(f32[384]{0:T(512)S(1)} %get-tuple-element.81) | copy-start | bytes 4612
  152.8 12.1 %collective-permute-start.7 = (f16[240,384]{1,0:T(8,128)(2,1)}, f16[240,384]{1,0:T(8,128)(2,1)}, u32[]{:S(2)}, u32[]{:S(2)}) collective-permute-start(f16[240,384]{1,0:T(8,128)(2,1)} %get-tuple-element.88), channel_id=1, source_target_pairs={{0,1},{1,2},{2,3},{3,0},{4,5},{5,6},{6,7},{7,4},{8,9},{9,10},{10,1... | collective-permute-start | bytes 552968 | tf_op jit(solution)/shard_map/ppermute | solution.py:327
  155.1 11.9 %collective-permute-start.8 = (f16[240,384]{1,0:T(8,128)(2,1)}, f16[240,384]{1,0:T(8,128)(2,1)}, u32[]{:S(2)}, u32[]{:S(2)}) collective-permute-start(f16[240,384]{1,0:T(8,128)(2,1)} %get-tuple-element.87), channel_id=1, source_target_pairs={{0,2},{1,3},{2,0},{3,1},{4,6},{5,7},{6,4},{7,5},{8,10},{9,11},{10,... | collective-permute-start | bytes 552968 | tf_op jit(solution)/shard_map/ppermute | solution.py:327
  157.5 2.8 %copy-start.3 = (f32[432,384]{1,0:T(8,128)S(1)}, f32[432,384]{1,0:T(8,128)}, u32[]{:S(2)}) copy-start(f32[432,384]{1,0:T(8,128)} %back.1) | copy-start | bytes 1990660
  157.5 9.5 %collective-permute-start.9 = (f16[240,384]{1,0:T(8,128)(2,1)}, f16[240,384]{1,0:T(8,128)(2,1)}, u32[]{:S(2)}, u32[]{:S(2)}) collective-permute-start(f16[240,384]{1,0:T(8,128)(2,1)} %get-tuple-element.86), channel_id=1, source_target_pairs={{0,3},{1,0},{2,1},{3,2},{4,7},{5,4},{6,5},{7,6},{8,11},{9,8},{10,9... | collective-permute-start | bytes 552968 | tf_op jit(solution)/shard_map/ppermute | solution.py:327
  159.3 7.7 %copy-start.12 = (f32[1,384]{1,0:T(1,128)S(1)}, f32[1,384]{1,0:T(1,128)}, u32[]{:S(2)}) copy-start(f32[1,384]{1,0:T(1,128)} %get-tuple-element.82) | copy-start | bytes 4612
  161.3 15.0 %all-to-all-start.1 = ((f32[8,54,384]{2,1,0:T(8,128)}), f32[8,54,384]{2,1,0:T(8,128)S(1)}, u32[]{:S(2)}, u32[]{:S(2)}) async-start(f32[8,54,384]{2,1,0:T(8,128)} %reshape.40), calls=%async_computation.1 | async-start | bytes 1376256 | tf_op jit(solution)/shard_map/all_to_all | solution.py:433
  167.8 14.0 %copy-start.13 = (pred[352]{0:T(512)(128)(4,1)S(1)}, pred[352]{0:T(512)(128)(4,1)}, u32[]{:S(2)}) copy-start(pred[352]{0:T(512)(128)(4,1)} %iota_compare_fusion.3) | copy-start | bytes 1060
  169.4 12.2 %collective-permute-start.10 = (f16[128,384]{1,0:T(8,128)(2,1)S(1)}, f16[128,384]{1,0:T(8,128)(2,1)S(1)}, u32[]{:S(2)}, u32[]{:S(2)}) collective-permute-start(f16[128,384]{1,0:T(8,128)(2,1)S(1)} %get-tuple-element.91), channel_id=1, source_target_pairs={{0,1},{1,2},{2,3},{3,0},{4,5},{5,6},{6,7},{7,4},{8,9},{9,10},{10,1... | collective-permute-start | bytes 294920 | tf_op jit(solution)/shard_map/ppermute | solution.py:327
  172.0 9.7 %collective-permute-start.11 = (f16[128,384]{1,0:T(8,128)(2,1)S(1)}, f16[128,384]{1,0:T(8,128)(2,1)S(1)}, u32[]{:S(2)}, u32[]{:S(2)}) collective-permute-start(f16[128,384]{1,0:T(8,128)(2,1)S(1)} %get-tuple-element.90), channel_id=1, source_target_pairs={{0,2},{1,3},{2,0},{3,1},{4,6},{5,7},{6,4},{7,5},{8,10},{9,11},{10,... | collective-permute-start | bytes 294920 | tf_op jit(solution)/shard_map/ppermute | solution.py:327
  173.7 8.0 %collective-permute-start.12 = (f16[128,384]{1,0:T(8,128)(2,1)S(1)}, f16[128,384]{1,0:T(8,128)(2,1)S(1)}, u32[]{:S(2)}, u32[]{:S(2)}) collective-permute-start(f16[128,384]{1,0:T(8,128)(2,1)S(1)} %get-tuple-element.89), channel_id=1, source_target_pairs={{0,3},{1,0},{2,1},{3,2},{4,7},{5,4},{6,5},{7,6},{8,11},{9,8},{10,9... | collective-permute-start | bytes 294920 | tf_op jit(solution)/shard_map/ppermute | solution.py:327
  177.1 35.5 %all-to-all-start.2 = ((f32[4,54,384]{2,1,0:T(8,128)}), f32[4,54,384]{2,1,0:T(8,128)S(1)}, u32[]{:S(2)}, u32[]{:S(2)}) async-start(f32[4,54,384]{2,1,0:T(8,128)} %broadcast_in_dim.83), calls=%async_computation.2 | async-start | bytes 688128 | tf_op jit(solution)/shard_map/all_to_all | solution.py:440
  181.9 12.3 %collective-permute-start.15 = (f16[352,384]{1,0:T(8,128)(2,1)S(1)}, f16[352,384]{1,0:T(8,128)(2,1)S(1)}, u32[]{:S(2)}, u32[]{:S(2)}) collective-permute-start(f16[352,384]{1,0:T(8,128)(2,1)S(1)} %fusion.5), channel_id=1, source_target_pairs={{0,3},{1,0},{2,1},{3,2},{4,7},{5,4},{6,5},{7,6},{8,11},{9,8},{10,9... | collective-permute-start | bytes 811016 | tf_op jit(solution)/shard_map/ppermute | solution.py:327
  185.8 26.8 %collective-permute-start.14 = (f16[352,384]{1,0:T(8,128)(2,1)S(1)}, f16[352,384]{1,0:T(8,128)(2,1)S(1)}, u32[]{:S(2)}, u32[]{:S(2)}) collective-permute-start(f16[352,384]{1,0:T(8,128)(2,1)S(1)} %fusion.5), channel_id=1, source_target_pairs={{0,2},{1,3},{2,0},{3,1},{4,6},{5,7},{6,4},{7,5},{8,10},{9,11},{10,... | collective-permute-start | bytes 811016 | tf_op jit(solution)/shard_map/ppermute | solution.py:327
  185.8 32.7 %collective-permute-start.13 = (f16[352,384]{1,0:T(8,128)(2,1)S(1)}, f16[352,384]{1,0:T(8,128)(2,1)S(1)}, u32[]{:S(2)}, u32[]{:S(2)}) collective-permute-start(f16[352,384]{1,0:T(8,128)(2,1)S(1)} %fusion.5), channel_id=1, source_target_pairs={{0,1},{1,2},{2,3},{3,0},{4,5},{5,6},{6,7},{7,4},{8,9},{9,10},{10,1... | collective-permute-start | bytes 811016 | tf_op jit(solution)/shard_map/ppermute | solution.py:327
  213.5 16.4 %all-to-all-start.3 = ((f32[8,54,384]{2,1,0:T(8,128)}), f32[8,54,384]{2,1,0:T(8,128)S(1)}, u32[]{:S(2)}, u32[]{:S(2)}) async-start(f32[8,54,384]{2,1,0:T(8,128)} %broadcast_in_dim.86), calls=%async_computation.3 | async-start | bytes 1376256 | tf_op jit(solution)/shard_map/all_to_all | solution.py:445
  219.9 11.0 %copy-start.1 = (bf16[1,8,8,32,16]{3,4,2,1,0:T(8,128)(2,1)S(1)}, bf16[1,8,8,32,16]{3,4,2,1,0:T(8,128)(2,1)}, u32[]{:S(2)}) copy-start(bf16[1,8,8,32,16]{3,4,2,1,0:T(8,128)(2,1)} %param.5) | copy-start | bytes 196612
  (3 other events, 2.1 us)
Sparse Core Ops, SparseCore 0:
  9.9 55.2 all-gather.1

commit v8 on v7

--- a/solution.py
+++ b/solution.py
@@ -441,7 +441,7 @@
     last = spread([(own_a, depth_a), (own_b, depth_b)], smalls, factors, total)
     in_sum = behind(in_got, last[0]).sum(axis=0)
     in_sum = jnp.broadcast_to(in_sum[None], (clips,) + in_sum.shape)
-    last[-1] = behind(last[-1], in_sum)
+    last[1:] = behind(last[1:], in_sum)
     grad_in = lax.all_to_all(in_sum, "clip", 0, 0, tiled=True).reshape(in_rows, chans)
     factors, _ = scales(last, sum(smalls), 0.0)
     pieces = assembled(last, factors, smalls, [2 * third, third])

time: 239 us -> 228 us (0.954)
  waiting for transfers between devices: 64.2 us -> 54.6 us
    ppermute x9, waiting for transfers between devices: 27.8 us -> 16.4 us  [around(): lax.ppermute(blocks, 'tm', [(i, (i + distance) % depth) for i in range(de...]
    all_to_all x1, waiting for transfers between devices: 0.01 us -> 6.89 us  [shards(): in_got = lax.all_to_all(in_sum, 'tm', 0, 0, tiled=True)]
    all_to_all x1, waiting for transfers between devices: 5.12 us -> 0.01 us  [shards(): lax.all_to_all(in_sum, 'clip', 0, 0, tiled=True).reshape(in_rows, chans)]
  transfers between devices with their start and end apart: 21 -> 21, of which waited for: 8 -> 7; matrix products, arithmetic and copies ran while one was open for 11% -> 11% of each run, Pallas kernels for 26% -> 28%
where the time goes in v8:
time: 228 us; the launch traced here: 227 us
  Pallas kernels  79.1 us (35%)
  waiting for transfers between devices  54.6 us (24%)
  starting transfers between devices  41.6 us (18%)
  other arithmetic  19.2 us (8%)
  between operations  17.7 us (8%)
  local copies, waits for them, and re-layouts  14.6 us (6%)
    all_gather x1, waiting for transfers between devices, shards(): w_full = lax.all_gather(w_mid, 'clip', axis=0, tiled=True)  22.8 us
    pallas_call x2, Pallas kernels, grad_chunk(): pl.pallas_call(lambda *refs: grad_kernel(*refs, units=units), grid_spec=p...  22.5 us
    pallas_call x2, Pallas kernels, front(): pl.pallas_call(lambda *refs: front_kernel(*refs, rows=rows, cols=cols, fi...  22.4 us
    pallas_call x1, Pallas kernels, back(): pl.pallas_call(lambda *refs: back_kernel(*refs, rows=rows, cols=cols), gr...  17.5 us
    pallas_call x1, Pallas kernels, middle(): pl.pallas_call(lambda *refs: middle_kernel(*refs, scale=scale), grid=(3,)...  16.7 us
    ppermute x9, waiting for transfers between devices, around(): lax.ppermute(blocks, 'tm', [(i, (i + distance) % depth) for i in range(de...  16.4 us
    ppermute x9, starting transfers between devices, around(): lax.ppermute(blocks, 'tm', [(i, (i + distance) % depth) for i in range(de...  16.2 us
    convert_element_type x5, other arithmetic, packed(): return jnp.where(row < rows, x * jnp.exp2(14.0 - power), power).astype(F16)  9.72 us
  transfers between devices with their start and end apart: 21, of which 7 were waited for; matrix products, arithmetic and copies ran while one was open for 11% of the time, Pallas kernels for 28%

profile of v8, /device:TPU:0, one launch (start us, length us, event | category | flops | bytes accessed | tf_op | source)
XLA Modules:
  0.0 226.8 jit_solution(2659212858326838746)
XLA Ops:
  9.1 4.9 %collective-permute-start = (bf16[16,512]{1,0:T(8,128)(2,1)S(1)}, bf16[16,512]{1,0:T(8,128)(2,1)S(1)}, u32[]{:S(2)}, u32[]{:S(2)}) collective-permute-start(bf16[16,512]{1,0:T(8,128)(2,1)S(1)} %slice.160), channel_id=1, source_target_pairs={{0,1},{1,2},{2,3},{4,5},{5,6},{6,7},{8,9},{9,10},{10,11},{12,13},{... | collective-permute-start | bytes 49160 | tf_op jit(solution)/shard_map/ppermute | solution.py:19
  14.1 1.4 collective-permute-done
  16.1 12.2 %front.2 = (bf16[432,1024]{1,0:T(8,128)(2,1)}, f32[1024,384]{1,0:T(8,128)}, bf16[3,10,10,16,384]{4,3,2,1,0:T(8,128)(2,1)}, bf16[27,384,1024]{2,1,0:T(8,128)(2,1)}, f32[384,128]{1,0:T(8,128)}) custom-call(bf16[16,1536]{1,0:T(8,128)(2,1)} %copy-done.8, bf16[432,384]{1,0:T(8,128)(2,1)} %refs_1_.3), custom_call_target="tpu_custom_call" | custom-call | tf_op jit(solution)/shard_map/front/pallas_call | solution.py:126
  28.4 1.6 reduce_max.18
  30.6 10.2 %front.3 = (bf16[27,384,1024]{2,1,0:T(8,128)(2,1)}, f32[384,128]{1,0:T(8,128)}) custom-call(bf16[16,1536]{1,0:T(8,128)(2,1)} %copy-done.10, bf16[432,384]{1,0:T(8,128)(2,1)} %refs_1_.3), custom_call_target="tpu_custom_call" | custom-call | tf_op jit(solution)/shard_map/front/pallas_call | solution.py:126
  40.7 1.7 reduce_max.19
  42.4 22.8 %all-gather.2.cloned.1.call-done = bf16[10368,384]{1,0:T(8,128)(2,1)} async-done(((bf16[1296,384]{1,0:T(8,128)(2,1)}), bf16[10368,384]{1,0:T(8,128)(2,1)}) %all-gather.2.cloned.1.call-update) | async-done | bytes 7962640 | tf_op jit(solution)/shard_map/all_gather | solution.py:394
  65.2 16.7 %middle.1 = (bf16[1040,384]{1,0:T(8,128)(2,1)}, bf16[256,384]{1,0:T(8,128)(2,1)}) custom-call(bf16[3,10,10,16,384]{4,3,2,1,0:T(8,128)(2,1)} %get-tuple-element.47.refs_0_, bf16[27,384,384]{2,1,0:T(8,128)(2,1)} %bitcast.46, bf16[1024,384]{1,0:T(8,128)(2,1)} %bitcast.48), custom_call_target="tpu_custom_call" | custom-call | tf_op jit(solution)/shard_map/middle/pallas_call | solution.py:171
  82.8 1.5 collective-permute-start.3
  88.2 13.7 %grad.2 = (f32[912,384]{1,0:T(8,128)}, f32[4,912,384]{2,1,0:T(8,128)}) custom-call(s32[4]{0:T(128)} %fusion.18.refs_0_, bf16[10368,1024]{1,0:T(8,128)(2,1)} %bitcast.38, bf16[10368,1024]{1,0:T(8,128)(2,1)} %bitcast.42, bf16[10368,1024]{1,0:T(8,128)(2,1)} %bitcast.39, bf16[10368,1024]{1,0:T(8,128)(2,1)} %bitcast.43, ...), custom_call_target="tpu_custom_call" | custom-call | tf_op jit(solution)/shard_map/grad/pallas_call | solution.py:228
  104.5 4.1 %fusion = (f16[912,384]{1,0:T(8,128)(2,1)}, f16[912,384]{1,0:T(8,128)(2,1)}, f16[912,384]{1,0:T(8,128)(2,1)}) fusion(f32[4,912,384]{2,1,0:T(8,128)} %get-tuple-element.53, f32[]{:T(128)} %bitcast.10, f32[]{:T(128)} %bitcast.8, pred[912]{0:T(1024)(128)(4,1)S(1)} %iota_compare_fusion.1), kind=kLoop, calls=%fused_computation.2 | loop fusion | flops 3151872 | bytes 6304664 | tf_op jit(solution)/shard_map/convert_element_type | solution.py:307
  108.5 1.5 collective-permute-start.4
  110.5 1.5 collective-permute-start.6
  112.0 8.8 %grad.3 = (f32[464,384]{1,0:T(8,128)}, f32[4,464,384]{2,1,0:T(8,128)}) custom-call(s32[4]{0:T(128)} %fusion.17.refs_0_, bf16[10368,1024]{1,0:T(8,128)(2,1)} %bitcast.40, bf16[10368,1024]{1,0:T(8,128)(2,1)} %bitcast.44, bf16[10368,1024]{1,0:T(8,128)(2,1)} %bitcast.41, bf16[10368,1024]{1,0:T(8,128)(2,1)} %bitcast.45, ...), custom_call_target="tpu_custom_call" | custom-call | tf_op jit(solution)/shard_map/grad/pallas_call | solution.py:228
  120.8 3.3 %select_convert_fusion = f16[4,464,384]{2,1,0:T(8,128)(2,1)} fusion(f32[4,464,384]{2,1,0:T(8,128)} %get-tuple-element.60, f32[]{:T(128)} %bitcast.10, f32[]{:T(128)} %bitcast.8, pred[464]{0:T(512)(128)(4,1)S(1)} %iota_compare_fusion.2), kind=kLoop, calls=%fused_computation | loop fusion | flops 2138112 | bytes 4276696 | tf_op jit(solution)/shard_map/convert_element_type | solution.py:307
  124.2 3.5 %all-to-all-start = ((f16[4,464,384]{2,1,0:T(8,128)(2,1)}), f16[4,464,384]{2,1,0:T(8,128)(2,1)S(1)}, u32[]{:S(2)}, u32[]{:S(2)}) async-start(f16[4,464,384]{2,1,0:T(8,128)(2,1)} %select_convert_fusion), calls=%async_computation | async-start | bytes 2850816 | tf_op jit(solution)/shard_map/all_to_all | solution.py:424
  128.9 17.5 %back.1 = f32[432,384]{1,0:T(8,128)} custom-call(bf16[1040,384]{1,0:T(8,128)(2,1)} %get-tuple-element.61.refs_5_.refs_0_, bf16[256,384]{1,0:T(8,128)(2,1)} %copy-done.9, bf16[27,384,384]{2,1,0:T(8,128)(2,1)} %bitcast.47, f32[1024,384]{1,0:T(8,128)} %get-tuple-element.63.refs_3_, bf16[432,1024]{1,0:T(8,128)(2,1)} %get-tuple-element.64.refs_4_), custom_call_target="tpu_custom_call" | custom-call | tf_op jit(solution)/shard_map/back/pallas_call | solution.py:283
  146.4 4.5 %collective-permute-done.5 = f16[912,384]{1,0:T(8,128)(2,1)S(1)} collective-permute-done((f16[912,384]{1,0:T(8,128)(2,1)}, f16[912,384]{1,0:T(8,128)(2,1)S(1)}, u32[]{:S(2)}, u32[]{:S(2)}) %collective-permute-start.5) | collective-permute-done | bytes 700448 | tf_op jit(solution)/shard_map/ppermute | solution.py:317
  152.8 2.4 %collective-permute-start.7 = (f16[240,384]{1,0:T(8,128)(2,1)}, f16[240,384]{1,0:T(8,128)(2,1)}, u32[]{:S(2)}, u32[]{:S(2)}) collective-permute-start(f16[240,384]{1,0:T(8,128)(2,1)} %get-tuple-element.92), channel_id=1, source_target_pairs={{0,1},{1,2},{2,3},{3,0},{4,5},{5,6},{6,7},{7,4},{8,9},{9,10},{10,1... | collective-permute-start | bytes 552968 | tf_op jit(solution)/shard_map/ppermute | solution.py:327
  155.1 2.4 %collective-permute-start.8 = (f16[240,384]{1,0:T(8,128)(2,1)}, f16[240,384]{1,0:T(8,128)(2,1)}, u32[]{:S(2)}, u32[]{:S(2)}) collective-permute-start(f16[240,384]{1,0:T(8,128)(2,1)} %get-tuple-element.91), channel_id=1, source_target_pairs={{0,2},{1,3},{2,0},{3,1},{4,6},{5,7},{6,4},{7,5},{8,10},{9,11},{10,... | collective-permute-start | bytes 552968 | tf_op jit(solution)/shard_map/ppermute | solution.py:327
  157.5 1.4 collective-permute-start.9
  161.3 3.5 %all-to-all-start.1 = ((f32[8,54,384]{2,1,0:T(8,128)}), f32[8,54,384]{2,1,0:T(8,128)S(1)}, u32[]{:S(2)}, u32[]{:S(2)}) async-start(f32[8,54,384]{2,1,0:T(8,128)} %reshape.40), calls=%async_computation.1 | async-start | bytes 1376256 | tf_op jit(solution)/shard_map/all_to_all | solution.py:433
  164.8 2.1 collective-permute-done.8
  167.8 1.6 fusion.6
  169.4 2.6 %collective-permute-start.10 = (f16[128,384]{1,0:T(8,128)(2,1)S(1)}, f16[128,384]{1,0:T(8,128)(2,1)S(1)}, u32[]{:S(2)}, u32[]{:S(2)}) collective-permute-start(f16[128,384]{1,0:T(8,128)(2,1)S(1)} %get-tuple-element.95), channel_id=1, source_target_pairs={{0,1},{1,2},{2,3},{3,0},{4,5},{5,6},{6,7},{7,4},{8,9},{9,10},{10,1... | collective-permute-start | bytes 294920 | tf_op jit(solution)/shard_map/ppermute | solution.py:327
  172.0 1.7 collective-permute-start.11
  174.4 1.8 all-to-all-done.1
  177.1 4.6 %all-to-all-start.2 = ((f32[4,54,384]{2,1,0:T(8,128)}), f32[4,54,384]{2,1,0:T(8,128)S(1)}, u32[]{:S(2)}, u32[]{:S(2)}) async-start(f32[4,54,384]{2,1,0:T(8,128)} %broadcast_in_dim.83), calls=%async_computation.2 | async-start | bytes 688128 | tf_op jit(solution)/shard_map/all_to_all | solution.py:440
  181.9 3.9 %collective-permute-start.13 = (f16[352,384]{1,0:T(8,128)(2,1)S(1)}, f16[352,384]{1,0:T(8,128)(2,1)S(1)}, u32[]{:S(2)}, u32[]{:S(2)}) collective-permute-start(f16[352,384]{1,0:T(8,128)(2,1)S(1)} %fusion.5), channel_id=1, source_target_pairs={{0,3},{1,0},{2,1},{3,2},{4,7},{5,4},{6,5},{7,6},{8,11},{9,8},{10,9... | collective-permute-start | bytes 811016 | tf_op jit(solution)/shard_map/ppermute | solution.py:327
  186.9 6.9 %all-to-all-done.2 = f32[4,54,384]{2,1,0:T(8,128)S(1)} async-done(((f32[4,54,384]{2,1,0:T(8,128)}), f32[4,54,384]{2,1,0:T(8,128)S(1)}, u32[]{:S(2)}, u32[]{:S(2)}) %all-to-all-start.2) | async-done | bytes 331808 | tf_op jit(solution)/shard_map/all_to_all | solution.py:440
  194.7 3.5 %all-to-all-start.3 = ((f32[8,54,384]{2,1,0:T(8,128)}), f32[8,54,384]{2,1,0:T(8,128)S(1)}, u32[]{:S(2)}, u32[]{:S(2)}) async-start(f32[8,54,384]{2,1,0:T(8,128)} %broadcast_in_dim.86), calls=%async_computation.3 | async-start | bytes 1376256 | tf_op jit(solution)/shard_map/all_to_all | solution.py:445
  198.3 14.3 %collective-permute-done.14 = f16[352,384]{1,0:T(8,128)(2,1)S(1)} collective-permute-done((f16[352,384]{1,0:T(8,128)(2,1)S(1)}, f16[352,384]{1,0:T(8,128)(2,1)S(1)}, u32[]{:S(2)}, u32[]{:S(2)}) %collective-permute-start.14) | collective-permute-done | bytes 270368 | tf_op jit(solution)/shard_map/ppermute | solution.py:327
  (94 shorter events, 25.0 us)
Async XLA Ops:
  7.2 1.4 copy-start
  7.2 58.0 %all-gather.2.cloned.1.call-start = ((), (), s32[]{:S(2)}) async-start(), calls=%async_computation.4 | async-start | bytes 8957952 | tf_op jit(solution)/shard_map/all_gather | solution.py:394
  9.1 6.4 %collective-permute-start = (bf16[16,512]{1,0:T(8,128)(2,1)S(1)}, bf16[16,512]{1,0:T(8,128)(2,1)S(1)}, u32[]{:S(2)}, u32[]{:S(2)}) collective-permute-start(bf16[16,512]{1,0:T(8,128)(2,1)S(1)} %slice.160), channel_id=1, source_target_pairs={{0,1},{1,2},{2,3},{4,5},{5,6},{6,7},{8,9},{9,10},{10,11},{12,13},{... | collective-permute-start | bytes 49160 | tf_op jit(solution)/shard_map/ppermute | solution.py:19
  15.5 14.5 %collective-permute-start.1 = (bf16[16,1536]{1,0:T(8,128)(2,1)S(1)}, bf16[16,1536]{1,0:T(8,128)(2,1)S(1)}, u32[]{:S(2)}, u32[]{:S(2)}) collective-permute-start(bf16[16,1536]{1,0:T(8,128)(2,1)S(1)} %pad_maximum_fusion.refs_0_), channel_id=1, source_target_pairs={{0,4},{4,0},{8,12},{12,8},{16,20},{20,16},{24,28},{28,24},{1,5},{5... | collective-permute-start | bytes 147464 | tf_op jit(solution)/shard_map/ppermute | solution.py:23
  82.0 5.4 %collective-permute-start.2 = (bf16[1040,384]{1,0:T(8,128)(2,1)}, bf16[1040,384]{1,0:T(8,128)(2,1)S(1)}, u32[]{:S(2)}, u32[]{:S(2)}) collective-permute-start(bf16[1040,384]{1,0:T(8,128)(2,1)} %get-tuple-element.61.refs_5_.refs_0_), channel_id=1, source_target_pairs={{0,4},{4,0},{8,12},{12,8},{16,20},{20,16},{24,28},{28,24},{1,5},{5... | collective-permute-start | bytes 2396168 | tf_op jit(solution)/shard_map/ppermute | solution.py:23
  82.8 19.1 %collective-permute-start.3 = (bf16[256,384]{1,0:T(8,128)(2,1)}, bf16[256,384]{1,0:T(8,128)(2,1)S(1)}, u32[]{:S(2)}, u32[]{:S(2)}) collective-permute-start(bf16[256,384]{1,0:T(8,128)(2,1)} %get-tuple-element.52), channel_id=1, source_target_pairs={{1,0},{2,1},{3,2},{5,4},{6,5},{7,6},{9,8},{10,9},{11,10},{13,12},{... | collective-permute-start | bytes 589832 | tf_op jit(solution)/shard_map/ppermute | solution.py:19
  101.9 6.6 %copy-start.9 = (bf16[256,384]{1,0:T(8,128)(2,1)}, bf16[256,384]{1,0:T(8,128)(2,1)S(1)}, u32[]{:S(2)}) copy-start(bf16[256,384]{1,0:T(8,128)(2,1)S(1)} %collective-permute-done.3.refs_1_) | copy-start | bytes 589828
  108.5 37.9 %collective-permute-start.4 = (f16[912,384]{1,0:T(8,128)(2,1)}, f16[912,384]{1,0:T(8,128)(2,1)S(1)}, u32[]{:S(2)}, u32[]{:S(2)}) collective-permute-start(f16[912,384]{1,0:T(8,128)(2,1)} %get-tuple-element.56), channel_id=1, source_target_pairs={{0,8},{4,12},{8,0},{12,4},{16,24},{20,28},{24,16},{28,20},{1,9},{5... | collective-permute-start | bytes 2101256 | tf_op jit(solution)/shard_map/ppermute | solution.py:317
  110.0 40.9 %collective-permute-start.5 = (f16[912,384]{1,0:T(8,128)(2,1)}, f16[912,384]{1,0:T(8,128)(2,1)S(1)}, u32[]{:S(2)}, u32[]{:S(2)}) collective-permute-start(f16[912,384]{1,0:T(8,128)(2,1)} %get-tuple-element.57), channel_id=1, source_target_pairs={{0,16},{4,20},{8,24},{12,28},{16,0},{20,4},{24,8},{28,12},{1,17},{... | collective-permute-start | bytes 2101256 | tf_op jit(solution)/shard_map/ppermute | solution.py:317
  110.5 40.3 %collective-permute-start.6 = (f16[912,384]{1,0:T(8,128)(2,1)}, f16[912,384]{1,0:T(8,128)(2,1)S(1)}, u32[]{:S(2)}, u32[]{:S(2)}) collective-permute-start(f16[912,384]{1,0:T(8,128)(2,1)} %get-tuple-element.58), channel_id=1, source_target_pairs={{0,24},{4,28},{8,16},{12,20},{16,8},{20,12},{24,0},{28,4},{1,25},{... | collective-permute-start | bytes 2101256 | tf_op jit(solution)/shard_map/ppermute | solution.py:317
  124.2 34.8 %all-to-all-start = ((f16[4,464,384]{2,1,0:T(8,128)(2,1)}), f16[4,464,384]{2,1,0:T(8,128)(2,1)S(1)}, u32[]{:S(2)}, u32[]{:S(2)}) async-start(f16[4,464,384]{2,1,0:T(8,128)(2,1)} %select_convert_fusion), calls=%async_computation | async-start | bytes 2850816 | tf_op jit(solution)/shard_map/all_to_all | solution.py:424
  128.9 22.6 %copy-start.4 = (f32[912,384]{1,0:T(8,128)S(1)}, f32[912,384]{1,0:T(8,128)}, u32[]{:S(2)}) copy-start(f32[912,384]{1,0:T(8,128)} %get-tuple-element.50) | copy-start | bytes 4202500
  146.4 11.2 %copy-start.5 = (f16[912,384]{1,0:T(8,128)(2,1)}, f16[912,384]{1,0:T(8,128)(2,1)S(1)}, u32[]{:S(2)}) copy-start(f16[912,384]{1,0:T(8,128)(2,1)S(1)} %collective-permute-done.4) | copy-start | bytes 2101252
  150.9 8.1 %copy-start.6 = (f16[912,384]{1,0:T(8,128)(2,1)}, f16[912,384]{1,0:T(8,128)(2,1)S(1)}, u32[]{:S(2)}) copy-start(f16[912,384]{1,0:T(8,128)(2,1)S(1)} %collective-permute-done.5) | copy-start | bytes 2101252
  150.9 8.1 %copy-start.7 = (f16[912,384]{1,0:T(8,128)(2,1)}, f16[912,384]{1,0:T(8,128)(2,1)S(1)}, u32[]{:S(2)}) copy-start(f16[912,384]{1,0:T(8,128)(2,1)S(1)} %collective-permute-done.6) | copy-start | bytes 2101252
  151.5 7.8 %copy-start.11 = (f32[384]{0:T(512)}, f32[384]{0:T(512)S(1)}, u32[]{:S(2)}) copy-start(f32[384]{0:T(512)S(1)} %get-tuple-element.85) | copy-start | bytes 4612
  152.8 12.1 %collective-permute-start.7 = (f16[240,384]{1,0:T(8,128)(2,1)}, f16[240,384]{1,0:T(8,128)(2,1)}, u32[]{:S(2)}, u32[]{:S(2)}) collective-permute-start(f16[240,384]{1,0:T(8,128)(2,1)} %get-tuple-element.92), channel_id=1, source_target_pairs={{0,1},{1,2},{2,3},{3,0},{4,5},{5,6},{6,7},{7,4},{8,9},{9,10},{10,1... | collective-permute-start | bytes 552968 | tf_op jit(solution)/shard_map/ppermute | solution.py:327
  155.1 11.9 %collective-permute-start.8 = (f16[240,384]{1,0:T(8,128)(2,1)}, f16[240,384]{1,0:T(8,128)(2,1)}, u32[]{:S(2)}, u32[]{:S(2)}) collective-permute-start(f16[240,384]{1,0:T(8,128)(2,1)} %get-tuple-element.91), channel_id=1, source_target_pairs={{0,2},{1,3},{2,0},{3,1},{4,6},{5,7},{6,4},{7,5},{8,10},{9,11},{10,... | collective-permute-start | bytes 552968 | tf_op jit(solution)/shard_map/ppermute | solution.py:327
  157.5 2.8 %copy-start.3 = (f32[432,384]{1,0:T(8,128)S(1)}, f32[432,384]{1,0:T(8,128)}, u32[]{:S(2)}) copy-start(f32[432,384]{1,0:T(8,128)} %back.1) | copy-start | bytes 1990660
  157.5 9.5 %collective-permute-start.9 = (f16[240,384]{1,0:T(8,128)(2,1)}, f16[240,384]{1,0:T(8,128)(2,1)}, u32[]{:S(2)}, u32[]{:S(2)}) collective-permute-start(f16[240,384]{1,0:T(8,128)(2,1)} %get-tuple-element.90), channel_id=1, source_target_pairs={{0,3},{1,0},{2,1},{3,2},{4,7},{5,4},{6,5},{7,6},{8,11},{9,8},{10,9... | collective-permute-start | bytes 552968 | tf_op jit(solution)/shard_map/ppermute | solution.py:327
  159.3 7.7 %copy-start.12 = (f32[1,384]{1,0:T(1,128)S(1)}, f32[1,384]{1,0:T(1,128)}, u32[]{:S(2)}) copy-start(f32[1,384]{1,0:T(1,128)} %get-tuple-element.86) | copy-start | bytes 4612
  161.3 15.0 %all-to-all-start.1 = ((f32[8,54,384]{2,1,0:T(8,128)}), f32[8,54,384]{2,1,0:T(8,128)S(1)}, u32[]{:S(2)}, u32[]{:S(2)}) async-start(f32[8,54,384]{2,1,0:T(8,128)} %reshape.40), calls=%async_computation.1 | async-start | bytes 1376256 | tf_op jit(solution)/shard_map/all_to_all | solution.py:433
  167.8 14.0 %copy-start.13 = (pred[352]{0:T(512)(128)(4,1)S(1)}, pred[352]{0:T(512)(128)(4,1)}, u32[]{:S(2)}) copy-start(pred[352]{0:T(512)(128)(4,1)} %iota_compare_fusion.3) | copy-start | bytes 1060
  169.4 12.2 %collective-permute-start.10 = (f16[128,384]{1,0:T(8,128)(2,1)S(1)}, f16[128,384]{1,0:T(8,128)(2,1)S(1)}, u32[]{:S(2)}, u32[]{:S(2)}) collective-permute-start(f16[128,384]{1,0:T(8,128)(2,1)S(1)} %get-tuple-element.95), channel_id=1, source_target_pairs={{0,1},{1,2},{2,3},{3,0},{4,5},{5,6},{6,7},{7,4},{8,9},{9,10},{10,1... | collective-permute-start | bytes 294920 | tf_op jit(solution)/shard_map/ppermute | solution.py:327
  172.0 9.7 %collective-permute-start.11 = (f16[128,384]{1,0:T(8,128)(2,1)S(1)}, f16[128,384]{1,0:T(8,128)(2,1)S(1)}, u32[]{:S(2)}, u32[]{:S(2)}) collective-permute-start(f16[128,384]{1,0:T(8,128)(2,1)S(1)} %get-tuple-element.94), channel_id=1, source_target_pairs={{0,2},{1,3},{2,0},{3,1},{4,6},{5,7},{6,4},{7,5},{8,10},{9,11},{10,... | collective-permute-start | bytes 294920 | tf_op jit(solution)/shard_map/ppermute | solution.py:327
  173.7 8.0 %collective-permute-start.12 = (f16[128,384]{1,0:T(8,128)(2,1)S(1)}, f16[128,384]{1,0:T(8,128)(2,1)S(1)}, u32[]{:S(2)}, u32[]{:S(2)}) collective-permute-start(f16[128,384]{1,0:T(8,128)(2,1)S(1)} %get-tuple-element.93), channel_id=1, source_target_pairs={{0,3},{1,0},{2,1},{3,2},{4,7},{5,4},{6,5},{7,6},{8,11},{9,8},{10,9... | collective-permute-start | bytes 294920 | tf_op jit(solution)/shard_map/ppermute | solution.py:327
  177.1 16.8 %all-to-all-start.2 = ((f32[4,54,384]{2,1,0:T(8,128)}), f32[4,54,384]{2,1,0:T(8,128)S(1)}, u32[]{:S(2)}, u32[]{:S(2)}) async-start(f32[4,54,384]{2,1,0:T(8,128)} %broadcast_in_dim.83), calls=%async_computation.2 | async-start | bytes 688128 | tf_op jit(solution)/shard_map/all_to_all | solution.py:440
  181.9 16.4 %collective-permute-start.13 = (f16[352,384]{1,0:T(8,128)(2,1)S(1)}, f16[352,384]{1,0:T(8,128)(2,1)S(1)}, u32[]{:S(2)}, u32[]{:S(2)}) collective-permute-start(f16[352,384]{1,0:T(8,128)(2,1)S(1)} %fusion.5), channel_id=1, source_target_pairs={{0,3},{1,0},{2,1},{3,2},{4,7},{5,4},{6,5},{7,6},{8,11},{9,8},{10,9... | collective-permute-start | bytes 811016 | tf_op jit(solution)/shard_map/ppermute | solution.py:327
  185.8 26.8 %collective-permute-start.14 = (f16[352,384]{1,0:T(8,128)(2,1)S(1)}, f16[352,384]{1,0:T(8,128)(2,1)S(1)}, u32[]{:S(2)}, u32[]{:S(2)}) collective-permute-start(f16[352,384]{1,0:T(8,128)(2,1)S(1)} %fusion.5), channel_id=1, source_target_pairs={{0,2},{1,3},{2,0},{3,1},{4,6},{5,7},{6,4},{7,5},{8,10},{9,11},{10,... | collective-permute-start | bytes 811016 | tf_op jit(solution)/shard_map/ppermute | solution.py:327
  185.8 26.8 %collective-permute-start.15 = (f16[352,384]{1,0:T(8,128)(2,1)S(1)}, f16[352,384]{1,0:T(8,128)(2,1)S(1)}, u32[]{:S(2)}, u32[]{:S(2)}) collective-permute-start(f16[352,384]{1,0:T(8,128)(2,1)S(1)} %fusion.5), channel_id=1, source_target_pairs={{0,1},{1,2},{2,3},{3,0},{4,5},{5,6},{6,7},{7,4},{8,9},{9,10},{10,1... | collective-permute-start | bytes 811016 | tf_op jit(solution)/shard_map/ppermute | solution.py:327
  194.7 24.3 %all-to-all-start.3 = ((f32[8,54,384]{2,1,0:T(8,128)}), f32[8,54,384]{2,1,0:T(8,128)S(1)}, u32[]{:S(2)}, u32[]{:S(2)}) async-start(f32[8,54,384]{2,1,0:T(8,128)} %broadcast_in_dim.86), calls=%async_computation.3 | async-start | bytes 1376256 | tf_op jit(solution)/shard_map/all_to_all | solution.py:445
  214.0 5.9 %copy-start.1 = (bf16[1,8,8,32,16]{3,4,2,1,0:T(8,128)(2,1)S(1)}, bf16[1,8,8,32,16]{3,4,2,1,0:T(8,128)(2,1)}, u32[]{:S(2)}) copy-start(bf16[1,8,8,32,16]{3,4,2,1,0:T(8,128)(2,1)} %param.5) | copy-start | bytes 196612
  (3 other events, 2.1 us)
Sparse Core Ops, SparseCore 0:
  9.9 55.2 all-gather.1

commit v9 on v8

--- a/solution.py
+++ b/solution.py
@@ -138,15 +138,17 @@
     )(crop_t, w_in)
 
 
-def middle_kernel(cells_ref, w_ref, teacher_ref, g_ref, head_ref, acc_ref, *, scale):
+def middle_kernel(cells_ref, wide_ref, thin_ref, teacher_ref, g_ref, head_ref, acc_ref, *, scale):
     depth = pl.program_id(0)
     frames = cells_ref.shape[1] - 2
     rows = cells_ref.shape[2] - 2
-    chans = w_ref.shape[2]
     left = jnp.concatenate(
         [window(cells_ref, k % 3, depth, k // 3, frames, rows) for k in range(9)], axis=1
     )
-    total = contract(left, w_ref[...].reshape(9 * chans, chans), ((1,), (0,)))
+    totals = []
+    for ref in (wide_ref, thin_ref):
+        totals.append(contract(left, ref[...].reshape(left.shape[1], ref.shape[2]), ((1,), (0,))))
+    total = jnp.concatenate(totals, axis=1)
 
     @pl.when(depth == 0)
     def _():
@@ -166,14 +168,15 @@
         g_ref[count:, :] = jnp.broadcast_to(size, (g_ref.shape[0] - count, g.shape[1])).astype(BF16)
 
 
-def middle(cells, w_taps, teacher, scale, head):
+def middle(cells, wide, thin, teacher, scale, head):
     count, chans = teacher.shape
     return pl.pallas_call(
         lambda *refs: middle_kernel(*refs, scale=scale),
         grid=(3,),
         in_specs=[
             pl.BlockSpec(cells.shape, lambda i: (0,) * 5),
-            pl.BlockSpec((9, chans, chans), lambda i: (i, 0, 0)),
+            pl.BlockSpec((9,) + wide.shape[1:], lambda i: (i, 0, 0)),
+            pl.BlockSpec((9,) + thin.shape[1:], lambda i: (i, 0, 0)),
             pl.BlockSpec((count, chans), lambda i: (0, 0)),
         ],
         out_specs=[
@@ -187,7 +190,7 @@
         scratch_shapes=[pltpu.VMEM((count, chans), F32)],
         compiler_params=pltpu.CompilerParams(vmem_limit_bytes=VMEM),
         name="middle",
-    )(cells, w_taps, teacher)
+    )(cells, wide, thin, teacher)
 
 
 def grad_kernel(order_ref, *refs, units):
@@ -245,7 +248,7 @@
     )(order, *(list(taps) * 2), *g)
 
 
-def back_kernel(g_ref, later_ref, w_ref, z_ref, patch_ref, out_ref, cells_ref, acc_ref, *, rows, cols):
+def back_kernel(g_ref, later_ref, wide_ref, thin_ref, z_ref, patch_ref, out_ref, cells_ref, acc_ref, *, rows, cols):
     depth = pl.program_id(0)
     frames = cells_ref.shape[1] - 2
 
@@ -254,10 +257,10 @@
         g = jnp.concatenate([g_ref[...], later_ref[...]], axis=0).astype(F32)
         fill_columns(cells_ref, g, rows, cols)
 
-    left = jnp.concatenate(
-        [window(cells_ref, 2 - k % 3, 2 - depth, 2 - k // 3, frames, rows) for k in range(9)], axis=1
-    )
-    right = jnp.concatenate([w_ref[k] for k in range(9)], axis=1)
+    taps = [window(cells_ref, 2 - k % 3, 2 - depth, 2 - k // 3, frames, rows) for k in range(9)]
+    cut = wide_ref.shape[2]
+    left = jnp.concatenate([x[:, :cut] for x in taps] + [x[:, cut:] for x in taps], axis=1)
+    right = jnp.concatenate([wide_ref[k] for k in range(9)] + [thin_ref[k] for k in range(9)], axis=1)
     total = contract(left, right, ((1,), (1,)))
 
     @pl.when(depth == 0)
@@ -276,7 +279,7 @@
         out_ref[...] = contract(patch_ref[...], dz, ((1,), (0,)))
 
 
-def back(g, later, w_taps, z, patch_t, rows, cols):
+def back(g, later, wide, thin, z, patch_t, rows, cols):
     count, chans = z.shape
     depth_in = patch_t.shape[0]
     frames = count // (rows * cols) + 2
@@ -286,7 +289,8 @@
         in_specs=[
             pl.BlockSpec((count, chans), lambda i: (0, 0)),
             pl.BlockSpec(later.shape, lambda i: (0, 0)),
-            pl.BlockSpec((9, chans, chans), lambda i: (i, 0, 0)),
+            pl.BlockSpec((9,) + wide.shape[1:], lambda i: (i, 0, 0)),
+            pl.BlockSpec((9,) + thin.shape[1:], lambda i: (i, 0, 0)),
             pl.BlockSpec((count, chans), lambda i: (0, 0)),
             pl.BlockSpec((depth_in, count), lambda i: (0, 0)),
         ],
@@ -298,7 +302,7 @@
         ],
         compiler_params=pltpu.CompilerParams(vmem_limit_bytes=VMEM),
         name="back",
-    )(g, later, w_taps, z, patch_t)
+    )(g, later, wide, thin, z, patch_t)
 
 
 def packed(x, rows, bound):
@@ -391,18 +395,33 @@
     clips = lax.axis_size("clip")
     total_cells = clips * lax.axis_size("tm") * count
     scale = 2.0 / math.sqrt(total_cells)
-    w_full = lax.all_gather(w_mid, "clip", axis=0, tiled=True)
+    me = lax.axis_index("clip")
+    cut = chans - 128
+    wide = lax.all_gather(w_mid[:, :cut], "clip", axis=0, tiled=True)
+    strip = w_mid[:, cut:]
+    strips = [strip]
+    for q in range(1, clips // 2):
+        strips.append(lax.ppermute(strip, "clip", [(i, i ^ (2 * q)) for i in range(clips)]))
     crop = lax.dynamic_slice_in_dim(latent[0], offsets[0], cols, axis=2).reshape(count, lat_chans).T
     earlier = passed_along(crop[:, count - 4 * plane :], "tm", 1)
     crop_ext = jnp.concatenate([earlier, crop], axis=1)
     patch_t, z, cells, taps, top = front(crop_ext, w_in, rows, cols, count, True)
-    pair_taps, pair_top = front(swapped(crop_ext), w_in, rows, cols, count, False)
+    mine = jnp.concatenate(behind(strips, top), axis=0)
+    theirs = swapped(mine)
+    pair_taps, pair_top = front(behind(swapped(crop_ext), mine), w_in, rows, cols, count, False)
     taps = taps.reshape(27 * chans, count)
     pair_taps = pair_taps.reshape(27 * chans, count)
     top, pair_top = jnp.max(top), jnp.max(pair_top)
-    w_full, pair_taps, top, pair_top = lax.optimization_barrier((w_full, pair_taps, top, pair_top))
-    w_taps = w_full.reshape(27, chans, chans)
-    g, head = middle(cells, w_taps, teacher[0].reshape(count, chans), scale, 2 * plane)
+    block_rows = strip.shape[0]
+    thin = jnp.zeros((clips * block_rows, 128), strip.dtype)
+    for k in range(clips):
+        source = theirs if k % 2 else mine
+        piece = source[k // 2 * block_rows : (k // 2 + 1) * block_rows]
+        thin = lax.dynamic_update_slice_in_dim(thin, piece, (me ^ k) * block_rows, axis=0)
+    wide, thin, pair_taps, top, pair_top = lax.optimization_barrier((wide, thin, pair_taps, top, pair_top))
+    wide = wide.reshape(27, chans, cut)
+    thin = thin.reshape(27, chans, chans - cut)
+    g, head = middle(cells, wide, thin, teacher[0].reshape(count, chans), scale, 2 * plane)
     pair_g = swapped(g)
     later = passed_along(head, "tm", -1)
 
@@ -412,7 +431,6 @@
     both = (taps, pair_taps)
     in_rows = patch_t.shape[0]
 
-    me = lax.axis_index("clip")
     chips = jnp.arange(clips // 2, dtype=jnp.int32)
     own_a, part = grad_chunk(me ^ (2 * chips), both, (g, pair_g), 0, 2)
     part, later = lax.optimization_barrier((part, later))
@@ -423,7 +441,7 @@
     groups = [[2 * p + core for p in range(clips // 2)] for core in range(2)]
     got_b = lax.all_to_all(payload, "clip", 0, 0, axis_index_groups=groups, tiled=True)
     got_b = [got_b[p] for p in range(clips // 2)]
-    in_part = back(g, later, w_taps, z, patch_t, rows, cols)
+    in_part = back(g, later, wide, thin, z, patch_t, rows, cols)
 
     got_a = behind(got_a, in_part)
     factors, total = scales(got_a, 2 * third, bound)

time: 228 us -> 224 us (0.982)
  waiting for transfers between devices: 54.6 us -> 29.6 us
  local copies, waits for them, and re-layouts: 14.6 us -> 27.2 us
  starting transfers between devices: 41.6 us -> 49.9 us
    all_gather x1, waiting for transfers between devices: 22.8 us -> 0.06 us  [shards(): wide = lax.all_gather(w_mid[:, :cut], 'clip', axis=0, tiled=True)]
    dynamic_update_slice x0 -> x7, local copies, waits for them, and re-layouts: none -> 5.22 us  [shards(): lax.dynamic_update_slice_in_dim(thin, piece, (me ^ k) * block_rows, axis=0)]
    ppermute x0 -> x3, starting transfers between devices: none -> 4.55 us  [shards(): lax.ppermute(strip, 'clip', [(i, i ^ 2 * q) for i in range(clips)])]
    ppermute x3, waiting for transfers between devices: 4.48 us -> 0.01 us  [across_plane(): got.append(lax.ppermute(payloads[q - 1], 'clip', route))]
    unnamed x35 -> x44, local copies, waits for them, and re-layouts: 7.19 us -> 11 us
    slice x0 -> x2, local copies, waits for them, and re-layouts: none -> 3.01 us  [the longest x1 2.01 us: shards(): wide = lax.all_gather(w_mid[:, :cut], 'clip', axis=0, tiled=True)]
    all_to_all x1, waiting for transfers between devices: 0.01 us -> 2.4 us  [shards(): lax.all_to_all(payload, 'clip', 0, 0, axis_index_groups=groups, tiled=True)]
    ppermute x9, starting transfers between devices: 16.2 us -> 18.6 us  [around(): lax.ppermute(blocks, 'tm', [(i, (i + distance) % depth) for i in range(de...]
  transfers between devices with their start and end apart: 21 -> 25, of which waited for: 7 -> 9; matrix products, arithmetic and copies ran while one was open for 11% -> 17% of each run, Pallas kernels for 28% -> 28%
where the time goes in v9:
time: 224 us; the launch traced here: 223 us
  Pallas kernels  79.1 us (35%)
  starting transfers between devices  49.9 us (22%)
  waiting for transfers between devices  29.6 us (13%)
  local copies, waits for them, and re-layouts  27.2 us (12%)
  other arithmetic  19.7 us (9%)
  between operations  17.6 us (8%)
    pallas_call x2, Pallas kernels, grad_chunk(): pl.pallas_call(lambda *refs: grad_kernel(*refs, units=units), grid_spec=p...  22.5 us
    pallas_call x2, Pallas kernels, front(): pl.pallas_call(lambda *refs: front_kernel(*refs, rows=rows, cols=cols, fi...  22.2 us
    ppermute x9, starting transfers between devices, around(): lax.ppermute(blocks, 'tm', [(i, (i + distance) % depth) for i in range(de...  18.6 us
    ppermute x9, waiting for transfers between devices, around(): lax.ppermute(blocks, 'tm', [(i, (i + distance) % depth) for i in range(de...  17.6 us
    pallas_call x1, Pallas kernels, back(): pl.pallas_call(lambda *refs: back_kernel(*refs, rows=rows, cols=cols), gr...  17.5 us
    pallas_call x1, Pallas kernels, middle(): pl.pallas_call(lambda *refs: middle_kernel(*refs, scale=scale), grid=(3,)...  16.8 us
    unnamed x44, local copies, waits for them, and re-layouts  11 us
    convert_element_type x5, other arithmetic, packed(): return jnp.where(row < rows, x * jnp.exp2(14.0 - power), power).astype(F16)  9.75 us
  transfers between devices with their start and end apart: 25, of which 9 were waited for; matrix products, arithmetic and copies ran while one was open for 17% of the time, Pallas kernels for 28%

profile of v9, /device:TPU:0, one launch (start us, length us, event | category | flops | bytes accessed | tf_op | source)
XLA Modules:
  0.0 223.0 jit_solution(1893064338930714507)
XLA Ops:
  7.2 2.0 slice.139
  10.3 3.0 %collective-permute-start.1 = (bf16[1296,128]{1,0:T(8,128)(2,1)S(1)}, bf16[1296,128]{1,0:T(8,128)(2,1)}, u32[]{:S(2)}, u32[]{:S(2)}) collective-permute-start(bf16[1296,128]{1,0:T(8,128)(2,1)S(1)} %slice.140), channel_id=1, source_target_pairs={{0,8},{4,12},{8,0},{12,4},{16,24},{20,28},{24,16},{28,20},{1,9},{5... | collective-permute-start | bytes 995336 | tf_op jit(solution)/shard_map/ppermute | solution.py:404
  13.3 1.5 collective-permute-start.2
  16.0 3.9 %collective-permute-start = (bf16[16,512]{1,0:T(8,128)(2,1)S(1)}, bf16[16,512]{1,0:T(8,128)(2,1)S(1)}, u32[]{:S(2)}, u32[]{:S(2)}) collective-permute-start(bf16[16,512]{1,0:T(8,128)(2,1)S(1)} %slice.184), channel_id=1, source_target_pairs={{0,1},{1,2},{2,3},{4,5},{5,6},{6,7},{8,9},{9,10},{10,11},{12,13},{... | collective-permute-start | bytes 49160 | tf_op jit(solution)/shard_map/ppermute | solution.py:19
  22.0 12.2 %front.2 = (bf16[432,1024]{1,0:T(8,128)(2,1)}, f32[1024,384]{1,0:T(8,128)}, bf16[3,10,10,16,384]{4,3,2,1,0:T(8,128)(2,1)}, bf16[27,384,1024]{2,1,0:T(8,128)(2,1)}, f32[384,128]{1,0:T(8,128)}) custom-call(bf16[16,1536]{1,0:T(8,128)(2,1)} %pad_maximum_fusion.refs_0_, bf16[432,384]{1,0:T(8,128)(2,1)} %refs_1_.3), custom_call_target="tpu_custom_call" | custom-call | tf_op jit(solution)/shard_map/front/pallas_call | solution.py:126
  37.2 1.7 constant_dynamic-update-slice_fusion.2
  40.9 1.6 reduce_max.18
  43.9 10.0 %front.3 = (bf16[27,384,1024]{2,1,0:T(8,128)(2,1)}, f32[384,128]{1,0:T(8,128)}) custom-call(bf16[16,1536]{1,0:T(8,128)(2,1)} %copy-done.13, bf16[432,384]{1,0:T(8,128)(2,1)} %refs_1_.3), custom_call_target="tpu_custom_call" | custom-call | tf_op jit(solution)/shard_map/front/pallas_call | solution.py:126
  53.9 1.6 reduce_max.19
  60.7 1.4 copy-done.2
  62.2 16.8 %middle.1 = (bf16[1040,384]{1,0:T(8,128)(2,1)}, bf16[256,384]{1,0:T(8,128)(2,1)}) custom-call(bf16[3,10,10,16,384]{4,3,2,1,0:T(8,128)(2,1)} %get-tuple-element.58.refs_0_, bf16[27,384,256]{2,1,0:T(8,128)(2,1)} %bitcast.49, bf16[27,384,128]{2,1,0:T(8,128)(2,1)} %bitcast.47, bf16[1024,384]{1,0:T(8,128)(2,1)} %bitcast.51), custom_call_target="tpu_custom_call" | custom-call | tf_op jit(solution)/shard_map/middle/pallas_call | solution.py:173
  80.0 1.5 collective-permute-start.7
  86.3 13.7 %grad.2 = (f32[912,384]{1,0:T(8,128)}, f32[4,912,384]{2,1,0:T(8,128)}) custom-call(s32[4]{0:T(128)} %fusion.18.refs_0_, bf16[10368,1024]{1,0:T(8,128)(2,1)} %bitcast.39, bf16[10368,1024]{1,0:T(8,128)(2,1)} %bitcast.43, bf16[10368,1024]{1,0:T(8,128)(2,1)} %bitcast.40, bf16[10368,1024]{1,0:T(8,128)(2,1)} %bitcast.44, ...), custom_call_target="tpu_custom_call" | custom-call | tf_op jit(solution)/shard_map/grad/pallas_call | solution.py:231
  100.0 4.1 %fusion = (f16[912,384]{1,0:T(8,128)(2,1)}, f16[912,384]{1,0:T(8,128)(2,1)}, f16[912,384]{1,0:T(8,128)(2,1)}) fusion(f32[4,912,384]{2,1,0:T(8,128)} %get-tuple-element.65, f32[]{:T(128)} %bitcast.11, f32[]{:T(128)} %bitcast.9, pred[912]{0:T(1024)(128)(4,1)S(1)} %iota_compare_fusion.1), kind=kLoop, calls=%fused_computation.2 | loop fusion | flops 3151872 | bytes 6304664 | tf_op jit(solution)/shard_map/convert_element_type | solution.py:311
  104.2 2.5 %collective-permute-start.10 = (f16[912,384]{1,0:T(8,128)(2,1)}, f16[912,384]{1,0:T(8,128)(2,1)S(1)}, u32[]{:S(2)}, u32[]{:S(2)}) collective-permute-start(f16[912,384]{1,0:T(8,128)(2,1)} %get-tuple-element.70), channel_id=1, source_target_pairs={{0,24},{4,28},{8,16},{12,20},{16,8},{20,12},{24,0},{28,4},{1,25},{... | collective-permute-start | bytes 2101256 | tf_op jit(solution)/shard_map/ppermute | solution.py:321
  108.0 8.8 %grad.3 = (f32[464,384]{1,0:T(8,128)}, f32[4,464,384]{2,1,0:T(8,128)}) custom-call(s32[4]{0:T(128)} %fusion.17.refs_0_, bf16[10368,1024]{1,0:T(8,128)(2,1)} %bitcast.41, bf16[10368,1024]{1,0:T(8,128)(2,1)} %bitcast.45, bf16[10368,1024]{1,0:T(8,128)(2,1)} %bitcast.42, bf16[10368,1024]{1,0:T(8,128)(2,1)} %bitcast.46, ...), custom_call_target="tpu_custom_call" | custom-call | tf_op jit(solution)/shard_map/grad/pallas_call | solution.py:231
  116.8 3.3 %select_convert_fusion = f16[4,464,384]{2,1,0:T(8,128)(2,1)} fusion(f32[4,464,384]{2,1,0:T(8,128)} %get-tuple-element.72, f32[]{:T(128)} %bitcast.11, f32[]{:T(128)} %bitcast.9, pred[464]{0:T(512)(128)(4,1)S(1)} %iota_compare_fusion.2), kind=kLoop, calls=%fused_computation | loop fusion | flops 2138112 | bytes 4276696 | tf_op jit(solution)/shard_map/convert_element_type | solution.py:311
  120.1 3.5 %all-to-all-start = ((f16[4,464,384]{2,1,0:T(8,128)(2,1)}), f16[4,464,384]{2,1,0:T(8,128)(2,1)S(1)}, u32[]{:S(2)}, u32[]{:S(2)}) async-start(f16[4,464,384]{2,1,0:T(8,128)(2,1)} %select_convert_fusion), calls=%async_computation | async-start | bytes 2850816 | tf_op jit(solution)/shard_map/all_to_all | solution.py:442
  124.8 17.5 %back.1 = f32[432,384]{1,0:T(8,128)} custom-call(bf16[1040,384]{1,0:T(8,128)(2,1)} %get-tuple-element.73.refs_5_.refs_0_, bf16[256,384]{1,0:T(8,128)(2,1)} %copy-done.12, bf16[27,384,256]{2,1,0:T(8,128)(2,1)} %bitcast.50, bf16[27,384,128]{2,1,0:T(8,128)(2,1)} %bitcast.48, f32[1024,384]{1,0:T(8,128)} %get-tuple-element.75.refs_4_, ...), custom_call_target="tpu_custom_call" | custom-call | tf_op jit(solution)/shard_map/back/pallas_call | solution.py:286
  144.2 2.7 %collective-permute-start.11 = (f16[240,384]{1,0:T(8,128)(2,1)}, f16[240,384]{1,0:T(8,128)(2,1)}, u32[]{:S(2)}, u32[]{:S(2)}) collective-permute-start(f16[240,384]{1,0:T(8,128)(2,1)} %get-tuple-element.104), channel_id=1, source_target_pairs={{0,1},{1,2},{2,3},{3,0},{4,5},{5,6},{6,7},{7,4},{8,9},{9,10},{10,1... | collective-permute-start | bytes 552968 | tf_op jit(solution)/shard_map/ppermute | solution.py:331
  146.9 2.8 %collective-permute-start.12 = (f16[240,384]{1,0:T(8,128)(2,1)}, f16[240,384]{1,0:T(8,128)(2,1)}, u32[]{:S(2)}, u32[]{:S(2)}) collective-permute-start(f16[240,384]{1,0:T(8,128)(2,1)} %get-tuple-element.103), channel_id=1, source_target_pairs={{0,2},{1,3},{2,0},{3,1},{4,6},{5,7},{6,4},{7,5},{8,10},{9,11},{10,... | collective-permute-start | bytes 552968 | tf_op jit(solution)/shard_map/ppermute | solution.py:331
  150.9 2.4 %all-to-all-done = f16[4,464,384]{2,1,0:T(8,128)(2,1)S(1)} async-done(((f16[4,464,384]{2,1,0:T(8,128)(2,1)}), f16[4,464,384]{2,1,0:T(8,128)(2,1)S(1)}, u32[]{:S(2)}, u32[]{:S(2)}) %all-to-all-start) | async-done | bytes 1425440 | tf_op jit(solution)/shard_map/all_to_all | solution.py:442
  155.6 3.8 %all-to-all-start.1 = ((f32[8,54,384]{2,1,0:T(8,128)}), f32[8,54,384]{2,1,0:T(8,128)S(1)}, u32[]{:S(2)}, u32[]{:S(2)}) async-start(f32[8,54,384]{2,1,0:T(8,128)} %reshape.44), calls=%async_computation.1 | async-start | bytes 1376256 | tf_op jit(solution)/shard_map/all_to_all | solution.py:451
  159.4 2.1 collective-permute-done.12
  162.2 1.6 fusion.6
  163.8 4.5 %collective-permute-start.14 = (f16[128,384]{1,0:T(8,128)(2,1)S(1)}, f16[128,384]{1,0:T(8,128)(2,1)S(1)}, u32[]{:S(2)}, u32[]{:S(2)}) collective-permute-start(f16[128,384]{1,0:T(8,128)(2,1)S(1)} %get-tuple-element.107), channel_id=1, source_target_pairs={{0,1},{1,2},{2,3},{3,0},{4,5},{5,6},{6,7},{7,4},{8,9},{9,10},{10,1... | collective-permute-start | bytes 294920 | tf_op jit(solution)/shard_map/ppermute | solution.py:331
  168.3 1.6 collective-permute-start.15
  171.7 5.7 %all-to-all-start.2 = ((f32[4,54,384]{2,1,0:T(8,128)}), f32[4,54,384]{2,1,0:T(8,128)S(1)}, u32[]{:S(2)}, u32[]{:S(2)}) async-start(f32[4,54,384]{2,1,0:T(8,128)} %broadcast_in_dim.87), calls=%async_computation.2 | async-start | bytes 688128 | tf_op jit(solution)/shard_map/all_to_all | solution.py:458
  177.7 3.9 %collective-permute-start.17 = (f16[352,384]{1,0:T(8,128)(2,1)S(1)}, f16[352,384]{1,0:T(8,128)(2,1)S(1)}, u32[]{:S(2)}, u32[]{:S(2)}) collective-permute-start(f16[352,384]{1,0:T(8,128)(2,1)S(1)} %fusion.5), channel_id=1, source_target_pairs={{0,3},{1,0},{2,1},{3,2},{4,7},{5,4},{6,5},{7,6},{8,11},{9,8},{10,9... | collective-permute-start | bytes 811016 | tf_op jit(solution)/shard_map/ppermute | solution.py:331
  182.7 6.1 %all-to-all-done.2 = f32[4,54,384]{2,1,0:T(8,128)S(1)} async-done(((f32[4,54,384]{2,1,0:T(8,128)}), f32[4,54,384]{2,1,0:T(8,128)S(1)}, u32[]{:S(2)}, u32[]{:S(2)}) %all-to-all-start.2) | async-done | bytes 331808 | tf_op jit(solution)/shard_map/all_to_all | solution.py:458
  189.8 3.5 %all-to-all-start.3 = ((f32[8,54,384]{2,1,0:T(8,128)}), f32[8,54,384]{2,1,0:T(8,128)S(1)}, u32[]{:S(2)}, u32[]{:S(2)}) async-start(f32[8,54,384]{2,1,0:T(8,128)} %broadcast_in_dim.90), calls=%async_computation.3 | async-start | bytes 1376256 | tf_op jit(solution)/shard_map/all_to_all | solution.py:463
  193.3 15.5 %collective-permute-done.18 = f16[352,384]{1,0:T(8,128)(2,1)S(1)} collective-permute-done((f16[352,384]{1,0:T(8,128)(2,1)S(1)}, f16[352,384]{1,0:T(8,128)(2,1)S(1)}, u32[]{:S(2)}, u32[]{:S(2)}) %collective-permute-start.18) | collective-permute-done | bytes 270368 | tf_op jit(solution)/shard_map/ppermute | solution.py:331
  (122 shorter events, 38.6 us)
Async XLA Ops:
  7.2 8.3 %copy-start = (bf16[1,8,8,32,16]{3,4,2,1,0:T(8,128)(2,1)S(1)}, bf16[1,8,8,32,16]{3,4,2,1,0:T(8,128)(2,1)}, u32[]{:S(2)}) copy-start(bf16[1,8,8,32,16]{3,4,2,1,0:T(8,128)(2,1)} %param.5) | copy-start | bytes 196612
  7.2 53.6 %all-gather.2.cloned.1.call-start = ((), (), s32[]{:S(2)}) async-start(), calls=%async_computation.4 | async-start | bytes 5971968 | tf_op jit(solution)/shard_map/all_gather | solution.py:400
  10.3 25.2 %copy-start.6 = (bf16[1296,128]{1,0:T(8,128)(2,1)}, bf16[1296,128]{1,0:T(8,128)(2,1)S(1)}, u32[]{:S(2)}) copy-start(bf16[1296,128]{1,0:T(8,128)(2,1)S(1)} %slice.140) | copy-start | bytes 995332
  10.3 24.0 %collective-permute-start.1 = (bf16[1296,128]{1,0:T(8,128)(2,1)S(1)}, bf16[1296,128]{1,0:T(8,128)(2,1)}, u32[]{:S(2)}, u32[]{:S(2)}) collective-permute-start(bf16[1296,128]{1,0:T(8,128)(2,1)S(1)} %slice.140), channel_id=1, source_target_pairs={{0,8},{4,12},{8,0},{12,4},{16,24},{20,28},{24,16},{28,20},{1,9},{5... | collective-permute-start | bytes 995336 | tf_op jit(solution)/shard_map/ppermute | solution.py:404
  13.3 21.0 %collective-permute-start.2 = (bf16[1296,128]{1,0:T(8,128)(2,1)S(1)}, bf16[1296,128]{1,0:T(8,128)(2,1)S(1)}, u32[]{:S(2)}, u32[]{:S(2)}) collective-permute-start(bf16[1296,128]{1,0:T(8,128)(2,1)S(1)} %slice.140), channel_id=1, source_target_pairs={{0,16},{4,20},{8,24},{12,28},{16,0},{20,4},{24,8},{28,12},{1,17},{... | collective-permute-start | bytes 995336 | tf_op jit(solution)/shard_map/ppermute | solution.py:404
  14.8 20.7 %collective-permute-start.3 = (bf16[1296,128]{1,0:T(8,128)(2,1)S(1)}, bf16[1296,128]{1,0:T(8,128)(2,1)S(1)}, u32[]{:S(2)}, u32[]{:S(2)}) collective-permute-start(bf16[1296,128]{1,0:T(8,128)(2,1)S(1)} %slice.140), channel_id=1, source_target_pairs={{0,24},{4,28},{8,16},{12,20},{16,8},{20,12},{24,0},{28,4},{1,25},{... | collective-permute-start | bytes 995336 | tf_op jit(solution)/shard_map/ppermute | solution.py:404
  16.0 5.4 %collective-permute-start = (bf16[16,512]{1,0:T(8,128)(2,1)S(1)}, bf16[16,512]{1,0:T(8,128)(2,1)S(1)}, u32[]{:S(2)}, u32[]{:S(2)}) collective-permute-start(bf16[16,512]{1,0:T(8,128)(2,1)S(1)} %slice.184), channel_id=1, source_target_pairs={{0,1},{1,2},{2,3},{4,5},{5,6},{6,7},{8,9},{9,10},{10,11},{12,13},{... | collective-permute-start | bytes 49160 | tf_op jit(solution)/shard_map/ppermute | solution.py:19
  40.4 15.0 %collective-permute-start.4 = (bf16[5184,128]{1,0:T(8,128)(2,1)}, bf16[5184,128]{1,0:T(8,128)(2,1)}, u32[]{:S(2)}, u32[]{:S(2)}) collective-permute-start(bf16[5184,128]{1,0:T(8,128)(2,1)} %constant_dynamic-update-slice_fusion), channel_id=1, source_target_pairs={{0,4},{4,0},{8,12},{12,8},{16,20},{20,16},{24,28},{28,24},{1,5},{5... | collective-permute-start | bytes 3981320 | tf_op jit(solution)/shard_map/ppermute | solution.py:23
  40.4 2.8 %collective-permute-start.5 = (bf16[16,1536]{1,0:T(8,128)(2,1)S(1)}, bf16[16,1536]{1,0:T(8,128)(2,1)S(1)}, u32[]{:S(2)}, u32[]{:S(2)}) collective-permute-start(bf16[16,1536]{1,0:T(8,128)(2,1)S(1)} %copy-done.11), channel_id=1, source_target_pairs={{0,4},{4,0},{8,12},{12,8},{16,20},{20,16},{24,28},{28,24},{1,5},{5... | collective-permute-start | bytes 147464 | tf_op jit(solution)/shard_map/ppermute | solution.py:23
  79.0 5.4 %collective-permute-start.6 = (bf16[1040,384]{1,0:T(8,128)(2,1)}, bf16[1040,384]{1,0:T(8,128)(2,1)S(1)}, u32[]{:S(2)}, u32[]{:S(2)}) collective-permute-start(bf16[1040,384]{1,0:T(8,128)(2,1)} %get-tuple-element.73.refs_5_.refs_0_), channel_id=1, source_target_pairs={{0,4},{4,0},{8,12},{12,8},{16,20},{20,16},{24,28},{28,24},{1,5},{5... | collective-permute-start | bytes 2396168 | tf_op jit(solution)/shard_map/ppermute | solution.py:23
  80.0 20.0 %collective-permute-start.7 = (bf16[256,384]{1,0:T(8,128)(2,1)}, bf16[256,384]{1,0:T(8,128)(2,1)S(1)}, u32[]{:S(2)}, u32[]{:S(2)}) collective-permute-start(bf16[256,384]{1,0:T(8,128)(2,1)} %get-tuple-element.64), channel_id=1, source_target_pairs={{1,0},{2,1},{3,2},{5,4},{6,5},{7,6},{9,8},{10,9},{11,10},{13,12},{... | collective-permute-start | bytes 589832 | tf_op jit(solution)/shard_map/ppermute | solution.py:19
  104.2 38.1 %collective-permute-start.10 = (f16[912,384]{1,0:T(8,128)(2,1)}, f16[912,384]{1,0:T(8,128)(2,1)S(1)}, u32[]{:S(2)}, u32[]{:S(2)}) collective-permute-start(f16[912,384]{1,0:T(8,128)(2,1)} %get-tuple-element.70), channel_id=1, source_target_pairs={{0,24},{4,28},{8,16},{12,20},{16,8},{20,12},{24,0},{28,4},{1,25},{... | collective-permute-start | bytes 2101256 | tf_op jit(solution)/shard_map/ppermute | solution.py:321
  106.6 35.7 %collective-permute-start.8 = (f16[912,384]{1,0:T(8,128)(2,1)}, f16[912,384]{1,0:T(8,128)(2,1)S(1)}, u32[]{:S(2)}, u32[]{:S(2)}) collective-permute-start(f16[912,384]{1,0:T(8,128)(2,1)} %get-tuple-element.68), channel_id=1, source_target_pairs={{0,8},{4,12},{8,0},{12,4},{16,24},{20,28},{24,16},{28,20},{1,9},{5... | collective-permute-start | bytes 2101256 | tf_op jit(solution)/shard_map/ppermute | solution.py:321
  106.6 35.7 %collective-permute-start.9 = (f16[912,384]{1,0:T(8,128)(2,1)}, f16[912,384]{1,0:T(8,128)(2,1)S(1)}, u32[]{:S(2)}, u32[]{:S(2)}) collective-permute-start(f16[912,384]{1,0:T(8,128)(2,1)} %get-tuple-element.69), channel_id=1, source_target_pairs={{0,16},{4,20},{8,24},{12,28},{16,0},{20,4},{24,8},{28,12},{1,17},{... | collective-permute-start | bytes 2101256 | tf_op jit(solution)/shard_map/ppermute | solution.py:321
  120.1 33.2 %all-to-all-start = ((f16[4,464,384]{2,1,0:T(8,128)(2,1)}), f16[4,464,384]{2,1,0:T(8,128)(2,1)S(1)}, u32[]{:S(2)}, u32[]{:S(2)}) async-start(f16[4,464,384]{2,1,0:T(8,128)(2,1)} %select_convert_fusion), calls=%async_computation | async-start | bytes 2850816 | tf_op jit(solution)/shard_map/all_to_all | solution.py:442
  124.8 18.2 %copy-start.5 = (f32[912,384]{1,0:T(8,128)S(1)}, f32[912,384]{1,0:T(8,128)}, u32[]{:S(2)}) copy-start(f32[912,384]{1,0:T(8,128)} %get-tuple-element.62) | copy-start | bytes 4202500
  142.3 8.6 %copy-start.9 = (f16[912,384]{1,0:T(8,128)(2,1)}, f16[912,384]{1,0:T(8,128)(2,1)S(1)}, u32[]{:S(2)}) copy-start(f16[912,384]{1,0:T(8,128)(2,1)S(1)} %collective-permute-done.8) | copy-start | bytes 2101252
  142.3 8.6 %copy-start.10 = (f16[912,384]{1,0:T(8,128)(2,1)}, f16[912,384]{1,0:T(8,128)(2,1)S(1)}, u32[]{:S(2)}) copy-start(f16[912,384]{1,0:T(8,128)(2,1)S(1)} %collective-permute-done.9) | copy-start | bytes 2101252
  143.0 10.6 %copy-start.14 = (f32[384]{0:T(512)}, f32[384]{0:T(512)S(1)}, u32[]{:S(2)}) copy-start(f32[384]{0:T(512)S(1)} %get-tuple-element.97) | copy-start | bytes 4612
  144.2 15.2 %collective-permute-start.11 = (f16[240,384]{1,0:T(8,128)(2,1)}, f16[240,384]{1,0:T(8,128)(2,1)}, u32[]{:S(2)}, u32[]{:S(2)}) collective-permute-start(f16[240,384]{1,0:T(8,128)(2,1)} %get-tuple-element.104), channel_id=1, source_target_pairs={{0,1},{1,2},{2,3},{3,0},{4,5},{5,6},{6,7},{7,4},{8,9},{9,10},{10,1... | collective-permute-start | bytes 552968 | tf_op jit(solution)/shard_map/ppermute | solution.py:331
  146.9 14.6 %collective-permute-start.12 = (f16[240,384]{1,0:T(8,128)(2,1)}, f16[240,384]{1,0:T(8,128)(2,1)}, u32[]{:S(2)}, u32[]{:S(2)}) collective-permute-start(f16[240,384]{1,0:T(8,128)(2,1)} %get-tuple-element.103), channel_id=1, source_target_pairs={{0,2},{1,3},{2,0},{3,1},{4,6},{5,7},{6,4},{7,5},{8,10},{9,11},{10,... | collective-permute-start | bytes 552968 | tf_op jit(solution)/shard_map/ppermute | solution.py:331
  149.6 11.8 %collective-permute-start.13 = (f16[240,384]{1,0:T(8,128)(2,1)}, f16[240,384]{1,0:T(8,128)(2,1)}, u32[]{:S(2)}, u32[]{:S(2)}) collective-permute-start(f16[240,384]{1,0:T(8,128)(2,1)} %get-tuple-element.102), channel_id=1, source_target_pairs={{0,3},{1,0},{2,1},{3,2},{4,7},{5,4},{6,5},{7,6},{8,11},{9,8},{10,9... | collective-permute-start | bytes 552968 | tf_op jit(solution)/shard_map/ppermute | solution.py:331
  155.6 15.3 %all-to-all-start.1 = ((f32[8,54,384]{2,1,0:T(8,128)}), f32[8,54,384]{2,1,0:T(8,128)S(1)}, u32[]{:S(2)}, u32[]{:S(2)}) async-start(f32[8,54,384]{2,1,0:T(8,128)} %reshape.44), calls=%async_computation.1 | async-start | bytes 1376256 | tf_op jit(solution)/shard_map/all_to_all | solution.py:451
  162.2 15.3 %copy-start.16 = (pred[352]{0:T(512)(128)(4,1)S(1)}, pred[352]{0:T(512)(128)(4,1)}, u32[]{:S(2)}) copy-start(pred[352]{0:T(512)(128)(4,1)} %iota_compare_fusion.3) | copy-start | bytes 1060
  163.8 13.6 %collective-permute-start.14 = (f16[128,384]{1,0:T(8,128)(2,1)S(1)}, f16[128,384]{1,0:T(8,128)(2,1)S(1)}, u32[]{:S(2)}, u32[]{:S(2)}) collective-permute-start(f16[128,384]{1,0:T(8,128)(2,1)S(1)} %get-tuple-element.107), channel_id=1, source_target_pairs={{0,1},{1,2},{2,3},{3,0},{4,5},{5,6},{6,7},{7,4},{8,9},{9,10},{10,1... | collective-permute-start | bytes 294920 | tf_op jit(solution)/shard_map/ppermute | solution.py:331
  168.3 9.1 %collective-permute-start.15 = (f16[128,384]{1,0:T(8,128)(2,1)S(1)}, f16[128,384]{1,0:T(8,128)(2,1)S(1)}, u32[]{:S(2)}, u32[]{:S(2)}) collective-permute-start(f16[128,384]{1,0:T(8,128)(2,1)S(1)} %get-tuple-element.106), channel_id=1, source_target_pairs={{0,2},{1,3},{2,0},{3,1},{4,6},{5,7},{6,4},{7,5},{8,10},{9,11},{10,... | collective-permute-start | bytes 294920 | tf_op jit(solution)/shard_map/ppermute | solution.py:331
  169.9 7.5 %collective-permute-start.16 = (f16[128,384]{1,0:T(8,128)(2,1)S(1)}, f16[128,384]{1,0:T(8,128)(2,1)S(1)}, u32[]{:S(2)}, u32[]{:S(2)}) collective-permute-start(f16[128,384]{1,0:T(8,128)(2,1)S(1)} %get-tuple-element.105), channel_id=1, source_target_pairs={{0,3},{1,0},{2,1},{3,2},{4,7},{5,4},{6,5},{7,6},{8,11},{9,8},{10,9... | collective-permute-start | bytes 294920 | tf_op jit(solution)/shard_map/ppermute | solution.py:331
  171.7 17.2 %all-to-all-start.2 = ((f32[4,54,384]{2,1,0:T(8,128)}), f32[4,54,384]{2,1,0:T(8,128)S(1)}, u32[]{:S(2)}, u32[]{:S(2)}) async-start(f32[4,54,384]{2,1,0:T(8,128)} %broadcast_in_dim.87), calls=%async_computation.2 | async-start | bytes 688128 | tf_op jit(solution)/shard_map/all_to_all | solution.py:458
  177.7 15.6 %collective-permute-start.17 = (f16[352,384]{1,0:T(8,128)(2,1)S(1)}, f16[352,384]{1,0:T(8,128)(2,1)S(1)}, u32[]{:S(2)}, u32[]{:S(2)}) collective-permute-start(f16[352,384]{1,0:T(8,128)(2,1)S(1)} %fusion.5), channel_id=1, source_target_pairs={{0,3},{1,0},{2,1},{3,2},{4,7},{5,4},{6,5},{7,6},{8,11},{9,8},{10,9... | collective-permute-start | bytes 811016 | tf_op jit(solution)/shard_map/ppermute | solution.py:331
  181.5 27.3 %collective-permute-start.18 = (f16[352,384]{1,0:T(8,128)(2,1)S(1)}, f16[352,384]{1,0:T(8,128)(2,1)S(1)}, u32[]{:S(2)}, u32[]{:S(2)}) collective-permute-start(f16[352,384]{1,0:T(8,128)(2,1)S(1)} %fusion.5), channel_id=1, source_target_pairs={{0,2},{1,3},{2,0},{3,1},{4,6},{5,7},{6,4},{7,5},{8,10},{9,11},{10,... | collective-permute-start | bytes 811016 | tf_op jit(solution)/shard_map/ppermute | solution.py:331
  181.6 27.3 %collective-permute-start.19 = (f16[352,384]{1,0:T(8,128)(2,1)S(1)}, f16[352,384]{1,0:T(8,128)(2,1)S(1)}, u32[]{:S(2)}, u32[]{:S(2)}) collective-permute-start(f16[352,384]{1,0:T(8,128)(2,1)S(1)} %fusion.5), channel_id=1, source_target_pairs={{0,1},{1,2},{2,3},{3,0},{4,5},{5,6},{6,7},{7,4},{8,9},{9,10},{10,1... | collective-permute-start | bytes 811016 | tf_op jit(solution)/shard_map/ppermute | solution.py:331
  189.8 25.5 %all-to-all-start.3 = ((f32[8,54,384]{2,1,0:T(8,128)}), f32[8,54,384]{2,1,0:T(8,128)S(1)}, u32[]{:S(2)}, u32[]{:S(2)}) async-start(f32[8,54,384]{2,1,0:T(8,128)} %broadcast_in_dim.90), calls=%async_computation.3 | async-start | bytes 1376256 | tf_op jit(solution)/shard_map/all_to_all | solution.py:463
  (10 other events, 39.2 us)
Sparse Core Ops, SparseCore 0:
  10.5 50.2 all-gather.1

commit v10 on v9

--- a/solution.py
+++ b/solution.py
@@ -451,13 +451,13 @@
     in_got = lax.all_to_all(in_part.reshape(clips, in_rows // clips, chans), "clip", 0, 0, tiled=True)
     z_total = total
     smalls = [piece_rows(2 * third), piece_rows(third)]
+    depth_a = behind(depth_a, depth_b)
     factors, total = scales(depth_a, smalls[0], z_total)
-    in_sum = behind(in_got, depth_a).sum(axis=0)
-    in_sum = jnp.broadcast_to(in_sum[None], (lax.axis_size("tm"),) + in_sum.shape)
-    depth_b = behind(depth_b, in_sum)
-    in_got = lax.all_to_all(in_sum, "tm", 0, 0, tiled=True)
     last = spread([(own_a, depth_a), (own_b, depth_b)], smalls, factors, total)
     in_sum = behind(in_got, last[0]).sum(axis=0)
+    in_sum = jnp.broadcast_to(in_sum[None], (lax.axis_size("tm"),) + in_sum.shape)
+    in_got = lax.all_to_all(in_sum, "tm", 0, 0, tiled=True)
+    in_sum = in_got.sum(axis=0)
     in_sum = jnp.broadcast_to(in_sum[None], (clips,) + in_sum.shape)
     last[1:] = behind(last[1:], in_sum)
     grad_in = lax.all_to_all(in_sum, "clip", 0, 0, tiled=True).reshape(in_rows, chans)

time: 224 us -> 234 us (1.045)
  waiting for transfers between devices: 29.6 us -> 36.7 us
  starting transfers between devices: 49.9 us -> 52.8 us
    all_to_all x1, starting transfers between devices: 5.71 us -> 9.26 us  [shards(): in_got = lax.all_to_all(in_sum, 'tm', 0, 0, tiled=True)]
    all_to_all x1, waiting for transfers between devices: 0.12 us -> 2.76 us  [shards(): lax.all_to_all(in_part.reshape(clips, in_rows // clips, chans), 'clip', 0...]
    unnamed x44 -> x40, local copies, waits for them, and re-layouts: 11 us -> 11 us
  transfers between devices with their start and end apart: 25 -> 25, of which waited for: 9 -> 9; matrix products, arithmetic and copies ran while one was open for 17% -> 15% of each run, Pallas kernels for 28% -> 27%
where the time goes in v10:
time: 234 us; the launch traced here: 232 us
  Pallas kernels  79.1 us (34%)
  starting transfers between devices  52.8 us (23%)
  waiting for transfers between devices  36.7 us (16%)
  local copies, waits for them, and re-layouts  27.1 us (12%)
  other arithmetic  18.5 us (8%)
  between operations  17.6 us (8%)
    pallas_call x2, Pallas kernels, grad_chunk(): pl.pallas_call(lambda *refs: grad_kernel(*refs, units=units), grid_spec=p...  22.5 us
    pallas_call x2, Pallas kernels, front(): pl.pallas_call(lambda *refs: front_kernel(*refs, rows=rows, cols=cols, fi...  22.2 us
    ppermute x9, waiting for transfers between devices, around(): lax.ppermute(blocks, 'tm', [(i, (i + distance) % depth) for i in range(de...  19.7 us
    ppermute x9, starting transfers between devices, around(): lax.ppermute(blocks, 'tm', [(i, (i + distance) % depth) for i in range(de...  18 us
    pallas_call x1, Pallas kernels, back(): pl.pallas_call(lambda *refs: back_kernel(*refs, rows=rows, cols=cols), gr...  17.5 us
    pallas_call x1, Pallas kernels, middle(): pl.pallas_call(lambda *refs: middle_kernel(*refs, scale=scale), grid=(3,)...  16.8 us
    unnamed x40, local copies, waits for them, and re-layouts  11 us
    all_to_all x1, starting transfers between devices, shards(): in_got = lax.all_to_all(in_sum, 'tm', 0, 0, tiled=True)  9.26 us
  transfers between devices with their start and end apart: 25, of which 9 were waited for; matrix products, arithmetic and copies ran while one was open for 15% of the time, Pallas kernels for 27%

profile of v10, /device:TPU:0, one launch (start us, length us, event | category | flops | bytes accessed | tf_op | source)
XLA Modules:
  0.0 231.9 jit_solution(15295596334439523)
XLA Ops:
  7.2 2.0 slice.139
  10.3 3.0 %collective-permute-start.1 = (bf16[1296,128]{1,0:T(8,128)(2,1)S(1)}, bf16[1296,128]{1,0:T(8,128)(2,1)}, u32[]{:S(2)}, u32[]{:S(2)}) collective-permute-start(bf16[1296,128]{1,0:T(8,128)(2,1)S(1)} %slice.140), channel_id=1, source_target_pairs={{0,8},{4,12},{8,0},{12,4},{16,24},{20,28},{24,16},{28,20},{1,9},{5... | collective-permute-start | bytes 995336 | tf_op jit(solution)/shard_map/ppermute | solution.py:404
  13.3 1.5 collective-permute-start.2
  16.0 3.9 %collective-permute-start = (bf16[16,512]{1,0:T(8,128)(2,1)S(1)}, bf16[16,512]{1,0:T(8,128)(2,1)S(1)}, u32[]{:S(2)}, u32[]{:S(2)}) collective-permute-start(bf16[16,512]{1,0:T(8,128)(2,1)S(1)} %slice.184), channel_id=1, source_target_pairs={{0,1},{1,2},{2,3},{4,5},{5,6},{6,7},{8,9},{9,10},{10,11},{12,13},{... | collective-permute-start | bytes 49160 | tf_op jit(solution)/shard_map/ppermute | solution.py:19
  22.0 12.2 %front.2 = (bf16[432,1024]{1,0:T(8,128)(2,1)}, f32[1024,384]{1,0:T(8,128)}, bf16[3,10,10,16,384]{4,3,2,1,0:T(8,128)(2,1)}, bf16[27,384,1024]{2,1,0:T(8,128)(2,1)}, f32[384,128]{1,0:T(8,128)}) custom-call(bf16[16,1536]{1,0:T(8,128)(2,1)} %pad_maximum_fusion.refs_0_, bf16[432,384]{1,0:T(8,128)(2,1)} %refs_1_.3), custom_call_target="tpu_custom_call" | custom-call | tf_op jit(solution)/shard_map/front/pallas_call | solution.py:126
  37.2 1.7 constant_dynamic-update-slice_fusion.2
  40.9 1.6 reduce_max.18
  43.9 10.0 %front.3 = (bf16[27,384,1024]{2,1,0:T(8,128)(2,1)}, f32[384,128]{1,0:T(8,128)}) custom-call(bf16[16,1536]{1,0:T(8,128)(2,1)} %copy-done.14, bf16[432,384]{1,0:T(8,128)(2,1)} %refs_1_.3), custom_call_target="tpu_custom_call" | custom-call | tf_op jit(solution)/shard_map/front/pallas_call | solution.py:126
  53.9 1.6 reduce_max.19
  62.2 16.8 %middle.1 = (bf16[1040,384]{1,0:T(8,128)(2,1)}, bf16[256,384]{1,0:T(8,128)(2,1)}) custom-call(bf16[3,10,10,16,384]{4,3,2,1,0:T(8,128)(2,1)} %get-tuple-element.57.refs_0_, bf16[27,384,256]{2,1,0:T(8,128)(2,1)} %bitcast.49, bf16[27,384,128]{2,1,0:T(8,128)(2,1)} %bitcast.47, bf16[1024,384]{1,0:T(8,128)(2,1)} %bitcast.51), custom_call_target="tpu_custom_call" | custom-call | tf_op jit(solution)/shard_map/middle/pallas_call | solution.py:173
  80.0 1.5 collective-permute-start.7
  86.3 13.7 %grad.2 = (f32[912,384]{1,0:T(8,128)}, f32[4,912,384]{2,1,0:T(8,128)}) custom-call(s32[4]{0:T(128)} %fusion.12.refs_0_, bf16[10368,1024]{1,0:T(8,128)(2,1)} %bitcast.39, bf16[10368,1024]{1,0:T(8,128)(2,1)} %bitcast.43, bf16[10368,1024]{1,0:T(8,128)(2,1)} %bitcast.40, bf16[10368,1024]{1,0:T(8,128)(2,1)} %bitcast.44, ...), custom_call_target="tpu_custom_call" | custom-call | tf_op jit(solution)/shard_map/grad/pallas_call | solution.py:231
  100.0 4.1 %fusion = (f16[912,384]{1,0:T(8,128)(2,1)}, f16[912,384]{1,0:T(8,128)(2,1)}, f16[912,384]{1,0:T(8,128)(2,1)}) fusion(f32[4,912,384]{2,1,0:T(8,128)} %get-tuple-element.64, f32[]{:T(128)} %bitcast.11, f32[]{:T(128)} %bitcast.9, pred[912]{0:T(1024)(128)(4,1)S(1)} %iota_compare_fusion.1), kind=kLoop, calls=%fused_computation.2 | loop fusion | flops 3151872 | bytes 6304664 | tf_op jit(solution)/shard_map/convert_element_type | solution.py:311
  104.2 2.5 %collective-permute-start.10 = (f16[912,384]{1,0:T(8,128)(2,1)}, f16[912,384]{1,0:T(8,128)(2,1)S(1)}, u32[]{:S(2)}, u32[]{:S(2)}) collective-permute-start(f16[912,384]{1,0:T(8,128)(2,1)} %get-tuple-element.69), channel_id=1, source_target_pairs={{0,24},{4,28},{8,16},{12,20},{16,8},{20,12},{24,0},{28,4},{1,25},{... | collective-permute-start | bytes 2101256 | tf_op jit(solution)/shard_map/ppermute | solution.py:321
  108.0 8.8 %grad.3 = (f32[464,384]{1,0:T(8,128)}, f32[4,464,384]{2,1,0:T(8,128)}) custom-call(s32[4]{0:T(128)} %fusion.11.refs_0_, bf16[10368,1024]{1,0:T(8,128)(2,1)} %bitcast.41, bf16[10368,1024]{1,0:T(8,128)(2,1)} %bitcast.45, bf16[10368,1024]{1,0:T(8,128)(2,1)} %bitcast.42, bf16[10368,1024]{1,0:T(8,128)(2,1)} %bitcast.46, ...), custom_call_target="tpu_custom_call" | custom-call | tf_op jit(solution)/shard_map/grad/pallas_call | solution.py:231
  116.8 3.3 %select_convert_fusion = f16[4,464,384]{2,1,0:T(8,128)(2,1)} fusion(f32[4,464,384]{2,1,0:T(8,128)} %get-tuple-element.71, f32[]{:T(128)} %bitcast.11, f32[]{:T(128)} %bitcast.9, pred[464]{0:T(512)(128)(4,1)S(1)} %iota_compare_fusion.2), kind=kLoop, calls=%fused_computation | loop fusion | flops 2138112 | bytes 4276696 | tf_op jit(solution)/shard_map/convert_element_type | solution.py:311
  120.1 3.5 %all-to-all-start = ((f16[4,464,384]{2,1,0:T(8,128)(2,1)}), f16[4,464,384]{2,1,0:T(8,128)(2,1)S(1)}, u32[]{:S(2)}, u32[]{:S(2)}) async-start(f16[4,464,384]{2,1,0:T(8,128)(2,1)} %select_convert_fusion), calls=%async_computation | async-start | bytes 2850816 | tf_op jit(solution)/shard_map/all_to_all | solution.py:442
  123.7 17.5 %back.1 = f32[432,384]{1,0:T(8,128)} custom-call(bf16[1040,384]{1,0:T(8,128)(2,1)} %get-tuple-element.72.refs_5_.refs_0_, bf16[256,384]{1,0:T(8,128)(2,1)} %copy-done.12, bf16[27,384,256]{2,1,0:T(8,128)(2,1)} %bitcast.50, bf16[27,384,128]{2,1,0:T(8,128)(2,1)} %bitcast.48, f32[1024,384]{1,0:T(8,128)} %get-tuple-element.74.refs_4_, ...), custom_call_target="tpu_custom_call" | custom-call | tf_op jit(solution)/shard_map/back/pallas_call | solution.py:286
  142.8 2.6 %collective-permute-start.11 = (f16[240,384]{1,0:T(8,128)(2,1)}, f16[240,384]{1,0:T(8,128)(2,1)}, u32[]{:S(2)}, u32[]{:S(2)}) collective-permute-start(f16[240,384]{1,0:T(8,128)(2,1)} %get-tuple-element.102), channel_id=1, source_target_pairs={{0,1},{1,2},{2,3},{3,0},{4,5},{5,6},{6,7},{7,4},{8,9},{9,10},{10,1... | collective-permute-start | bytes 552968 | tf_op jit(solution)/shard_map/ppermute | solution.py:331
  145.4 2.8 %collective-permute-start.12 = (f16[240,384]{1,0:T(8,128)(2,1)}, f16[240,384]{1,0:T(8,128)(2,1)}, u32[]{:S(2)}, u32[]{:S(2)}) collective-permute-start(f16[240,384]{1,0:T(8,128)(2,1)} %get-tuple-element.101), channel_id=1, source_target_pairs={{0,2},{1,3},{2,0},{3,1},{4,6},{5,7},{6,4},{7,5},{8,10},{9,11},{10,... | collective-permute-start | bytes 552968 | tf_op jit(solution)/shard_map/ppermute | solution.py:331
  149.5 3.8 %all-to-all-done = f16[4,464,384]{2,1,0:T(8,128)(2,1)S(1)} async-done(((f16[4,464,384]{2,1,0:T(8,128)(2,1)}), f16[4,464,384]{2,1,0:T(8,128)(2,1)S(1)}, u32[]{:S(2)}, u32[]{:S(2)}) %all-to-all-start) | async-done | bytes 1425440 | tf_op jit(solution)/shard_map/all_to_all | solution.py:442
  153.9 2.4 %collective-permute-start.14 = (f16[128,384]{1,0:T(8,128)(2,1)S(1)}, f16[128,384]{1,0:T(8,128)(2,1)S(1)}, u32[]{:S(2)}, u32[]{:S(2)}) collective-permute-start(f16[128,384]{1,0:T(8,128)(2,1)S(1)} %get-tuple-element.103), channel_id=1, source_target_pairs={{0,1},{1,2},{2,3},{3,0},{4,5},{5,6},{6,7},{7,4},{8,9},{9,10},{10,1... | collective-permute-start | bytes 294920 | tf_op jit(solution)/shard_map/ppermute | solution.py:331
  156.4 2.8 %collective-permute-start.15 = (f16[128,384]{1,0:T(8,128)(2,1)S(1)}, f16[128,384]{1,0:T(8,128)(2,1)S(1)}, u32[]{:S(2)}, u32[]{:S(2)}) collective-permute-start(f16[128,384]{1,0:T(8,128)(2,1)S(1)} %get-tuple-element.104), channel_id=1, source_target_pairs={{0,2},{1,3},{2,0},{3,1},{4,6},{5,7},{6,4},{7,5},{8,10},{9,11},{10,... | collective-permute-start | bytes 294920 | tf_op jit(solution)/shard_map/ppermute | solution.py:331
  161.3 3.7 %all-to-all-start.1 = ((f32[8,54,384]{2,1,0:T(8,128)}), f32[8,54,384]{2,1,0:T(8,128)S(1)}, u32[]{:S(2)}, u32[]{:S(2)}) async-start(f32[8,54,384]{2,1,0:T(8,128)} %reshape.44), calls=%async_computation.1 | async-start | bytes 1376256 | tf_op jit(solution)/shard_map/all_to_all | solution.py:451
  165.1 5.1 %collective-permute-done.15 = f16[128,384]{1,0:T(8,128)(2,1)S(1)} collective-permute-done((f16[128,384]{1,0:T(8,128)(2,1)S(1)}, f16[128,384]{1,0:T(8,128)(2,1)S(1)}, u32[]{:S(2)}, u32[]{:S(2)}) %collective-permute-start.15) | collective-permute-done | bytes 98336 | tf_op jit(solution)/shard_map/ppermute | solution.py:331
  172.0 1.6 fusion.6
  173.8 2.8 %all-to-all-done.1 = f32[8,54,384]{2,1,0:T(8,128)S(1)} async-done(((f32[8,54,384]{2,1,0:T(8,128)}), f32[8,54,384]{2,1,0:T(8,128)S(1)}, u32[]{:S(2)}, u32[]{:S(2)}) %all-to-all-start.1) | async-done | bytes 663584 | tf_op jit(solution)/shard_map/all_to_all | solution.py:451
  177.3 9.3 %all-to-all-start.2 = ((f32[4,54,384]{2,1,0:T(8,128)}), f32[4,54,384]{2,1,0:T(8,128)S(1)}, u32[]{:S(2)}, u32[]{:S(2)}) async-start(f32[4,54,384]{2,1,0:T(8,128)} %broadcast_in_dim.89), calls=%async_computation.2 | async-start | bytes 688128 | tf_op jit(solution)/shard_map/all_to_all | solution.py:459
  186.6 3.8 %collective-permute-start.17 = (f16[352,384]{1,0:T(8,128)(2,1)S(1)}, f16[352,384]{1,0:T(8,128)(2,1)S(1)}, u32[]{:S(2)}, u32[]{:S(2)}) collective-permute-start(f16[352,384]{1,0:T(8,128)(2,1)S(1)} %fusion.5), channel_id=1, source_target_pairs={{0,3},{1,0},{2,1},{3,2},{4,7},{5,4},{6,5},{7,6},{8,11},{9,8},{10,9... | collective-permute-start | bytes 811016 | tf_op jit(solution)/shard_map/ppermute | solution.py:331
  191.6 7.1 %all-to-all-done.2 = f32[4,54,384]{2,1,0:T(8,128)S(1)} async-done(((f32[4,54,384]{2,1,0:T(8,128)}), f32[4,54,384]{2,1,0:T(8,128)S(1)}, u32[]{:S(2)}, u32[]{:S(2)}) %all-to-all-start.2) | async-done | bytes 331808 | tf_op jit(solution)/shard_map/all_to_all | solution.py:459
  199.6 3.5 %all-to-all-start.3 = ((f32[8,54,384]{2,1,0:T(8,128)}), f32[8,54,384]{2,1,0:T(8,128)S(1)}, u32[]{:S(2)}, u32[]{:S(2)}) async-start(f32[8,54,384]{2,1,0:T(8,128)} %broadcast_in_dim.90), calls=%async_computation.3 | async-start | bytes 1376256 | tf_op jit(solution)/shard_map/all_to_all | solution.py:463
  203.1 14.5 %collective-permute-done.18 = f16[352,384]{1,0:T(8,128)(2,1)S(1)} collective-permute-done((f16[352,384]{1,0:T(8,128)(2,1)S(1)}, f16[352,384]{1,0:T(8,128)(2,1)S(1)}, u32[]{:S(2)}, u32[]{:S(2)}) %collective-permute-start.18) | collective-permute-done | bytes 270368 | tf_op jit(solution)/shard_map/ppermute | solution.py:331
  (118 shorter events, 39.1 us)
Async XLA Ops:
  7.2 8.3 %copy-start = (bf16[1,8,8,32,16]{3,4,2,1,0:T(8,128)(2,1)S(1)}, bf16[1,8,8,32,16]{3,4,2,1,0:T(8,128)(2,1)}, u32[]{:S(2)}) copy-start(bf16[1,8,8,32,16]{3,4,2,1,0:T(8,128)(2,1)} %param.5) | copy-start | bytes 196612
  7.2 53.6 %all-gather.2.cloned.1.call-start = ((), (), s32[]{:S(2)}) async-start(), calls=%async_computation.4 | async-start | bytes 5971968 | tf_op jit(solution)/shard_map/all_gather | solution.py:400
  10.3 25.2 %copy-start.6 = (bf16[1296,128]{1,0:T(8,128)(2,1)}, bf16[1296,128]{1,0:T(8,128)(2,1)S(1)}, u32[]{:S(2)}) copy-start(bf16[1296,128]{1,0:T(8,128)(2,1)S(1)} %slice.140) | copy-start | bytes 995332
  10.3 24.0 %collective-permute-start.1 = (bf16[1296,128]{1,0:T(8,128)(2,1)S(1)}, bf16[1296,128]{1,0:T(8,128)(2,1)}, u32[]{:S(2)}, u32[]{:S(2)}) collective-permute-start(bf16[1296,128]{1,0:T(8,128)(2,1)S(1)} %slice.140), channel_id=1, source_target_pairs={{0,8},{4,12},{8,0},{12,4},{16,24},{20,28},{24,16},{28,20},{1,9},{5... | collective-permute-start | bytes 995336 | tf_op jit(solution)/shard_map/ppermute | solution.py:404
  13.3 21.0 %collective-permute-start.2 = (bf16[1296,128]{1,0:T(8,128)(2,1)S(1)}, bf16[1296,128]{1,0:T(8,128)(2,1)S(1)}, u32[]{:S(2)}, u32[]{:S(2)}) collective-permute-start(bf16[1296,128]{1,0:T(8,128)(2,1)S(1)} %slice.140), channel_id=1, source_target_pairs={{0,16},{4,20},{8,24},{12,28},{16,0},{20,4},{24,8},{28,12},{1,17},{... | collective-permute-start | bytes 995336 | tf_op jit(solution)/shard_map/ppermute | solution.py:404
  14.8 20.7 %collective-permute-start.3 = (bf16[1296,128]{1,0:T(8,128)(2,1)S(1)}, bf16[1296,128]{1,0:T(8,128)(2,1)S(1)}, u32[]{:S(2)}, u32[]{:S(2)}) collective-permute-start(bf16[1296,128]{1,0:T(8,128)(2,1)S(1)} %slice.140), channel_id=1, source_target_pairs={{0,24},{4,28},{8,16},{12,20},{16,8},{20,12},{24,0},{28,4},{1,25},{... | collective-permute-start | bytes 995336 | tf_op jit(solution)/shard_map/ppermute | solution.py:404
  16.0 5.4 %collective-permute-start = (bf16[16,512]{1,0:T(8,128)(2,1)S(1)}, bf16[16,512]{1,0:T(8,128)(2,1)S(1)}, u32[]{:S(2)}, u32[]{:S(2)}) collective-permute-start(bf16[16,512]{1,0:T(8,128)(2,1)S(1)} %slice.184), channel_id=1, source_target_pairs={{0,1},{1,2},{2,3},{4,5},{5,6},{6,7},{8,9},{9,10},{10,11},{12,13},{... | collective-permute-start | bytes 49160 | tf_op jit(solution)/shard_map/ppermute | solution.py:19
  40.4 15.0 %collective-permute-start.4 = (bf16[5184,128]{1,0:T(8,128)(2,1)}, bf16[5184,128]{1,0:T(8,128)(2,1)}, u32[]{:S(2)}, u32[]{:S(2)}) collective-permute-start(bf16[5184,128]{1,0:T(8,128)(2,1)} %constant_dynamic-update-slice_fusion), channel_id=1, source_target_pairs={{0,4},{4,0},{8,12},{12,8},{16,20},{20,16},{24,28},{28,24},{1,5},{5... | collective-permute-start | bytes 3981320 | tf_op jit(solution)/shard_map/ppermute | solution.py:23
  40.4 2.8 %collective-permute-start.5 = (bf16[16,1536]{1,0:T(8,128)(2,1)S(1)}, bf16[16,1536]{1,0:T(8,128)(2,1)S(1)}, u32[]{:S(2)}, u32[]{:S(2)}) collective-permute-start(bf16[16,1536]{1,0:T(8,128)(2,1)S(1)} %copy-done.11), channel_id=1, source_target_pairs={{0,4},{4,0},{8,12},{12,8},{16,20},{20,16},{24,28},{28,24},{1,5},{5... | collective-permute-start | bytes 147464 | tf_op jit(solution)/shard_map/ppermute | solution.py:23
  79.0 5.4 %collective-permute-start.6 = (bf16[1040,384]{1,0:T(8,128)(2,1)}, bf16[1040,384]{1,0:T(8,128)(2,1)S(1)}, u32[]{:S(2)}, u32[]{:S(2)}) collective-permute-start(bf16[1040,384]{1,0:T(8,128)(2,1)} %get-tuple-element.72.refs_5_.refs_0_), channel_id=1, source_target_pairs={{0,4},{4,0},{8,12},{12,8},{16,20},{20,16},{24,28},{28,24},{1,5},{5... | collective-permute-start | bytes 2396168 | tf_op jit(solution)/shard_map/ppermute | solution.py:23
  80.0 20.0 %collective-permute-start.7 = (bf16[256,384]{1,0:T(8,128)(2,1)}, bf16[256,384]{1,0:T(8,128)(2,1)S(1)}, u32[]{:S(2)}, u32[]{:S(2)}) collective-permute-start(bf16[256,384]{1,0:T(8,128)(2,1)} %get-tuple-element.63), channel_id=1, source_target_pairs={{1,0},{2,1},{3,2},{5,4},{6,5},{7,6},{9,8},{10,9},{11,10},{13,12},{... | collective-permute-start | bytes 589832 | tf_op jit(solution)/shard_map/ppermute | solution.py:19
  104.2 37.1 %collective-permute-start.10 = (f16[912,384]{1,0:T(8,128)(2,1)}, f16[912,384]{1,0:T(8,128)(2,1)S(1)}, u32[]{:S(2)}, u32[]{:S(2)}) collective-permute-start(f16[912,384]{1,0:T(8,128)(2,1)} %get-tuple-element.69), channel_id=1, source_target_pairs={{0,24},{4,28},{8,16},{12,20},{16,8},{20,12},{24,0},{28,4},{1,25},{... | collective-permute-start | bytes 2101256 | tf_op jit(solution)/shard_map/ppermute | solution.py:321
  106.6 34.7 %collective-permute-start.8 = (f16[912,384]{1,0:T(8,128)(2,1)}, f16[912,384]{1,0:T(8,128)(2,1)S(1)}, u32[]{:S(2)}, u32[]{:S(2)}) collective-permute-start(f16[912,384]{1,0:T(8,128)(2,1)} %get-tuple-element.67), channel_id=1, source_target_pairs={{0,8},{4,12},{8,0},{12,4},{16,24},{20,28},{24,16},{28,20},{1,9},{5... | collective-permute-start | bytes 2101256 | tf_op jit(solution)/shard_map/ppermute | solution.py:321
  106.6 34.7 %collective-permute-start.9 = (f16[912,384]{1,0:T(8,128)(2,1)}, f16[912,384]{1,0:T(8,128)(2,1)S(1)}, u32[]{:S(2)}, u32[]{:S(2)}) collective-permute-start(f16[912,384]{1,0:T(8,128)(2,1)} %get-tuple-element.68), channel_id=1, source_target_pairs={{0,16},{4,20},{8,24},{12,28},{16,0},{20,4},{24,8},{28,12},{1,17},{... | collective-permute-start | bytes 2101256 | tf_op jit(solution)/shard_map/ppermute | solution.py:321
  120.1 33.2 %all-to-all-start = ((f16[4,464,384]{2,1,0:T(8,128)(2,1)}), f16[4,464,384]{2,1,0:T(8,128)(2,1)S(1)}, u32[]{:S(2)}, u32[]{:S(2)}) async-start(f16[4,464,384]{2,1,0:T(8,128)(2,1)} %select_convert_fusion), calls=%async_computation | async-start | bytes 2850816 | tf_op jit(solution)/shard_map/all_to_all | solution.py:442
  123.7 17.7 %copy-start.5 = (f32[912,384]{1,0:T(8,128)S(1)}, f32[912,384]{1,0:T(8,128)}, u32[]{:S(2)}) copy-start(f32[912,384]{1,0:T(8,128)} %get-tuple-element.61) | copy-start | bytes 4202500
  141.3 6.9 %copy-start.8 = (f16[912,384]{1,0:T(8,128)(2,1)}, f16[912,384]{1,0:T(8,128)(2,1)S(1)}, u32[]{:S(2)}) copy-start(f16[912,384]{1,0:T(8,128)(2,1)S(1)} %collective-permute-done.10) | copy-start | bytes 2101252
  141.3 8.2 %copy-start.9 = (f16[912,384]{1,0:T(8,128)(2,1)}, f16[912,384]{1,0:T(8,128)(2,1)S(1)}, u32[]{:S(2)}) copy-start(f16[912,384]{1,0:T(8,128)(2,1)S(1)} %collective-permute-done.8) | copy-start | bytes 2101252
  141.3 8.1 %copy-start.10 = (f16[912,384]{1,0:T(8,128)(2,1)}, f16[912,384]{1,0:T(8,128)(2,1)S(1)}, u32[]{:S(2)}) copy-start(f16[912,384]{1,0:T(8,128)(2,1)S(1)} %collective-permute-done.9) | copy-start | bytes 2101252
  142.8 16.3 %collective-permute-start.11 = (f16[240,384]{1,0:T(8,128)(2,1)}, f16[240,384]{1,0:T(8,128)(2,1)}, u32[]{:S(2)}, u32[]{:S(2)}) collective-permute-start(f16[240,384]{1,0:T(8,128)(2,1)} %get-tuple-element.102), channel_id=1, source_target_pairs={{0,1},{1,2},{2,3},{3,0},{4,5},{5,6},{6,7},{7,4},{8,9},{9,10},{10,1... | collective-permute-start | bytes 552968 | tf_op jit(solution)/shard_map/ppermute | solution.py:331
  145.4 19.6 %collective-permute-start.12 = (f16[240,384]{1,0:T(8,128)(2,1)}, f16[240,384]{1,0:T(8,128)(2,1)}, u32[]{:S(2)}, u32[]{:S(2)}) collective-permute-start(f16[240,384]{1,0:T(8,128)(2,1)} %get-tuple-element.101), channel_id=1, source_target_pairs={{0,2},{1,3},{2,0},{3,1},{4,6},{5,7},{6,4},{7,5},{8,10},{9,11},{10,... | collective-permute-start | bytes 552968 | tf_op jit(solution)/shard_map/ppermute | solution.py:331
  148.2 12.2 %copy-start.4 = (f32[432,384]{1,0:T(8,128)S(1)}, f32[432,384]{1,0:T(8,128)}, u32[]{:S(2)}) copy-start(f32[432,384]{1,0:T(8,128)} %back.1) | copy-start | bytes 1990660
  148.2 16.8 %collective-permute-start.13 = (f16[240,384]{1,0:T(8,128)(2,1)}, f16[240,384]{1,0:T(8,128)(2,1)}, u32[]{:S(2)}, u32[]{:S(2)}) collective-permute-start(f16[240,384]{1,0:T(8,128)(2,1)} %get-tuple-element.100), channel_id=1, source_target_pairs={{0,3},{1,0},{2,1},{3,2},{4,7},{5,4},{6,5},{7,6},{8,11},{9,8},{10,9... | collective-permute-start | bytes 552968 | tf_op jit(solution)/shard_map/ppermute | solution.py:331
  153.9 11.1 %collective-permute-start.14 = (f16[128,384]{1,0:T(8,128)(2,1)S(1)}, f16[128,384]{1,0:T(8,128)(2,1)S(1)}, u32[]{:S(2)}, u32[]{:S(2)}) collective-permute-start(f16[128,384]{1,0:T(8,128)(2,1)S(1)} %get-tuple-element.103), channel_id=1, source_target_pairs={{0,1},{1,2},{2,3},{3,0},{4,5},{5,6},{6,7},{7,4},{8,9},{9,10},{10,1... | collective-permute-start | bytes 294920 | tf_op jit(solution)/shard_map/ppermute | solution.py:331
  156.4 13.8 %collective-permute-start.15 = (f16[128,384]{1,0:T(8,128)(2,1)S(1)}, f16[128,384]{1,0:T(8,128)(2,1)S(1)}, u32[]{:S(2)}, u32[]{:S(2)}) collective-permute-start(f16[128,384]{1,0:T(8,128)(2,1)S(1)} %get-tuple-element.104), channel_id=1, source_target_pairs={{0,2},{1,3},{2,0},{3,1},{4,6},{5,7},{6,4},{7,5},{8,10},{9,11},{10,... | collective-permute-start | bytes 294920 | tf_op jit(solution)/shard_map/ppermute | solution.py:331
  159.1 11.1 %collective-permute-start.16 = (f16[128,384]{1,0:T(8,128)(2,1)S(1)}, f16[128,384]{1,0:T(8,128)(2,1)S(1)}, u32[]{:S(2)}, u32[]{:S(2)}) collective-permute-start(f16[128,384]{1,0:T(8,128)(2,1)S(1)} %get-tuple-element.105), channel_id=1, source_target_pairs={{0,3},{1,0},{2,1},{3,2},{4,7},{5,4},{6,5},{7,6},{8,11},{9,8},{10,9... | collective-permute-start | bytes 294920 | tf_op jit(solution)/shard_map/ppermute | solution.py:331
  161.3 15.2 %all-to-all-start.1 = ((f32[8,54,384]{2,1,0:T(8,128)}), f32[8,54,384]{2,1,0:T(8,128)S(1)}, u32[]{:S(2)}, u32[]{:S(2)}) async-start(f32[8,54,384]{2,1,0:T(8,128)} %reshape.44), calls=%async_computation.1 | async-start | bytes 1376256 | tf_op jit(solution)/shard_map/all_to_all | solution.py:451
  177.3 21.3 %all-to-all-start.2 = ((f32[4,54,384]{2,1,0:T(8,128)}), f32[4,54,384]{2,1,0:T(8,128)S(1)}, u32[]{:S(2)}, u32[]{:S(2)}) async-start(f32[4,54,384]{2,1,0:T(8,128)} %broadcast_in_dim.89), calls=%async_computation.2 | async-start | bytes 688128 | tf_op jit(solution)/shard_map/all_to_all | solution.py:459
  186.6 16.5 %collective-permute-start.17 = (f16[352,384]{1,0:T(8,128)(2,1)S(1)}, f16[352,384]{1,0:T(8,128)(2,1)S(1)}, u32[]{:S(2)}, u32[]{:S(2)}) collective-permute-start(f16[352,384]{1,0:T(8,128)(2,1)S(1)} %fusion.5), channel_id=1, source_target_pairs={{0,3},{1,0},{2,1},{3,2},{4,7},{5,4},{6,5},{7,6},{8,11},{9,8},{10,9... | collective-permute-start | bytes 811016 | tf_op jit(solution)/shard_map/ppermute | solution.py:331
  190.4 27.2 %collective-permute-start.18 = (f16[352,384]{1,0:T(8,128)(2,1)S(1)}, f16[352,384]{1,0:T(8,128)(2,1)S(1)}, u32[]{:S(2)}, u32[]{:S(2)}) collective-permute-start(f16[352,384]{1,0:T(8,128)(2,1)S(1)} %fusion.5), channel_id=1, source_target_pairs={{0,2},{1,3},{2,0},{3,1},{4,6},{5,7},{6,4},{7,5},{8,10},{9,11},{10,... | collective-permute-start | bytes 811016 | tf_op jit(solution)/shard_map/ppermute | solution.py:331
  190.4 27.2 %collective-permute-start.19 = (f16[352,384]{1,0:T(8,128)(2,1)S(1)}, f16[352,384]{1,0:T(8,128)(2,1)S(1)}, u32[]{:S(2)}, u32[]{:S(2)}) collective-permute-start(f16[352,384]{1,0:T(8,128)(2,1)S(1)} %fusion.5), channel_id=1, source_target_pairs={{0,1},{1,2},{2,3},{3,0},{4,5},{5,6},{6,7},{7,4},{8,9},{9,10},{10,1... | collective-permute-start | bytes 811016 | tf_op jit(solution)/shard_map/ppermute | solution.py:331
  199.6 24.5 %all-to-all-start.3 = ((f32[8,54,384]{2,1,0:T(8,128)}), f32[8,54,384]{2,1,0:T(8,128)S(1)}, u32[]{:S(2)}, u32[]{:S(2)}) async-start(f32[8,54,384]{2,1,0:T(8,128)} %broadcast_in_dim.90), calls=%async_computation.3 | async-start | bytes 1376256 | tf_op jit(solution)/shard_map/all_to_all | solution.py:463
  (8 other events, 19.8 us)
Sparse Core Ops, SparseCore 0:
  10.5 50.2 all-gather.1

commit v11 on v9

--- a/solution.py
+++ b/solution.py
@@ -432,25 +432,25 @@
     in_rows = patch_t.shape[0]
 
     chips = jnp.arange(clips // 2, dtype=jnp.int32)
-    own_a, part = grad_chunk(me ^ (2 * chips), both, (g, pair_g), 0, 2)
+    own_a, part = grad_chunk(me ^ (2 * chips), both, (g, pair_g), 0, 1)
     part, later = lax.optimization_barrier((part, later))
-    got_a, g = across_plane(part, 2 * third, bound, g)
-    _, part = grad_chunk(2 * chips + me % 2, both, (g, pair_g), 2, 1)
-    payload = packed(part, third, bound)
+    got_a, g = across_plane(part, third, bound, g)
+    _, part = grad_chunk(2 * chips + me % 2, both, (g, pair_g), 1, 2)
+    payload = packed(behind(part, got_a), 2 * third, bound)
     payload, g = lax.optimization_barrier((payload, g))
     groups = [[2 * p + core for p in range(clips // 2)] for core in range(2)]
     got_b = lax.all_to_all(payload, "clip", 0, 0, axis_index_groups=groups, tiled=True)
     got_b = [got_b[p] for p in range(clips // 2)]
+    got_a = behind(got_a, payload)
+    factors, total = scales(got_a, third, bound)
+    (own_a, depth_a), g = across_depth(own_a, got_a, third, factors, total, g)
     in_part = back(g, later, wide, thin, z, patch_t, rows, cols)
-
-    got_a = behind(got_a, in_part)
-    factors, total = scales(got_a, 2 * third, bound)
-    (own_a, depth_a), got_b = across_depth(own_a, got_a, 2 * third, factors, total, got_b)
-    factors, _ = scales(got_b, third, 0.0)
-    (own_b, depth_b), in_part = across_depth(None, got_b, third, factors, total, in_part)
+    got_b = behind(got_b, in_part)
+    factors, _ = scales(got_b, 2 * third, 0.0)
+    (own_b, depth_b), in_part = across_depth(None, got_b, 2 * third, factors, total, in_part)
     in_got = lax.all_to_all(in_part.reshape(clips, in_rows // clips, chans), "clip", 0, 0, tiled=True)
     z_total = total
-    smalls = [piece_rows(2 * third), piece_rows(third)]
+    smalls = [piece_rows(third), piece_rows(2 * third)]
     factors, total = scales(depth_a, smalls[0], z_total)
     in_sum = behind(in_got, depth_a).sum(axis=0)
     in_sum = jnp.broadcast_to(in_sum[None], (lax.axis_size("tm"),) + in_sum.shape)
@@ -462,7 +462,7 @@
     last[1:] = behind(last[1:], in_sum)
     grad_in = lax.all_to_all(in_sum, "clip", 0, 0, tiled=True).reshape(in_rows, chans)
     factors, _ = scales(last, sum(smalls), 0.0)
-    pieces = assembled(last, factors, smalls, [2 * third, third])
+    pieces = assembled(last, factors, smalls, [third, 2 * third])
     return (jnp.concatenate(pieces, axis=0), grad_in)
 
 

time: 224 us -> 233 us (1.040)
  starting transfers between devices: 49.9 us -> 56 us
  waiting for transfers between devices: 29.6 us -> 32.5 us
    all_to_all x1, waiting for transfers between devices: 6.14 us -> 0.01 us  [shards(): in_got = lax.all_to_all(in_sum, 'tm', 0, 0, tiled=True)]
    ppermute x9, starting transfers between devices: 18.6 us -> 23.7 us  [around(): lax.ppermute(blocks, 'tm', [(i, (i + distance) % depth) for i in range(de...]
    all_to_all x1, waiting for transfers between devices: 2.4 us -> 6.65 us  [shards(): lax.all_to_all(payload, 'clip', 0, 0, axis_index_groups=groups, tiled=True)]
    all_to_all x1, waiting for transfers between devices: 0.12 us -> 2.85 us  [shards(): lax.all_to_all(in_part.reshape(clips, in_rows // clips, chans), 'clip', 0...]
    unnamed x44 -> x52, local copies, waits for them, and re-layouts: 11 us -> 10.9 us
  transfers between devices with their start and end apart: 25 -> 25, of which waited for: 9 -> 10; matrix products, arithmetic and copies ran while one was open for 17% -> 14% of each run, Pallas kernels for 28% -> 27%
where the time goes in v11:
time: 233 us; the launch traced here: 232 us
  Pallas kernels  79.1 us (34%)
  starting transfers between devices  56 us (24%)
  waiting for transfers between devices  32.5 us (14%)
  local copies, waits for them, and re-layouts  28.5 us (12%)
  other arithmetic  18.3 us (8%)
  between operations  17.8 us (8%)
    ppermute x9, starting transfers between devices, around(): lax.ppermute(blocks, 'tm', [(i, (i + distance) % depth) for i in range(de...  23.7 us
    pallas_call x2, Pallas kernels, grad_chunk(): pl.pallas_call(lambda *refs: grad_kernel(*refs, units=units), grid_spec=p...  22.6 us
    pallas_call x2, Pallas kernels, front(): pl.pallas_call(lambda *refs: front_kernel(*refs, rows=rows, cols=cols, fi...  22.3 us
    ppermute x9, waiting for transfers between devices, around(): lax.ppermute(blocks, 'tm', [(i, (i + distance) % depth) for i in range(de...  18.1 us
    pallas_call x1, Pallas kernels, back(): pl.pallas_call(lambda *refs: back_kernel(*refs, rows=rows, cols=cols), gr...  17.4 us
    pallas_call x1, Pallas kernels, middle(): pl.pallas_call(lambda *refs: middle_kernel(*refs, scale=scale), grid=(3,)...  16.8 us
    unnamed x52, local copies, waits for them, and re-layouts  10.9 us
    convert_element_type x5, other arithmetic, packed(): return jnp.where(row < rows, x * jnp.exp2(14.0 - power), power).astype(F16)  9.25 us
  transfers between devices with their start and end apart: 25, of which 10 were waited for; matrix products, arithmetic and copies ran while one was open for 14% of the time, Pallas kernels for 27%

profile of v11, /device:TPU:0, one launch (start us, length us, event | category | flops | bytes accessed | tf_op | source)
XLA Modules:
  0.0 232.2 jit_solution(7224437770976456630)
XLA Ops:
  7.2 2.0 slice.139
  10.3 3.0 %collective-permute-start.1 = (bf16[1296,128]{1,0:T(8,128)(2,1)S(1)}, bf16[1296,128]{1,0:T(8,128)(2,1)S(1)}, u32[]{:S(2)}, u32[]{:S(2)}) collective-permute-start(bf16[1296,128]{1,0:T(8,128)(2,1)S(1)} %slice.140), channel_id=1, source_target_pairs={{0,8},{4,12},{8,0},{12,4},{16,24},{20,28},{24,16},{28,20},{1,9},{5... | collective-permute-start | bytes 995336 | tf_op jit(solution)/shard_map/ppermute | solution.py:404
  13.3 1.5 collective-permute-start.2
  16.0 3.9 %collective-permute-start = (bf16[16,512]{1,0:T(8,128)(2,1)S(1)}, bf16[16,512]{1,0:T(8,128)(2,1)S(1)}, u32[]{:S(2)}, u32[]{:S(2)}) collective-permute-start(bf16[16,512]{1,0:T(8,128)(2,1)S(1)} %slice.184), channel_id=1, source_target_pairs={{0,1},{1,2},{2,3},{4,5},{5,6},{6,7},{8,9},{9,10},{10,11},{12,13},{... | collective-permute-start | bytes 49160 | tf_op jit(solution)/shard_map/ppermute | solution.py:19
  20.0 1.4 collective-permute-done
  22.0 12.2 %front.2 = (bf16[432,1024]{1,0:T(8,128)(2,1)}, f32[1024,384]{1,0:T(8,128)}, bf16[3,10,10,16,384]{4,3,2,1,0:T(8,128)(2,1)}, bf16[27,384,1024]{2,1,0:T(8,128)(2,1)}, f32[384,128]{1,0:T(8,128)}) custom-call(bf16[16,1536]{1,0:T(8,128)(2,1)} %pad_maximum_fusion.refs_0_, bf16[432,384]{1,0:T(8,128)(2,1)} %refs_1_.3), custom_call_target="tpu_custom_call" | custom-call | tf_op jit(solution)/shard_map/front/pallas_call | solution.py:126
  40.7 1.5 collective-permute-done.5.refs_0_
  42.9 10.1 %front.3 = (bf16[27,384,1024]{2,1,0:T(8,128)(2,1)}, f32[384,128]{1,0:T(8,128)}) custom-call(bf16[16,1536]{1,0:T(8,128)(2,1)} %copy-done.20, bf16[432,384]{1,0:T(8,128)(2,1)} %refs_1_.3), custom_call_target="tpu_custom_call" | custom-call | tf_op jit(solution)/shard_map/front/pallas_call | solution.py:126
  52.9 1.6 reduce_max.19
  60.8 1.5 copy-done.2
  62.2 16.8 %middle.1 = (bf16[1040,384]{1,0:T(8,128)(2,1)}, bf16[256,384]{1,0:T(8,128)(2,1)}) custom-call(bf16[3,10,10,16,384]{4,3,2,1,0:T(8,128)(2,1)} %get-tuple-element.60.refs_0_, bf16[27,384,256]{2,1,0:T(8,128)(2,1)} %bitcast.49, bf16[27,384,128]{2,1,0:T(8,128)(2,1)} %bitcast.47, bf16[1024,384]{1,0:T(8,128)(2,1)} %bitcast.51), custom_call_target="tpu_custom_call" | custom-call | tf_op jit(solution)/shard_map/middle/pallas_call | solution.py:173
  79.5 1.5 collective-permute-start.7
  86.2 8.9 %grad.2 = (f32[464,384]{1,0:T(8,128)}, f32[4,464,384]{2,1,0:T(8,128)}) custom-call(s32[4]{0:T(128)} %fusion.18.refs_0_, bf16[10368,1024]{1,0:T(8,128)(2,1)} %bitcast.39, bf16[10368,1024]{1,0:T(8,128)(2,1)} %bitcast.43, bf16[10368,1024]{1,0:T(8,128)(2,1)} %bitcast.40, bf16[10368,1024]{1,0:T(8,128)(2,1)} %bitcast.44, ...), custom_call_target="tpu_custom_call" | custom-call | tf_op jit(solution)/shard_map/grad/pallas_call | solution.py:231
  95.1 1.9 fusion
  97.0 2.6 %collective-permute-start.10 = (f16[464,384]{1,0:T(8,128)(2,1)S(1)}, f16[464,384]{1,0:T(8,128)(2,1)S(1)}, u32[]{:S(2)}, u32[]{:S(2)}) collective-permute-start(f16[464,384]{1,0:T(8,128)(2,1)S(1)} %get-tuple-element.72), channel_id=1, source_target_pairs={{0,24},{4,28},{8,16},{12,20},{16,8},{20,12},{24,0},{28,4},{1,25},{... | collective-permute-start | bytes 1069064 | tf_op jit(solution)/shard_map/ppermute | solution.py:321
  101.5 13.7 %grad.3 = (f32[912,384]{1,0:T(8,128)}, f32[4,912,384]{2,1,0:T(8,128)}) custom-call(s32[4]{0:T(128)} %fusion.17.refs_0_, bf16[10368,1024]{1,0:T(8,128)(2,1)} %bitcast.41, bf16[10368,1024]{1,0:T(8,128)(2,1)} %bitcast.45, bf16[10368,1024]{1,0:T(8,128)(2,1)} %bitcast.42, bf16[10368,1024]{1,0:T(8,128)(2,1)} %bitcast.46, ...), custom_call_target="tpu_custom_call" | custom-call | tf_op jit(solution)/shard_map/grad/pallas_call | solution.py:231
  115.9 5.0 %select_convert_fusion = f16[4,912,384]{2,1,0:T(8,128)(2,1)} fusion(f32[4,912,384]{2,1,0:T(8,128)} %get-tuple-element.75, f32[]{:T(128)} %bitcast.11, f32[]{:T(128)} %bitcast.9, pred[912]{0:T(1024)(128)(4,1)S(1)} %iota_compare_fusion.1), kind=kLoop, calls=%fused_computation | loop fusion | flops 4202496 | bytes 8405912 | tf_op jit(solution)/shard_map/convert_element_type | solution.py:311
  121.0 3.9 %all-to-all-start = ((f16[4,912,384]{2,1,0:T(8,128)(2,1)}), f16[4,912,384]{2,1,0:T(8,128)(2,1)S(1)}, u32[]{:S(2)}, u32[]{:S(2)}) async-start(f16[4,912,384]{2,1,0:T(8,128)(2,1)} %select_convert_fusion), calls=%async_computation | async-start | bytes 5603328 | tf_op jit(solution)/shard_map/all_to_all | solution.py:442
  125.6 1.6 select_convert_fusion.4
  127.3 2.8 %collective-permute-start.11 = (f16[128,384]{1,0:T(8,128)(2,1)S(1)}, f16[128,384]{1,0:T(8,128)(2,1)}, u32[]{:S(2)}, u32[]{:S(2)}) collective-permute-start(f16[128,384]{1,0:T(8,128)(2,1)S(1)} %get-tuple-element.115), channel_id=1, source_target_pairs={{0,1},{1,2},{2,3},{3,0},{4,5},{5,6},{6,7},{7,4},{8,9},{9,10},{10,1... | collective-permute-start | bytes 294920 | tf_op jit(solution)/shard_map/ppermute | solution.py:331
  130.0 2.7 %collective-permute-start.12 = (f16[128,384]{1,0:T(8,128)(2,1)S(1)}, f16[128,384]{1,0:T(8,128)(2,1)}, u32[]{:S(2)}, u32[]{:S(2)}) collective-permute-start(f16[128,384]{1,0:T(8,128)(2,1)S(1)} %get-tuple-element.114), channel_id=1, source_target_pairs={{0,2},{1,3},{2,0},{3,1},{4,6},{5,7},{6,4},{7,5},{8,10},{9,11},{10,... | collective-permute-start | bytes 294920 | tf_op jit(solution)/shard_map/ppermute | solution.py:331
  134.1 17.4 %back.1 = f32[432,384]{1,0:T(8,128)} custom-call(bf16[1040,384]{1,0:T(8,128)(2,1)} %get-tuple-element.81.refs_5_.refs_0_, bf16[256,384]{1,0:T(8,128)(2,1)} %copy-done.19, bf16[27,384,256]{2,1,0:T(8,128)(2,1)} %bitcast.50, bf16[27,384,128]{2,1,0:T(8,128)(2,1)} %bitcast.48, f32[1024,384]{1,0:T(8,128)} %get-tuple-element.83.refs_4_, ...), custom_call_target="tpu_custom_call" | custom-call | tf_op jit(solution)/shard_map/back/pallas_call | solution.py:286
  151.6 6.6 %all-to-all-done = f16[4,912,384]{2,1,0:T(8,128)(2,1)S(1)} async-done(((f16[4,912,384]{2,1,0:T(8,128)(2,1)}), f16[4,912,384]{2,1,0:T(8,128)(2,1)S(1)}, u32[]{:S(2)}, u32[]{:S(2)}) %all-to-all-start) | async-done | bytes 2801696 | tf_op jit(solution)/shard_map/all_to_all | solution.py:442
  161.4 3.5 %all-to-all-start.1 = ((f32[8,54,384]{2,1,0:T(8,128)}), f32[8,54,384]{2,1,0:T(8,128)S(1)}, u32[]{:S(2)}, u32[]{:S(2)}) async-start(f32[8,54,384]{2,1,0:T(8,128)} %reshape.44), calls=%async_computation.1 | async-start | bytes 1376256 | tf_op jit(solution)/shard_map/all_to_all | solution.py:451
  165.7 2.4 %collective-permute-start.14 = (f16[240,384]{1,0:T(8,128)(2,1)S(1)}, f16[240,384]{1,0:T(8,128)(2,1)S(1)}, u32[]{:S(2)}, u32[]{:S(2)}) collective-permute-start(f16[240,384]{1,0:T(8,128)(2,1)S(1)} %get-tuple-element.108), channel_id=1, source_target_pairs={{0,1},{1,2},{2,3},{3,0},{4,5},{5,6},{6,7},{7,4},{8,9},{9,10},{10,1... | collective-permute-start | bytes 552968 | tf_op jit(solution)/shard_map/ppermute | solution.py:331
  168.2 2.8 %collective-permute-start.15 = (f16[240,384]{1,0:T(8,128)(2,1)S(1)}, f16[240,384]{1,0:T(8,128)(2,1)S(1)}, u32[]{:S(2)}, u32[]{:S(2)}) collective-permute-start(f16[240,384]{1,0:T(8,128)(2,1)S(1)} %get-tuple-element.107), channel_id=1, source_target_pairs={{0,2},{1,3},{2,0},{3,1},{4,6},{5,7},{6,4},{7,5},{8,10},{9,11},{10,... | collective-permute-start | bytes 552968 | tf_op jit(solution)/shard_map/ppermute | solution.py:331
  173.5 2.9 %all-to-all-done.1 = f32[8,54,384]{2,1,0:T(8,128)S(1)} async-done(((f32[8,54,384]{2,1,0:T(8,128)}), f32[8,54,384]{2,1,0:T(8,128)S(1)}, u32[]{:S(2)}, u32[]{:S(2)}) %all-to-all-start.1) | async-done | bytes 663584 | tf_op jit(solution)/shard_map/all_to_all | solution.py:451
  177.1 5.8 %all-to-all-start.2 = ((f32[4,54,384]{2,1,0:T(8,128)}), f32[4,54,384]{2,1,0:T(8,128)S(1)}, u32[]{:S(2)}, u32[]{:S(2)}) async-start(f32[4,54,384]{2,1,0:T(8,128)} %broadcast_in_dim.87), calls=%async_computation.2 | async-start | bytes 688128 | tf_op jit(solution)/shard_map/all_to_all | solution.py:458
  183.6 1.4 add_add_fusion
  185.1 9.7 %collective-permute-start.17 = (f16[352,384]{1,0:T(8,128)(2,1)S(1)}, f16[352,384]{1,0:T(8,128)(2,1)S(1)}, u32[]{:S(2)}, u32[]{:S(2)}) collective-permute-start(f16[352,384]{1,0:T(8,128)(2,1)S(1)} %fusion.5), channel_id=1, source_target_pairs={{0,3},{1,0},{2,1},{3,2},{4,7},{5,4},{6,5},{7,6},{8,11},{9,8},{10,9... | collective-permute-start | bytes 811016 | tf_op jit(solution)/shard_map/ppermute | solution.py:331
  196.4 4.2 %all-to-all-start.3 = ((f32[8,54,384]{2,1,0:T(8,128)}), f32[8,54,384]{2,1,0:T(8,128)S(1)}, u32[]{:S(2)}, u32[]{:S(2)}) async-start(f32[8,54,384]{2,1,0:T(8,128)} %broadcast_in_dim.90), calls=%async_computation.3 | async-start | bytes 1376256 | tf_op jit(solution)/shard_map/all_to_all | solution.py:463
  201.8 16.2 %collective-permute-done.18 = f16[352,384]{1,0:T(8,128)(2,1)S(1)} collective-permute-done((f16[352,384]{1,0:T(8,128)(2,1)S(1)}, f16[352,384]{1,0:T(8,128)(2,1)S(1)}, u32[]{:S(2)}, u32[]{:S(2)}) %collective-permute-start.18) | collective-permute-done | bytes 270368 | tf_op jit(solution)/shard_map/ppermute | solution.py:331
  (130 shorter events, 41.3 us)
Async XLA Ops:
  7.2 8.3 %copy-start = (bf16[1,8,8,32,16]{3,4,2,1,0:T(8,128)(2,1)S(1)}, bf16[1,8,8,32,16]{3,4,2,1,0:T(8,128)(2,1)}, u32[]{:S(2)}) copy-start(bf16[1,8,8,32,16]{3,4,2,1,0:T(8,128)(2,1)} %param.5) | copy-start | bytes 196612
  7.2 53.6 %all-gather.2.cloned.1.call-start = ((), (), s32[]{:S(2)}) async-start(), calls=%async_computation.4 | async-start | bytes 5971968 | tf_op jit(solution)/shard_map/all_gather | solution.py:400
  10.3 25.2 %copy-start.13 = (bf16[1296,128]{1,0:T(8,128)(2,1)}, bf16[1296,128]{1,0:T(8,128)(2,1)S(1)}, u32[]{:S(2)}) copy-start(bf16[1296,128]{1,0:T(8,128)(2,1)S(1)} %slice.140) | copy-start | bytes 995332
  10.3 24.0 %collective-permute-start.1 = (bf16[1296,128]{1,0:T(8,128)(2,1)S(1)}, bf16[1296,128]{1,0:T(8,128)(2,1)S(1)}, u32[]{:S(2)}, u32[]{:S(2)}) collective-permute-start(bf16[1296,128]{1,0:T(8,128)(2,1)S(1)} %slice.140), channel_id=1, source_target_pairs={{0,8},{4,12},{8,0},{12,4},{16,24},{20,28},{24,16},{28,20},{1,9},{5... | collective-permute-start | bytes 995336 | tf_op jit(solution)/shard_map/ppermute | solution.py:404
  13.3 21.0 %collective-permute-start.2 = (bf16[1296,128]{1,0:T(8,128)(2,1)S(1)}, bf16[1296,128]{1,0:T(8,128)(2,1)S(1)}, u32[]{:S(2)}, u32[]{:S(2)}) collective-permute-start(bf16[1296,128]{1,0:T(8,128)(2,1)S(1)} %slice.140), channel_id=1, source_target_pairs={{0,16},{4,20},{8,24},{12,28},{16,0},{20,4},{24,8},{28,12},{1,17},{... | collective-permute-start | bytes 995336 | tf_op jit(solution)/shard_map/ppermute | solution.py:404
  14.8 20.7 %collective-permute-start.3 = (bf16[1296,128]{1,0:T(8,128)(2,1)S(1)}, bf16[1296,128]{1,0:T(8,128)(2,1)S(1)}, u32[]{:S(2)}, u32[]{:S(2)}) collective-permute-start(bf16[1296,128]{1,0:T(8,128)(2,1)S(1)} %slice.140), channel_id=1, source_target_pairs={{0,24},{4,28},{8,16},{12,20},{16,8},{20,12},{24,0},{28,4},{1,25},{... | collective-permute-start | bytes 995336 | tf_op jit(solution)/shard_map/ppermute | solution.py:404
  16.0 5.4 %collective-permute-start = (bf16[16,512]{1,0:T(8,128)(2,1)S(1)}, bf16[16,512]{1,0:T(8,128)(2,1)S(1)}, u32[]{:S(2)}, u32[]{:S(2)}) collective-permute-start(bf16[16,512]{1,0:T(8,128)(2,1)S(1)} %slice.184), channel_id=1, source_target_pairs={{0,1},{1,2},{2,3},{4,5},{5,6},{6,7},{8,9},{9,10},{10,11},{12,13},{... | collective-permute-start | bytes 49160 | tf_op jit(solution)/shard_map/ppermute | solution.py:19
  36.4 3.6 %copy-start.18 = (f32[384,128]{1,0:T(8,128)S(1)}, f32[384,128]{1,0:T(8,128)}, u32[]{:S(2)}) copy-start(f32[384,128]{1,0:T(8,128)} %get-tuple-element.51) | copy-start | bytes 589828
  39.5 15.0 %collective-permute-start.4 = (bf16[5184,128]{1,0:T(8,128)(2,1)}, bf16[5184,128]{1,0:T(8,128)(2,1)}, u32[]{:S(2)}, u32[]{:S(2)}) collective-permute-start(bf16[5184,128]{1,0:T(8,128)(2,1)} %constant_dynamic-update-slice_fusion), channel_id=1, source_target_pairs={{0,4},{4,0},{8,12},{12,8},{16,20},{20,16},{24,28},{28,24},{1,5},{5... | collective-permute-start | bytes 3981320 | tf_op jit(solution)/shard_map/ppermute | solution.py:23
  39.5 2.8 %collective-permute-start.5 = (bf16[16,1536]{1,0:T(8,128)(2,1)S(1)}, bf16[16,1536]{1,0:T(8,128)(2,1)S(1)}, u32[]{:S(2)}, u32[]{:S(2)}) collective-permute-start(bf16[16,1536]{1,0:T(8,128)(2,1)S(1)} %copy-done.17), channel_id=1, source_target_pairs={{0,4},{4,0},{8,12},{12,8},{16,20},{20,16},{24,28},{28,24},{1,5},{5... | collective-permute-start | bytes 147464 | tf_op jit(solution)/shard_map/ppermute | solution.py:23
  79.1 5.1 %collective-permute-start.6 = (bf16[1040,384]{1,0:T(8,128)(2,1)}, bf16[1040,384]{1,0:T(8,128)(2,1)S(1)}, u32[]{:S(2)}, u32[]{:S(2)}) collective-permute-start(bf16[1040,384]{1,0:T(8,128)(2,1)} %get-tuple-element.81.refs_5_.refs_0_), channel_id=1, source_target_pairs={{0,4},{4,0},{8,12},{12,8},{16,20},{20,16},{24,28},{28,24},{1,5},{5... | collective-permute-start | bytes 2396168 | tf_op jit(solution)/shard_map/ppermute | solution.py:23
  79.5 15.6 %collective-permute-start.7 = (bf16[256,384]{1,0:T(8,128)(2,1)}, bf16[256,384]{1,0:T(8,128)(2,1)S(1)}, u32[]{:S(2)}, u32[]{:S(2)}) collective-permute-start(bf16[256,384]{1,0:T(8,128)(2,1)} %get-tuple-element.66), channel_id=1, source_target_pairs={{1,0},{2,1},{3,2},{5,4},{6,5},{7,6},{9,8},{10,9},{11,10},{13,12},{... | collective-permute-start | bytes 589832 | tf_op jit(solution)/shard_map/ppermute | solution.py:19
  95.0 20.2 %copy-start.19 = (bf16[256,384]{1,0:T(8,128)(2,1)}, bf16[256,384]{1,0:T(8,128)(2,1)S(1)}, u32[]{:S(2)}) copy-start(bf16[256,384]{1,0:T(8,128)(2,1)S(1)} %collective-permute-done.7.refs_1_) | copy-start | bytes 589828
  97.0 18.2 %collective-permute-start.10 = (f16[464,384]{1,0:T(8,128)(2,1)S(1)}, f16[464,384]{1,0:T(8,128)(2,1)S(1)}, u32[]{:S(2)}, u32[]{:S(2)}) collective-permute-start(f16[464,384]{1,0:T(8,128)(2,1)S(1)} %get-tuple-element.72), channel_id=1, source_target_pairs={{0,24},{4,28},{8,16},{12,20},{16,8},{20,12},{24,0},{28,4},{1,25},{... | collective-permute-start | bytes 1069064 | tf_op jit(solution)/shard_map/ppermute | solution.py:321
  99.5 16.3 %collective-permute-start.8 = (f16[464,384]{1,0:T(8,128)(2,1)S(1)}, f16[464,384]{1,0:T(8,128)(2,1)S(1)}, u32[]{:S(2)}, u32[]{:S(2)}) collective-permute-start(f16[464,384]{1,0:T(8,128)(2,1)S(1)} %get-tuple-element.70), channel_id=1, source_target_pairs={{0,8},{4,12},{8,0},{12,4},{16,24},{20,28},{24,16},{28,20},{1,9},{5... | collective-permute-start | bytes 1069064 | tf_op jit(solution)/shard_map/ppermute | solution.py:321
  99.8 16.1 %collective-permute-start.9 = (f16[464,384]{1,0:T(8,128)(2,1)S(1)}, f16[464,384]{1,0:T(8,128)(2,1)S(1)}, u32[]{:S(2)}, u32[]{:S(2)}) collective-permute-start(f16[464,384]{1,0:T(8,128)(2,1)S(1)} %get-tuple-element.71), channel_id=1, source_target_pairs={{0,16},{4,20},{8,24},{12,28},{16,0},{20,4},{24,8},{28,12},{1,17},{... | collective-permute-start | bytes 1069064 | tf_op jit(solution)/shard_map/ppermute | solution.py:321
  115.8 5.1 %copy-start.15 = (f16[464,384]{1,0:T(8,128)(2,1)}, f16[464,384]{1,0:T(8,128)(2,1)S(1)}, u32[]{:S(2)}) copy-start(f16[464,384]{1,0:T(8,128)(2,1)S(1)} %collective-permute-done.8) | copy-start | bytes 1069060
  115.9 5.0 %copy-start.16 = (f16[464,384]{1,0:T(8,128)(2,1)}, f16[464,384]{1,0:T(8,128)(2,1)S(1)}, u32[]{:S(2)}) copy-start(f16[464,384]{1,0:T(8,128)(2,1)S(1)} %collective-permute-done.9) | copy-start | bytes 1069060
  121.0 37.2 %all-to-all-start = ((f16[4,912,384]{2,1,0:T(8,128)(2,1)}), f16[4,912,384]{2,1,0:T(8,128)(2,1)S(1)}, u32[]{:S(2)}, u32[]{:S(2)}) async-start(f16[4,912,384]{2,1,0:T(8,128)(2,1)} %select_convert_fusion), calls=%async_computation | async-start | bytes 5603328 | tf_op jit(solution)/shard_map/all_to_all | solution.py:442
  127.3 37.6 %collective-permute-start.11 = (f16[128,384]{1,0:T(8,128)(2,1)S(1)}, f16[128,384]{1,0:T(8,128)(2,1)}, u32[]{:S(2)}, u32[]{:S(2)}) collective-permute-start(f16[128,384]{1,0:T(8,128)(2,1)S(1)} %get-tuple-element.115), channel_id=1, source_target_pairs={{0,1},{1,2},{2,3},{3,0},{4,5},{5,6},{6,7},{7,4},{8,9},{9,10},{10,1... | collective-permute-start | bytes 294920 | tf_op jit(solution)/shard_map/ppermute | solution.py:331
  130.0 34.9 %collective-permute-start.12 = (f16[128,384]{1,0:T(8,128)(2,1)S(1)}, f16[128,384]{1,0:T(8,128)(2,1)}, u32[]{:S(2)}, u32[]{:S(2)}) collective-permute-start(f16[128,384]{1,0:T(8,128)(2,1)S(1)} %get-tuple-element.114), channel_id=1, source_target_pairs={{0,2},{1,3},{2,0},{3,1},{4,6},{5,7},{6,4},{7,5},{8,10},{9,11},{10,... | collective-permute-start | bytes 294920 | tf_op jit(solution)/shard_map/ppermute | solution.py:331
  132.8 32.2 %collective-permute-start.13 = (f16[128,384]{1,0:T(8,128)(2,1)S(1)}, f16[128,384]{1,0:T(8,128)(2,1)}, u32[]{:S(2)}, u32[]{:S(2)}) collective-permute-start(f16[128,384]{1,0:T(8,128)(2,1)S(1)} %get-tuple-element.113), channel_id=1, source_target_pairs={{0,3},{1,0},{2,1},{3,2},{4,7},{5,4},{6,5},{7,6},{8,11},{9,8},{10,9... | collective-permute-start | bytes 294920 | tf_op jit(solution)/shard_map/ppermute | solution.py:331
  161.4 15.0 %all-to-all-start.1 = ((f32[8,54,384]{2,1,0:T(8,128)}), f32[8,54,384]{2,1,0:T(8,128)S(1)}, u32[]{:S(2)}, u32[]{:S(2)}) async-start(f32[8,54,384]{2,1,0:T(8,128)} %reshape.44), calls=%async_computation.1 | async-start | bytes 1376256 | tf_op jit(solution)/shard_map/all_to_all | solution.py:451
  165.7 17.2 %collective-permute-start.14 = (f16[240,384]{1,0:T(8,128)(2,1)S(1)}, f16[240,384]{1,0:T(8,128)(2,1)S(1)}, u32[]{:S(2)}, u32[]{:S(2)}) collective-permute-start(f16[240,384]{1,0:T(8,128)(2,1)S(1)} %get-tuple-element.108), channel_id=1, source_target_pairs={{0,1},{1,2},{2,3},{3,0},{4,5},{5,6},{6,7},{7,4},{8,9},{9,10},{10,1... | collective-permute-start | bytes 552968 | tf_op jit(solution)/shard_map/ppermute | solution.py:331
  168.2 15.4 %collective-permute-start.15 = (f16[240,384]{1,0:T(8,128)(2,1)S(1)}, f16[240,384]{1,0:T(8,128)(2,1)S(1)}, u32[]{:S(2)}, u32[]{:S(2)}) collective-permute-start(f16[240,384]{1,0:T(8,128)(2,1)S(1)} %get-tuple-element.107), channel_id=1, source_target_pairs={{0,2},{1,3},{2,0},{3,1},{4,6},{5,7},{6,4},{7,5},{8,10},{9,11},{10,... | collective-permute-start | bytes 552968 | tf_op jit(solution)/shard_map/ppermute | solution.py:331
  171.0 12.7 %collective-permute-start.16 = (f16[240,384]{1,0:T(8,128)(2,1)S(1)}, f16[240,384]{1,0:T(8,128)(2,1)S(1)}, u32[]{:S(2)}, u32[]{:S(2)}) collective-permute-start(f16[240,384]{1,0:T(8,128)(2,1)S(1)} %get-tuple-element.106), channel_id=1, source_target_pairs={{0,3},{1,0},{2,1},{3,2},{4,7},{5,4},{6,5},{7,6},{8,11},{9,8},{10,9... | collective-permute-start | bytes 552968 | tf_op jit(solution)/shard_map/ppermute | solution.py:331
  177.1 18.3 %all-to-all-start.2 = ((f32[4,54,384]{2,1,0:T(8,128)}), f32[4,54,384]{2,1,0:T(8,128)S(1)}, u32[]{:S(2)}, u32[]{:S(2)}) async-start(f32[4,54,384]{2,1,0:T(8,128)} %broadcast_in_dim.87), calls=%async_computation.2 | async-start | bytes 688128 | tf_op jit(solution)/shard_map/all_to_all | solution.py:458
  185.1 16.6 %collective-permute-start.17 = (f16[352,384]{1,0:T(8,128)(2,1)S(1)}, f16[352,384]{1,0:T(8,128)(2,1)S(1)}, u32[]{:S(2)}, u32[]{:S(2)}) collective-permute-start(f16[352,384]{1,0:T(8,128)(2,1)S(1)} %fusion.5), channel_id=1, source_target_pairs={{0,3},{1,0},{2,1},{3,2},{4,7},{5,4},{6,5},{7,6},{8,11},{9,8},{10,9... | collective-permute-start | bytes 811016 | tf_op jit(solution)/shard_map/ppermute | solution.py:331
  194.8 23.2 %collective-permute-start.18 = (f16[352,384]{1,0:T(8,128)(2,1)S(1)}, f16[352,384]{1,0:T(8,128)(2,1)S(1)}, u32[]{:S(2)}, u32[]{:S(2)}) collective-permute-start(f16[352,384]{1,0:T(8,128)(2,1)S(1)} %fusion.5), channel_id=1, source_target_pairs={{0,2},{1,3},{2,0},{3,1},{4,6},{5,7},{6,4},{7,5},{8,10},{9,11},{10,... | collective-permute-start | bytes 811016 | tf_op jit(solution)/shard_map/ppermute | solution.py:331
  194.8 23.2 %collective-permute-start.19 = (f16[352,384]{1,0:T(8,128)(2,1)S(1)}, f16[352,384]{1,0:T(8,128)(2,1)S(1)}, u32[]{:S(2)}, u32[]{:S(2)}) collective-permute-start(f16[352,384]{1,0:T(8,128)(2,1)S(1)} %fusion.5), channel_id=1, source_target_pairs={{0,1},{1,2},{2,3},{3,0},{4,5},{5,6},{6,7},{7,4},{8,9},{9,10},{10,1... | collective-permute-start | bytes 811016 | tf_op jit(solution)/shard_map/ppermute | solution.py:331
  196.4 28.0 %all-to-all-start.3 = ((f32[8,54,384]{2,1,0:T(8,128)}), f32[8,54,384]{2,1,0:T(8,128)S(1)}, u32[]{:S(2)}, u32[]{:S(2)}) async-start(f32[8,54,384]{2,1,0:T(8,128)} %broadcast_in_dim.90), calls=%async_computation.3 | async-start | bytes 1376256 | tf_op jit(solution)/shard_map/all_to_all | solution.py:463
  220.7 4.6 %copy-start.1 = (bf16[1,8,8,32,16]{3,4,2,1,0:T(8,128)(2,1)S(1)}, bf16[1,8,8,32,16]{3,4,2,1,0:T(8,128)(2,1)}, u32[]{:S(2)}) copy-start(bf16[1,8,8,32,16]{3,4,2,1,0:T(8,128)(2,1)} %param.5) | copy-start | bytes 196612
  (14 other events, 21.6 us)
Sparse Core Ops, SparseCore 0:
  10.5 50.2 all-gather.1

commit v12 on v9

--- a/solution.py
+++ b/solution.py
@@ -193,27 +193,34 @@
     )(cells, wide, thin, teacher)
 
 
-def grad_kernel(order_ref, *refs, units):
-    own_ref, out_ref = refs[-2:]
-    g_refs = refs[-4:-2]
+def grad_kernel(order_ref, *refs, units, apart):
+    out_ref = refs[-1]
+    g_refs = refs[-4:-2] if apart else refs[-3:-1]
     at_once = out_ref.shape[0]
     rows = refs[0].shape[0]
-    spare = own_ref.shape[0] - units * rows
-    zero = jnp.zeros((spare, own_ref.shape[1]), F32)
+    zero = jnp.zeros((out_ref.shape[1] - units * rows, out_ref.shape[2]), F32)
     for i in range(at_once):
+        totals = []
         for k in range(units):
             at = 2 * (i * units + k)
             total = contract(refs[at][...], g_refs[0][...], ((1,), (0,)))
             total += contract(refs[at + 1][...], g_refs[1][...], ((1,), (0,)))
-            out_ref[i, k * rows : (k + 1) * rows, :] = total
-        out_ref[i, units * rows :, :] = zero
-
-    @pl.when(pl.program_id(0) == 0)
-    def _():
-        own_ref[...] = out_ref[0]
-
-
-def grad_chunk(order, taps, g, first, units):
+            totals.append(total)
+        block = jnp.concatenate(totals + [zero], axis=0)
+        if apart:
+            @pl.when(pl.program_id(0) == 0)
+            def _():
+                refs[-2][...] = block
+
+            @pl.when(pl.program_id(0) > 0)
+            def _():
+                out_ref[0] = block
+
+        else:
+            out_ref[i] = block
+
+
+def grad_chunk(order, taps, g, first, units, apart):
     blocks = order.shape[0]
     total, count = taps[0].shape
     chans = g[0].shape[1]
@@ -228,21 +235,20 @@
             tap_specs += [spec, spec]
     whole = pl.BlockSpec((count, chans), lambda s, order: (0, 0))
     size = padded(rows * units)
+    out_specs = [pl.BlockSpec((at_once, size, chans), lambda s, order: (jnp.maximum(s - apart, 0), 0, 0))]
+    out_shape = [jax.ShapeDtypeStruct((blocks - apart, size, chans), F32)]
+    if apart:
+        out_specs = [pl.BlockSpec((size, chans), lambda s, order: (0, 0))] + out_specs
+        out_shape = [jax.ShapeDtypeStruct((size, chans), F32)] + out_shape
     return pl.pallas_call(
-        lambda *refs: grad_kernel(*refs, units=units),
+        lambda *refs: grad_kernel(*refs, units=units, apart=apart),
         grid_spec=pltpu.PrefetchScalarGridSpec(
             num_scalar_prefetch=1,
             grid=(blocks // at_once,),
             in_specs=tap_specs + [whole, whole],
-            out_specs=[
-                pl.BlockSpec((size, chans), lambda s, order: (0, 0)),
-                pl.BlockSpec((at_once, size, chans), lambda s, order: (s, 0, 0)),
-            ],
+            out_specs=out_specs,
         ),
-        out_shape=[
-            jax.ShapeDtypeStruct((size, chans), F32),
-            jax.ShapeDtypeStruct((blocks, size, chans), F32),
-        ],
+        out_shape=out_shape,
         compiler_params=pltpu.CompilerParams(vmem_limit_bytes=VMEM),
         name="grad",
     )(order, *(list(taps) * 2), *g)
@@ -313,7 +319,7 @@
 
 def across_plane(part, rows, bound, after):
     clips = lax.axis_size("clip")
-    payloads = [packed(part[q], rows, bound) for q in range(1, clips // 2)]
+    payloads = [packed(part[q - 1], rows, bound) for q in range(1, clips // 2)]
     payloads, after = lax.optimization_barrier((payloads, after))
     got = []
     for q in range(1, clips // 2):
@@ -432,10 +438,10 @@
     in_rows = patch_t.shape[0]
 
     chips = jnp.arange(clips // 2, dtype=jnp.int32)
-    own_a, part = grad_chunk(me ^ (2 * chips), both, (g, pair_g), 0, 2)
+    own_a, part = grad_chunk(me ^ (2 * chips), both, (g, pair_g), 0, 2, 1)
     part, later = lax.optimization_barrier((part, later))
     got_a, g = across_plane(part, 2 * third, bound, g)
-    _, part = grad_chunk(2 * chips + me % 2, both, (g, pair_g), 2, 1)
+    (part,) = grad_chunk(2 * chips + me % 2, both, (g, pair_g), 2, 1, 0)
     payload = packed(part, third, bound)
     payload, g = lax.optimization_barrier((payload, g))
     groups = [[2 * p + core for p in range(clips // 2)] for core in range(2)]

time: 224 us -> 225 us (level)
    unnamed x44 -> x48, local copies, waits for them, and re-layouts: 11 us -> 10.7 us
  transfers between devices with their start and end apart: 25 -> 25, of which waited for: 9 -> 8; matrix products, arithmetic and copies ran while one was open for 17% -> 16% of each run, Pallas kernels for 28% -> 28%
where the time goes in v12:
time: 225 us; the launch traced here: 223 us
  Pallas kernels  78.9 us (35%)
  starting transfers between devices  50.3 us (22%)
  waiting for transfers between devices  29.4 us (13%)
  local copies, waits for them, and re-layouts  27.8 us (12%)
  other arithmetic  19.4 us (9%)
  between operations  17.7 us (8%)
    pallas_call x2, Pallas kernels, grad_chunk(): pl.pallas_call(lambda *refs: grad_kernel(*refs, units=units, apart=apart)...  22.3 us
    pallas_call x2, Pallas kernels, front(): pl.pallas_call(lambda *refs: front_kernel(*refs, rows=rows, cols=cols, fi...  22.2 us
    ppermute x9, starting transfers between devices, around(): lax.ppermute(blocks, 'tm', [(i, (i + distance) % depth) for i in range(de...  18.6 us
    pallas_call x1, Pallas kernels, back(): pl.pallas_call(lambda *refs: back_kernel(*refs, rows=rows, cols=cols), gr...  17.5 us
    ppermute x9, waiting for transfers between devices, around(): lax.ppermute(blocks, 'tm', [(i, (i + distance) % depth) for i in range(de...  17.4 us
    pallas_call x1, Pallas kernels, middle(): pl.pallas_call(lambda *refs: middle_kernel(*refs, scale=scale), grid=(3,)...  16.8 us
    unnamed x48, local copies, waits for them, and re-layouts  10.7 us
    convert_element_type x5, other arithmetic, packed(): return jnp.where(row < rows, x * jnp.exp2(14.0 - power), power).astype(F16)  10.3 us
  transfers between devices with their start and end apart: 25, of which 8 were waited for; matrix products, arithmetic and copies ran while one was open for 16% of the time, Pallas kernels for 28%

profile of v12, /device:TPU:0, one launch (start us, length us, event | category | flops | bytes accessed | tf_op | source)
XLA Modules:
  0.0 223.4 jit_solution(5638883498860078014)
XLA Ops:
  7.2 2.0 slice.139
  10.3 3.0 %collective-permute-start.1 = (bf16[1296,128]{1,0:T(8,128)(2,1)S(1)}, bf16[1296,128]{1,0:T(8,128)(2,1)S(1)}, u32[]{:S(2)}, u32[]{:S(2)}) collective-permute-start(bf16[1296,128]{1,0:T(8,128)(2,1)S(1)} %slice.140), channel_id=1, source_target_pairs={{0,8},{4,12},{8,0},{12,4},{16,24},{20,28},{24,16},{28,20},{1,9},{5... | collective-permute-start | bytes 995336 | tf_op jit(solution)/shard_map/ppermute | solution.py:410
  13.3 1.5 collective-permute-start.2
  16.0 3.9 %collective-permute-start = (bf16[16,512]{1,0:T(8,128)(2,1)S(1)}, bf16[16,512]{1,0:T(8,128)(2,1)S(1)}, u32[]{:S(2)}, u32[]{:S(2)}) collective-permute-start(bf16[16,512]{1,0:T(8,128)(2,1)S(1)} %slice.184), channel_id=1, source_target_pairs={{0,1},{1,2},{2,3},{4,5},{5,6},{6,7},{8,9},{9,10},{10,11},{12,13},{... | collective-permute-start | bytes 49160 | tf_op jit(solution)/shard_map/ppermute | solution.py:19
  22.0 12.2 %front.2 = (bf16[432,1024]{1,0:T(8,128)(2,1)}, f32[1024,384]{1,0:T(8,128)}, bf16[3,10,10,16,384]{4,3,2,1,0:T(8,128)(2,1)}, bf16[27,384,1024]{2,1,0:T(8,128)(2,1)}, f32[384,128]{1,0:T(8,128)}) custom-call(bf16[16,1536]{1,0:T(8,128)(2,1)} %pad_maximum_fusion.refs_0_, bf16[432,384]{1,0:T(8,128)(2,1)} %refs_1_.3), custom_call_target="tpu_custom_call" | custom-call | tf_op jit(solution)/shard_map/front/pallas_call | solution.py:126
  40.7 1.6 collective-permute-done.5.refs_0_
  42.9 10.0 %front.3 = (bf16[27,384,1024]{2,1,0:T(8,128)(2,1)}, f32[384,128]{1,0:T(8,128)}) custom-call(bf16[16,1536]{1,0:T(8,128)(2,1)} %copy-done.18, bf16[432,384]{1,0:T(8,128)(2,1)} %refs_1_.3), custom_call_target="tpu_custom_call" | custom-call | tf_op jit(solution)/shard_map/front/pallas_call | solution.py:126
  52.8 1.6 reduce_max.19
  60.7 1.4 copy-done.2
  62.2 16.8 %middle.1 = (bf16[1040,384]{1,0:T(8,128)(2,1)}, bf16[256,384]{1,0:T(8,128)(2,1)}) custom-call(bf16[3,10,10,16,384]{4,3,2,1,0:T(8,128)(2,1)} %get-tuple-element.57.refs_0_, bf16[27,384,256]{2,1,0:T(8,128)(2,1)} %bitcast.49, bf16[27,384,128]{2,1,0:T(8,128)(2,1)} %bitcast.47, bf16[1024,384]{1,0:T(8,128)(2,1)} %bitcast.51), custom_call_target="tpu_custom_call" | custom-call | tf_op jit(solution)/shard_map/middle/pallas_call | solution.py:173
  80.0 1.5 collective-permute-start.7
  86.4 13.7 %grad.2 = (f32[912,384]{1,0:T(8,128)}, f32[3,912,384]{2,1,0:T(8,128)}) custom-call(s32[4]{0:T(128)} %fusion.18.refs_0_, bf16[10368,1024]{1,0:T(8,128)(2,1)} %bitcast.39, bf16[10368,1024]{1,0:T(8,128)(2,1)} %bitcast.43, bf16[10368,1024]{1,0:T(8,128)(2,1)} %bitcast.40, bf16[10368,1024]{1,0:T(8,128)(2,1)} %bitcast.44, ...), custom_call_target="tpu_custom_call" | custom-call | tf_op jit(solution)/shard_map/grad/pallas_call | solution.py:243
  100.2 4.2 %fusion = (f16[912,384]{1,0:T(8,128)(2,1)}, f16[912,384]{1,0:T(8,128)(2,1)}, f16[912,384]{1,0:T(8,128)(2,1)}) fusion(f32[3,912,384]{2,1,0:T(8,128)} %get-tuple-element.64, f32[]{:T(128)} %bitcast.11, f32[]{:T(128)} %bitcast.9, pred[912]{0:T(1024)(128)(4,1)S(1)} %iota_compare_fusion.1), kind=kLoop, calls=%fused_computation.2 | loop fusion | flops 3151872 | bytes 6304664 | tf_op jit(solution)/shard_map/convert_element_type | solution.py:317
  104.3 2.5 %collective-permute-start.10 = (f16[912,384]{1,0:T(8,128)(2,1)}, f16[912,384]{1,0:T(8,128)(2,1)S(1)}, u32[]{:S(2)}, u32[]{:S(2)}) collective-permute-start(f16[912,384]{1,0:T(8,128)(2,1)} %get-tuple-element.69), channel_id=1, source_target_pairs={{0,24},{4,28},{8,16},{12,20},{16,8},{20,12},{24,0},{28,4},{1,25},{... | collective-permute-start | bytes 2101256 | tf_op jit(solution)/shard_map/ppermute | solution.py:327
  108.3 8.6 %grad.3 = f32[4,464,384]{2,1,0:T(8,128)} custom-call(s32[4]{0:T(128)} %fusion.17.refs_0_, bf16[10368,1024]{1,0:T(8,128)(2,1)} %bitcast.41, bf16[10368,1024]{1,0:T(8,128)(2,1)} %bitcast.45, bf16[10368,1024]{1,0:T(8,128)(2,1)} %bitcast.42, bf16[10368,1024]{1,0:T(8,128)(2,1)} %bitcast.46, bf16[1040,384]{1,0:T(8,128)(2,1)} %get-tuple-element.71.refs_5_.refs_0_, ...), custom_call_target="tpu_custom_call" | custom-call | tf_op jit(solution)/shard_map/grad/pallas_call | solution.py:243
  116.8 3.3 %select_convert_fusion = f16[4,464,384]{2,1,0:T(8,128)(2,1)} fusion(f32[4,464,384]{2,1,0:T(8,128)} %grad.3, f32[]{:T(128)} %bitcast.11, f32[]{:T(128)} %bitcast.9, pred[464]{0:T(512)(128)(4,1)S(1)} %iota_compare_fusion.2), kind=kLoop, calls=%fused_computation | loop fusion | flops 2138112 | bytes 4276696 | tf_op jit(solution)/shard_map/convert_element_type | solution.py:317
  120.2 3.5 %all-to-all-start = ((f16[4,464,384]{2,1,0:T(8,128)(2,1)}), f16[4,464,384]{2,1,0:T(8,128)(2,1)S(1)}, u32[]{:S(2)}, u32[]{:S(2)}) async-start(f16[4,464,384]{2,1,0:T(8,128)(2,1)} %select_convert_fusion), calls=%async_computation | async-start | bytes 2850816 | tf_op jit(solution)/shard_map/all_to_all | solution.py:448
  123.8 17.5 %back.1 = f32[432,384]{1,0:T(8,128)} custom-call(bf16[1040,384]{1,0:T(8,128)(2,1)} %get-tuple-element.71.refs_5_.refs_0_, bf16[256,384]{1,0:T(8,128)(2,1)} %copy-done.17, bf16[27,384,256]{2,1,0:T(8,128)(2,1)} %bitcast.50, bf16[27,384,128]{2,1,0:T(8,128)(2,1)} %bitcast.48, f32[1024,384]{1,0:T(8,128)} %get-tuple-element.73.refs_4_, ...), custom_call_target="tpu_custom_call" | custom-call | tf_op jit(solution)/shard_map/back/pallas_call | solution.py:292
  142.2 2.4 %select_convert_fusion.1 = (f16[240,384]{1,0:T(8,128)(2,1)S(1)}, f16[240,384]{1,0:T(8,128)(2,1)}, f16[240,384]{1,0:T(8,128)(2,1)}) fusion(f32[912,384]{1,0:T(8,128)S(1)} %copy-done.6, s32[]{:T(128)S(6)} %select_n.259, f16[912,384]{1,0:T(8,128)(2,1)S(1)} %collective-permute-done.10, f16[912,384]{1,0:T(8,128)(2,1)} %collective-permute-done.9, ...), kind=kLoop, calls=%fused_computation.20 | loop fusion | flops 3317760 | bytes 3325692 | tf_op jit(solution)/shard_map/convert_element_type | solution.py:317
  144.6 2.7 %collective-permute-start.11 = (f16[240,384]{1,0:T(8,128)(2,1)}, f16[240,384]{1,0:T(8,128)(2,1)}, u32[]{:S(2)}, u32[]{:S(2)}) collective-permute-start(f16[240,384]{1,0:T(8,128)(2,1)} %get-tuple-element.102), channel_id=1, source_target_pairs={{0,1},{1,2},{2,3},{3,0},{4,5},{5,6},{6,7},{7,4},{8,9},{9,10},{10,1... | collective-permute-start | bytes 552968 | tf_op jit(solution)/shard_map/ppermute | solution.py:337
  147.2 2.8 %collective-permute-start.12 = (f16[240,384]{1,0:T(8,128)(2,1)}, f16[240,384]{1,0:T(8,128)(2,1)}, u32[]{:S(2)}, u32[]{:S(2)}) collective-permute-start(f16[240,384]{1,0:T(8,128)(2,1)} %get-tuple-element.101), channel_id=1, source_target_pairs={{0,2},{1,3},{2,0},{3,1},{4,6},{5,7},{6,4},{7,5},{8,10},{9,11},{10,... | collective-permute-start | bytes 552968 | tf_op jit(solution)/shard_map/ppermute | solution.py:337
  151.2 2.2 all-to-all-done
  155.7 3.9 %all-to-all-start.1 = ((f32[8,54,384]{2,1,0:T(8,128)}), f32[8,54,384]{2,1,0:T(8,128)S(1)}, u32[]{:S(2)}, u32[]{:S(2)}) async-start(f32[8,54,384]{2,1,0:T(8,128)} %reshape.44), calls=%async_computation.1 | async-start | bytes 1376256 | tf_op jit(solution)/shard_map/all_to_all | solution.py:457
  159.6 2.2 collective-permute-done.12
  162.6 1.6 fusion.6
  164.2 4.5 %collective-permute-start.14 = (f16[128,384]{1,0:T(8,128)(2,1)S(1)}, f16[128,384]{1,0:T(8,128)(2,1)S(1)}, u32[]{:S(2)}, u32[]{:S(2)}) collective-permute-start(f16[128,384]{1,0:T(8,128)(2,1)S(1)} %get-tuple-element.105), channel_id=1, source_target_pairs={{0,1},{1,2},{2,3},{3,0},{4,5},{5,6},{6,7},{7,4},{8,9},{9,10},{10,1... | collective-permute-start | bytes 294920 | tf_op jit(solution)/shard_map/ppermute | solution.py:337
  168.7 1.5 collective-permute-start.15
  171.9 6.0 %all-to-all-start.2 = ((f32[4,54,384]{2,1,0:T(8,128)}), f32[4,54,384]{2,1,0:T(8,128)S(1)}, u32[]{:S(2)}, u32[]{:S(2)}) async-start(f32[4,54,384]{2,1,0:T(8,128)} %broadcast_in_dim.87), calls=%async_computation.2 | async-start | bytes 688128 | tf_op jit(solution)/shard_map/all_to_all | solution.py:464
  179.1 3.9 %collective-permute-start.17 = (f16[352,384]{1,0:T(8,128)(2,1)S(1)}, f16[352,384]{1,0:T(8,128)(2,1)S(1)}, u32[]{:S(2)}, u32[]{:S(2)}) collective-permute-start(f16[352,384]{1,0:T(8,128)(2,1)S(1)} %fusion.5), channel_id=1, source_target_pairs={{0,3},{1,0},{2,1},{3,2},{4,7},{5,4},{6,5},{7,6},{8,11},{9,8},{10,9... | collective-permute-start | bytes 811016 | tf_op jit(solution)/shard_map/ppermute | solution.py:337
  184.1 5.5 %all-to-all-done.2 = f32[4,54,384]{2,1,0:T(8,128)S(1)} async-done(((f32[4,54,384]{2,1,0:T(8,128)}), f32[4,54,384]{2,1,0:T(8,128)S(1)}, u32[]{:S(2)}, u32[]{:S(2)}) %all-to-all-start.2) | async-done | bytes 331808 | tf_op jit(solution)/shard_map/all_to_all | solution.py:464
  190.6 3.5 %all-to-all-start.3 = ((f32[8,54,384]{2,1,0:T(8,128)}), f32[8,54,384]{2,1,0:T(8,128)S(1)}, u32[]{:S(2)}, u32[]{:S(2)}) async-start(f32[8,54,384]{2,1,0:T(8,128)} %broadcast_in_dim.90), calls=%async_computation.3 | async-start | bytes 1376256 | tf_op jit(solution)/shard_map/all_to_all | solution.py:469
  194.1 15.1 %collective-permute-done.18 = f16[352,384]{1,0:T(8,128)(2,1)S(1)} collective-permute-done((f16[352,384]{1,0:T(8,128)(2,1)S(1)}, f16[352,384]{1,0:T(8,128)(2,1)S(1)}, u32[]{:S(2)}, u32[]{:S(2)}) %collective-permute-start.18) | collective-permute-done | bytes 270368 | tf_op jit(solution)/shard_map/ppermute | solution.py:337
  (126 shorter events, 39.0 us)
Async XLA Ops:
  7.2 8.3 %copy-start = (bf16[1,8,8,32,16]{3,4,2,1,0:T(8,128)(2,1)S(1)}, bf16[1,8,8,32,16]{3,4,2,1,0:T(8,128)(2,1)}, u32[]{:S(2)}) copy-start(bf16[1,8,8,32,16]{3,4,2,1,0:T(8,128)(2,1)} %param.5) | copy-start | bytes 196612
  7.2 53.6 %all-gather.2.cloned.1.call-start = ((), (), s32[]{:S(2)}) async-start(), calls=%async_computation.4 | async-start | bytes 5971968 | tf_op jit(solution)/shard_map/all_gather | solution.py:406
  10.3 25.2 %copy-start.11 = (bf16[1296,128]{1,0:T(8,128)(2,1)}, bf16[1296,128]{1,0:T(8,128)(2,1)S(1)}, u32[]{:S(2)}) copy-start(bf16[1296,128]{1,0:T(8,128)(2,1)S(1)} %slice.140) | copy-start | bytes 995332
  10.3 24.0 %collective-permute-start.1 = (bf16[1296,128]{1,0:T(8,128)(2,1)S(1)}, bf16[1296,128]{1,0:T(8,128)(2,1)S(1)}, u32[]{:S(2)}, u32[]{:S(2)}) collective-permute-start(bf16[1296,128]{1,0:T(8,128)(2,1)S(1)} %slice.140), channel_id=1, source_target_pairs={{0,8},{4,12},{8,0},{12,4},{16,24},{20,28},{24,16},{28,20},{1,9},{5... | collective-permute-start | bytes 995336 | tf_op jit(solution)/shard_map/ppermute | solution.py:410
  13.3 21.0 %collective-permute-start.2 = (bf16[1296,128]{1,0:T(8,128)(2,1)S(1)}, bf16[1296,128]{1,0:T(8,128)(2,1)S(1)}, u32[]{:S(2)}, u32[]{:S(2)}) collective-permute-start(bf16[1296,128]{1,0:T(8,128)(2,1)S(1)} %slice.140), channel_id=1, source_target_pairs={{0,16},{4,20},{8,24},{12,28},{16,0},{20,4},{24,8},{28,12},{1,17},{... | collective-permute-start | bytes 995336 | tf_op jit(solution)/shard_map/ppermute | solution.py:410
  14.8 20.7 %collective-permute-start.3 = (bf16[1296,128]{1,0:T(8,128)(2,1)S(1)}, bf16[1296,128]{1,0:T(8,128)(2,1)S(1)}, u32[]{:S(2)}, u32[]{:S(2)}) collective-permute-start(bf16[1296,128]{1,0:T(8,128)(2,1)S(1)} %slice.140), channel_id=1, source_target_pairs={{0,24},{4,28},{8,16},{12,20},{16,8},{20,12},{24,0},{28,4},{1,25},{... | collective-permute-start | bytes 995336 | tf_op jit(solution)/shard_map/ppermute | solution.py:410
  16.0 5.4 %collective-permute-start = (bf16[16,512]{1,0:T(8,128)(2,1)S(1)}, bf16[16,512]{1,0:T(8,128)(2,1)S(1)}, u32[]{:S(2)}, u32[]{:S(2)}) collective-permute-start(bf16[16,512]{1,0:T(8,128)(2,1)S(1)} %slice.184), channel_id=1, source_target_pairs={{0,1},{1,2},{2,3},{4,5},{5,6},{6,7},{8,9},{9,10},{10,11},{12,13},{... | collective-permute-start | bytes 49160 | tf_op jit(solution)/shard_map/ppermute | solution.py:19
  39.5 14.9 %collective-permute-start.4 = (bf16[5184,128]{1,0:T(8,128)(2,1)}, bf16[5184,128]{1,0:T(8,128)(2,1)}, u32[]{:S(2)}, u32[]{:S(2)}) collective-permute-start(bf16[5184,128]{1,0:T(8,128)(2,1)} %constant_dynamic-update-slice_fusion), channel_id=1, source_target_pairs={{0,4},{4,0},{8,12},{12,8},{16,20},{20,16},{24,28},{28,24},{1,5},{5... | collective-permute-start | bytes 3981320 | tf_op jit(solution)/shard_map/ppermute | solution.py:23
  39.5 2.8 %collective-permute-start.5 = (bf16[16,1536]{1,0:T(8,128)(2,1)S(1)}, bf16[16,1536]{1,0:T(8,128)(2,1)S(1)}, u32[]{:S(2)}, u32[]{:S(2)}) collective-permute-start(bf16[16,1536]{1,0:T(8,128)(2,1)S(1)} %copy-done.15), channel_id=1, source_target_pairs={{0,4},{4,0},{8,12},{12,8},{16,20},{20,16},{24,28},{28,24},{1,5},{5... | collective-permute-start | bytes 147464 | tf_op jit(solution)/shard_map/ppermute | solution.py:23
  79.0 5.5 %collective-permute-start.6 = (bf16[1040,384]{1,0:T(8,128)(2,1)}, bf16[1040,384]{1,0:T(8,128)(2,1)S(1)}, u32[]{:S(2)}, u32[]{:S(2)}) collective-permute-start(bf16[1040,384]{1,0:T(8,128)(2,1)} %get-tuple-element.71.refs_5_.refs_0_), channel_id=1, source_target_pairs={{0,4},{4,0},{8,12},{12,8},{16,20},{20,16},{24,28},{28,24},{1,5},{5... | collective-permute-start | bytes 2396168 | tf_op jit(solution)/shard_map/ppermute | solution.py:23
  80.0 20.2 %collective-permute-start.7 = (bf16[256,384]{1,0:T(8,128)(2,1)}, bf16[256,384]{1,0:T(8,128)(2,1)S(1)}, u32[]{:S(2)}, u32[]{:S(2)}) collective-permute-start(bf16[256,384]{1,0:T(8,128)(2,1)} %get-tuple-element.63), channel_id=1, source_target_pairs={{1,0},{2,1},{3,2},{5,4},{6,5},{7,6},{9,8},{10,9},{11,10},{13,12},{... | collective-permute-start | bytes 589832 | tf_op jit(solution)/shard_map/ppermute | solution.py:19
  104.3 37.0 %collective-permute-start.10 = (f16[912,384]{1,0:T(8,128)(2,1)}, f16[912,384]{1,0:T(8,128)(2,1)S(1)}, u32[]{:S(2)}, u32[]{:S(2)}) collective-permute-start(f16[912,384]{1,0:T(8,128)(2,1)} %get-tuple-element.69), channel_id=1, source_target_pairs={{0,24},{4,28},{8,16},{12,20},{16,8},{20,12},{24,0},{28,4},{1,25},{... | collective-permute-start | bytes 2101256 | tf_op jit(solution)/shard_map/ppermute | solution.py:327
  106.8 34.5 %collective-permute-start.8 = (f16[912,384]{1,0:T(8,128)(2,1)}, f16[912,384]{1,0:T(8,128)(2,1)S(1)}, u32[]{:S(2)}, u32[]{:S(2)}) collective-permute-start(f16[912,384]{1,0:T(8,128)(2,1)} %get-tuple-element.67), channel_id=1, source_target_pairs={{0,8},{4,12},{8,0},{12,4},{16,24},{20,28},{24,16},{28,20},{1,9},{5... | collective-permute-start | bytes 2101256 | tf_op jit(solution)/shard_map/ppermute | solution.py:327
  107.1 34.3 %collective-permute-start.9 = (f16[912,384]{1,0:T(8,128)(2,1)}, f16[912,384]{1,0:T(8,128)(2,1)}, u32[]{:S(2)}, u32[]{:S(2)}) collective-permute-start(f16[912,384]{1,0:T(8,128)(2,1)} %get-tuple-element.68), channel_id=1, source_target_pairs={{0,16},{4,20},{8,24},{12,28},{16,0},{20,4},{24,8},{28,12},{1,17},{... | collective-permute-start | bytes 2101256 | tf_op jit(solution)/shard_map/ppermute | solution.py:327
  120.2 33.3 %all-to-all-start = ((f16[4,464,384]{2,1,0:T(8,128)(2,1)}), f16[4,464,384]{2,1,0:T(8,128)(2,1)S(1)}, u32[]{:S(2)}, u32[]{:S(2)}) async-start(f16[4,464,384]{2,1,0:T(8,128)(2,1)} %select_convert_fusion), calls=%async_computation | async-start | bytes 2850816 | tf_op jit(solution)/shard_map/all_to_all | solution.py:448
  123.8 18.4 %copy-start.6 = (f32[912,384]{1,0:T(8,128)S(1)}, f32[912,384]{1,0:T(8,128)}, u32[]{:S(2)}) copy-start(f32[912,384]{1,0:T(8,128)} %get-tuple-element.61) | copy-start | bytes 4202500
  141.4 9.9 %copy-start.13 = (f16[912,384]{1,0:T(8,128)(2,1)}, f16[912,384]{1,0:T(8,128)(2,1)S(1)}, u32[]{:S(2)}) copy-start(f16[912,384]{1,0:T(8,128)(2,1)S(1)} %collective-permute-done.10) | copy-start | bytes 2101252
  141.4 8.6 %copy-start.14 = (f16[912,384]{1,0:T(8,128)(2,1)}, f16[912,384]{1,0:T(8,128)(2,1)S(1)}, u32[]{:S(2)}) copy-start(f16[912,384]{1,0:T(8,128)(2,1)S(1)} %collective-permute-done.8) | copy-start | bytes 2101252
  144.6 15.0 %collective-permute-start.11 = (f16[240,384]{1,0:T(8,128)(2,1)}, f16[240,384]{1,0:T(8,128)(2,1)}, u32[]{:S(2)}, u32[]{:S(2)}) collective-permute-start(f16[240,384]{1,0:T(8,128)(2,1)} %get-tuple-element.102), channel_id=1, source_target_pairs={{0,1},{1,2},{2,3},{3,0},{4,5},{5,6},{6,7},{7,4},{8,9},{9,10},{10,1... | collective-permute-start | bytes 552968 | tf_op jit(solution)/shard_map/ppermute | solution.py:337
  147.2 14.6 %collective-permute-start.12 = (f16[240,384]{1,0:T(8,128)(2,1)}, f16[240,384]{1,0:T(8,128)(2,1)}, u32[]{:S(2)}, u32[]{:S(2)}) collective-permute-start(f16[240,384]{1,0:T(8,128)(2,1)} %get-tuple-element.101), channel_id=1, source_target_pairs={{0,2},{1,3},{2,0},{3,1},{4,6},{5,7},{6,4},{7,5},{8,10},{9,11},{10,... | collective-permute-start | bytes 552968 | tf_op jit(solution)/shard_map/ppermute | solution.py:337
  150.0 4.8 %copy-start.4 = (f32[432,384]{1,0:T(8,128)S(1)}, f32[432,384]{1,0:T(8,128)}, u32[]{:S(2)}) copy-start(f32[432,384]{1,0:T(8,128)} %back.1) | copy-start | bytes 1990660
  150.0 11.8 %collective-permute-start.13 = (f16[240,384]{1,0:T(8,128)(2,1)S(1)}, f16[240,384]{1,0:T(8,128)(2,1)}, u32[]{:S(2)}, u32[]{:S(2)}) collective-permute-start(f16[240,384]{1,0:T(8,128)(2,1)S(1)} %get-tuple-element.100), channel_id=1, source_target_pairs={{0,3},{1,0},{2,1},{3,2},{4,7},{5,4},{6,5},{7,6},{8,11},{9,8},{10,9... | collective-permute-start | bytes 552968 | tf_op jit(solution)/shard_map/ppermute | solution.py:337
  155.7 15.4 %all-to-all-start.1 = ((f32[8,54,384]{2,1,0:T(8,128)}), f32[8,54,384]{2,1,0:T(8,128)S(1)}, u32[]{:S(2)}, u32[]{:S(2)}) async-start(f32[8,54,384]{2,1,0:T(8,128)} %reshape.44), calls=%async_computation.1 | async-start | bytes 1376256 | tf_op jit(solution)/shard_map/all_to_all | solution.py:457
  164.2 13.8 %collective-permute-start.14 = (f16[128,384]{1,0:T(8,128)(2,1)S(1)}, f16[128,384]{1,0:T(8,128)(2,1)S(1)}, u32[]{:S(2)}, u32[]{:S(2)}) collective-permute-start(f16[128,384]{1,0:T(8,128)(2,1)S(1)} %get-tuple-element.105), channel_id=1, source_target_pairs={{0,1},{1,2},{2,3},{3,0},{4,5},{5,6},{6,7},{7,4},{8,9},{9,10},{10,1... | collective-permute-start | bytes 294920 | tf_op jit(solution)/shard_map/ppermute | solution.py:337
  168.7 9.3 %collective-permute-start.15 = (f16[128,384]{1,0:T(8,128)(2,1)S(1)}, f16[128,384]{1,0:T(8,128)(2,1)S(1)}, u32[]{:S(2)}, u32[]{:S(2)}) collective-permute-start(f16[128,384]{1,0:T(8,128)(2,1)S(1)} %get-tuple-element.104), channel_id=1, source_target_pairs={{0,2},{1,3},{2,0},{3,1},{4,6},{5,7},{6,4},{7,5},{8,10},{9,11},{10,... | collective-permute-start | bytes 294920 | tf_op jit(solution)/shard_map/ppermute | solution.py:337
  170.2 7.8 %collective-permute-start.16 = (f16[128,384]{1,0:T(8,128)(2,1)S(1)}, f16[128,384]{1,0:T(8,128)(2,1)S(1)}, u32[]{:S(2)}, u32[]{:S(2)}) collective-permute-start(f16[128,384]{1,0:T(8,128)(2,1)S(1)} %get-tuple-element.103), channel_id=1, source_target_pairs={{0,3},{1,0},{2,1},{3,2},{4,7},{5,4},{6,5},{7,6},{8,11},{9,8},{10,9... | collective-permute-start | bytes 294920 | tf_op jit(solution)/shard_map/ppermute | solution.py:337
  171.9 17.7 %all-to-all-start.2 = ((f32[4,54,384]{2,1,0:T(8,128)}), f32[4,54,384]{2,1,0:T(8,128)S(1)}, u32[]{:S(2)}, u32[]{:S(2)}) async-start(f32[4,54,384]{2,1,0:T(8,128)} %broadcast_in_dim.87), calls=%async_computation.2 | async-start | bytes 688128 | tf_op jit(solution)/shard_map/all_to_all | solution.py:464
  179.1 15.0 %collective-permute-start.17 = (f16[352,384]{1,0:T(8,128)(2,1)S(1)}, f16[352,384]{1,0:T(8,128)(2,1)S(1)}, u32[]{:S(2)}, u32[]{:S(2)}) collective-permute-start(f16[352,384]{1,0:T(8,128)(2,1)S(1)} %fusion.5), channel_id=1, source_target_pairs={{0,3},{1,0},{2,1},{3,2},{4,7},{5,4},{6,5},{7,6},{8,11},{9,8},{10,9... | collective-permute-start | bytes 811016 | tf_op jit(solution)/shard_map/ppermute | solution.py:337
  183.0 26.3 %collective-permute-start.18 = (f16[352,384]{1,0:T(8,128)(2,1)S(1)}, f16[352,384]{1,0:T(8,128)(2,1)S(1)}, u32[]{:S(2)}, u32[]{:S(2)}) collective-permute-start(f16[352,384]{1,0:T(8,128)(2,1)S(1)} %fusion.5), channel_id=1, source_target_pairs={{0,2},{1,3},{2,0},{3,1},{4,6},{5,7},{6,4},{7,5},{8,10},{9,11},{10,... | collective-permute-start | bytes 811016 | tf_op jit(solution)/shard_map/ppermute | solution.py:337
  183.0 26.3 %collective-permute-start.19 = (f16[352,384]{1,0:T(8,128)(2,1)S(1)}, f16[352,384]{1,0:T(8,128)(2,1)S(1)}, u32[]{:S(2)}, u32[]{:S(2)}) collective-permute-start(f16[352,384]{1,0:T(8,128)(2,1)S(1)} %fusion.5), channel_id=1, source_target_pairs={{0,1},{1,2},{2,3},{3,0},{4,5},{5,6},{6,7},{7,4},{8,9},{9,10},{10,1... | collective-permute-start | bytes 811016 | tf_op jit(solution)/shard_map/ppermute | solution.py:337
  190.6 25.1 %all-to-all-start.3 = ((f32[8,54,384]{2,1,0:T(8,128)}), f32[8,54,384]{2,1,0:T(8,128)S(1)}, u32[]{:S(2)}, u32[]{:S(2)}) async-start(f32[8,54,384]{2,1,0:T(8,128)} %broadcast_in_dim.90), calls=%async_computation.3 | async-start | bytes 1376256 | tf_op jit(solution)/shard_map/all_to_all | solution.py:469
  210.7 5.9 %copy-start.1 = (bf16[1,8,8,32,16]{3,4,2,1,0:T(8,128)(2,1)S(1)}, bf16[1,8,8,32,16]{3,4,2,1,0:T(8,128)(2,1)}, u32[]{:S(2)}) copy-start(bf16[1,8,8,32,16]{3,4,2,1,0:T(8,128)(2,1)} %param.5) | copy-start | bytes 196612
  (12 other events, 23.2 us)
Sparse Core Ops, SparseCore 0:
  10.5 50.2 all-gather.1
